TPU v7x, 32 devices: a whole 2x2x4 slice. The times are simulated.
32 devices in a mesh: sim: 8 (over y, x, core), ana: 4 (over z).
Axes of the slice: x: 2, y: 2, z: 4, core: 2. Of those that a mesh axis runs over, the one named last changes fastest.
Arguments:
- initial_disp: float32 [256, 512, 128], P('ana', 'sim'), may hold values from -24 to 24
- initial_vel: float32 [256, 512, 128], P('ana', 'sim'), may hold values from -2 to 2
- stiffness: float32 [512, 128], P('sim'), may hold values from 0.05 to 0.35
- basis: float32 [512, 128, 512], P(('sim', 'ana')), may hold values from -5 to 5
- rotation: float32 [768, 512], replicated, may hold values from -0.21875 to 0.21875
Outputs:
- basis_out: float32 [512, 128, 512], P(('sim', 'ana'))
- coords: float32 [512, 256], replicated
All inputs are finite; a program needn't handle non-finite values.
Results may differ from a plain program's by a relative error of at most 0.000054.
Values sent between devices are 32-bit elements; how exact they have to be, the bound alone decides.
No kernel may reach another device: no remote copies, remote signals or barrier semaphores. Data moves between devices by JAX's collectives and lax.ppermute only.
A program may use at most 64 MiB of HBM per device.

v0:
```python
import math

import jax
import jax.numpy as jnp
from jax import lax
from jax.sharding import PartitionSpec as P

M = 256
K = 512
STEPS = 4


epsilon = 1e-06


def with_halo(value, sides, width):
    for axis, dim in sides:
        size, length = (lax.axis_size(axis), value.shape[dim])
        up = [(i, (i + 1) % size) for i in range(size - 1)]
        down = [(j, i) for i, j in up]
        last = lax.slice_in_dim(value, length - width, length, axis=dim)
        initial = lax.slice_in_dim(value, 0, width, axis=dim)
        before = lax.ppermute(last, axis, up)
        after = lax.ppermute(initial, axis, down)
        value = jnp.concatenate([before, value, after], axis=dim)
    return value


def accelerate(displace, stiffness):
    padded = with_halo(displace, (("sim", 1),), 1)
    padded = jnp.pad(padded, ((0, 0), (0, 0), (1, 1)))
    laplace = (
        padded[:, 2:, 1:-1]
        + padded[:, :-2, 1:-1]
        + padded[:, 1:-1, 2:]
        + padded[:, 1:-1, :-2]
        - 4.0 * displace
    )
    return stiffness[None] * (
        laplace - 0.5 * displace * displace * displace / (1.0 + displace * displace)
    )


def contract(left, right, left_dim, right_dim):
    return lax.dot_general(
        left,
        right,
        (((left_dim,), (right_dim,)), ((), ())),
        precision=lax.Precision.HIGHEST,
        preferred_element_type=jnp.float32,
    )


def per_device(initial_disp, initial_vel, stiffness, basis, rotation):
    displace = initial_disp
    velocity = initial_vel
    for step_index in range(STEPS):
        velocity = velocity + accelerate(displace, stiffness)
        displace = displace + velocity
    row_count = basis.shape[0] * basis.shape[1] * lax.axis_size("sim") * lax.axis_size("ana")
    basis_rows = basis.reshape(-1, K)
    totals = lax.psum(jnp.sum(displace * displace, axis=(1, 2)), "sim")
    member_scale = jnp.sqrt(totals / row_count + epsilon)
    outgoing = displace / member_scale[:, None, None]
    arrived = lax.all_to_all(outgoing, "ana", split_axis=1, concat_axis=0, tiled=True)
    unscaled = arrived.reshape(M, -1)
    coefficients = lax.psum(contract(basis_rows, unscaled, 0, 1), ("sim", "ana")) / row_count
    remainder = unscaled - contract(coefficients, basis_rows, 0, 1)
    gram_matrix = lax.psum(contract(remainder, remainder, 1, 1), ("sim", "ana")) / row_count
    factor = jnp.linalg.cholesky(gram_matrix)
    fresh_basis = jax.scipy.linalg.solve_triangular(factor, remainder, lower=True)
    top_rows = rotation[:K]
    bottom_rows = rotation[K:]
    basis_out = contract(basis_rows, top_rows, 1, 0) + contract(fresh_basis, bottom_rows, 0, 0)
    coords = (
        contract(top_rows, coefficients, 0, 0) + contract(bottom_rows, factor, 0, 1)
    ) * math.sqrt(K)
    return (basis_out.reshape(basis.shape), coords)


def solution(mesh):
    in_specs = (
        P("ana", "sim", None),
        P("ana", "sim", None),
        P("sim", None),
        P(("sim", "ana"), None, None),
        P(),
    )
    out_specs = (P(("sim", "ana"), None, None), P())
    return jax.shard_map(
        per_device, mesh=mesh, in_specs=in_specs, out_specs=out_specs, check_vma=False
    )
```

profile of v0, /device:TPU:0, one launch (start us, length us, event | category | flops | bytes accessed | tf_op | source)
XLA Modules:
  0.0 476.7 jit_solution(9723111592130537525)
XLA Ops:
  7.2 2.8 copy.23
  10.0 1.3 collective-permute-start
  11.4 3.3 collective-permute-start.1
  14.7 0.8 collective-permute-done.1
  15.5 1.2 select_maximum_fusion.6
  16.7 5.5 %copy_add_fusion = (f32[64,64,128]{2,0,1:T(8,128)S(1)}, f32[64,64,128]{2,0,1:T(8,128)S(1)}) fusion(f32[64,64,128]{2,1,0:T(8,128)S(1)} %copy-done.3, f32[64,64,128]{2,0,1:T(8,128)S(1)} %copy.23, f32[64,66,130]{2,0,1:T(8,128)S(1)} %select_maximum_fusion.6, f32[64,1,128]{2,0,1:T(8,128)S(1)} %collective-permute-done.1, ...), kind=kLoop, calls=%fused_computation.118 | loop fusion | flops 8912896 | bytes 14778368 | tf_op jit(solution)/shard_map/add | solution.py:59
  22.2 1.3 collective-permute-start.2
  23.5 5.3 %collective-permute-start.3 = (f32[64,1,128]{2,0,1:T(8,128)S(1)}, f32[64,1,128]{2,0,1:T(8,128)S(1)}, u32[]{:S(2)}, u32[]{:S(2)}) collective-permute-start(f32[64,1,128]{2,0,1:T(8,128)S(1)} %get-tuple-element.36), channel_id=1, source_target_pairs={{0,4},{4,8},{8,12},{12,16},{16,20},{20,24},{24,28},{1,5},{5,9},{9,... | collective-permute-start | bytes 98312 | tf_op jit(solution)/shard_map/ppermute | solution.py:23
  28.8 0.8 collective-permute-done.3
  29.6 1.2 select_maximum_fusion.4
  30.8 1.9 fusion.67
  32.7 1.3 collective-permute-start.4
  34.0 5.0 %collective-permute-start.5 = (f32[64,1,128]{2,0,1:T(8,128)S(1)}, f32[64,1,128]{2,0,1:T(8,128)S(1)}, u32[]{:S(2)}, u32[]{:S(2)}) collective-permute-start(f32[64,1,128]{2,0,1:T(8,128)S(1)} %get-tuple-element.34), channel_id=1, source_target_pairs={{0,4},{4,8},{8,12},{12,16},{16,20},{20,24},{24,28},{1,5},{5,9},{9,... | collective-permute-start | bytes 98312 | tf_op jit(solution)/shard_map/ppermute | solution.py:23
  39.1 0.8 collective-permute-done.5
  39.9 1.2 select_maximum_fusion.2
  41.1 1.8 fusion.65
  42.9 1.3 collective-permute-start.6
  44.2 5.0 %collective-permute-start.7 = (f32[64,1,128]{2,0,1:T(8,128)S(1)}, f32[64,1,128]{2,0,1:T(8,128)S(1)}, u32[]{:S(2)}, u32[]{:S(2)}) collective-permute-start(f32[64,1,128]{2,0,1:T(8,128)S(1)} %get-tuple-element.32), channel_id=1, source_target_pairs={{0,4},{4,8},{8,12},{12,16},{16,20},{20,24},{24,28},{1,5},{5,9},{9,... | collective-permute-start | bytes 98312 | tf_op jit(solution)/shard_map/ppermute | solution.py:23
  49.3 0.8 collective-permute-done.7
  50.1 1.2 select_maximum_fusion
  51.3 2.0 multiply_reduce_fusion
  53.3 17.2 %psum.21 = f32[64]{0:T(128)S(1)} all-reduce(f32[64]{0:T(128)S(1)} %get-tuple-element.22), channel_id=1, replica_groups=mesh['sim'=8,'ana'=4] {'sim'}, use_global_device_ids=true, to_apply=%region_1.2 | all-reduce | flops 64 | bytes 512 | tf_op jit(solution)/shard_map/psum | solution.py:62
  70.8 53.3 %all_to_all.15 = f32[64,64,128]{2,0,1:T(8,128)S(1)} all-to-all(f32[64,64,128]{2,0,1:T(8,128)S(1)} %broadcast_divide_fusion), channel_id=1, replica_groups=mesh['sim'=8,'ana'=4] {'ana'}, dimensions={1} | all-to-all | bytes 4194304 | tf_op jit(solution)/shard_map/all_to_all | solution.py:65
  124.1 1.2 copy.24
  125.4 1.3 copy-done.2
  126.7 4.9 %fusion.34 = f32[512,256]{0,1:T(8,128)} fusion(f32[2048,512]{1,0:T(8,128)S(1)} %bitcast.54, f32[32,8,16,128]{3,2,1,0:T(8,128)S(1)} %bitcast.55), kind=kOutput, calls=%fused_computation.71 | convolution fusion | flops 3221225472 | bytes 6815744 | tf_op jit(solution)/shard_map/dot_general | solution.py:45
  131.6 128.3 %all-reduce.8.cloned.1.call-done = f32[512,256]{0,1:T(8,128)} async-done(((f32[512,256]{0,1:T(8,128)}), f32[512,256]{0,1:T(8,128)}) %all-reduce.8.cloned.1.call-update) | async-done | bytes 524304 | tf_op jit(solution)/shard_map/psum | solution.py:67
  260.0 7.1 %convolution_subtract_fusion = f32[256,2048]{1,0:T(8,128)S(1)} fusion(f32[2048,512]{1,0:T(8,128)} %bitcast.52, f32[32,8,16,128]{3,2,1,0:T(8,128)} %bitcast.56, f32[512,256]{0,1:T(8,128)} %all-reduce.8.cloned.1.call-done), kind=kOutput, calls=%fused_computation.18 | convolution fusion | flops 3221880832 | bytes 8912896 | tf_op jit(solution)/shard_map/dot_general | solution.py:45
  267.0 2.6 fusion.75
  269.6 18.5 %fusion.40 = f32[2048,512]{1,0:T(8,128)} fusion(f32[2048,512]{1,0:T(8,128)} %bitcast.53, f32[768,512]{1,0:T(8,128)} %param.9), kind=kOutput, calls=%fused_computation.77 | convolution fusion | flops 6442450944 | bytes 9437184 | tf_op jit(solution)/shard_map/dot_general | solution.py:45
  288.2 105.5 %all-reduce.10.cloned.1.call-done = f32[256,256]{0,1:T(8,128)} async-done(((f32[256,256]{0,1:T(8,128)}), f32[256,256]{0,1:T(8,128)}) %all-reduce.10.cloned.1.call-update) | async-done | bytes 262160 | tf_op jit(solution)/shard_map/psum | solution.py:69
  393.7 1.0 broadcast_multiply_fusion
  394.9 1.0 fusion.47
  395.9 11.7 %cholesky.50 = f32[128,128]{1,0:T(8,128)S(1)} custom-call(f32[128,128]{1,0:T(8,128)S(1)} %cholesky.118), custom_call_target="Cholesky" | custom-call | tf_op jit(solution)/shard_map/jit(cholesky)/cholesky | solution.py:70
  407.7 9.8 %custom-call.15 = f32[1,128,128]{1,2,0:T(8,128)S(1)} custom-call(f32[1,128,128]{2,1,0:T(8,128)S(1)} %get-tuple-element.43), custom_call_target="InvertDiagBlocksLowerTriangular" | custom-call | tf_op jit(solution)/shard_map/jit(cholesky)/cholesky | solution.py:70
  418.0 11.7 %cholesky.105 = f32[128,128]{1,0:T(8,128)S(1)} custom-call(f32[128,128]{1,0:T(8,128)S(1)} %convolution_subtract_fusion.2), custom_call_target="Cholesky" | custom-call | tf_op jit(solution)/shard_map/jit(cholesky)/cholesky | solution.py:70
  431.8 1.8 fusion.42
  433.6 0.7 fusion.50
  434.3 1.1 fusion.33
  435.4 1.0 copy.27
  436.4 4.0 while.1
  437.2 1.3 bitcast_dynamic-update-slice_fusion.2
  439.1 1.3 bitcast_dynamic-update-slice_fusion.2
  440.4 19.7 %custom-call.16 = f32[2,128,128]{1,2,0:T(8,128)S(1)} custom-call(f32[2,128,128]{2,1,0:T(8,128)S(1)} %get-tuple-element.9), custom_call_target="InvertDiagBlocksLowerTriangular" | custom-call | tf_op jit(solution)/shard_map/jit(_solve_triangular)/triangular_solve | solution.py:71
  460.1 1.1 fusion.37
  461.2 1.0 convolution_subtract_fusion.1
  462.2 1.0 fusion.55
  463.4 6.3 %convolution_add_fusion = f32[2048,512]{1,0:T(8,128)} fusion(f32[2048,512]{1,0:T(8,128)S(1)} %copy-done.1, f32[128,2048]{1,0:T(8,128)S(1)} %fusion.55, f32[128,2048]{1,0:T(8,128)S(1)} %fusion.37, f32[768,512]{1,0:T(8,128)} %param.9), kind=kOutput, calls=%fused_computation.13 | convolution fusion | flops 3222798336 | bytes 11010048 | tf_op jit(solution)/shard_map/dot_general | solution.py:45
  (46 shorter events, 3.3 us)
Async XLA Ops:
  7.2 252.8 %all-reduce.8.cloned.1.call-start = ((), (), s32[]{:S(2)}) async-start(), calls=%async_computation.1 | async-start | bytes 1048576 | tf_op jit(solution)/shard_map/psum | solution.py:67
  10.0 4.6 collective-permute-start
  11.3 5.4 %copy-start.3 = (f32[64,64,128]{2,1,0:T(8,128)S(1)}, f32[64,64,128]{2,1,0:T(8,128)}, u32[]{:S(2)}) copy-start(f32[64,64,128]{2,1,0:T(8,128)} %param.5) | copy-start | bytes 6291460
  11.3 5.4 %copy-start.5 = (f32[64,64,128]{2,1,0:T(8,128)S(1)}, f32[64,64,128]{2,1,0:T(8,128)}, u32[]{:S(2)}) copy-start(f32[64,64,128]{2,1,0:T(8,128)} %param.6) | copy-start | bytes 6291460
  11.4 5.4 %copy-start.8 = (f32[64,128]{1,0:T(8,128)S(1)}, f32[64,128]{1,0:T(8,128)}, u32[]{:S(2)}) copy-start(f32[64,128]{1,0:T(8,128)} %param.7) | copy-start | bytes 98308
  11.4 4.1 collective-permute-start.1
  22.2 6.6 %collective-permute-start.2 = (f32[64,1,128]{2,0,1:T(8,128)S(1)}, f32[64,1,128]{2,0,1:T(8,128)S(1)}, u32[]{:S(2)}, u32[]{:S(2)}) collective-permute-start(f32[64,1,128]{2,0,1:T(8,128)S(1)} %get-tuple-element.37), channel_id=1, source_target_pairs={{4,0},{8,4},{12,8},{16,12},{20,16},{24,20},{28,24},{5,1},{9,5},{13... | collective-permute-start | bytes 98312 | tf_op jit(solution)/shard_map/ppermute | solution.py:24
  23.5 6.1 %collective-permute-start.3 = (f32[64,1,128]{2,0,1:T(8,128)S(1)}, f32[64,1,128]{2,0,1:T(8,128)S(1)}, u32[]{:S(2)}, u32[]{:S(2)}) collective-permute-start(f32[64,1,128]{2,0,1:T(8,128)S(1)} %get-tuple-element.36), channel_id=1, source_target_pairs={{0,4},{4,8},{8,12},{12,16},{16,20},{20,24},{24,28},{1,5},{5,9},{9,... | collective-permute-start | bytes 98312 | tf_op jit(solution)/shard_map/ppermute | solution.py:23
  32.7 6.3 %collective-permute-start.4 = (f32[64,1,128]{2,0,1:T(8,128)S(1)}, f32[64,1,128]{2,0,1:T(8,128)S(1)}, u32[]{:S(2)}, u32[]{:S(2)}) collective-permute-start(f32[64,1,128]{2,0,1:T(8,128)S(1)} %get-tuple-element.35), channel_id=1, source_target_pairs={{4,0},{8,4},{12,8},{16,12},{20,16},{24,20},{28,24},{5,1},{9,5},{13... | collective-permute-start | bytes 98312 | tf_op jit(solution)/shard_map/ppermute | solution.py:24
  34.0 5.9 %collective-permute-start.5 = (f32[64,1,128]{2,0,1:T(8,128)S(1)}, f32[64,1,128]{2,0,1:T(8,128)S(1)}, u32[]{:S(2)}, u32[]{:S(2)}) collective-permute-start(f32[64,1,128]{2,0,1:T(8,128)S(1)} %get-tuple-element.34), channel_id=1, source_target_pairs={{0,4},{4,8},{8,12},{12,16},{16,20},{20,24},{24,28},{1,5},{5,9},{9,... | collective-permute-start | bytes 98312 | tf_op jit(solution)/shard_map/ppermute | solution.py:23
  42.9 6.3 %collective-permute-start.6 = (f32[64,1,128]{2,0,1:T(8,128)S(1)}, f32[64,1,128]{2,0,1:T(8,128)S(1)}, u32[]{:S(2)}, u32[]{:S(2)}) collective-permute-start(f32[64,1,128]{2,0,1:T(8,128)S(1)} %get-tuple-element.33), channel_id=1, source_target_pairs={{4,0},{8,4},{12,8},{16,12},{20,16},{24,20},{28,24},{5,1},{9,5},{13... | collective-permute-start | bytes 98312 | tf_op jit(solution)/shard_map/ppermute | solution.py:24
  44.2 5.9 %collective-permute-start.7 = (f32[64,1,128]{2,0,1:T(8,128)S(1)}, f32[64,1,128]{2,0,1:T(8,128)S(1)}, u32[]{:S(2)}, u32[]{:S(2)}) collective-permute-start(f32[64,1,128]{2,0,1:T(8,128)S(1)} %get-tuple-element.32), channel_id=1, source_target_pairs={{0,4},{4,8},{8,12},{12,16},{16,20},{20,24},{24,28},{1,5},{5,9},{9,... | collective-permute-start | bytes 98312 | tf_op jit(solution)/shard_map/ppermute | solution.py:23
  124.1 2.5 copy-start
  125.3 1.3 copy-start.2
  131.6 262.1 %all-reduce.10.cloned.1.call-start = ((), (), s32[]{:S(2)}) async-start(), calls=%async_computation.2 | async-start | bytes 524288 | tf_op jit(solution)/shard_map/psum | solution.py:69
  394.7 39.6 %copy-start.6 = (f32[512,256]{0,1:T(8,128)S(1)}, f32[512,256]{0,1:T(8,128)}, u32[]{:S(2)}) copy-start(f32[512,256]{0,1:T(8,128)} %all-reduce.8.cloned.1.call-done) | copy-start | bytes 1572868
  431.7 2.6 copy-start.4
  434.3 2.1 copy-start.7
  461.2 2.2 copy-start.1
Sparse Core Ops, SparseCore 0:
  131.7 128.2 all-reduce.7
  269.8 123.9 all-reduce.9
where the time goes:
time: 486 us; the launch traced here: 477 us
  waiting for transfers between devices  237 us (49%)
  other arithmetic  72.6 us (15%)
  blocking collectives  70.5 us (15%)
  matrix products  45.8 us (9%)
  starting transfers between devices  23.8 us (5%)
  between operations  16 us (3%)
  local copies, waits for them, and re-layouts  10.5 us (2%)
    psum x1, waiting for transfers between devices, per_device(): lax.psum(contract(basis_rows, unscaled, 0, 1), ('sim', 'ana')) / row_count  128 us
    psum x1, waiting for transfers between devices, per_device(): lax.psum(contract(remainder, remainder, 1, 1), ('sim', 'ana')) / row_count  106 us
    all_to_all x1, blocking collectives, per_device(): lax.all_to_all(outgoing, 'ana', split_axis=1, concat_axis=0, tiled=True)  53.3 us
    dot_general x7, matrix products, contract(): lax.dot_general(left, right, (((left_dim,), (right_dim,)), ((), ())), pre...  42.2 us
    another operation x6, other arithmetic, per_device(): factor = jnp.linalg.cholesky(gram_matrix)  34 us
    another operation x3, other arithmetic, per_device(): jax.scipy.linalg.solve_triangular(factor, remainder, lower=True)  20.4 us
    ppermute x4, starting transfers between devices, with_halo(): before = lax.ppermute(last, axis, up)  18.6 us
    psum x1, blocking collectives, per_device(): totals = lax.psum(jnp.sum(displace * displace, axis=(1, 2)), 'sim')  17.2 us
  transfers between devices with their start and end apart: 10, of which 6 were waited for; matrix products, arithmetic and copies ran while one was open for 4% of the time, Pallas kernels for 0%

commit v1 on v0

v1 whole, which is shorter than its diff:
```python
import functools
import math

import jax
import jax.numpy as jnp
from jax import lax
from jax.experimental import pallas as pl
from jax.experimental.pallas import tpu as pltpu
from jax.sharding import PartitionSpec as P

STEPS = 4
EPS = 1e-06
MIB = 1024 * 1024
HI = lax.Precision.HIGHEST
SCALARS = pl.BlockSpec(memory_space=pltpu.SMEM)


def mm(left, right, dims, precision=HI):
    return lax.dot_general(left, right, (dims, ((), ())), precision=precision, preferred_element_type=jnp.float32)


def shape(*dims, dtype=jnp.float32):
    return jax.ShapeDtypeStruct(dims, dtype)


def params(mib):
    return pltpu.CompilerParams(vmem_limit_bytes=mib * MIB)


def xor_permute(value, axis, mask):
    size = lax.axis_size(axis)
    return lax.ppermute(value, axis, [(i, i ^ mask) for i in range(size)])


def to_lines_kernel(disp_ref, vel_ref, stiff_ref, disp_out, vel_out, last_ref, first_ref):
    lines, group, _ = disp_out.shape
    for line in range(lines):
        disp_out[line] = disp_ref[pl.ds(line, group, stride=lines), :]
        vel_out[line] = vel_ref[pl.ds(line, group, stride=lines), :]
    w = STEPS
    for ref, start in ((last_ref, lines - w), (first_ref, 0)):
        for i in range(w):
            ref[i] = disp_ref[pl.ds(start + i, group, stride=lines), :]
            ref[w + i] = vel_ref[pl.ds(start + i, group, stride=lines), :]
        ref[2 * w] = jnp.zeros_like(ref[2 * w])
        ref[2 * w, :w, :] = stiff_ref[start:start + w, :]


def to_lines(disp, vel, stiff):
    members, lines, width = disp.shape
    group = 16
    w = STEPS
    flat = pl.BlockSpec((group * lines, width), lambda i: (i, 0))
    out = pl.BlockSpec((lines, group, width), lambda i: (0, i, 0))
    edge = pl.BlockSpec((2 * w + 1, group, width), lambda i: (0, i, 0))
    return pl.pallas_call(
        to_lines_kernel,
        grid=(members // group,),
        in_specs=[flat, flat, pl.BlockSpec((lines, width), lambda i: (0, 0))],
        out_specs=[out, out, edge, edge],
        out_shape=[shape(lines, members, width)] * 2 + [shape(2 * w + 1, members, width)] * 2,
        compiler_params=params(32),
        name="to_lines",
    )(disp.reshape(members * lines, width), vel.reshape(members * lines, width), stiff)


def evolve_kernel(index_ref, disp_ref, vel_ref, stiff_ref, before_ref, after_ref, *rest, masks, size):
    outs, (disp_pad, vel_pad, stiff_pad) = rest[:len(masks)], rest[len(masks):]
    lines, members, width = disp_ref.shape
    w = STEPS
    blocks = lines // size
    lane = lax.broadcasted_iota(jnp.int32, (8, width), 1)
    for mask, out in zip(masks, outs):
        block = index_ref[0] ^ mask
        start = block * size
        disp_pad[w:w + size] = disp_ref[pl.ds(start, size)]
        vel_pad[w:w + size] = vel_ref[pl.ds(start, size)]
        stiff_pad[8:8 + size, :] = stiff_ref[pl.ds(pl.multiple_of(start, 8), size), :]

        @pl.when(block == 0)
        def _():
            disp_pad[:w] = before_ref[:w]
            vel_pad[:w] = before_ref[w:2 * w]
            stiff_pad[8 - w:8, :] = before_ref[2 * w, :w, :]

        @pl.when(block > 0)
        def _():
            low = jnp.maximum(start - w, 0)
            disp_pad[:w] = disp_ref[pl.ds(low, w)]
            vel_pad[:w] = vel_ref[pl.ds(low, w)]
            stiff_pad[:8, :] = stiff_ref[pl.ds(pl.multiple_of(jnp.maximum(start - 8, 0), 8), 8), :]

        @pl.when(block == blocks - 1)
        def _():
            disp_pad[w + size:] = after_ref[:w]
            vel_pad[w + size:] = after_ref[w:2 * w]
            stiff_pad[8 + size:8 + size + w, :] = after_ref[2 * w, :w, :]

        @pl.when(block < blocks - 1)
        def _():
            high = jnp.minimum(start + size, lines - 8)
            disp_pad[w + size:] = disp_ref[pl.ds(high, w)]
            vel_pad[w + size:] = vel_ref[pl.ds(high, w)]
            stiff_pad[8 + size:, :] = stiff_ref[pl.ds(pl.multiple_of(high, 8), 8), :]

        def group_step(g, carry):
            at = pl.ds(pl.multiple_of(g * 8, 8), 8)
            disp = {i: disp_pad[i, at, :] for i in range(size + 2 * w)}
            vel = {i: vel_pad[i, at, :] for i in range(1, size + 2 * w - 1)}
            for step in range(1, w + 1):
                new = {}
                for i in range(step, size + 2 * w - step):
                    u = disp[i]
                    right = jnp.where(lane == width - 1, 0.0, pltpu.roll(u, width - 1, 1))
                    left = jnp.where(lane == 0, 0.0, pltpu.roll(u, 1, 1))
                    laplace = disp[i + 1] + disp[i - 1] + right + left - 4.0 * u
                    square = u * u
                    stiff = jnp.broadcast_to(stiff_pad[8 - w + i:8 - w + i + 1, :], (8, width))
                    vel[i] = vel[i] + stiff * (laplace - 0.5 * u * (square / (1.0 + square)))
                    new[i] = u + vel[i]
                disp = new
            for i in range(size):
                out[i, at, :] = disp[w + i]
            return carry

        lax.fori_loop(0, members // 8, group_step, 0)


def evolve(index, disp, vel, stiff, before, after, masks, size):
    lines, members, width = disp.shape
    w = STEPS
    return pl.pallas_call(
        functools.partial(evolve_kernel, masks=masks, size=size),
        in_specs=[SCALARS] + [pl.BlockSpec(memory_space=pltpu.VMEM)] * 5,
        out_shape=[shape(size, members, width)] * len(masks),
        scratch_shapes=[pltpu.VMEM((size + 2 * w, members, width), jnp.float32)] * 2
        + [pltpu.VMEM((size + 16, width), jnp.float32)],
        compiler_params=params(32),
        name="evolve" + "".join(str(m) for m in masks),
    )(index, disp, vel, stiff, before, after)


def products_kernel(index_ref, basis_ref, *rest):
    pieces, (send_ref, keep_ref, snap_ref, sum_ref) = rest[:-4], rest[-4:]
    lines, members, width = pieces[0].shape
    rank = basis_ref.shape[-1]
    step = pl.program_id(0)
    for k, piece in enumerate(pieces):
        at = pl.multiple_of((index_ref[0] ^ k) * members, members)
        for line in range(lines):
            snap_ref[pl.ds(at, members), line * width:(line + 1) * width] = piece[line]

    @pl.when(step == 0)
    def _():
        sum_ref[...] = jnp.zeros_like(sum_ref)

    snap = snap_ref[...]
    rows = basis_ref[...].reshape(lines * width, rank)
    sum_ref[:, :rank] += mm(snap, rows, ((1,), (0,)))
    sum_ref[:, rank:] += mm(snap, snap, ((1,), (1,)))

    @pl.when(step == pl.num_programs(0) - 1)
    def _():
        half = keep_ref.shape[0]
        core = index_ref[1]
        keep_ref[...] = sum_ref[pl.ds(pl.multiple_of(core * half, half), half), :]
        send_ref[...] = sum_ref[pl.ds(pl.multiple_of((1 - core) * half, half), half), :]


def products(index, basis, pieces):
    lines, width, rank = basis.shape
    members = pieces[0].shape[1]
    total = members * len(pieces)
    block = 2
    half = pl.BlockSpec((total // 2, rank + total), lambda i: (0, 0))
    return pl.pallas_call(
        products_kernel,
        grid=(lines // block,),
        in_specs=[SCALARS, pl.BlockSpec((block, width, rank), lambda i: (i, 0, 0))]
        + [pl.BlockSpec((block, members, width), lambda i: (i, 0, 0))] * len(pieces),
        out_specs=[half, half],
        out_shape=[shape(total // 2, rank + total)] * 2,
        scratch_shapes=[pltpu.VMEM((total, block * width), jnp.float32), pltpu.VMEM((total, rank + total), jnp.float32)],
        compiler_params=params(32),
        name="products",
    )(index, basis, *pieces)


def split_kernel(index_ref, keep_ref, got_ref, *outs):
    rows = outs[0].shape[0]
    for k, out in enumerate(outs):
        at = pl.ds(pl.multiple_of((index_ref[2] ^ k) * rows, rows), rows)
        out[...] = keep_ref[at, :] + got_ref[at, :]


def split(index, keep, got, chips):
    rows, cols = keep.shape
    return pl.pallas_call(
        split_kernel,
        in_specs=[SCALARS] + [pl.BlockSpec(memory_space=pltpu.VMEM)] * 2,
        out_shape=[shape(rows // chips, cols)] * chips,
        compiler_params=params(16),
        name="split",
    )(index, keep, got)


def tree_sum(values):
    while len(values) > 1:
        values = [a + b for a, b in zip(values[::2], values[1::2])]
    return values[0]


def chip_scatter(index, send, keep):
    chips = lax.axis_size("sim") // 2
    got = xor_permute(send, "sim", 1)
    pieces = split(index, keep, got, chips)
    return tree_sum([pieces[0]] + [xor_permute(pieces[k], "sim", 2 * k) for k in range(1, chips)])


def ana_sum(value):
    return tree_sum([value] + [xor_permute(value, "ana", k) for k in range(1, lax.axis_size("ana"))])


def chip_gather(value):
    chips = lax.axis_size("sim") // 2
    mine = jnp.concatenate([value] + [xor_permute(value, "sim", 2 * k) for k in range(1, chips)], axis=0)
    return mine, xor_permute(mine, "sim", 1)


PANEL = 32

def eliminate(work_ref, members):
    tiles = work_ref.shape[1] // 128
    groups = PANEL // 8
    sub = lax.broadcasted_iota(jnp.int32, (8, 128), 0)

    def panel_step(k, carry):
        start = pl.multiple_of(k * PANEL, PANEL)
        at = pl.multiple_of((k * PANEL) // 128 * 128, 128)
        diag = work_ref[pl.ds(start, PANEL), pl.ds(at, 128)]
        diag = pltpu.roll(diag, (128 - (k * PANEL) % 128) % 128, 1)
        rows = work_ref[pl.ds(start, PANEL), :]
        x = [[rows[8 * g:8 * g + 8, 128 * t:128 * t + 128] for t in range(tiles)] + [diag[8 * g:8 * g + 8]]
             for g in range(groups)]
        for b in range(groups):
            cols = {g: [jnp.broadcast_to(x[g][tiles][:, 8 * b + j:8 * b + j + 1], (8, 128)) for j in range(8)]
                    for g in range(b, groups)}
            pivots = jnp.ones((8, 128), jnp.float32)
            for r in range(8):
                pivot = jnp.broadcast_to(cols[b][r][r:r + 1], (8, 128))
                pivots = jnp.where(sub == r, pivot, pivots)
                inverse = 1.0 / pivot
                raw = [jnp.broadcast_to(v[r:r + 1], (8, 128)) for v in x[b]]
                craw = [jnp.broadcast_to(cols[b][j][r:r + 1], (8, 128)) if j > r else None for j in range(8)]
                for g in range(b, groups):
                    coef = cols[g][r] * inverse
                    if g == b:
                        coef = jnp.where(sub > r, coef, 0.0)
                    x[g] = [v - coef * w for v, w in zip(x[g], raw)]
                    cols[g] = [cols[g][j] - coef * craw[j] if j > r else cols[g][j] for j in range(8)]
            x[b] = [v * lax.rsqrt(pivots) for v in x[b]]
        done = jnp.concatenate([jnp.concatenate(v[:tiles], axis=1) for v in x], axis=0)
        lane = lax.broadcasted_iota(jnp.int32, (PANEL, members), 1)
        lower = jnp.where(lane >= start + PANEL, done[:, :members], 0.0)
        work_ref[...] = work_ref[...] - mm(lower, done, ((0,), (0,)))
        work_ref[pl.ds(start, PANEL), :] = done
        return carry

    lax.fori_loop(0, members // PANEL, panel_step, 0)


def ordered(index_ref, mine_ref, other_ref, out_ref, chips):
    half = mine_ref.shape[0]
    rows = half // chips
    for k in range(chips):
        at = (index_ref[2] ^ k) * rows
        piece = slice(k * rows, (k + 1) * rows)
        out_ref[pl.ds(pl.multiple_of(index_ref[1] * half + at, rows), rows), :] = mine_ref[piece, :]
        out_ref[pl.ds(pl.multiple_of((1 - index_ref[1]) * half + at, rows), rows), :] = other_ref[piece, :]


def solve_kernel(index_ref, sums_ref, sums2_ref, gram_ref, gram2_ref, rot_ref, w_ref, coords_ref,
                 work_ref, all_ref, basis_ref, *, count, chips):
    members, rank = coords_ref.shape
    ordered(index_ref, sums_ref, sums2_ref, all_ref, chips)
    ordered(index_ref, gram_ref, gram2_ref, basis_ref, chips)
    row = lax.broadcasted_iota(jnp.int32, (members, members), 0)
    col = lax.broadcasted_iota(jnp.int32, (members, members), 1)
    eye = row == col
    inner = all_ref[:, rank:]
    diag = jnp.where(eye, inner, 0.0)
    across = lax.rsqrt(jnp.sum(diag, axis=0, keepdims=True) / count + EPS)
    along = lax.rsqrt(jnp.sum(diag, axis=1, keepdims=True) / count + EPS)
    coef = all_ref[:, :rank] * (along / count)
    correct = 2.0 * coef - mm(coef, basis_ref[...], ((1,), (0,))) / count
    work_ref[:, :members] = inner * (along / count) * across - mm(correct, coef, ((1,), (1,)))
    work_ref[:, members:] = jnp.where(eye, 1.0, 0.0)
    eliminate(work_ref, members)
    top, bottom = rot_ref[:rank, :], rot_ref[rank:, :]
    upper = jnp.where(row <= col, work_ref[:, :members], 0.0)
    mix = mm(work_ref[:, members:], bottom, ((0,), (0,)))
    w_ref[:rank, :] = top - mm(coef, mix, ((0,), (0,)))
    w_ref[rank:, :] = mix * along
    coords_ref[...] = (mm(coef, top, ((1,), (0,))) + mm(upper, bottom, ((0,), (0,)))) * math.sqrt(rank)


def solve(index, sums, gram, rotation, count, chips):
    rank = gram[0].shape[1]
    members = rotation.shape[0] - rank
    return pl.pallas_call(
        functools.partial(solve_kernel, count=float(count), chips=chips),
        in_specs=[SCALARS] + [pl.BlockSpec(memory_space=pltpu.VMEM)] * 5,
        out_shape=(shape(members + rank, rank), shape(members, rank)),
        scratch_shapes=[pltpu.VMEM((members, 2 * members), jnp.float32),
                        pltpu.VMEM((members, rank + members), jnp.float32),
                        pltpu.VMEM((rank, rank), jnp.float32)],
        compiler_params=params(40),
        name="solve",
    )(index, *sums, *gram, rotation)


def rotate_kernel(index_ref, weights_ref, basis_ref, *rest):
    pieces, (out_ref, snap_ref) = rest[:-2], rest[-2:]
    lines, members, width = pieces[0].shape
    rank = basis_ref.shape[-1]
    for k, piece in enumerate(pieces):
        at = pl.multiple_of((index_ref[0] ^ k) * members, members)
        for line in range(lines):
            snap_ref[pl.ds(at, members), line * width:(line + 1) * width] = piece[line]
    rows = basis_ref[...].reshape(lines * width, rank)
    out = mm(rows, weights_ref[:rank, :], ((1,), (0,))) + mm(snap_ref[...], weights_ref[rank:, :], ((0,), (0,)))
    out_ref[...] = out.reshape(out_ref.shape)


def rotate(index, weights, basis, pieces):
    lines, width, rank = basis.shape
    members = pieces[0].shape[1]
    block = 2
    rows = pl.BlockSpec((block, width, rank), lambda i: (i, 0, 0))
    return pl.pallas_call(
        rotate_kernel,
        grid=(lines // block,),
        in_specs=[SCALARS, pl.BlockSpec(weights.shape, lambda i: (0, 0)), rows]
        + [pl.BlockSpec((block, members, width), lambda i: (i, 0, 0))] * len(pieces),
        out_specs=rows,
        out_shape=shape(lines, width, rank),
        scratch_shapes=[pltpu.VMEM((members * len(pieces), block * width), jnp.float32)],
        compiler_params=params(32),
        name="rotate",
    )(index, weights, basis, *pieces)


def per_device(initial_disp, initial_vel, stiffness, basis, rotation):
    ranks, sims = lax.axis_size("ana"), lax.axis_size("sim")
    ana, sim = lax.axis_index("ana"), lax.axis_index("sim")
    lines, width, rank = basis.shape
    count = lines * width * sims * ranks
    chips = sims // 2
    core = sim % 2
    index = jnp.stack([ana, core, sim // 2]).astype(jnp.int32)

    disp, vel, last, first = to_lines(initial_disp, initial_vel, stiffness)
    up = [(i, i + 1) for i in range(sims - 1)]
    before = lax.ppermute(last, "sim", up)
    after = lax.ppermute(first, "sim", [(j, i) for i, j in up])

    rows = basis.reshape(lines * width, rank)
    gram = mm(rows, rows, ((0,), (0,)))
    half = rank // 2
    keep = lax.dynamic_slice_in_dim(gram, core * half, half, axis=0)
    send = lax.dynamic_slice_in_dim(gram, (1 - core) * half, half, axis=0)
    gram = chip_scatter(index, send, keep)

    far = tuple(range(ranks // 2, ranks))
    near = tuple(range(ranks // 2))
    pieces = {}
    for masks in (far, near):
        found = evolve(index, disp, vel, stiffness, before, after, masks, lines)
        for mask, piece in zip(masks, found):
            pieces[mask] = xor_permute(piece, "ana", mask) if mask else piece
    pieces = [pieces[k] for k in range(ranks)]

    send, keep = products(index, basis, pieces)
    sums = chip_gather(ana_sum(chip_scatter(index, send, keep)))
    gram = chip_gather(ana_sum(gram))
    weights, coords = solve(index, sums, gram, rotation, count, chips)
    return rotate(index, weights, basis, pieces), coords.T


def solution(mesh):
    in_specs = (
        P("ana", "sim", None),
        P("ana", "sim", None),
        P("sim", None),
        P(("sim", "ana"), None, None),
        P(),
    )
    out_specs = (P(("sim", "ana"), None, None), P())
    return jax.shard_map(
        per_device, mesh=mesh, in_specs=in_specs, out_specs=out_specs, check_vma=False
    )
```

time: 486 us -> 171 us (0.35); the launches traced: 477 us -> 171 us
  waiting for transfers between devices: 237 us -> 38.7 us
  other arithmetic: 72.6 us -> 0.26 us
  blocking collectives: 70.5 us -> 0 us
  Pallas kernels: 0 us -> 59 us
  matrix products: 45.8 us -> 7.03 us
  starting transfers between devices: 23.8 us -> 48.1 us
  between operations: 16 us -> 0.84 us
  local copies, waits for them, and re-layouts: 10.5 us -> 16.7 us
    psum x2 -> x0, waiting for transfers between devices: 234 us -> none  [the longest x1 128 us: per_device(): lax.psum(contract(basis_rows, unscaled, 0, 1), ('sim', 'ana')) / row_count]
    pallas_call x0 -> x8, Pallas kernels: none -> 59 us  [the longest x1 17.6 us: solve(): pl.pallas_call(functools.partial(solve_kernel, count=float(count), chips=...]
    another operation x9 -> x1, other arithmetic: 54.4 us -> 0.08 us  [per_device(): index = jnp.stack([ana, core, sim // 2]).astype(jnp.int32)]
    all_to_all x1 -> x0, blocking collectives: 53.3 us -> none  [per_device(): lax.all_to_all(outgoing, 'ana', split_axis=1, concat_axis=0, tiled=True)]
    ppermute x8 -> x27, waiting for transfers between devices: 3.33 us -> 38.7 us  [the longest x25 34.5 us: xor_permute(): return lax.ppermute(value, axis, [(i, i ^ mask) for i in range(size)])]
    dot_general x7 -> x1, matrix products: 42.2 us -> 7.03 us  [mm(): lax.dot_general(left, right, (dims, ((), ())), precision=precision, prefe...]
    ppermute x8 -> x27, starting transfers between devices: 23.7 us -> 48.1 us  [the longest x25 44.4 us: xor_permute(): return lax.ppermute(value, axis, [(i, i ^ mask) for i in range(size)])]
    psum x1 -> x0, blocking collectives: 17.2 us -> none  [per_device(): totals = lax.psum(jnp.sum(displace * displace, axis=(1, 2)), 'sim')]
  transfers between devices with their start and end apart: 10 -> 27, of which waited for: 6 -> 13; matrix products, arithmetic and copies ran while one was open for 4% -> 4% of each run, Pallas kernels for 0% -> 10%
where the time goes in v1:
time: 171 us
  Pallas kernels  59 us (35%)
  starting transfers between devices  48.1 us (28%)
  waiting for transfers between devices  38.7 us (23%)
  local copies, waits for them, and re-layouts  16.7 us (10%)
  matrix products  7.03 us (4%)
    ppermute x25, starting transfers between devices, xor_permute(): return lax.ppermute(value, axis, [(i, i ^ mask) for i in range(size)])  44.4 us
    ppermute x25, waiting for transfers between devices, xor_permute(): return lax.ppermute(value, axis, [(i, i ^ mask) for i in range(size)])  34.5 us
    pallas_call x1, Pallas kernels, solve(): pl.pallas_call(functools.partial(solve_kernel, count=float(count), chips=...  17.6 us
    unnamed x33, local copies, waits for them, and re-layouts  16.6 us
    pallas_call x2, Pallas kernels, evolve(): pl.pallas_call(functools.partial(evolve_kernel, masks=masks, size=size),...  15.9 us
    pallas_call x1, Pallas kernels, rotate(): pl.pallas_call(rotate_kernel, grid=(lines // block,), in_specs=[SCALARS,...  13.9 us
    pallas_call x1, Pallas kernels, products(): pl.pallas_call(products_kernel, grid=(lines // block,), in_specs=[SCALARS...  7.49 us
    dot_general x1, matrix products, mm(): lax.dot_general(left, right, (dims, ((), ())), precision=precision, prefe...  7.03 us
  transfers between devices with their start and end apart: 27, of which 13 were waited for; matrix products, arithmetic and copies ran while one was open for 4% of the time, Pallas kernels for 10%

profile of v1, /device:TPU:0, one launch (start us, length us, event | category | flops | bytes accessed | tf_op | source)
XLA Modules:
  0.0 170.6 jit_solution(11629867613044766860)
XLA Ops:
  0.6 1.6 copy-done.7
  2.2 1.6 copy-done.8
  4.6 3.0 %to_lines.1 = (f32[64,64,128]{2,1,0:T(8,128)S(1)}, f32[64,64,128]{2,1,0:T(8,128)S(1)}, f32[9,64,128]{2,1,0:T(8,128)S(1)}, f32[9,64,128]{2,1,0:T(8,128)S(1)}) custom-call(f32[4096,128]{1,0:T(8,128)S(1)} %bitcast.10, f32[4096,128]{1,0:T(8,128)S(1)} %bitcast.11, f32[64,128]{1,0:T(8,128)S(1)} %copy-done.14), custom_call_target="tpu_custom_call" | custom-call | tf_op jit(solution)/shard_map/to_lines/pallas_call | solution.py:56
  7.6 1.3 copy-done.3
  8.9 2.4 %collective-permute-start = (f32[9,64,128]{2,1,0:T(8,128)S(1)}, f32[9,64,128]{2,1,0:T(8,128)S(1)}, u32[]{:S(2)}, u32[]{:S(2)}) collective-permute-start(f32[9,64,128]{2,1,0:T(8,128)S(1)} %get-tuple-element.24), channel_id=1, source_target_pairs={{0,4},{4,8},{8,12},{12,16},{16,20},{20,24},{24,28},{1,5},{5,9},{9,... | collective-permute-start | bytes 884744 | tf_op jit(solution)/shard_map/ppermute | solution.py:364
  11.3 1.3 collective-permute-start.1
  12.7 4.2 %collective-permute-done.1.after_ref = f32[9,64,128]{2,1,0:T(8,128)S(1)} collective-permute-done((f32[9,64,128]{2,1,0:T(8,128)S(1)}, f32[9,64,128]{2,1,0:T(8,128)S(1)}, u32[]{:S(2)}, u32[]{:S(2)}) %collective-permute-start.1) | collective-permute-done | bytes 294944 | tf_op jit(solution)/shard_map/ppermute | solution.py:365
  16.8 1.7 copy-done.4
  18.5 8.0 %evolve23.1 = (f32[16,64,128]{2,1,0:T(8,128)}, f32[16,64,128]{2,1,0:T(8,128)}) custom-call(s32[3]{0:T(128)S(1)} %pad_add_fusion.index_ref, f32[64,64,128]{2,1,0:T(8,128)S(1)} %get-tuple-element.22.disp_ref, f32[64,64,128]{2,1,0:T(8,128)S(1)} %copy-done.4, f32[64,128]{1,0:T(8,128)S(1)} %copy-done.15, f32[9,64,128]{2,1,0:T(8,128)S(1)} %collective-permute-done.before_ref, ...), custom_call_target="tpu_custom_call" | custom-call | tf_op jit(solution)/shard_map/evolve23/pallas_call | solution.py:132
  26.5 2.6 %collective-permute-start.3 = (f32[16,64,128]{2,1,0:T(8,128)}, f32[16,64,128]{2,1,0:T(8,128)S(1)}, u32[]{:S(2)}, u32[]{:S(2)}) collective-permute-start(f32[16,64,128]{2,1,0:T(8,128)} %get-tuple-element.28), channel_id=1, source_target_pairs={{0,2},{1,3},{2,0},{3,1},{4,6},{5,7},{6,4},{7,5},{8,10},{9,11},{10,... | collective-permute-start | bytes 1572872 | tf_op jit(solution)/shard_map/ppermute | solution.py:32
  29.1 1.3 collective-permute-start.4
  30.4 1.0 copy-done.13
  31.4 7.9 %evolve01.1 = (f32[16,64,128]{2,1,0:T(8,128)S(1)}, f32[16,64,128]{2,1,0:T(8,128)}) custom-call(s32[3]{0:T(128)S(1)} %pad_add_fusion.index_ref, f32[64,64,128]{2,1,0:T(8,128)S(1)} %get-tuple-element.22.disp_ref, f32[64,64,128]{2,1,0:T(8,128)S(1)} %copy-done.4, f32[64,128]{1,0:T(8,128)S(1)} %copy-done.15, f32[9,64,128]{2,1,0:T(8,128)S(1)} %collective-permute-done.before_ref, ...), custom_call_target="tpu_custom_call" | custom-call | tf_op jit(solution)/shard_map/evolve01/pallas_call | solution.py:132
  40.4 7.0 %convolution_bitcast_fusion = f32[512,512]{1,0:T(8,128)S(1)} fusion(f32[16,128,512]{2,1,0:T(8,128)S(1)} %copy-done), kind=kOutput, calls=%fused_computation | convolution fusion | flops 6442450944 | bytes 5242880 | tf_op jit(solution)/shard_map/dot_general | solution.py:19
  47.5 5.0 %collective-permute-start.16 = (f32[256,512]{1,0:T(8,128)S(1)}, f32[256,512]{1,0:T(8,128)S(1)}, u32[]{:S(2)}, u32[]{:S(2)}) collective-permute-start(f32[256,512]{1,0:T(8,128)S(1)} %get-tuple-element.44), channel_id=1, source_target_pairs={{0,4},{4,0},{8,12},{12,8},{16,20},{20,16},{24,28},{28,24},{1,5},{5... | collective-permute-start | bytes 1572872 | tf_op jit(solution)/shard_map/ppermute | solution.py:32
  52.5 11.3 %collective-permute-done.3.rest_2_ = f32[16,64,128]{2,1,0:T(8,128)S(1)} collective-permute-done((f32[16,64,128]{2,1,0:T(8,128)}, f32[16,64,128]{2,1,0:T(8,128)S(1)}, u32[]{:S(2)}, u32[]{:S(2)}) %collective-permute-start.3) | collective-permute-done | bytes 524320 | tf_op jit(solution)/shard_map/ppermute | solution.py:32
  63.8 8.2 %collective-permute-done.2.rest_1_ = f32[16,64,128]{2,1,0:T(8,128)S(1)} collective-permute-done((f32[16,64,128]{2,1,0:T(8,128)}, f32[16,64,128]{2,1,0:T(8,128)S(1)}, u32[]{:S(2)}, u32[]{:S(2)}) %collective-permute-start.2) | collective-permute-done | bytes 524320 | tf_op jit(solution)/shard_map/ppermute | solution.py:32
  72.0 2.2 %copy-done.1 = f32[16,128,512]{2,1,0:T(8,128)S(1)} copy-done((f32[16,128,512]{2,1,0:T(8,128)S(1)}, f32[16,128,512]{2,1,0:T(8,128)}, u32[]{:S(2)}) %copy-start.1) | copy-done | bytes 4194328
  74.2 7.5 %products.1 = (f32[128,768]{1,0:T(8,128)S(1)}, f32[128,768]{1,0:T(8,128)S(1)}) custom-call(s32[3]{0:T(128)S(1)} %pad_add_fusion.index_ref, f32[16,128,512]{2,1,0:T(8,128)S(1)} %copy-done.1, f32[16,64,128]{2,1,0:T(8,128)S(1)} %copy-done.6, f32[16,64,128]{2,1,0:T(8,128)S(1)} %collective-permute-done.2.rest_1_, ...), custom_call_target="tpu_custom_call" | custom-call | tf_op jit(solution)/shard_map/products/pallas_call | solution.py:176
  81.7 1.9 %collective-permute-start.5 = (f32[128,768]{1,0:T(8,128)S(1)}, f32[128,768]{1,0:T(8,128)S(1)}, u32[]{:S(2)}, u32[]{:S(2)}) collective-permute-start(f32[128,768]{1,0:T(8,128)S(1)} %get-tuple-element.31), channel_id=1, source_target_pairs={{0,4},{4,0},{8,12},{12,8},{16,20},{20,16},{24,28},{28,24},{1,5},{5... | collective-permute-start | bytes 1179656 | tf_op jit(solution)/shard_map/ppermute | solution.py:32
  84.2 6.9 %collective-permute-start.17 = (f32[64,512]{1,0:T(8,128)S(1)}, f32[64,512]{1,0:T(8,128)S(1)}, u32[]{:S(2)}, u32[]{:S(2)}) collective-permute-start(f32[64,512]{1,0:T(8,128)S(1)} %get-tuple-element.37), channel_id=1, source_target_pairs={{0,8},{4,12},{8,0},{12,4},{16,24},{20,28},{24,16},{28,20},{1,9},{5... | collective-permute-start | bytes 393224 | tf_op jit(solution)/shard_map/ppermute | solution.py:32
  91.1 0.9 collective-permute-start.18
  92.1 1.4 collective-permute-start.19
  94.1 1.2 collective-permute-start.6
  95.3 0.9 collective-permute-start.7
  96.3 1.5 collective-permute-start.8
  97.7 0.8 collective-permute-done.18
  98.6 2.0 %collective-permute-done.19 = f32[64,512]{1,0:T(8,128)S(1)} collective-permute-done((f32[64,512]{1,0:T(8,128)S(1)}, f32[64,512]{1,0:T(8,128)S(1)}, u32[]{:S(2)}, u32[]{:S(2)}) %collective-permute-start.19) | collective-permute-done | bytes 131104 | tf_op jit(solution)/shard_map/ppermute | solution.py:32
  100.6 3.6 %collective-permute-start.22 = (f32[64,512]{1,0:T(8,128)S(1)}, f32[64,512]{1,0:T(8,128)S(1)}, u32[]{:S(2)}, u32[]{:S(2)}) collective-permute-start(f32[64,512]{1,0:T(8,128)S(1)} %add_add_fusion.1), channel_id=1, source_target_pairs={{0,3},{1,2},{2,1},{3,0},{4,7},{5,6},{6,5},{7,4},{8,11},{9,10},{10,... | collective-permute-start | bytes 393224 | tf_op jit(solution)/shard_map/ppermute | solution.py:32
  104.2 0.9 collective-permute-start.20
  105.1 3.6 %collective-permute-start.11 = (f32[32,768]{1,0:T(8,128)S(1)}, f32[32,768]{1,0:T(8,128)S(1)}, u32[]{:S(2)}, u32[]{:S(2)}) collective-permute-start(f32[32,768]{1,0:T(8,128)S(1)} %add_add_fusion.3), channel_id=1, source_target_pairs={{0,3},{1,2},{2,1},{3,0},{4,7},{5,6},{6,5},{7,4},{8,11},{9,10},{10,... | collective-permute-start | bytes 294920 | tf_op jit(solution)/shard_map/ppermute | solution.py:32
  108.9 6.1 %collective-permute-start.9 = (f32[32,768]{1,0:T(8,128)S(1)}, f32[32,768]{1,0:T(8,128)S(1)}, u32[]{:S(2)}, u32[]{:S(2)}) collective-permute-start(f32[32,768]{1,0:T(8,128)S(1)} %add_add_fusion.3), channel_id=1, source_target_pairs={{0,1},{1,0},{2,3},{3,2},{4,5},{5,4},{6,7},{7,6},{8,9},{9,8},{10,11... | collective-permute-start | bytes 294920 | tf_op jit(solution)/shard_map/ppermute | solution.py:32
  115.0 5.0 %collective-permute-done.21 = f32[64,512]{1,0:T(8,128)S(1)} collective-permute-done((f32[64,512]{1,0:T(8,128)S(1)}, f32[64,512]{1,0:T(8,128)S(1)}, u32[]{:S(2)}, u32[]{:S(2)}) %collective-permute-start.21) | collective-permute-done | bytes 131104 | tf_op jit(solution)/shard_map/ppermute | solution.py:32
  120.0 1.4 collective-permute-start.25
  121.4 2.2 %collective-permute-start.23 = (f32[64,512]{1,0:T(8,128)S(1)}, f32[64,512]{1,0:T(8,128)S(1)}, u32[]{:S(2)}, u32[]{:S(2)}) collective-permute-start(f32[64,512]{1,0:T(8,128)S(1)} %add_add_fusion), channel_id=1, source_target_pairs={{0,8},{4,12},{8,0},{12,4},{16,24},{20,28},{24,16},{28,20},{1,9},{5... | collective-permute-start | bytes 393224 | tf_op jit(solution)/shard_map/ppermute | solution.py:32
  123.6 1.4 collective-permute-start.14
  125.2 0.9 collective-permute-done.25
  126.1 1.1 collective-permute-start.12
  127.2 2.6 %collective-permute-done.24 = f32[64,512]{1,0:T(8,128)S(1)} collective-permute-done((f32[64,512]{1,0:T(8,128)S(1)}, f32[64,512]{1,0:T(8,128)S(1)}, u32[]{:S(2)}, u32[]{:S(2)}) %collective-permute-start.24) | collective-permute-done | bytes 131104 | tf_op jit(solution)/shard_map/ppermute | solution.py:32
  129.9 0.8 collective-permute-done.14
  130.7 0.8 collective-permute-done.13
  131.8 1.6 collective-permute-done.15.sums2_ref
  133.4 17.6 %solve.1 = (f32[768,512]{1,0:T(8,128)S(1)}, f32[256,512]{1,0:T(8,128)S(1)}) custom-call(s32[3]{0:T(128)S(1)} %pad_add_fusion.index_ref, f32[128,768]{1,0:T(8,128)S(1)} %pad_maximum_fusion.1.sums_ref, f32[128,768]{1,0:T(8,128)S(1)} %collective-permute-done.15.sums2_ref, f32[256,512]{1,0:T(8,128)S(1)} %pad_maximum_fusion.gram_ref, ...), custom_call_target="tpu_custom_call" | custom-call | tf_op jit(solution)/shard_map/solve/pallas_call | solution.py:310
  151.0 1.1 copy-done.9
  152.1 1.0 copy.8
  153.1 2.2 %copy-done.2 = f32[16,128,512]{2,1,0:T(8,128)S(1)} copy-done((f32[16,128,512]{2,1,0:T(8,128)S(1)}, f32[16,128,512]{2,1,0:T(8,128)}, u32[]{:S(2)}) %copy-start.2) | copy-done | bytes 4194328
  155.3 1.4 copy-done.10
  156.7 13.9 %rotate.1 = f32[16,128,512]{2,1,0:T(8,128)} custom-call(s32[3]{0:T(128)S(1)} %pad_add_fusion.index_ref, f32[768,512]{1,0:T(8,128)S(1)} %copy-done.10, f32[16,128,512]{2,1,0:T(8,128)S(1)} %copy-done.2, f32[16,64,128]{2,1,0:T(8,128)S(1)} %copy-done.6, f32[16,64,128]{2,1,0:T(8,128)S(1)} %collective-permute-done.2.rest_1_, ...), custom_call_target="tpu_custom_call" | custom-call | tf_op jit(solution)/shard_map/rotate/pallas_call | solution.py:340
  (56 shorter events, 4.0 us)
Async XLA Ops:
  0.6 1.6 copy-start.7
  2.2 1.6 copy-start.8
  3.8 0.8 copy-start.14
  4.6 12.3 %copy-start.15 = (f32[64,128]{1,0:T(8,128)S(1)}, f32[64,128]{1,0:T(8,128)}, u32[]{:S(2)}) copy-start(f32[64,128]{1,0:T(8,128)} %stiff_ref.5) | copy-start | bytes 98308
  7.6 1.3 copy-start.3
  8.9 3.8 %collective-permute-start = (f32[9,64,128]{2,1,0:T(8,128)S(1)}, f32[9,64,128]{2,1,0:T(8,128)S(1)}, u32[]{:S(2)}, u32[]{:S(2)}) collective-permute-start(f32[9,64,128]{2,1,0:T(8,128)S(1)} %get-tuple-element.24), channel_id=1, source_target_pairs={{0,4},{4,8},{8,12},{12,16},{16,20},{20,24},{24,28},{1,5},{5,9},{9,... | collective-permute-start | bytes 884744 | tf_op jit(solution)/shard_map/ppermute | solution.py:364
  11.3 5.6 %collective-permute-start.1 = (f32[9,64,128]{2,1,0:T(8,128)S(1)}, f32[9,64,128]{2,1,0:T(8,128)S(1)}, u32[]{:S(2)}, u32[]{:S(2)}) collective-permute-start(f32[9,64,128]{2,1,0:T(8,128)S(1)} %get-tuple-element.25), channel_id=1, source_target_pairs={{4,0},{8,4},{12,8},{16,12},{20,16},{24,20},{28,24},{5,1},{9,5},{13... | collective-permute-start | bytes 884744 | tf_op jit(solution)/shard_map/ppermute | solution.py:365
  16.8 9.7 %copy-start.12 = (f32[9,64,128]{2,1,0:T(8,128)}, f32[9,64,128]{2,1,0:T(8,128)S(1)}, u32[]{:S(2)}) copy-start(f32[9,64,128]{2,1,0:T(8,128)S(1)} %collective-permute-done.1.after_ref) | copy-start | bytes 884740
  16.8 1.7 copy-start.4
  18.5 21.8 %copy-start = (f32[16,128,512]{2,1,0:T(8,128)S(1)}, f32[16,128,512]{2,1,0:T(8,128)}, u32[]{:S(2)}) copy-start(f32[16,128,512]{2,1,0:T(8,128)} %basis_ref.3) | copy-start | bytes 12582916
  26.5 37.3 %collective-permute-start.3 = (f32[16,64,128]{2,1,0:T(8,128)}, f32[16,64,128]{2,1,0:T(8,128)S(1)}, u32[]{:S(2)}, u32[]{:S(2)}) collective-permute-start(f32[16,64,128]{2,1,0:T(8,128)} %get-tuple-element.28), channel_id=1, source_target_pairs={{0,2},{1,3},{2,0},{3,1},{4,6},{5,7},{6,4},{7,5},{8,10},{9,11},{10,... | collective-permute-start | bytes 1572872 | tf_op jit(solution)/shard_map/ppermute | solution.py:32
  29.1 34.7 %collective-permute-start.4 = (f32[16,64,128]{2,1,0:T(8,128)}, f32[16,64,128]{2,1,0:T(8,128)S(1)}, u32[]{:S(2)}, u32[]{:S(2)}) collective-permute-start(f32[16,64,128]{2,1,0:T(8,128)} %get-tuple-element.29), channel_id=1, source_target_pairs={{0,3},{1,2},{2,1},{3,0},{4,7},{5,6},{6,5},{7,4},{8,11},{9,10},{10,... | collective-permute-start | bytes 1572872 | tf_op jit(solution)/shard_map/ppermute | solution.py:32
  30.4 1.0 copy-start.13
  39.3 0.8 copy-start.5
  40.1 31.9 %copy-start.6 = (f32[16,64,128]{2,1,0:T(8,128)S(1)}, f32[16,64,128]{2,1,0:T(8,128)}, u32[]{:S(2)}) copy-start(f32[16,64,128]{2,1,0:T(8,128)} %copy-done.5) | copy-start | bytes 1572868
  40.1 31.9 %collective-permute-start.2 = (f32[16,64,128]{2,1,0:T(8,128)}, f32[16,64,128]{2,1,0:T(8,128)S(1)}, u32[]{:S(2)}, u32[]{:S(2)}) collective-permute-start(f32[16,64,128]{2,1,0:T(8,128)} %get-tuple-element.27), channel_id=1, source_target_pairs={{0,1},{1,0},{2,3},{3,2},{4,5},{5,4},{6,7},{7,6},{8,9},{9,8},{10,11... | collective-permute-start | bytes 1572872 | tf_op jit(solution)/shard_map/ppermute | solution.py:32
  47.5 36.1 %collective-permute-start.16 = (f32[256,512]{1,0:T(8,128)S(1)}, f32[256,512]{1,0:T(8,128)S(1)}, u32[]{:S(2)}, u32[]{:S(2)}) collective-permute-start(f32[256,512]{1,0:T(8,128)S(1)} %get-tuple-element.44), channel_id=1, source_target_pairs={{0,4},{4,0},{8,12},{12,8},{16,20},{20,16},{24,28},{28,24},{1,5},{5... | collective-permute-start | bytes 1572872 | tf_op jit(solution)/shard_map/ppermute | solution.py:32
  72.0 2.2 %copy-start.1 = (f32[16,128,512]{2,1,0:T(8,128)S(1)}, f32[16,128,512]{2,1,0:T(8,128)}, u32[]{:S(2)}) copy-start(f32[16,128,512]{2,1,0:T(8,128)} %basis_ref.3) | copy-start | bytes 12582916
  81.7 51.7 %copy-start.11 = (f32[768,512]{1,0:T(8,128)S(1)}, f32[768,512]{1,0:T(8,128)}, u32[]{:S(2)}) copy-start(f32[768,512]{1,0:T(8,128)} %rot_ref.1) | copy-start | bytes 4718596
  81.7 11.8 %collective-permute-start.5 = (f32[128,768]{1,0:T(8,128)S(1)}, f32[128,768]{1,0:T(8,128)S(1)}, u32[]{:S(2)}, u32[]{:S(2)}) collective-permute-start(f32[128,768]{1,0:T(8,128)S(1)} %get-tuple-element.31), channel_id=1, source_target_pairs={{0,4},{4,0},{8,12},{12,8},{16,20},{20,16},{24,28},{28,24},{1,5},{5... | collective-permute-start | bytes 1179656 | tf_op jit(solution)/shard_map/ppermute | solution.py:32
  84.2 12.0 %collective-permute-start.17 = (f32[64,512]{1,0:T(8,128)S(1)}, f32[64,512]{1,0:T(8,128)S(1)}, u32[]{:S(2)}, u32[]{:S(2)}) collective-permute-start(f32[64,512]{1,0:T(8,128)S(1)} %get-tuple-element.37), channel_id=1, source_target_pairs={{0,8},{4,12},{8,0},{12,4},{16,24},{20,28},{24,16},{28,20},{1,9},{5... | collective-permute-start | bytes 393224 | tf_op jit(solution)/shard_map/ppermute | solution.py:32
  91.1 7.4 %collective-permute-start.18 = (f32[64,512]{1,0:T(8,128)S(1)}, f32[64,512]{1,0:T(8,128)S(1)}, u32[]{:S(2)}, u32[]{:S(2)}) collective-permute-start(f32[64,512]{1,0:T(8,128)S(1)} %get-tuple-element.38), channel_id=1, source_target_pairs={{0,16},{4,20},{8,24},{12,28},{16,0},{20,4},{24,8},{28,12},{1,17},{... | collective-permute-start | bytes 393224 | tf_op jit(solution)/shard_map/ppermute | solution.py:32
  92.1 8.5 %collective-permute-start.19 = (f32[64,512]{1,0:T(8,128)S(1)}, f32[64,512]{1,0:T(8,128)S(1)}, u32[]{:S(2)}, u32[]{:S(2)}) collective-permute-start(f32[64,512]{1,0:T(8,128)S(1)} %get-tuple-element.39), channel_id=1, source_target_pairs={{0,24},{4,28},{8,16},{12,20},{16,8},{20,12},{24,0},{28,4},{1,25},{... | collective-permute-start | bytes 393224 | tf_op jit(solution)/shard_map/ppermute | solution.py:32
  94.1 10.1 %collective-permute-start.6 = (f32[32,768]{1,0:T(8,128)S(1)}, f32[32,768]{1,0:T(8,128)S(1)}, u32[]{:S(2)}, u32[]{:S(2)}) collective-permute-start(f32[32,768]{1,0:T(8,128)S(1)} %get-tuple-element.33), channel_id=1, source_target_pairs={{0,8},{4,12},{8,0},{12,4},{16,24},{20,28},{24,16},{28,20},{1,9},{5... | collective-permute-start | bytes 294920 | tf_op jit(solution)/shard_map/ppermute | solution.py:32
  95.3 9.8 %collective-permute-start.7 = (f32[32,768]{1,0:T(8,128)S(1)}, f32[32,768]{1,0:T(8,128)S(1)}, u32[]{:S(2)}, u32[]{:S(2)}) collective-permute-start(f32[32,768]{1,0:T(8,128)S(1)} %get-tuple-element.34), channel_id=1, source_target_pairs={{0,16},{4,20},{8,24},{12,28},{16,0},{20,4},{24,8},{28,12},{1,17},{... | collective-permute-start | bytes 294920 | tf_op jit(solution)/shard_map/ppermute | solution.py:32
  96.3 8.8 %collective-permute-start.8 = (f32[32,768]{1,0:T(8,128)S(1)}, f32[32,768]{1,0:T(8,128)S(1)}, u32[]{:S(2)}, u32[]{:S(2)}) collective-permute-start(f32[32,768]{1,0:T(8,128)S(1)} %get-tuple-element.35), channel_id=1, source_target_pairs={{0,24},{4,28},{8,16},{12,20},{16,8},{20,12},{24,0},{28,4},{1,25},{... | collective-permute-start | bytes 294920 | tf_op jit(solution)/shard_map/ppermute | solution.py:32
  100.6 8.2 %collective-permute-start.22 = (f32[64,512]{1,0:T(8,128)S(1)}, f32[64,512]{1,0:T(8,128)S(1)}, u32[]{:S(2)}, u32[]{:S(2)}) collective-permute-start(f32[64,512]{1,0:T(8,128)S(1)} %add_add_fusion.1), channel_id=1, source_target_pairs={{0,3},{1,2},{2,1},{3,0},{4,7},{5,6},{6,5},{7,4},{8,11},{9,10},{10,... | collective-permute-start | bytes 393224 | tf_op jit(solution)/shard_map/ppermute | solution.py:32
  104.2 15.8 %collective-permute-start.21 = (f32[64,512]{1,0:T(8,128)S(1)}, f32[64,512]{1,0:T(8,128)S(1)}, u32[]{:S(2)}, u32[]{:S(2)}) collective-permute-start(f32[64,512]{1,0:T(8,128)S(1)} %add_add_fusion.1), channel_id=1, source_target_pairs={{0,2},{1,3},{2,0},{3,1},{4,6},{5,7},{6,4},{7,5},{8,10},{9,11},{10,... | collective-permute-start | bytes 393224 | tf_op jit(solution)/shard_map/ppermute | solution.py:32
  104.2 15.8 %collective-permute-start.20 = (f32[64,512]{1,0:T(8,128)S(1)}, f32[64,512]{1,0:T(8,128)S(1)}, u32[]{:S(2)}, u32[]{:S(2)}) collective-permute-start(f32[64,512]{1,0:T(8,128)S(1)} %add_add_fusion.1), channel_id=1, source_target_pairs={{0,1},{1,0},{2,3},{3,2},{4,5},{5,4},{6,7},{7,6},{8,9},{9,8},{10,11... | collective-permute-start | bytes 393224 | tf_op jit(solution)/shard_map/ppermute | solution.py:32
  105.1 16.3 %collective-permute-start.11 = (f32[32,768]{1,0:T(8,128)S(1)}, f32[32,768]{1,0:T(8,128)S(1)}, u32[]{:S(2)}, u32[]{:S(2)}) collective-permute-start(f32[32,768]{1,0:T(8,128)S(1)} %add_add_fusion.3), channel_id=1, source_target_pairs={{0,3},{1,2},{2,1},{3,0},{4,7},{5,6},{6,5},{7,4},{8,11},{9,10},{10,... | collective-permute-start | bytes 294920 | tf_op jit(solution)/shard_map/ppermute | solution.py:32
  108.7 14.9 %collective-permute-start.10 = (f32[32,768]{1,0:T(8,128)S(1)}, f32[32,768]{1,0:T(8,128)S(1)}, u32[]{:S(2)}, u32[]{:S(2)}) collective-permute-start(f32[32,768]{1,0:T(8,128)S(1)} %add_add_fusion.3), channel_id=1, source_target_pairs={{0,2},{1,3},{2,0},{3,1},{4,6},{5,7},{6,4},{7,5},{8,10},{9,11},{10,... | collective-permute-start | bytes 294920 | tf_op jit(solution)/shard_map/ppermute | solution.py:32
  108.9 14.7 %collective-permute-start.9 = (f32[32,768]{1,0:T(8,128)S(1)}, f32[32,768]{1,0:T(8,128)S(1)}, u32[]{:S(2)}, u32[]{:S(2)}) collective-permute-start(f32[32,768]{1,0:T(8,128)S(1)} %add_add_fusion.3), channel_id=1, source_target_pairs={{0,1},{1,0},{2,3},{3,2},{4,5},{5,4},{6,7},{7,6},{8,9},{9,8},{10,11... | collective-permute-start | bytes 294920 | tf_op jit(solution)/shard_map/ppermute | solution.py:32
  120.0 6.0 %collective-permute-start.25 = (f32[64,512]{1,0:T(8,128)S(1)}, f32[64,512]{1,0:T(8,128)S(1)}, u32[]{:S(2)}, u32[]{:S(2)}) collective-permute-start(f32[64,512]{1,0:T(8,128)S(1)} %add_add_fusion), channel_id=1, source_target_pairs={{0,24},{4,28},{8,16},{12,20},{16,8},{20,12},{24,0},{28,4},{1,25},{... | collective-permute-start | bytes 393224 | tf_op jit(solution)/shard_map/ppermute | solution.py:32
  121.4 8.4 %collective-permute-start.24 = (f32[64,512]{1,0:T(8,128)S(1)}, f32[64,512]{1,0:T(8,128)S(1)}, u32[]{:S(2)}, u32[]{:S(2)}) collective-permute-start(f32[64,512]{1,0:T(8,128)S(1)} %add_add_fusion), channel_id=1, source_target_pairs={{0,16},{4,20},{8,24},{12,28},{16,0},{20,4},{24,8},{28,12},{1,17},{... | collective-permute-start | bytes 393224 | tf_op jit(solution)/shard_map/ppermute | solution.py:32
  121.4 8.3 %collective-permute-start.23 = (f32[64,512]{1,0:T(8,128)S(1)}, f32[64,512]{1,0:T(8,128)S(1)}, u32[]{:S(2)}, u32[]{:S(2)}) collective-permute-start(f32[64,512]{1,0:T(8,128)S(1)} %add_add_fusion), channel_id=1, source_target_pairs={{0,8},{4,12},{8,0},{12,4},{16,24},{20,28},{24,16},{28,20},{1,9},{5... | collective-permute-start | bytes 393224 | tf_op jit(solution)/shard_map/ppermute | solution.py:32
  123.6 7.1 %collective-permute-start.14 = (f32[32,768]{1,0:T(8,128)S(1)}, f32[32,768]{1,0:T(8,128)S(1)}, u32[]{:S(2)}, u32[]{:S(2)}) collective-permute-start(f32[32,768]{1,0:T(8,128)S(1)} %add_add_fusion.2), channel_id=1, source_target_pairs={{0,24},{4,28},{8,16},{12,20},{16,8},{20,12},{24,0},{28,4},{1,25},{... | collective-permute-start | bytes 294920 | tf_op jit(solution)/shard_map/ppermute | solution.py:32
  125.0 6.6 %collective-permute-start.13 = (f32[32,768]{1,0:T(8,128)S(1)}, f32[32,768]{1,0:T(8,128)S(1)}, u32[]{:S(2)}, u32[]{:S(2)}) collective-permute-start(f32[32,768]{1,0:T(8,128)S(1)} %add_add_fusion.2), channel_id=1, source_target_pairs={{0,16},{4,20},{8,24},{12,28},{16,0},{20,4},{24,8},{28,12},{1,17},{... | collective-permute-start | bytes 294920 | tf_op jit(solution)/shard_map/ppermute | solution.py:32
  126.1 5.5 %collective-permute-start.12 = (f32[32,768]{1,0:T(8,128)S(1)}, f32[32,768]{1,0:T(8,128)S(1)}, u32[]{:S(2)}, u32[]{:S(2)}) collective-permute-start(f32[32,768]{1,0:T(8,128)S(1)} %add_add_fusion.2), channel_id=1, source_target_pairs={{0,8},{4,12},{8,0},{12,4},{16,24},{20,28},{24,16},{28,20},{1,9},{5... | collective-permute-start | bytes 294920 | tf_op jit(solution)/shard_map/ppermute | solution.py:32
  129.8 2.0 %collective-permute-start.26 = (f32[256,512]{1,0:T(8,128)S(1)}, f32[256,512]{1,0:T(8,128)S(1)}, u32[]{:S(2)}, u32[]{:S(2)}) collective-permute-start(f32[256,512]{1,0:T(8,128)S(1)} %pad_maximum_fusion.gram_ref), channel_id=1, source_target_pairs={{0,4},{4,0},{8,12},{12,8},{16,20},{20,16},{24,28},{28,24},{1,5},{5... | collective-permute-start | bytes 1572872 | tf_op jit(solution)/shard_map/ppermute | solution.py:32
  131.6 1.8 %collective-permute-start.15 = (f32[128,768]{1,0:T(8,128)S(1)}, f32[128,768]{1,0:T(8,128)S(1)}, u32[]{:S(2)}, u32[]{:S(2)}) collective-permute-start(f32[128,768]{1,0:T(8,128)S(1)} %pad_maximum_fusion.1.sums_ref), channel_id=1, source_target_pairs={{0,4},{4,0},{8,12},{12,8},{16,20},{20,16},{24,28},{28,24},{1,5},{5... | collective-permute-start | bytes 1179656 | tf_op jit(solution)/shard_map/ppermute | solution.py:32
  151.0 1.1 copy-start.9
  153.1 2.2 %copy-start.2 = (f32[16,128,512]{2,1,0:T(8,128)S(1)}, f32[16,128,512]{2,1,0:T(8,128)}, u32[]{:S(2)}) copy-start(f32[16,128,512]{2,1,0:T(8,128)} %basis_ref.3) | copy-start | bytes 12582916
  155.3 1.4 copy-start.10

commit v2 on v1

--- a/solution.py
+++ b/solution.py
@@ -12,6 +12,7 @@
 EPS = 1e-06
 MIB = 1024 * 1024
 HI = lax.Precision.HIGHEST
+FIRST = 4
 SCALARS = pl.BlockSpec(memory_space=pltpu.SMEM)
 
 
@@ -25,6 +26,20 @@
 
 def params(mib):
     return pltpu.CompilerParams(vmem_limit_bytes=mib * MIB)
+
+
+def in_hbm(value):
+    return pltpu.with_memory_space_constraint(value, pltpu.HBM)
+
+
+def halves(value):
+    high = value.astype(jnp.bfloat16)
+    return high, (value - high.astype(jnp.float32)).astype(jnp.bfloat16)
+
+
+def mm3(left, right, dims):
+    (lh, ll), (rh, rl) = left, right
+    return mm(lh, rh, dims, None) + (mm(lh, rl, dims, None) + mm(ll, rh, dims, None))
 
 
 def xor_permute(value, axis, mask):
@@ -61,83 +76,119 @@
         out_shape=[shape(lines, members, width)] * 2 + [shape(2 * w + 1, members, width)] * 2,
         compiler_params=params(32),
         name="to_lines",
-    )(disp.reshape(members * lines, width), vel.reshape(members * lines, width), stiff)
-
-
-def evolve_kernel(index_ref, disp_ref, vel_ref, stiff_ref, before_ref, after_ref, *rest, masks, size):
-    outs, (disp_pad, vel_pad, stiff_pad) = rest[:len(masks)], rest[len(masks):]
+    )(in_hbm(disp.reshape(members * lines, width)), in_hbm(vel.reshape(members * lines, width)), stiff)
+
+
+def evolve_kernel(index_ref, disp_ref, vel_ref, stiff_ref, before_ref, after_ref, out, disp_pad, vel_pad, stiff_pad, *, slot):
+    size = out.shape[0]
     lines, members, width = disp_ref.shape
     w = STEPS
     blocks = lines // size
     lane = lax.broadcasted_iota(jnp.int32, (8, width), 1)
-    for mask, out in zip(masks, outs):
-        block = index_ref[0] ^ mask
-        start = block * size
-        disp_pad[w:w + size] = disp_ref[pl.ds(start, size)]
-        vel_pad[w:w + size] = vel_ref[pl.ds(start, size)]
-        stiff_pad[8:8 + size, :] = stiff_ref[pl.ds(pl.multiple_of(start, 8), size), :]
-
-        @pl.when(block == 0)
-        def _():
-            disp_pad[:w] = before_ref[:w]
-            vel_pad[:w] = before_ref[w:2 * w]
-            stiff_pad[8 - w:8, :] = before_ref[2 * w, :w, :]
-
-        @pl.when(block > 0)
-        def _():
-            low = jnp.maximum(start - w, 0)
-            disp_pad[:w] = disp_ref[pl.ds(low, w)]
-            vel_pad[:w] = vel_ref[pl.ds(low, w)]
-            stiff_pad[:8, :] = stiff_ref[pl.ds(pl.multiple_of(jnp.maximum(start - 8, 0), 8), 8), :]
-
-        @pl.when(block == blocks - 1)
-        def _():
-            disp_pad[w + size:] = after_ref[:w]
-            vel_pad[w + size:] = after_ref[w:2 * w]
-            stiff_pad[8 + size:8 + size + w, :] = after_ref[2 * w, :w, :]
-
-        @pl.when(block < blocks - 1)
-        def _():
-            high = jnp.minimum(start + size, lines - 8)
-            disp_pad[w + size:] = disp_ref[pl.ds(high, w)]
-            vel_pad[w + size:] = vel_ref[pl.ds(high, w)]
-            stiff_pad[8 + size:, :] = stiff_ref[pl.ds(pl.multiple_of(high, 8), 8), :]
-
-        def group_step(g, carry):
-            at = pl.ds(pl.multiple_of(g * 8, 8), 8)
-            disp = {i: disp_pad[i, at, :] for i in range(size + 2 * w)}
-            vel = {i: vel_pad[i, at, :] for i in range(1, size + 2 * w - 1)}
-            for step in range(1, w + 1):
-                new = {}
-                for i in range(step, size + 2 * w - step):
-                    u = disp[i]
-                    right = jnp.where(lane == width - 1, 0.0, pltpu.roll(u, width - 1, 1))
-                    left = jnp.where(lane == 0, 0.0, pltpu.roll(u, 1, 1))
-                    laplace = disp[i + 1] + disp[i - 1] + right + left - 4.0 * u
-                    square = u * u
-                    stiff = jnp.broadcast_to(stiff_pad[8 - w + i:8 - w + i + 1, :], (8, width))
-                    vel[i] = vel[i] + stiff * (laplace - 0.5 * u * (square / (1.0 + square)))
-                    new[i] = u + vel[i]
-                disp = new
-            for i in range(size):
-                out[i, at, :] = disp[w + i]
-            return carry
-
-        lax.fori_loop(0, members // 8, group_step, 0)
-
-
-def evolve(index, disp, vel, stiff, before, after, masks, size):
+    block = index_ref[0] ^ index_ref[FIRST + slot]
+    start = block * size
+    disp_pad[w:w + size] = disp_ref[pl.ds(start, size)]
+    vel_pad[w:w + size] = vel_ref[pl.ds(start, size)]
+    stiff_pad[8:8 + size, :] = stiff_ref[pl.ds(pl.multiple_of(start, 8), size), :]
+
+    @pl.when(block == 0)
+    def _():
+        disp_pad[:w] = before_ref[:w]
+        vel_pad[:w] = before_ref[w:2 * w]
+        stiff_pad[8 - w:8, :] = before_ref[2 * w, :w, :]
+
+    @pl.when(block > 0)
+    def _():
+        low = jnp.maximum(start - w, 0)
+        disp_pad[:w] = disp_ref[pl.ds(low, w)]
+        vel_pad[:w] = vel_ref[pl.ds(low, w)]
+        stiff_pad[:8, :] = stiff_ref[pl.ds(pl.multiple_of(jnp.maximum(start - 8, 0), 8), 8), :]
+
+    @pl.when(block == blocks - 1)
+    def _():
+        disp_pad[w + size:] = after_ref[:w]
+        vel_pad[w + size:] = after_ref[w:2 * w]
+        stiff_pad[8 + size:8 + size + w, :] = after_ref[2 * w, :w, :]
+
+    @pl.when(block < blocks - 1)
+    def _():
+        high = jnp.minimum(start + size, lines - 8)
+        disp_pad[w + size:] = disp_ref[pl.ds(high, w)]
+        vel_pad[w + size:] = vel_ref[pl.ds(high, w)]
+        stiff_pad[8 + size:, :] = stiff_ref[pl.ds(pl.multiple_of(high, 8), 8), :]
+
+    def group_step(g, carry):
+        at = pl.ds(pl.multiple_of(g * 8, 8), 8)
+        disp = {i: disp_pad[i, at, :] for i in range(size + 2 * w)}
+        vel = {i: vel_pad[i, at, :] for i in range(1, size + 2 * w - 1)}
+        for step in range(1, w + 1):
+            new = {}
+            for i in range(step, size + 2 * w - step):
+                u = disp[i]
+                right = jnp.where(lane == width - 1, 0.0, pltpu.roll(u, width - 1, 1))
+                left = jnp.where(lane == 0, 0.0, pltpu.roll(u, 1, 1))
+                around = (disp[i + 1] + disp[i - 1]) + (right + left)
+                stiff = jnp.broadcast_to(stiff_pad[8 - w + i:8 - w + i + 1, :], (8, width))
+                vel[i] = vel[i] + stiff * (around + u * (0.5 * pl.reciprocal(1.0 + u * u) - 4.5))
+                new[i] = u + vel[i]
+            disp = new
+        for i in range(size):
+            out[i, at, :] = disp[w + i]
+        return carry
+
+    lax.fori_loop(0, members // 8, group_step, 0)
+
+
+def evolve(index, disp, vel, stiff, before, after, slot, size):
     lines, members, width = disp.shape
     w = STEPS
     return pl.pallas_call(
-        functools.partial(evolve_kernel, masks=masks, size=size),
+        functools.partial(evolve_kernel, slot=slot),
         in_specs=[SCALARS] + [pl.BlockSpec(memory_space=pltpu.VMEM)] * 5,
-        out_shape=[shape(size, members, width)] * len(masks),
+        out_shape=shape(size, members, width),
         scratch_shapes=[pltpu.VMEM((size + 2 * w, members, width), jnp.float32)] * 2
         + [pltpu.VMEM((size + 16, width), jnp.float32)],
-        compiler_params=params(32),
-        name="evolve" + "".join(str(m) for m in masks),
+        compiler_params=params(16),
+        name="evolve%d" % slot,
     )(index, disp, vel, stiff, before, after)
+
+
+def basis_gram_kernel(index_ref, basis_ref, send_ref, keep_ref, sum_ref, mixed_ref):
+    lines, width, rank = basis_ref.shape
+    step = pl.program_id(0)
+
+    @pl.when(step == 0)
+    def _():
+        sum_ref[...] = jnp.zeros_like(sum_ref)
+        mixed_ref[...] = jnp.zeros_like(mixed_ref)
+
+    high, low = halves(basis_ref[...].reshape(lines * width, rank))
+    sum_ref[...] += mm(high, high, ((0,), (0,)), None)
+    mixed_ref[...] += mm(high, low, ((0,), (0,)), None)
+
+    @pl.when(step == pl.num_programs(0) - 1)
+    def _():
+        sum_ref[...] += mixed_ref[...] + mixed_ref[...].T
+        half = keep_ref.shape[0]
+        core = index_ref[1]
+        keep_ref[...] = sum_ref[pl.ds(pl.multiple_of(core * half, half), half), :]
+        send_ref[...] = sum_ref[pl.ds(pl.multiple_of((1 - core) * half, half), half), :]
+
+
+def basis_gram(index, basis):
+    lines, width, rank = basis.shape
+    block = 2
+    half = pl.BlockSpec((rank // 2, rank), lambda i: (0, 0))
+    return pl.pallas_call(
+        basis_gram_kernel,
+        grid=(lines // block,),
+        in_specs=[SCALARS, pl.BlockSpec((block, width, rank), lambda i: (i, 0, 0))],
+        out_specs=[half, half],
+        out_shape=[shape(rank // 2, rank)] * 2,
+        scratch_shapes=[pltpu.VMEM((rank, rank), jnp.float32)] * 2,
+        compiler_params=params(24),
+        name="basis_gram",
+    )(index, in_hbm(basis))
 
 
 def products_kernel(index_ref, basis_ref, *rest):
@@ -146,7 +197,7 @@
     rank = basis_ref.shape[-1]
     step = pl.program_id(0)
     for k, piece in enumerate(pieces):
-        at = pl.multiple_of((index_ref[0] ^ k) * members, members)
+        at = pl.multiple_of((index_ref[0] ^ index_ref[FIRST + k]) * members, members)
         for line in range(lines):
             snap_ref[pl.ds(at, members), line * width:(line + 1) * width] = piece[line]
 
@@ -156,7 +207,7 @@
 
     snap = snap_ref[...]
     rows = basis_ref[...].reshape(lines * width, rank)
-    sum_ref[:, :rank] += mm(snap, rows, ((1,), (0,)))
+    sum_ref[:, :rank] += mm3(halves(snap), halves(rows), ((1,), (0,)))
     sum_ref[:, rank:] += mm(snap, snap, ((1,), (1,)))
 
     @pl.when(step == pl.num_programs(0) - 1)
@@ -183,7 +234,7 @@
         scratch_shapes=[pltpu.VMEM((total, block * width), jnp.float32), pltpu.VMEM((total, rank + total), jnp.float32)],
         compiler_params=params(32),
         name="products",
-    )(index, basis, *pieces)
+    )(index, in_hbm(basis), *pieces)
 
 
 def split_kernel(index_ref, keep_ref, got_ref, *outs):
@@ -219,6 +270,19 @@
 
 def ana_sum(value):
     return tree_sum([value] + [xor_permute(value, "ana", k) for k in range(1, lax.axis_size("ana"))])
+
+
+def ana_sum_halved(value):
+    ranks = lax.axis_size("ana")
+    top = lax.axis_index("ana") // (ranks // 2)
+    half = value.shape[0] // 2
+    send = lax.dynamic_slice_in_dim(value, (1 - top) * half, half, axis=0)
+    total = lax.dynamic_slice_in_dim(value, top * half, half, axis=0) + xor_permute(send, "ana", ranks // 2)
+    bit = 1
+    while bit < ranks // 2:
+        total = total + xor_permute(total, "ana", bit)
+        bit *= 2
+    return jnp.concatenate([total, xor_permute(total, "ana", ranks // 2)], axis=0)
 
 
 def chip_gather(value):
@@ -269,21 +333,23 @@
     lax.fori_loop(0, members // PANEL, panel_step, 0)
 
 
-def ordered(index_ref, mine_ref, other_ref, out_ref, chips):
+def ordered(index_ref, mine_ref, other_ref, out_ref, chips, parts):
     half = mine_ref.shape[0]
-    rows = half // chips
-    for k in range(chips):
-        at = (index_ref[2] ^ k) * rows
+    rows = half // chips // parts
+    for k in range(chips * parts):
+        at = (index_ref[2] ^ (k // parts)) * (rows * parts)
+        if parts > 1:
+            at = at + (index_ref[3] ^ (k % parts)) * rows
         piece = slice(k * rows, (k + 1) * rows)
         out_ref[pl.ds(pl.multiple_of(index_ref[1] * half + at, rows), rows), :] = mine_ref[piece, :]
         out_ref[pl.ds(pl.multiple_of((1 - index_ref[1]) * half + at, rows), rows), :] = other_ref[piece, :]
 
 
-def solve_kernel(index_ref, sums_ref, sums2_ref, gram_ref, gram2_ref, rot_ref, w_ref, coords_ref,
+def solve_kernel(index_ref, sums_ref, sums2_ref, gram_ref, gram2_ref, rot_ref, high_ref, low_ref, coords_ref,
                  work_ref, all_ref, basis_ref, *, count, chips):
-    members, rank = coords_ref.shape
-    ordered(index_ref, sums_ref, sums2_ref, all_ref, chips)
-    ordered(index_ref, gram_ref, gram2_ref, basis_ref, chips)
+    rank, members = coords_ref.shape
+    ordered(index_ref, sums_ref, sums2_ref, all_ref, chips, 1)
+    ordered(index_ref, gram_ref, gram2_ref, basis_ref, chips, 2)
     row = lax.broadcasted_iota(jnp.int32, (members, members), 0)
     col = lax.broadcasted_iota(jnp.int32, (members, members), 1)
     eye = row == col
@@ -299,9 +365,10 @@
     top, bottom = rot_ref[:rank, :], rot_ref[rank:, :]
     upper = jnp.where(row <= col, work_ref[:, :members], 0.0)
     mix = mm(work_ref[:, members:], bottom, ((0,), (0,)))
-    w_ref[:rank, :] = top - mm(coef, mix, ((0,), (0,)))
-    w_ref[rank:, :] = mix * along
-    coords_ref[...] = (mm(coef, top, ((1,), (0,))) + mm(upper, bottom, ((0,), (0,)))) * math.sqrt(rank)
+    high_ref[:rank, :], low_ref[:rank, :] = halves(top - mm(coef, mix, ((0,), (0,))))
+    high_ref[rank:, :], low_ref[rank:, :] = halves(mix * along)
+    coords = (mm(coef, top, ((1,), (0,))) + mm(upper, bottom, ((0,), (0,)))) * math.sqrt(rank)
+    coords_ref[...] = coords.T
 
 
 def solve(index, sums, gram, rotation, count, chips):
@@ -310,7 +377,7 @@
     return pl.pallas_call(
         functools.partial(solve_kernel, count=float(count), chips=chips),
         in_specs=[SCALARS] + [pl.BlockSpec(memory_space=pltpu.VMEM)] * 5,
-        out_shape=(shape(members + rank, rank), shape(members, rank)),
+        out_shape=[shape(members + rank, rank, dtype=jnp.bfloat16)] * 2 + [shape(rank, members)],
         scratch_shapes=[pltpu.VMEM((members, 2 * members), jnp.float32),
                         pltpu.VMEM((members, rank + members), jnp.float32),
                         pltpu.VMEM((rank, rank), jnp.float32)],
@@ -319,20 +386,21 @@
     )(index, *sums, *gram, rotation)
 
 
-def rotate_kernel(index_ref, weights_ref, basis_ref, *rest):
+def rotate_kernel(index_ref, high_ref, low_ref, basis_ref, *rest):
     pieces, (out_ref, snap_ref) = rest[:-2], rest[-2:]
     lines, members, width = pieces[0].shape
     rank = basis_ref.shape[-1]
     for k, piece in enumerate(pieces):
-        at = pl.multiple_of((index_ref[0] ^ k) * members, members)
+        at = pl.multiple_of((index_ref[0] ^ index_ref[FIRST + k]) * members, members)
         for line in range(lines):
             snap_ref[pl.ds(at, members), line * width:(line + 1) * width] = piece[line]
     rows = basis_ref[...].reshape(lines * width, rank)
-    out = mm(rows, weights_ref[:rank, :], ((1,), (0,))) + mm(snap_ref[...], weights_ref[rank:, :], ((0,), (0,)))
+    out = mm3(halves(rows), (high_ref[:rank, :], low_ref[:rank, :]), ((1,), (0,)))
+    out = out + mm3(halves(snap_ref[...].T), (high_ref[rank:, :], low_ref[rank:, :]), ((1,), (0,)))
     out_ref[...] = out.reshape(out_ref.shape)
 
 
-def rotate(index, weights, basis, pieces):
+def rotate(index, high, low, basis, pieces):
     lines, width, rank = basis.shape
     members = pieces[0].shape[1]
     block = 2
@@ -340,14 +408,14 @@
     return pl.pallas_call(
         rotate_kernel,
         grid=(lines // block,),
-        in_specs=[SCALARS, pl.BlockSpec(weights.shape, lambda i: (0, 0)), rows]
+        in_specs=[SCALARS] + [pl.BlockSpec(high.shape, lambda i: (0, 0))] * 2 + [rows]
         + [pl.BlockSpec((block, members, width), lambda i: (i, 0, 0))] * len(pieces),
         out_specs=rows,
         out_shape=shape(lines, width, rank),
         scratch_shapes=[pltpu.VMEM((members * len(pieces), block * width), jnp.float32)],
         compiler_params=params(32),
         name="rotate",
-    )(index, weights, basis, *pieces)
+    )(index, high, low, in_hbm(basis), *pieces)
 
 
 def per_device(initial_disp, initial_vel, stiffness, basis, rotation):
@@ -357,34 +425,37 @@
     count = lines * width * sims * ranks
     chips = sims // 2
     core = sim % 2
-    index = jnp.stack([ana, core, sim // 2]).astype(jnp.int32)
+    near, far = list(range(1, ranks // 2)), list(range(ranks // 2, ranks))
+    orders = (near + far[::-1] + [0], far[::-1] + near + [0])
+    masks = jnp.where(core == 0, jnp.array(orders[0]), jnp.array(orders[1]))
+    first_index = jnp.stack([ana, core, sim // 2, ana // (ranks // 2)])
+    index = jnp.concatenate([first_index, masks]).astype(jnp.int32)
 
     disp, vel, last, first = to_lines(initial_disp, initial_vel, stiffness)
     up = [(i, i + 1) for i in range(sims - 1)]
     before = lax.ppermute(last, "sim", up)
     after = lax.ppermute(first, "sim", [(j, i) for i, j in up])
 
-    rows = basis.reshape(lines * width, rank)
-    gram = mm(rows, rows, ((0,), (0,)))
-    half = rank // 2
-    keep = lax.dynamic_slice_in_dim(gram, core * half, half, axis=0)
-    send = lax.dynamic_slice_in_dim(gram, (1 - core) * half, half, axis=0)
+    basis_late, _ = lax.optimization_barrier((basis, last[0, 0, 0]))
+    send, keep = basis_gram(index, basis_late)
+    before, after, send = lax.optimization_barrier((before, after, send))
+
+    pieces = []
+    for slot in range(ranks):
+        piece = evolve(index, disp, vel, stiffness, before, after, slot, lines)
+        if slot < ranks - 1:
+            pairs = [(s * ranks + a, s * ranks + (a ^ orders[s % 2][slot])) for s in range(sims) for a in range(ranks)]
+            piece = lax.ppermute(piece, ("sim", "ana"), pairs)
+        pieces.append(piece)
+    pieces[-1], send = lax.optimization_barrier((pieces[-1], send))
     gram = chip_scatter(index, send, keep)
-
-    far = tuple(range(ranks // 2, ranks))
-    near = tuple(range(ranks // 2))
-    pieces = {}
-    for masks in (far, near):
-        found = evolve(index, disp, vel, stiffness, before, after, masks, lines)
-        for mask, piece in zip(masks, found):
-            pieces[mask] = xor_permute(piece, "ana", mask) if mask else piece
-    pieces = [pieces[k] for k in range(ranks)]
+    gram = chip_gather(ana_sum_halved(gram))
+    pieces, gram = lax.optimization_barrier((pieces, gram))
 
     send, keep = products(index, basis, pieces)
     sums = chip_gather(ana_sum(chip_scatter(index, send, keep)))
-    gram = chip_gather(ana_sum(gram))
-    weights, coords = solve(index, sums, gram, rotation, count, chips)
-    return rotate(index, weights, basis, pieces), coords.T
+    high, low, coords = solve(index, sums, gram, rotation, count, chips)
+    return rotate(index, high, low, basis, pieces), coords
 
 
 def solution(mesh):

time: 171 us -> 180 us (1.053)
  waiting for transfers between devices: 38.7 us -> 70.1 us
  local copies, waits for them, and re-layouts: 16.7 us -> 3.82 us
  starting transfers between devices: 48.1 us -> 38.8 us
  matrix products: 7.03 us -> 0 us
  Pallas kernels: 59 us -> 64.1 us
    ppermute x0 -> x3, waiting for transfers between devices: none -> 31.8 us  [per_device(): piece = lax.ppermute(piece, ('sim', 'ana'), pairs)]
    ppermute x25 -> x22, starting transfers between devices: 44.4 us -> 30.2 us  [xor_permute(): return lax.ppermute(value, axis, [(i, i ^ mask) for i in range(size)])]
    unnamed x33 -> x19, local copies, waits for them, and re-layouts: 16.6 us -> 3.71 us
    dot_general x1 -> x0, matrix products: 7.03 us -> none  [mm(): lax.dot_general(left, right, (dims, ((), ())), precision=precision, prefe...]
    ppermute x0 -> x3, starting transfers between devices: none -> 4.88 us  [per_device(): piece = lax.ppermute(piece, ('sim', 'ana'), pairs)]
    ppermute x1, waiting for transfers between devices: 4.17 us -> 0.01 us  [per_device(): after = lax.ppermute(first, 'sim', [(j, i) for i, j in up])]
    ppermute x25 -> x22, waiting for transfers between devices: 34.5 us -> 38.3 us  [xor_permute(): return lax.ppermute(value, axis, [(i, i ^ mask) for i in range(size)])]
    pallas_call x1, Pallas kernels: 2.99 us -> 5.38 us  [to_lines(): pl.pallas_call(to_lines_kernel, grid=(members // group,), in_specs=[flat,...]
  transfers between devices with their start and end apart: 27 -> 27, of which waited for: 13 -> 21; matrix products, arithmetic and copies ran while one was open for 4% -> 0% of each run, Pallas kernels for 10% -> 10%
where the time goes in v2:
time: 180 us; the launch traced here: 179 us
  waiting for transfers between devices  70.1 us (39%)
  Pallas kernels  64.1 us (36%)
  starting transfers between devices  38.8 us (22%)
  local copies, waits for them, and re-layouts  3.82 us (2%)
    ppermute x22, waiting for transfers between devices, xor_permute(): return lax.ppermute(value, axis, [(i, i ^ mask) for i in range(size)])  38.3 us
    ppermute x3, waiting for transfers between devices, per_device(): piece = lax.ppermute(piece, ('sim', 'ana'), pairs)  31.8 us
    ppermute x22, starting transfers between devices, xor_permute(): return lax.ppermute(value, axis, [(i, i ^ mask) for i in range(size)])  30.2 us
    pallas_call x1, Pallas kernels, solve(): pl.pallas_call(functools.partial(solve_kernel, count=float(count), chips=...  18.6 us
    pallas_call x4, Pallas kernels, evolve(): pl.pallas_call(functools.partial(evolve_kernel, slot=slot), in_specs=[SCA...  13.5 us
    pallas_call x1, Pallas kernels, rotate(): pl.pallas_call(rotate_kernel, grid=(lines // block,), in_specs=[SCALARS]...  9.79 us
    pallas_call x1, Pallas kernels, products(): pl.pallas_call(products_kernel, grid=(lines // block,), in_specs=[SCALARS...  7.58 us
    pallas_call x1, Pallas kernels, basis_gram(): pl.pallas_call(basis_gram_kernel, grid=(lines // block,), in_specs=[SCALA...  7.4 us
  transfers between devices with their start and end apart: 27, of which 21 were waited for; matrix products, arithmetic and copies ran while one was open for 0% of the time, Pallas kernels for 10%

profile of v2, /device:TPU:0, one launch (start us, length us, event | category | flops | bytes accessed | tf_op | source)
XLA Modules:
  0.0 178.8 jit_solution(6522526663693900306)
XLA Ops:
  1.4 5.4 %to_lines.1 = (f32[64,64,128]{2,1,0:T(8,128)S(1)}, f32[64,64,128]{2,1,0:T(8,128)S(1)}, f32[9,64,128]{2,1,0:T(8,128)}, f32[9,64,128]{2,1,0:T(8,128)S(1)}) custom-call(f32[4096,128]{1,0:T(8,128)} %bitcast.6, f32[4096,128]{1,0:T(8,128)} %bitcast.7, f32[64,128]{1,0:T(8,128)S(1)} %copy-done.4), custom_call_target="tpu_custom_call" | custom-call | tf_op jit(solution)/shard_map/to_lines/pallas_call | solution.py:71
  6.8 1.3 copy-done
  8.1 2.4 %collective-permute-start = (f32[9,64,128]{2,1,0:T(8,128)}, f32[9,64,128]{2,1,0:T(8,128)S(1)}, u32[]{:S(2)}, u32[]{:S(2)}) collective-permute-start(f32[9,64,128]{2,1,0:T(8,128)} %get-tuple-element.34), channel_id=1, source_target_pairs={{0,4},{4,8},{8,12},{12,16},{16,20},{20,24},{24,28},{1,5},{5,9},{9,... | collective-permute-start | bytes 884744 | tf_op jit(solution)/shard_map/ppermute | solution.py:436
  10.5 1.3 collective-permute-start.1
  11.9 7.4 %basis_gram.1 = (f32[256,512]{1,0:T(8,128)S(1)}, f32[256,512]{1,0:T(8,128)S(1)}) custom-call(s32[8]{0:T(128)S(1)} %concatenate.13.index_ref, f32[16,128,512]{2,1,0:T(8,128)} %basis_ref.4), custom_call_target="tpu_custom_call" | custom-call | tf_op jit(solution)/shard_map/basis_gram/pallas_call | solution.py:182
  19.4 3.3 %evolve3.1.rest_3_ = f32[16,64,128]{2,1,0:T(8,128)S(1)} custom-call(s32[8]{0:T(128)S(1)} %concatenate.13.index_ref, f32[64,64,128]{2,1,0:T(8,128)S(1)} %get-tuple-element.32.disp_ref, f32[64,64,128]{2,1,0:T(8,128)S(1)} %copy-done.1, f32[64,128]{1,0:T(8,128)S(1)} %copy-done.5, f32[9,64,128]{2,1,0:T(8,128)S(1)} %collective-permute-done.before_ref, ...), custom_call_target="tpu_custom_call" | custom-call | tf_op jit(solution)/shard_map/evolve3/pallas_call | solution.py:145
  22.7 3.3 %collective-permute-start.5 = (f32[256,512]{1,0:T(8,128)S(1)}, f32[256,512]{1,0:T(8,128)S(1)}, u32[]{:S(2)}, u32[]{:S(2)}) collective-permute-start(f32[256,512]{1,0:T(8,128)S(1)} %get-tuple-element.42), channel_id=1, source_target_pairs={{0,4},{4,0},{8,12},{12,8},{16,20},{20,16},{24,28},{28,24},{1,5},{5... | collective-permute-start | bytes 1572872 | tf_op jit(solution)/shard_map/ppermute | solution.py:47
  26.0 1.5 collective-permute-done.5.got_ref
  27.5 1.3 split.2
  28.8 2.0 %collective-permute-start.6 = (f32[64,512]{1,0:T(8,128)}, f32[64,512]{1,0:T(8,128)}, u32[]{:S(2)}, u32[]{:S(2)}) collective-permute-start(f32[64,512]{1,0:T(8,128)} %get-tuple-element.44), channel_id=1, source_target_pairs={{0,8},{4,12},{8,0},{12,4},{16,24},{20,28},{24,16},{28,20},{1,9},{5... | collective-permute-start | bytes 393224 | tf_op jit(solution)/shard_map/ppermute | solution.py:47
  30.8 1.5 collective-permute-start.7
  33.2 2.0 %collective-permute-done.6 = f32[64,512]{1,0:T(8,128)} collective-permute-done((f32[64,512]{1,0:T(8,128)}, f32[64,512]{1,0:T(8,128)}, u32[]{:S(2)}, u32[]{:S(2)}) %collective-permute-start.6) | collective-permute-done | bytes 131104 | tf_op jit(solution)/shard_map/ppermute | solution.py:47
  35.2 3.0 %collective-permute-done.7 = f32[64,512]{1,0:T(8,128)} collective-permute-done((f32[64,512]{1,0:T(8,128)}, f32[64,512]{1,0:T(8,128)}, u32[]{:S(2)}, u32[]{:S(2)}) %collective-permute-start.7) | collective-permute-done | bytes 131104 | tf_op jit(solution)/shard_map/ppermute | solution.py:47
  38.2 1.6 collective-permute-done.8
  40.9 2.7 %collective-permute-start.9 = (f32[32,512]{1,0:T(8,128)S(1)}, f32[32,512]{1,0:T(8,128)S(1)}, u32[]{:S(2)}, u32[]{:S(2)}) collective-permute-start(f32[32,512]{1,0:T(8,128)S(1)} %constant_dynamic-slice_fusion), channel_id=1, source_target_pairs={{0,2},{1,3},{2,0},{3,1},{4,6},{5,7},{6,4},{7,5},{8,10},{9,11},{10,... | collective-permute-start | bytes 196616 | tf_op jit(solution)/shard_map/ppermute | solution.py:47
  43.6 2.6 %collective-permute-done.9 = f32[32,512]{1,0:T(8,128)S(1)} collective-permute-done((f32[32,512]{1,0:T(8,128)S(1)}, f32[32,512]{1,0:T(8,128)S(1)}, u32[]{:S(2)}, u32[]{:S(2)}) %collective-permute-start.9) | collective-permute-done | bytes 65568 | tf_op jit(solution)/shard_map/ppermute | solution.py:47
  46.2 1.6 collective-permute-start.10
  47.8 2.7 %collective-permute-done.10 = f32[32,512]{1,0:T(8,128)S(1)} collective-permute-done((f32[32,512]{1,0:T(8,128)S(1)}, f32[32,512]{1,0:T(8,128)S(1)}, u32[]{:S(2)}, u32[]{:S(2)}) %collective-permute-start.10) | collective-permute-done | bytes 65568 | tf_op jit(solution)/shard_map/ppermute | solution.py:47
  50.6 2.8 %collective-permute-start.11 = (f32[32,512]{1,0:T(8,128)S(1)}, f32[32,512]{1,0:T(8,128)S(1)}, u32[]{:S(2)}, u32[]{:S(2)}) collective-permute-start(f32[32,512]{1,0:T(8,128)S(1)} %get-tuple-element.63), channel_id=1, source_target_pairs={{0,2},{1,3},{2,0},{3,1},{4,6},{5,7},{6,4},{7,5},{8,10},{9,11},{10,... | collective-permute-start | bytes 196616 | tf_op jit(solution)/shard_map/ppermute | solution.py:47
  53.4 2.4 %collective-permute-done.11 = f32[32,512]{1,0:T(8,128)S(1)} collective-permute-done((f32[32,512]{1,0:T(8,128)S(1)}, f32[32,512]{1,0:T(8,128)S(1)}, u32[]{:S(2)}, u32[]{:S(2)}) %collective-permute-start.11) | collective-permute-done | bytes 65568 | tf_op jit(solution)/shard_map/ppermute | solution.py:47
  56.5 1.6 copy-done.2
  58.1 3.3 %evolve2.1 = f32[16,64,128]{2,1,0:T(8,128)S(1)} custom-call(s32[8]{0:T(128)S(1)} %concatenate.13.index_ref, f32[64,64,128]{2,1,0:T(8,128)S(1)} %get-tuple-element.32.disp_ref, f32[64,64,128]{2,1,0:T(8,128)S(1)} %copy-done.2, f32[64,128]{1,0:T(8,128)S(1)} %copy-done.5, f32[9,64,128]{2,1,0:T(8,128)S(1)} %collective-permute-done.before_ref, ...), custom_call_target="tpu_custom_call" | custom-call | tf_op jit(solution)/shard_map/evolve2/pallas_call | solution.py:145
  61.4 3.3 %evolve1.1 = f32[16,64,128]{2,1,0:T(8,128)S(1)} custom-call(s32[8]{0:T(128)S(1)} %concatenate.13.index_ref, f32[64,64,128]{2,1,0:T(8,128)S(1)} %get-tuple-element.32.disp_ref, f32[64,64,128]{2,1,0:T(8,128)S(1)} %copy-done.2, f32[64,128]{1,0:T(8,128)S(1)} %copy-done.5, f32[9,64,128]{2,1,0:T(8,128)S(1)} %collective-permute-done.before_ref, ...), custom_call_target="tpu_custom_call" | custom-call | tf_op jit(solution)/shard_map/evolve1/pallas_call | solution.py:145
  64.8 3.5 %evolve0.1 = f32[16,64,128]{2,1,0:T(8,128)S(1)} custom-call(s32[8]{0:T(128)S(1)} %concatenate.13.index_ref, f32[64,64,128]{2,1,0:T(8,128)S(1)} %get-tuple-element.32.disp_ref, f32[64,64,128]{2,1,0:T(8,128)S(1)} %copy-done.2, f32[64,128]{1,0:T(8,128)S(1)} %copy-done.5, f32[9,64,128]{2,1,0:T(8,128)S(1)} %collective-permute-done.before_ref, ...), custom_call_target="tpu_custom_call" | custom-call | tf_op jit(solution)/shard_map/evolve0/pallas_call | solution.py:145
  68.3 1.8 %collective-permute-start.2 = (f32[16,64,128]{2,1,0:T(8,128)S(1)}, f32[16,64,128]{2,1,0:T(8,128)S(1)}, u32[]{:S(2)}, u32[]{:S(2)}) collective-permute-start(f32[16,64,128]{2,1,0:T(8,128)S(1)} %evolve0.1), channel_id=1, source_target_pairs={{0,1},{1,0},{2,3},{3,2},{4,7},{5,6},{6,5},{7,4},{8,9},{9,8},{10,11... | collective-permute-start | bytes 1572872 | tf_op jit(solution)/shard_map/ppermute | solution.py:448
  70.1 2.6 %collective-permute-start.3 = (f32[16,64,128]{2,1,0:T(8,128)S(1)}, f32[16,64,128]{2,1,0:T(8,128)S(1)}, u32[]{:S(2)}, u32[]{:S(2)}) collective-permute-start(f32[16,64,128]{2,1,0:T(8,128)S(1)} %evolve1.1), channel_id=1, source_target_pairs={{0,3},{1,2},{2,1},{3,0},{4,6},{5,7},{6,4},{7,5},{8,11},{9,10},{10,... | collective-permute-start | bytes 1572872 | tf_op jit(solution)/shard_map/ppermute | solution.py:448
  73.2 2.0 %collective-permute-start.13 = (f32[64,512]{1,0:T(8,128)S(1)}, f32[64,512]{1,0:T(8,128)S(1)}, u32[]{:S(2)}, u32[]{:S(2)}) collective-permute-start(f32[64,512]{1,0:T(8,128)S(1)} %pad_maximum_fusion.1), channel_id=1, source_target_pairs={{0,16},{4,20},{8,24},{12,28},{16,0},{20,4},{24,8},{28,12},{1,17},{... | collective-permute-start | bytes 393224 | tf_op jit(solution)/shard_map/ppermute | solution.py:47
  76.2 2.8 %collective-permute-done.13 = f32[64,512]{1,0:T(8,128)S(1)} collective-permute-done((f32[64,512]{1,0:T(8,128)S(1)}, f32[64,512]{1,0:T(8,128)S(1)}, u32[]{:S(2)}, u32[]{:S(2)}) %collective-permute-start.13) | collective-permute-done | bytes 131104 | tf_op jit(solution)/shard_map/ppermute | solution.py:47
  79.1 2.0 %collective-permute-done.14 = f32[64,512]{1,0:T(8,128)S(1)} collective-permute-done((f32[64,512]{1,0:T(8,128)S(1)}, f32[64,512]{1,0:T(8,128)S(1)}, u32[]{:S(2)}, u32[]{:S(2)}) %collective-permute-start.14) | collective-permute-done | bytes 131104 | tf_op jit(solution)/shard_map/ppermute | solution.py:47
  81.2 5.9 %collective-permute-done.2.rest_0_ = f32[16,64,128]{2,1,0:T(8,128)S(1)} collective-permute-done((f32[16,64,128]{2,1,0:T(8,128)S(1)}, f32[16,64,128]{2,1,0:T(8,128)S(1)}, u32[]{:S(2)}, u32[]{:S(2)}) %collective-permute-start.2) | collective-permute-done | bytes 524320 | tf_op jit(solution)/shard_map/ppermute | solution.py:448
  87.1 9.6 %collective-permute-done.3.rest_1_ = f32[16,64,128]{2,1,0:T(8,128)S(1)} collective-permute-done((f32[16,64,128]{2,1,0:T(8,128)S(1)}, f32[16,64,128]{2,1,0:T(8,128)S(1)}, u32[]{:S(2)}, u32[]{:S(2)}) %collective-permute-start.3) | collective-permute-done | bytes 524320 | tf_op jit(solution)/shard_map/ppermute | solution.py:448
  96.7 16.3 %collective-permute-done.4.rest_2_ = f32[16,64,128]{2,1,0:T(8,128)S(1)} collective-permute-done((f32[16,64,128]{2,1,0:T(8,128)S(1)}, f32[16,64,128]{2,1,0:T(8,128)S(1)}, u32[]{:S(2)}, u32[]{:S(2)}) %collective-permute-start.4) | collective-permute-done | bytes 524320 | tf_op jit(solution)/shard_map/ppermute | solution.py:448
  113.0 7.6 %products.1 = (f32[128,768]{1,0:T(8,128)S(1)}, f32[128,768]{1,0:T(8,128)S(1)}) custom-call(s32[8]{0:T(128)S(1)} %concatenate.13.index_ref, f32[16,128,512]{2,1,0:T(8,128)} %basis_ref.4, f32[16,64,128]{2,1,0:T(8,128)S(1)} %collective-permute-done.2.rest_0_, f32[16,64,128]{2,1,0:T(8,128)S(1)} %collective-permute-done.3.rest_1_, ...), custom_call_target="tpu_custom_call" | custom-call | tf_op jit(solution)/shard_map/products/pallas_call | solution.py:227
  120.7 1.7 collective-permute-done.16.got_ref
  123.0 1.5 collective-permute-start.17
  125.3 1.2 collective-permute-start.19
  126.5 1.3 collective-permute-done.17
  127.9 2.3 %collective-permute-done.18 = f32[32,768]{1,0:T(8,128)S(1)} collective-permute-done((f32[32,768]{1,0:T(8,128)S(1)}, f32[32,768]{1,0:T(8,128)S(1)}, u32[]{:S(2)}, u32[]{:S(2)}) %collective-permute-start.18) | collective-permute-done | bytes 98336 | tf_op jit(solution)/shard_map/ppermute | solution.py:47
  131.2 2.4 %collective-permute-start.22 = (f32[32,768]{1,0:T(8,128)S(1)}, f32[32,768]{1,0:T(8,128)S(1)}, u32[]{:S(2)}, u32[]{:S(2)}) collective-permute-start(f32[32,768]{1,0:T(8,128)S(1)} %add_add_fusion.2), channel_id=1, source_target_pairs={{0,3},{1,2},{2,1},{3,0},{4,7},{5,6},{6,5},{7,4},{8,11},{9,10},{10,... | collective-permute-start | bytes 294920 | tf_op jit(solution)/shard_map/ppermute | solution.py:47
  133.6 2.0 %collective-permute-start.20 = (f32[32,768]{1,0:T(8,128)S(1)}, f32[32,768]{1,0:T(8,128)S(1)}, u32[]{:S(2)}, u32[]{:S(2)}) collective-permute-start(f32[32,768]{1,0:T(8,128)S(1)} %add_add_fusion.2), channel_id=1, source_target_pairs={{0,1},{1,0},{2,3},{3,2},{4,5},{5,4},{6,7},{7,6},{8,9},{9,8},{10,11... | collective-permute-start | bytes 294920 | tf_op jit(solution)/shard_map/ppermute | solution.py:47
  135.6 3.2 %collective-permute-done.22 = f32[32,768]{1,0:T(8,128)S(1)} collective-permute-done((f32[32,768]{1,0:T(8,128)S(1)}, f32[32,768]{1,0:T(8,128)S(1)}, u32[]{:S(2)}, u32[]{:S(2)}) %collective-permute-start.22) | collective-permute-done | bytes 98336 | tf_op jit(solution)/shard_map/ppermute | solution.py:47
  138.8 2.3 %collective-permute-done.21 = f32[32,768]{1,0:T(8,128)S(1)} collective-permute-done((f32[32,768]{1,0:T(8,128)S(1)}, f32[32,768]{1,0:T(8,128)S(1)}, u32[]{:S(2)}, u32[]{:S(2)}) %collective-permute-start.21) | collective-permute-done | bytes 98336 | tf_op jit(solution)/shard_map/ppermute | solution.py:47
  141.2 1.6 collective-permute-start.25
  143.7 1.1 collective-permute-start.23
  144.8 2.8 %collective-permute-done.25 = f32[32,768]{1,0:T(8,128)S(1)} collective-permute-done((f32[32,768]{1,0:T(8,128)S(1)}, f32[32,768]{1,0:T(8,128)S(1)}, u32[]{:S(2)}, u32[]{:S(2)}) %collective-permute-start.25) | collective-permute-done | bytes 98336 | tf_op jit(solution)/shard_map/ppermute | solution.py:47
  148.7 1.7 collective-permute-done.26.sums2_ref
  150.5 18.6 %solve.1 = (bf16[768,512]{1,0:T(8,128)(2,1)S(1)}, bf16[768,512]{1,0:T(8,128)(2,1)S(1)}, f32[512,256]{1,0:T(8,128)}) custom-call(s32[8]{0:T(128)S(1)} %concatenate.13.index_ref, f32[128,768]{1,0:T(8,128)S(1)} %pad_maximum_fusion.sums_ref, f32[128,768]{1,0:T(8,128)S(1)} %collective-permute-done.26.sums2_ref, ...), custom_call_target="tpu_custom_call" | custom-call | tf_op jit(solution)/shard_map/solve/pallas_call | solution.py:377
  169.0 9.8 %rotate.1 = f32[16,128,512]{2,1,0:T(8,128)} custom-call(s32[8]{0:T(128)S(1)} %concatenate.13.index_ref, bf16[768,512]{1,0:T(8,128)(2,1)S(1)} %get-tuple-element.59.high_ref, bf16[768,512]{1,0:T(8,128)(2,1)S(1)} %get-tuple-element.60.low_ref, f32[16,128,512]{2,1,0:T(8,128)} %basis_ref.4, f32[16,64,128]{2,1,0:T(8,128)S(1)} %collective-permute-done.2.rest_0_, ...), custom_call_target="tpu_custom_call" | custom-call | tf_op jit(solution)/shard_map/rotate/pallas_call | solution.py:408
  (47 shorter events, 9.7 us)
Async XLA Ops:
  0.6 0.8 copy-start.4
  1.4 10.4 %copy-start.6 = (s32[4]{0:T(128)S(1)}, s32[4]{0:T(128)}, u32[]{:S(2)}) copy-start(s32[4]{0:T(128)} %constant.53.clone) | copy-start | bytes 52
  1.4 10.4 %copy-start.7 = (s32[4]{0:T(128)S(1)}, s32[4]{0:T(128)}, u32[]{:S(2)}) copy-start(s32[4]{0:T(128)} %constant.52.clone) | copy-start | bytes 52
  6.8 1.3 copy-start
  8.1 11.2 %collective-permute-start = (f32[9,64,128]{2,1,0:T(8,128)}, f32[9,64,128]{2,1,0:T(8,128)S(1)}, u32[]{:S(2)}, u32[]{:S(2)}) collective-permute-start(f32[9,64,128]{2,1,0:T(8,128)} %get-tuple-element.34), channel_id=1, source_target_pairs={{0,4},{4,8},{8,12},{12,16},{16,20},{20,24},{24,28},{1,5},{5,9},{9,... | collective-permute-start | bytes 884744 | tf_op jit(solution)/shard_map/ppermute | solution.py:436
  10.5 8.9 %collective-permute-start.1 = (f32[9,64,128]{2,1,0:T(8,128)S(1)}, f32[9,64,128]{2,1,0:T(8,128)S(1)}, u32[]{:S(2)}, u32[]{:S(2)}) collective-permute-start(f32[9,64,128]{2,1,0:T(8,128)S(1)} %get-tuple-element.35), channel_id=1, source_target_pairs={{4,0},{8,4},{12,8},{16,12},{20,16},{24,20},{28,24},{5,1},{9,5},{13... | collective-permute-start | bytes 884744 | tf_op jit(solution)/shard_map/ppermute | solution.py:437
  11.9 7.4 %copy-start.1 = (f32[64,64,128]{2,1,0:T(8,128)S(1)}, f32[64,64,128]{2,1,0:T(8,128)}, u32[]{:S(2)}) copy-start(f32[64,64,128]{2,1,0:T(8,128)} %copy-done) | copy-start | bytes 6291460
  11.9 7.4 %copy-start.5 = (f32[64,128]{1,0:T(8,128)S(1)}, f32[64,128]{1,0:T(8,128)}, u32[]{:S(2)}) copy-start(f32[64,128]{1,0:T(8,128)} %stiff_ref.9) | copy-start | bytes 98308
  22.7 4.8 %collective-permute-start.5 = (f32[256,512]{1,0:T(8,128)S(1)}, f32[256,512]{1,0:T(8,128)S(1)}, u32[]{:S(2)}, u32[]{:S(2)}) collective-permute-start(f32[256,512]{1,0:T(8,128)S(1)} %get-tuple-element.42), channel_id=1, source_target_pairs={{0,4},{4,0},{8,12},{12,8},{16,20},{20,16},{24,28},{28,24},{1,5},{5... | collective-permute-start | bytes 1572872 | tf_op jit(solution)/shard_map/ppermute | solution.py:47
  28.8 6.4 %collective-permute-start.6 = (f32[64,512]{1,0:T(8,128)}, f32[64,512]{1,0:T(8,128)}, u32[]{:S(2)}, u32[]{:S(2)}) collective-permute-start(f32[64,512]{1,0:T(8,128)} %get-tuple-element.44), channel_id=1, source_target_pairs={{0,8},{4,12},{8,0},{12,4},{16,24},{20,28},{24,16},{28,20},{1,9},{5... | collective-permute-start | bytes 393224 | tf_op jit(solution)/shard_map/ppermute | solution.py:47
  30.8 7.4 %collective-permute-start.7 = (f32[64,512]{1,0:T(8,128)}, f32[64,512]{1,0:T(8,128)}, u32[]{:S(2)}, u32[]{:S(2)}) collective-permute-start(f32[64,512]{1,0:T(8,128)} %get-tuple-element.45), channel_id=1, source_target_pairs={{0,16},{4,20},{8,24},{12,28},{16,0},{20,4},{24,8},{28,12},{1,17},{... | collective-permute-start | bytes 393224 | tf_op jit(solution)/shard_map/ppermute | solution.py:47
  32.3 7.5 %collective-permute-start.8 = (f32[64,512]{1,0:T(8,128)S(1)}, f32[64,512]{1,0:T(8,128)}, u32[]{:S(2)}, u32[]{:S(2)}) collective-permute-start(f32[64,512]{1,0:T(8,128)S(1)} %get-tuple-element.46), channel_id=1, source_target_pairs={{0,24},{4,28},{8,16},{12,20},{16,8},{20,12},{24,0},{28,4},{1,25},{... | collective-permute-start | bytes 393224 | tf_op jit(solution)/shard_map/ppermute | solution.py:47
  40.9 5.3 %collective-permute-start.9 = (f32[32,512]{1,0:T(8,128)S(1)}, f32[32,512]{1,0:T(8,128)S(1)}, u32[]{:S(2)}, u32[]{:S(2)}) collective-permute-start(f32[32,512]{1,0:T(8,128)S(1)} %constant_dynamic-slice_fusion), channel_id=1, source_target_pairs={{0,2},{1,3},{2,0},{3,1},{4,6},{5,7},{6,4},{7,5},{8,10},{9,11},{10,... | collective-permute-start | bytes 196616 | tf_op jit(solution)/shard_map/ppermute | solution.py:47
  46.2 4.3 %collective-permute-start.10 = (f32[32,512]{1,0:T(8,128)S(1)}, f32[32,512]{1,0:T(8,128)S(1)}, u32[]{:S(2)}, u32[]{:S(2)}) collective-permute-start(f32[32,512]{1,0:T(8,128)S(1)} %dynamic-slice_add_fusion), channel_id=1, source_target_pairs={{0,1},{1,0},{2,3},{3,2},{4,5},{5,4},{6,7},{7,6},{8,9},{9,8},{10,11... | collective-permute-start | bytes 196616 | tf_op jit(solution)/shard_map/ppermute | solution.py:47
  50.6 5.2 %collective-permute-start.11 = (f32[32,512]{1,0:T(8,128)S(1)}, f32[32,512]{1,0:T(8,128)S(1)}, u32[]{:S(2)}, u32[]{:S(2)}) collective-permute-start(f32[32,512]{1,0:T(8,128)S(1)} %get-tuple-element.63), channel_id=1, source_target_pairs={{0,2},{1,3},{2,0},{3,1},{4,6},{5,7},{6,4},{7,5},{8,10},{9,11},{10,... | collective-permute-start | bytes 196616 | tf_op jit(solution)/shard_map/ppermute | solution.py:47
  55.8 19.3 %collective-permute-start.12 = (f32[64,512]{1,0:T(8,128)S(1)}, f32[64,512]{1,0:T(8,128)S(1)}, u32[]{:S(2)}, u32[]{:S(2)}) collective-permute-start(f32[64,512]{1,0:T(8,128)S(1)} %pad_maximum_fusion.1), channel_id=1, source_target_pairs={{0,8},{4,12},{8,0},{12,4},{16,24},{20,28},{24,16},{28,20},{1,9},{5... | collective-permute-start | bytes 393224 | tf_op jit(solution)/shard_map/ppermute | solution.py:47
  56.5 1.6 copy-start.2
  68.3 18.8 %collective-permute-start.2 = (f32[16,64,128]{2,1,0:T(8,128)S(1)}, f32[16,64,128]{2,1,0:T(8,128)S(1)}, u32[]{:S(2)}, u32[]{:S(2)}) collective-permute-start(f32[16,64,128]{2,1,0:T(8,128)S(1)} %evolve0.1), channel_id=1, source_target_pairs={{0,1},{1,0},{2,3},{3,2},{4,7},{5,6},{6,5},{7,4},{8,9},{9,8},{10,11... | collective-permute-start | bytes 1572872 | tf_op jit(solution)/shard_map/ppermute | solution.py:448
  70.1 26.6 %collective-permute-start.3 = (f32[16,64,128]{2,1,0:T(8,128)S(1)}, f32[16,64,128]{2,1,0:T(8,128)S(1)}, u32[]{:S(2)}, u32[]{:S(2)}) collective-permute-start(f32[16,64,128]{2,1,0:T(8,128)S(1)} %evolve1.1), channel_id=1, source_target_pairs={{0,3},{1,2},{2,1},{3,0},{4,6},{5,7},{6,4},{7,5},{8,11},{9,10},{10,... | collective-permute-start | bytes 1572872 | tf_op jit(solution)/shard_map/ppermute | solution.py:448
  72.7 40.3 %collective-permute-start.4 = (f32[16,64,128]{2,1,0:T(8,128)S(1)}, f32[16,64,128]{2,1,0:T(8,128)S(1)}, u32[]{:S(2)}, u32[]{:S(2)}) collective-permute-start(f32[16,64,128]{2,1,0:T(8,128)S(1)} %evolve2.1), channel_id=1, source_target_pairs={{0,2},{1,3},{2,0},{3,1},{4,5},{5,4},{6,7},{7,6},{8,10},{9,11},{10,... | collective-permute-start | bytes 1572872 | tf_op jit(solution)/shard_map/ppermute | solution.py:448
  73.2 5.9 %collective-permute-start.13 = (f32[64,512]{1,0:T(8,128)S(1)}, f32[64,512]{1,0:T(8,128)S(1)}, u32[]{:S(2)}, u32[]{:S(2)}) collective-permute-start(f32[64,512]{1,0:T(8,128)S(1)} %pad_maximum_fusion.1), channel_id=1, source_target_pairs={{0,16},{4,20},{8,24},{12,28},{16,0},{20,4},{24,8},{28,12},{1,17},{... | collective-permute-start | bytes 393224 | tf_op jit(solution)/shard_map/ppermute | solution.py:47
  75.2 5.9 %collective-permute-start.14 = (f32[64,512]{1,0:T(8,128)S(1)}, f32[64,512]{1,0:T(8,128)S(1)}, u32[]{:S(2)}, u32[]{:S(2)}) collective-permute-start(f32[64,512]{1,0:T(8,128)S(1)} %pad_maximum_fusion.1), channel_id=1, source_target_pairs={{0,24},{4,28},{8,16},{12,20},{16,8},{20,12},{24,0},{28,4},{1,25},{... | collective-permute-start | bytes 393224 | tf_op jit(solution)/shard_map/ppermute | solution.py:47
  81.1 31.9 %collective-permute-start.15 = (f32[256,512]{1,0:T(8,128)S(1)}, f32[256,512]{1,0:T(8,128)S(1)}, u32[]{:S(2)}, u32[]{:S(2)}) collective-permute-start(f32[256,512]{1,0:T(8,128)S(1)} %constant_dynamic-update-slice_fusion.gram_ref), channel_id=1, source_target_pairs={{0,4},{4,0},{8,12},{12,8},{16,20},{20,16},{24,28},{28,24},{1,5},{5... | collective-permute-start | bytes 1572872 | tf_op jit(solution)/shard_map/ppermute | solution.py:47
  120.6 29.9 %copy-start.3 = (f32[768,512]{1,0:T(8,128)S(1)}, f32[768,512]{1,0:T(8,128)}, u32[]{:S(2)}) copy-start(f32[768,512]{1,0:T(8,128)} %rot_ref.1) | copy-start | bytes 4718596
  120.6 1.8 %collective-permute-start.16 = (f32[128,768]{1,0:T(8,128)S(1)}, f32[128,768]{1,0:T(8,128)S(1)}, u32[]{:S(2)}, u32[]{:S(2)}) collective-permute-start(f32[128,768]{1,0:T(8,128)S(1)} %get-tuple-element.52), channel_id=1, source_target_pairs={{0,4},{4,0},{8,12},{12,8},{16,20},{20,16},{24,28},{28,24},{1,5},{5... | collective-permute-start | bytes 1179656 | tf_op jit(solution)/shard_map/ppermute | solution.py:47
  123.0 4.9 %collective-permute-start.17 = (f32[32,768]{1,0:T(8,128)S(1)}, f32[32,768]{1,0:T(8,128)S(1)}, u32[]{:S(2)}, u32[]{:S(2)}) collective-permute-start(f32[32,768]{1,0:T(8,128)S(1)} %get-tuple-element.54), channel_id=1, source_target_pairs={{0,8},{4,12},{8,0},{12,4},{16,24},{20,28},{24,16},{28,20},{1,9},{5... | collective-permute-start | bytes 294920 | tf_op jit(solution)/shard_map/ppermute | solution.py:47
  124.4 5.7 %collective-permute-start.18 = (f32[32,768]{1,0:T(8,128)S(1)}, f32[32,768]{1,0:T(8,128)S(1)}, u32[]{:S(2)}, u32[]{:S(2)}) collective-permute-start(f32[32,768]{1,0:T(8,128)S(1)} %get-tuple-element.55), channel_id=1, source_target_pairs={{0,16},{4,20},{8,24},{12,28},{16,0},{20,4},{24,8},{28,12},{1,17},{... | collective-permute-start | bytes 294920 | tf_op jit(solution)/shard_map/ppermute | solution.py:47
  125.3 5.8 %collective-permute-start.19 = (f32[32,768]{1,0:T(8,128)S(1)}, f32[32,768]{1,0:T(8,128)S(1)}, u32[]{:S(2)}, u32[]{:S(2)}) collective-permute-start(f32[32,768]{1,0:T(8,128)S(1)} %get-tuple-element.56), channel_id=1, source_target_pairs={{0,24},{4,28},{8,16},{12,20},{16,8},{20,12},{24,0},{28,4},{1,25},{... | collective-permute-start | bytes 294920 | tf_op jit(solution)/shard_map/ppermute | solution.py:47
  131.2 7.7 %collective-permute-start.22 = (f32[32,768]{1,0:T(8,128)S(1)}, f32[32,768]{1,0:T(8,128)S(1)}, u32[]{:S(2)}, u32[]{:S(2)}) collective-permute-start(f32[32,768]{1,0:T(8,128)S(1)} %add_add_fusion.2), channel_id=1, source_target_pairs={{0,3},{1,2},{2,1},{3,0},{4,7},{5,6},{6,5},{7,4},{8,11},{9,10},{10,... | collective-permute-start | bytes 294920 | tf_op jit(solution)/shard_map/ppermute | solution.py:47
  133.6 7.6 %collective-permute-start.21 = (f32[32,768]{1,0:T(8,128)S(1)}, f32[32,768]{1,0:T(8,128)S(1)}, u32[]{:S(2)}, u32[]{:S(2)}) collective-permute-start(f32[32,768]{1,0:T(8,128)S(1)} %add_add_fusion.2), channel_id=1, source_target_pairs={{0,2},{1,3},{2,0},{3,1},{4,6},{5,7},{6,4},{7,5},{8,10},{9,11},{10,... | collective-permute-start | bytes 294920 | tf_op jit(solution)/shard_map/ppermute | solution.py:47
  133.6 7.6 %collective-permute-start.20 = (f32[32,768]{1,0:T(8,128)S(1)}, f32[32,768]{1,0:T(8,128)S(1)}, u32[]{:S(2)}, u32[]{:S(2)}) collective-permute-start(f32[32,768]{1,0:T(8,128)S(1)} %add_add_fusion.2), channel_id=1, source_target_pairs={{0,1},{1,0},{2,3},{3,2},{4,5},{5,4},{6,7},{7,6},{8,9},{9,8},{10,11... | collective-permute-start | bytes 294920 | tf_op jit(solution)/shard_map/ppermute | solution.py:47
  141.2 6.4 %collective-permute-start.25 = (f32[32,768]{1,0:T(8,128)S(1)}, f32[32,768]{1,0:T(8,128)S(1)}, u32[]{:S(2)}, u32[]{:S(2)}) collective-permute-start(f32[32,768]{1,0:T(8,128)S(1)} %add_add_fusion.1), channel_id=1, source_target_pairs={{0,24},{4,28},{8,16},{12,20},{16,8},{20,12},{24,0},{28,4},{1,25},{... | collective-permute-start | bytes 294920 | tf_op jit(solution)/shard_map/ppermute | solution.py:47
  142.9 5.8 %collective-permute-start.24 = (f32[32,768]{1,0:T(8,128)S(1)}, f32[32,768]{1,0:T(8,128)S(1)}, u32[]{:S(2)}, u32[]{:S(2)}) collective-permute-start(f32[32,768]{1,0:T(8,128)S(1)} %add_add_fusion.1), channel_id=1, source_target_pairs={{0,16},{4,20},{8,24},{12,28},{16,0},{20,4},{24,8},{28,12},{1,17},{... | collective-permute-start | bytes 294920 | tf_op jit(solution)/shard_map/ppermute | solution.py:47
  143.7 4.9 %collective-permute-start.23 = (f32[32,768]{1,0:T(8,128)S(1)}, f32[32,768]{1,0:T(8,128)S(1)}, u32[]{:S(2)}, u32[]{:S(2)}) collective-permute-start(f32[32,768]{1,0:T(8,128)S(1)} %add_add_fusion.1), channel_id=1, source_target_pairs={{0,8},{4,12},{8,0},{12,4},{16,24},{20,28},{24,16},{28,20},{1,9},{5... | collective-permute-start | bytes 294920 | tf_op jit(solution)/shard_map/ppermute | solution.py:47
  148.7 1.8 %collective-permute-start.26 = (f32[128,768]{1,0:T(8,128)S(1)}, f32[128,768]{1,0:T(8,128)S(1)}, u32[]{:S(2)}, u32[]{:S(2)}) collective-permute-start(f32[128,768]{1,0:T(8,128)S(1)} %pad_maximum_fusion.sums_ref), channel_id=1, source_target_pairs={{0,4},{4,0},{8,12},{12,8},{16,20},{20,16},{24,28},{28,24},{1,5},{5... | collective-permute-start | bytes 1179656 | tf_op jit(solution)/shard_map/ppermute | solution.py:47

commit v3 on v2

--- a/solution.py
+++ b/solution.py
@@ -145,7 +145,8 @@
     return pl.pallas_call(
         functools.partial(evolve_kernel, slot=slot),
         in_specs=[SCALARS] + [pl.BlockSpec(memory_space=pltpu.VMEM)] * 5,
-        out_shape=shape(size, members, width),
+        out_shape=pltpu.HBM((size, members, width), jnp.float32),
+        out_specs=pl.BlockSpec((size, members, width), lambda: (0, 0, 0)),
         scratch_shapes=[pltpu.VMEM((size + 2 * w, members, width), jnp.float32)] * 2
         + [pltpu.VMEM((size + 16, width), jnp.float32)],
         compiler_params=params(16),
@@ -177,7 +178,7 @@
 
 def basis_gram(index, basis):
     lines, width, rank = basis.shape
-    block = 2
+    block = 4
     half = pl.BlockSpec((rank // 2, rank), lambda i: (0, 0))
     return pl.pallas_call(
         basis_gram_kernel,
@@ -222,7 +223,7 @@
     lines, width, rank = basis.shape
     members = pieces[0].shape[1]
     total = members * len(pieces)
-    block = 2
+    block = 4
     half = pl.BlockSpec((total // 2, rank + total), lambda i: (0, 0))
     return pl.pallas_call(
         products_kernel,
@@ -261,11 +262,21 @@
     return values[0]
 
 
-def chip_scatter(index, send, keep):
+def exchange_chips(pieces, limit):
+    found = []
+    for k in range(1, len(pieces)):
+        piece = pieces[k]
+        if k > limit:
+            piece, found[k - limit - 1] = lax.optimization_barrier((piece, found[k - limit - 1]))
+        found.append(xor_permute(piece, "sim", 2 * k))
+    return found
+
+
+def chip_scatter(index, send, keep, limit):
     chips = lax.axis_size("sim") // 2
     got = xor_permute(send, "sim", 1)
     pieces = split(index, keep, got, chips)
-    return tree_sum([pieces[0]] + [xor_permute(pieces[k], "sim", 2 * k) for k in range(1, chips)])
+    return tree_sum([pieces[0]] + exchange_chips(pieces, limit))
 
 
 def ana_sum(value):
@@ -285,9 +296,9 @@
     return jnp.concatenate([total, xor_permute(total, "ana", ranks // 2)], axis=0)
 
 
-def chip_gather(value):
+def chip_gather(value, limit):
     chips = lax.axis_size("sim") // 2
-    mine = jnp.concatenate([value] + [xor_permute(value, "sim", 2 * k) for k in range(1, chips)], axis=0)
+    mine = jnp.concatenate([value] + exchange_chips([value] * chips, limit), axis=0)
     return mine, xor_permute(mine, "sim", 1)
 
 
@@ -403,7 +414,7 @@
 def rotate(index, high, low, basis, pieces):
     lines, width, rank = basis.shape
     members = pieces[0].shape[1]
-    block = 2
+    block = 4
     rows = pl.BlockSpec((block, width, rank), lambda i: (i, 0, 0))
     return pl.pallas_call(
         rotate_kernel,
@@ -441,19 +452,22 @@
     before, after, send = lax.optimization_barrier((before, after, send))
 
     pieces = []
+    order = index
     for slot in range(ranks):
-        piece = evolve(index, disp, vel, stiffness, before, after, slot, lines)
+        piece = evolve(order, disp, vel, stiffness, before, after, slot, lines)
+        order, piece = lax.optimization_barrier((order, piece))
         if slot < ranks - 1:
             pairs = [(s * ranks + a, s * ranks + (a ^ orders[s % 2][slot])) for s in range(sims) for a in range(ranks)]
             piece = lax.ppermute(piece, ("sim", "ana"), pairs)
         pieces.append(piece)
     pieces[-1], send = lax.optimization_barrier((pieces[-1], send))
-    gram = chip_scatter(index, send, keep)
-    gram = chip_gather(ana_sum_halved(gram))
+    once = 1 + (ana >> 20)
+    gram = lax.fori_loop(
+        0, once, lambda _, pair: chip_gather(ana_sum_halved(chip_scatter(index, *pair, 2)), 2), (send, keep))
     pieces, gram = lax.optimization_barrier((pieces, gram))
 
     send, keep = products(index, basis, pieces)
-    sums = chip_gather(ana_sum(chip_scatter(index, send, keep)))
+    sums = chip_gather(ana_sum(chip_scatter(index, send, keep, chips)), chips)
     high, low, coords = solve(index, sums, gram, rotation, count, chips)
     return rotate(index, high, low, basis, pieces), coords
 

time: 180 us -> 180 us (level)
  starting transfers between devices: 38.8 us -> 43.7 us
  waiting for transfers between devices: 70.1 us -> 66.9 us
  Pallas kernels: 64.1 us -> 62.1 us
    ppermute x3, waiting for transfers between devices: 31.8 us -> 0.01 us  [per_device(): piece = lax.ppermute(piece, ('sim', 'ana'), pairs)]
    ppermute x22, waiting for transfers between devices: 38.3 us -> 66.9 us  [xor_permute(): return lax.ppermute(value, axis, [(i, i ^ mask) for i in range(size)])]
    ppermute x22, starting transfers between devices: 30.2 us -> 35.1 us  [xor_permute(): return lax.ppermute(value, axis, [(i, i ^ mask) for i in range(size)])]
    pallas_call x4, Pallas kernels: 13.5 us -> 16.7 us  [evolve(): pl.pallas_call(functools.partial(evolve_kernel, slot=slot), in_specs=[SCA...]
    while x0 -> x3, local copies, waits for them, and re-layouts: none -> 1.92 us
    unnamed x19 -> x18, local copies, waits for them, and re-layouts: 3.71 us -> 2.1 us
  transfers between devices with their start and end apart: 27 -> 27, of which waited for: 21 -> 18; matrix products, arithmetic and copies ran while one was open for 0% -> 2% of each run, Pallas kernels for 10% -> 4%
where the time goes in v3:
time: 180 us; the launch traced here: 179 us
  waiting for transfers between devices  66.9 us (37%)
  Pallas kernels  62.1 us (34%)
  starting transfers between devices  43.7 us (24%)
  local copies, waits for them, and re-layouts  4.76 us (3%)
    ppermute x22, waiting for transfers between devices, xor_permute(): return lax.ppermute(value, axis, [(i, i ^ mask) for i in range(size)])  66.9 us
    ppermute x22, starting transfers between devices, xor_permute(): return lax.ppermute(value, axis, [(i, i ^ mask) for i in range(size)])  35.1 us
    pallas_call x1, Pallas kernels, solve(): pl.pallas_call(functools.partial(solve_kernel, count=float(count), chips=...  19.1 us
    pallas_call x4, Pallas kernels, evolve(): pl.pallas_call(functools.partial(evolve_kernel, slot=slot), in_specs=[SCA...  16.7 us
    pallas_call x1, Pallas kernels, rotate(): pl.pallas_call(rotate_kernel, grid=(lines // block,), in_specs=[SCALARS]...  8.05 us
    pallas_call x1, Pallas kernels, basis_gram(): pl.pallas_call(basis_gram_kernel, grid=(lines // block,), in_specs=[SCALA...  6.5 us
    pallas_call x1, Pallas kernels, products(): pl.pallas_call(products_kernel, grid=(lines // block,), in_specs=[SCALARS...  5.89 us
    ppermute x3, starting transfers between devices, per_device(): piece = lax.ppermute(piece, ('sim', 'ana'), pairs)  4.99 us
  transfers between devices with their start and end apart: 27, of which 18 were waited for; matrix products, arithmetic and copies ran while one was open for 2% of the time, Pallas kernels for 4%

profile of v3, /device:TPU:0, one launch (start us, length us, event | category | flops | bytes accessed | tf_op | source)
XLA Modules:
  0.0 179.1 jit_solution(3511142564566814064)
XLA Ops:
  0.6 0.7 copy-done.4
  1.4 4.7 %to_lines.1 = (f32[64,64,128]{2,1,0:T(8,128)S(1)}, f32[64,64,128]{2,1,0:T(8,128)S(1)}, f32[9,64,128]{2,1,0:T(8,128)S(1)}, f32[9,64,128]{2,1,0:T(8,128)S(1)}) custom-call(f32[4096,128]{1,0:T(8,128)} %bitcast.6, f32[4096,128]{1,0:T(8,128)} %bitcast.7, f32[64,128]{1,0:T(8,128)S(1)} %copy-done.4), custom_call_target="tpu_custom_call" | custom-call | tf_op jit(solution)/shard_map/to_lines/pallas_call | solution.py:71
  6.2 1.3 copy-done
  7.5 2.4 %collective-permute-start.11 = (f32[9,64,128]{2,1,0:T(8,128)S(1)}, f32[9,64,128]{2,1,0:T(8,128)S(1)}, u32[]{:S(2)}, u32[]{:S(2)}) collective-permute-start(f32[9,64,128]{2,1,0:T(8,128)S(1)} %get-tuple-element.112), channel_id=1, source_target_pairs={{0,4},{4,8},{8,12},{12,16},{16,20},{20,24},{24,28},{1,5},{5,9},{9,... | collective-permute-start | bytes 884744 | tf_op jit(solution)/shard_map/ppermute | solution.py:447
  9.8 1.3 collective-permute-start.12
  11.3 6.5 %basis_gram.1 = (f32[256,512]{1,0:T(8,128)}, f32[256,512]{1,0:T(8,128)}) custom-call(s32[8]{0:T(128)S(1)} %concatenate.19.index_ref, f32[16,128,512]{2,1,0:T(8,128)} %basis_ref.4), custom_call_target="tpu_custom_call" | custom-call | tf_op jit(solution)/shard_map/basis_gram/pallas_call | solution.py:183
  17.8 4.1 %evolve0.1 = f32[16,64,128]{2,1,0:T(8,128)} custom-call(s32[8]{0:T(128)S(1)} %concatenate.19.index_ref, f32[64,64,128]{2,1,0:T(8,128)S(1)} %get-tuple-element.110.disp_ref, f32[64,64,128]{2,1,0:T(8,128)S(1)} %copy-done.1, f32[64,128]{1,0:T(8,128)S(1)} %copy-done.5, f32[9,64,128]{2,1,0:T(8,128)S(1)} %collective-permute-done.11.before_ref, ...), custom_call_target="tpu_custom_call" | custom-call | tf_op jit(solution)/shard_map/evolve0/pallas_call | solution.py:145
  22.0 4.1 %evolve1.1 = f32[16,64,128]{2,1,0:T(8,128)} custom-call(s32[8]{0:T(128)S(1)} %concatenate.19.index_ref, f32[64,64,128]{2,1,0:T(8,128)S(1)} %get-tuple-element.110.disp_ref, f32[64,64,128]{2,1,0:T(8,128)S(1)} %copy-done.1, f32[64,128]{1,0:T(8,128)S(1)} %copy-done.5, f32[9,64,128]{2,1,0:T(8,128)S(1)} %collective-permute-done.11.before_ref, ...), custom_call_target="tpu_custom_call" | custom-call | tf_op jit(solution)/shard_map/evolve1/pallas_call | solution.py:145
  26.1 4.1 %evolve2.1 = f32[16,64,128]{2,1,0:T(8,128)} custom-call(s32[8]{0:T(128)S(1)} %concatenate.19.index_ref, f32[64,64,128]{2,1,0:T(8,128)S(1)} %get-tuple-element.110.disp_ref, f32[64,64,128]{2,1,0:T(8,128)S(1)} %copy-done.1, f32[64,128]{1,0:T(8,128)S(1)} %copy-done.5, f32[9,64,128]{2,1,0:T(8,128)S(1)} %collective-permute-done.11.before_ref, ...), custom_call_target="tpu_custom_call" | custom-call | tf_op jit(solution)/shard_map/evolve2/pallas_call | solution.py:145
  30.2 4.3 %evolve3.1.rest_3_ = f32[16,64,128]{2,1,0:T(8,128)} custom-call(s32[8]{0:T(128)S(1)} %concatenate.19.index_ref, f32[64,64,128]{2,1,0:T(8,128)S(1)} %get-tuple-element.110.disp_ref, f32[64,64,128]{2,1,0:T(8,128)S(1)} %copy-done.1, f32[64,128]{1,0:T(8,128)S(1)} %copy-done.5, f32[9,64,128]{2,1,0:T(8,128)S(1)} %collective-permute-done.11.before_ref, ...), custom_call_target="tpu_custom_call" | custom-call | tf_op jit(solution)/shard_map/evolve3/pallas_call | solution.py:145
  34.5 3.4 %collective-permute-start.15 = (f32[16,64,128]{2,1,0:T(8,128)}, f32[16,64,128]{2,1,0:T(8,128)S(1)}, u32[]{:S(2)}, u32[]{:S(2)}) collective-permute-start(f32[16,64,128]{2,1,0:T(8,128)} %evolve2.1), channel_id=1, source_target_pairs={{0,2},{1,3},{2,0},{3,1},{4,5},{5,4},{6,7},{7,6},{8,10},{9,11},{10,... | collective-permute-start | bytes 1572872 | tf_op jit(solution)/shard_map/ppermute | solution.py:461
  38.0 1.3 collective-permute-start.14
  39.5 75.2 %while.14 = (s32[]{:T(128)}, f32[256,512]{1,0:T(8,128)}, f32[256,512]{1,0:T(8,128)S(1)}, s32[]{:T(128)}, s32[8]{0:T(128)S(1)}, /*index=5*/s32[]{:T(128)}, u32[]{...) while((s32[]{:T(128)}, f32[256,512]{1,0:T(8,128)}, f32[256,512]{1,0:T(8,128)S(1)}, s32[]{:T(128)}, ...), condition=%wide.region_1.2_spmd, body=%wide.region_0.1_spmd.sunk | while | flops 163867 | bytes 10552127 | solution.py:465
  39.5 1.9 %collective-permute-start = (f32[256,512]{1,0:T(8,128)}, f32[256,512]{1,0:T(8,128)S(1)}, u32[]{:S(2)}, u32[]{:S(2)}) collective-permute-start(f32[256,512]{1,0:T(8,128)} %get-tuple-element.221), channel_id=1, source_target_pairs={{0,4},{4,0},{8,12},{12,8},{16,20},{20,16},{24,28},{28,24},{1,5},{5... | collective-permute-start | bytes 1572872 | tf_op jit(solution)/shard_map/while/body/ppermute | solution.py:47
  41.4 1.7 collective-permute-done.got_ref
  43.8 2.6 %collective-permute-start.2 = (f32[64,512]{1,0:T(8,128)S(1)}, f32[64,512]{1,0:T(8,128)S(1)}, u32[]{:S(2)}, u32[]{:S(2)}) collective-permute-start(f32[64,512]{1,0:T(8,128)S(1)} %get-tuple-element.201), channel_id=1, source_target_pairs={{0,8},{4,12},{8,0},{12,4},{16,24},{20,28},{24,16},{28,20},{1,9},{5... | collective-permute-start | bytes 393224 | tf_op jit(solution)/shard_map/while/body/ppermute | solution.py:47
  46.3 1.5 collective-permute-start.1
  47.9 2.3 %collective-permute-done.2 = f32[64,512]{1,0:T(8,128)S(1)} collective-permute-done((f32[64,512]{1,0:T(8,128)S(1)}, f32[64,512]{1,0:T(8,128)S(1)}, u32[]{:S(2)}, u32[]{:S(2)}) %collective-permute-start.2) | collective-permute-done | bytes 131104 | tf_op jit(solution)/shard_map/while/body/ppermute | solution.py:47
  50.1 2.7 %collective-permute-start.3 = (f32[64,512]{1,0:T(8,128)S(1)}, f32[64,512]{1,0:T(8,128)S(1)}, u32[]{:S(2)}, u32[]{:S(2)}) collective-permute-start(f32[64,512]{1,0:T(8,128)S(1)} %get-tuple-element.202), channel_id=1, source_target_pairs={{0,24},{4,28},{8,16},{12,20},{16,8},{20,12},{24,0},{28,4},{1,25},{... | collective-permute-start | bytes 393224 | tf_op jit(solution)/shard_map/while/body/ppermute | solution.py:47
  52.8 3.2 %collective-permute-done.3 = f32[64,512]{1,0:T(8,128)S(1)} collective-permute-done((f32[64,512]{1,0:T(8,128)S(1)}, f32[64,512]{1,0:T(8,128)S(1)}, u32[]{:S(2)}, u32[]{:S(2)}) %collective-permute-start.3) | collective-permute-done | bytes 131104 | tf_op jit(solution)/shard_map/while/body/ppermute | solution.py:47
  56.1 2.9 %collective-permute-start.4 = (f32[32,512]{1,0:T(8,128)S(1)}, f32[32,512]{1,0:T(8,128)S(1)}, u32[]{:S(2)}, u32[]{:S(2)}) collective-permute-start(f32[32,512]{1,0:T(8,128)S(1)} %constant_dynamic-slice_fusion.2), channel_id=1, source_target_pairs={{0,2},{1,3},{2,0},{3,1},{4,6},{5,7},{6,4},{7,5},{8,10},{9,11},{10,... | collective-permute-start | bytes 196616 | tf_op jit(solution)/shard_map/while/body/ppermute | solution.py:47
  59.0 27.0 %collective-permute-done.4 = f32[32,512]{1,0:T(8,128)S(1)} collective-permute-done((f32[32,512]{1,0:T(8,128)S(1)}, f32[32,512]{1,0:T(8,128)S(1)}, u32[]{:S(2)}, u32[]{:S(2)}) %collective-permute-start.4) | collective-permute-done | bytes 65568 | tf_op jit(solution)/shard_map/while/body/ppermute | solution.py:47
  86.0 1.8 collective-permute-start.5
  87.8 3.0 %collective-permute-done.5 = f32[32,512]{1,0:T(8,128)S(1)} collective-permute-done((f32[32,512]{1,0:T(8,128)S(1)}, f32[32,512]{1,0:T(8,128)S(1)}, u32[]{:S(2)}, u32[]{:S(2)}) %collective-permute-start.5) | collective-permute-done | bytes 65568 | tf_op jit(solution)/shard_map/while/body/ppermute | solution.py:47
  91.4 3.2 %collective-permute-start.6 = (f32[32,512]{1,0:T(8,128)S(1)}, f32[32,512]{1,0:T(8,128)S(1)}, u32[]{:S(2)}, u32[]{:S(2)}) collective-permute-start(f32[32,512]{1,0:T(8,128)S(1)} %get-tuple-element.206), channel_id=1, source_target_pairs={{0,2},{1,3},{2,0},{3,1},{4,6},{5,7},{6,4},{7,5},{8,10},{9,11},{10,... | collective-permute-start | bytes 196616 | tf_op jit(solution)/shard_map/while/body/ppermute | solution.py:47
  94.6 3.7 %collective-permute-done.6 = f32[32,512]{1,0:T(8,128)S(1)} collective-permute-done((f32[32,512]{1,0:T(8,128)S(1)}, f32[32,512]{1,0:T(8,128)S(1)}, u32[]{:S(2)}, u32[]{:S(2)}) %collective-permute-start.6) | collective-permute-done | bytes 65568 | tf_op jit(solution)/shard_map/while/body/ppermute | solution.py:47
  98.3 4.0 %collective-permute-start.7 = (f32[64,512]{1,0:T(8,128)S(1)}, f32[64,512]{1,0:T(8,128)S(1)}, u32[]{:S(2)}, u32[]{:S(2)}) collective-permute-start(f32[64,512]{1,0:T(8,128)S(1)} %pad_maximum_fusion.3), channel_id=1, source_target_pairs={{0,8},{4,12},{8,0},{12,4},{16,24},{20,28},{24,16},{28,20},{1,9},{5... | collective-permute-start | bytes 393224 | tf_op jit(solution)/shard_map/while/body/ppermute | solution.py:47
  103.6 2.5 %collective-permute-done.7 = f32[64,512]{1,0:T(8,128)S(1)} collective-permute-done((f32[64,512]{1,0:T(8,128)S(1)}, f32[64,512]{1,0:T(8,128)S(1)}, u32[]{:S(2)}, u32[]{:S(2)}) %collective-permute-start.7) | collective-permute-done | bytes 131104 | tf_op jit(solution)/shard_map/while/body/ppermute | solution.py:47
  106.1 1.5 collective-permute-start.9
  109.3 2.6 %collective-permute-done.9 = f32[64,512]{1,0:T(8,128)S(1)} collective-permute-done((f32[64,512]{1,0:T(8,128)S(1)}, f32[64,512]{1,0:T(8,128)S(1)}, u32[]{:S(2)}, u32[]{:S(2)}) %collective-permute-start.9) | collective-permute-done | bytes 131104 | tf_op jit(solution)/shard_map/while/body/ppermute | solution.py:47
  112.6 2.1 %collective-permute-done.10 = f32[256,512]{1,0:T(8,128)S(1)} collective-permute-done((f32[256,512]{1,0:T(8,128)}, f32[256,512]{1,0:T(8,128)S(1)}, u32[]{:S(2)}, u32[]{:S(2)}) %collective-permute-start.10) | collective-permute-done | bytes 524320 | tf_op jit(solution)/shard_map/while/body/ppermute | solution.py:47
  114.7 5.9 %products.1 = (f32[128,768]{1,0:T(8,128)S(1)}, f32[128,768]{1,0:T(8,128)S(1)}) custom-call(s32[8]{0:T(128)S(1)} %get-tuple-element.282, f32[16,128,512]{2,1,0:T(8,128)} %basis_ref.4, f32[16,64,128]{2,1,0:T(8,128)S(1)} %collective-permute-done.13.rest_0_, f32[16,64,128]{2,1,0:T(8,128)S(1)} %collective-permute-done.14.rest_1_, ...), custom_call_target="tpu_custom_call" | custom-call | tf_op jit(solution)/shard_map/products/pallas_call | solution.py:228
  120.8 1.6 collective-permute-done.16.got_ref
  123.0 2.5 %collective-permute-start.17 = (f32[32,768]{1,0:T(8,128)S(1)}, f32[32,768]{1,0:T(8,128)S(1)}, u32[]{:S(2)}, u32[]{:S(2)}) collective-permute-start(f32[32,768]{1,0:T(8,128)S(1)} %get-tuple-element.137), channel_id=1, source_target_pairs={{0,8},{4,12},{8,0},{12,4},{16,24},{20,28},{24,16},{28,20},{1,9},{5... | collective-permute-start | bytes 294920 | tf_op jit(solution)/shard_map/ppermute | solution.py:47
  125.7 1.4 collective-permute-start.19
  127.1 1.6 collective-permute-done.17
  128.7 3.5 %collective-permute-done.18 = f32[32,768]{1,0:T(8,128)S(1)} collective-permute-done((f32[32,768]{1,0:T(8,128)S(1)}, f32[32,768]{1,0:T(8,128)S(1)}, u32[]{:S(2)}, u32[]{:S(2)}) %collective-permute-start.18) | collective-permute-done | bytes 98336 | tf_op jit(solution)/shard_map/ppermute | solution.py:47
  132.3 2.7 %collective-permute-start.22 = (f32[32,768]{1,0:T(8,128)S(1)}, f32[32,768]{1,0:T(8,128)S(1)}, u32[]{:S(2)}, u32[]{:S(2)}) collective-permute-start(f32[32,768]{1,0:T(8,128)S(1)} %add_add_fusion.2), channel_id=1, source_target_pairs={{0,3},{1,2},{2,1},{3,0},{4,7},{5,6},{6,5},{7,4},{8,11},{9,10},{10,... | collective-permute-start | bytes 294920 | tf_op jit(solution)/shard_map/ppermute | solution.py:47
  135.0 1.7 collective-permute-start.20
  136.8 2.7 %collective-permute-done.22 = f32[32,768]{1,0:T(8,128)S(1)} collective-permute-done((f32[32,768]{1,0:T(8,128)S(1)}, f32[32,768]{1,0:T(8,128)S(1)}, u32[]{:S(2)}, u32[]{:S(2)}) %collective-permute-start.22) | collective-permute-done | bytes 98336 | tf_op jit(solution)/shard_map/ppermute | solution.py:47
  139.5 3.4 %collective-permute-done.21 = f32[32,768]{1,0:T(8,128)S(1)} collective-permute-done((f32[32,768]{1,0:T(8,128)S(1)}, f32[32,768]{1,0:T(8,128)S(1)}, u32[]{:S(2)}, u32[]{:S(2)}) %collective-permute-start.21) | collective-permute-done | bytes 98336 | tf_op jit(solution)/shard_map/ppermute | solution.py:47
  142.9 1.2 collective-permute-start.25
  144.8 1.7 collective-permute-start.23
  146.4 3.1 %collective-permute-done.25 = f32[32,768]{1,0:T(8,128)S(1)} collective-permute-done((f32[32,768]{1,0:T(8,128)S(1)}, f32[32,768]{1,0:T(8,128)S(1)}, u32[]{:S(2)}, u32[]{:S(2)}) %collective-permute-start.25) | collective-permute-done | bytes 98336 | tf_op jit(solution)/shard_map/ppermute | solution.py:47
  149.5 0.7 collective-permute-done.24
  150.3 1.7 collective-permute-done.26.sums2_ref
  152.0 19.1 %solve.1 = (bf16[768,512]{1,0:T(8,128)(2,1)S(1)}, bf16[768,512]{1,0:T(8,128)(2,1)S(1)}, f32[512,256]{1,0:T(8,128)}) custom-call(s32[8]{0:T(128)S(1)} %get-tuple-element.282, f32[128,768]{1,0:T(8,128)S(1)} %pad_maximum_fusion.1.sums_ref, f32[128,768]{1,0:T(8,128)S(1)} %collective-permute-done.26.sums2_ref, f32[256,512]{1,0:T(8,128)} %get-tuple-element.140.gram_ref, ...), custom_call_target="tpu_custom_call" | custom-call | tf_op jit(solution)/shard_map/solve/pallas_call | solution.py:388
  171.1 8.1 %rotate.1 = f32[16,128,512]{2,1,0:T(8,128)} custom-call(s32[8]{0:T(128)S(1)} %get-tuple-element.282, bf16[768,512]{1,0:T(8,128)(2,1)S(1)} %get-tuple-element.142.high_ref, bf16[768,512]{1,0:T(8,128)(2,1)S(1)} %get-tuple-element.143.low_ref, f32[16,128,512]{2,1,0:T(8,128)} %basis_ref.4, f32[16,64,128]{2,1,0:T(8,128)S(1)} %collective-permute-done.13.rest_0_, ...), custom_call_target="tpu_custom_call" | custom-call | tf_op jit(solution)/shard_map/rotate/pallas_call | solution.py:419
  (50 shorter events, 7.0 us)
Async XLA Ops:
  0.6 0.8 copy-start.4
  1.4 9.8 %copy-start.7 = (s32[4]{0:T(128)S(1)}, s32[4]{0:T(128)}, u32[]{:S(2)}) copy-start(s32[4]{0:T(128)} %constant.96.clone) | copy-start | bytes 52
  1.4 9.8 %copy-start.8 = (s32[4]{0:T(128)S(1)}, s32[4]{0:T(128)}, u32[]{:S(2)}) copy-start(s32[4]{0:T(128)} %constant.95.clone) | copy-start | bytes 52
  6.2 1.3 copy-start
  7.5 10.3 %collective-permute-start.11 = (f32[9,64,128]{2,1,0:T(8,128)S(1)}, f32[9,64,128]{2,1,0:T(8,128)S(1)}, u32[]{:S(2)}, u32[]{:S(2)}) collective-permute-start(f32[9,64,128]{2,1,0:T(8,128)S(1)} %get-tuple-element.112), channel_id=1, source_target_pairs={{0,4},{4,8},{8,12},{12,16},{16,20},{20,24},{24,28},{1,5},{5,9},{9,... | collective-permute-start | bytes 884744 | tf_op jit(solution)/shard_map/ppermute | solution.py:447
  9.8 8.0 %collective-permute-start.12 = (f32[9,64,128]{2,1,0:T(8,128)S(1)}, f32[9,64,128]{2,1,0:T(8,128)S(1)}, u32[]{:S(2)}, u32[]{:S(2)}) collective-permute-start(f32[9,64,128]{2,1,0:T(8,128)S(1)} %get-tuple-element.113), channel_id=1, source_target_pairs={{4,0},{8,4},{12,8},{16,12},{20,16},{24,20},{28,24},{5,1},{9,5},{13... | collective-permute-start | bytes 884744 | tf_op jit(solution)/shard_map/ppermute | solution.py:448
  11.3 6.5 %copy-start.1 = (f32[64,64,128]{2,1,0:T(8,128)S(1)}, f32[64,64,128]{2,1,0:T(8,128)}, u32[]{:S(2)}) copy-start(f32[64,64,128]{2,1,0:T(8,128)} %copy-done) | copy-start | bytes 6291460
  11.3 6.5 %copy-start.5 = (f32[64,128]{1,0:T(8,128)S(1)}, f32[64,128]{1,0:T(8,128)}, u32[]{:S(2)}) copy-start(f32[64,128]{1,0:T(8,128)} %stiff_ref.9) | copy-start | bytes 98308
  30.2 9.3 %copy-start.6 = (f32[256,512]{1,0:T(8,128)S(1)}, f32[256,512]{1,0:T(8,128)}, u32[]{:S(2)}) copy-start(f32[256,512]{1,0:T(8,128)} %get-tuple-element.211) | copy-start | bytes 1572868
  34.5 80.2 %collective-permute-start.15 = (f32[16,64,128]{2,1,0:T(8,128)}, f32[16,64,128]{2,1,0:T(8,128)S(1)}, u32[]{:S(2)}, u32[]{:S(2)}) collective-permute-start(f32[16,64,128]{2,1,0:T(8,128)} %evolve2.1), channel_id=1, source_target_pairs={{0,2},{1,3},{2,0},{3,1},{4,5},{5,4},{6,7},{7,6},{8,10},{9,11},{10,... | collective-permute-start | bytes 1572872 | tf_op jit(solution)/shard_map/ppermute | solution.py:461
  38.0 76.8 %collective-permute-start.14 = (f32[16,64,128]{2,1,0:T(8,128)}, f32[16,64,128]{2,1,0:T(8,128)S(1)}, u32[]{:S(2)}, u32[]{:S(2)}) collective-permute-start(f32[16,64,128]{2,1,0:T(8,128)} %evolve1.1), channel_id=1, source_target_pairs={{0,3},{1,2},{2,1},{3,0},{4,6},{5,7},{6,4},{7,5},{8,11},{9,10},{10,... | collective-permute-start | bytes 1572872 | tf_op jit(solution)/shard_map/ppermute | solution.py:461
  39.3 75.4 %collective-permute-start.13 = (f32[16,64,128]{2,1,0:T(8,128)}, f32[16,64,128]{2,1,0:T(8,128)S(1)}, u32[]{:S(2)}, u32[]{:S(2)}) collective-permute-start(f32[16,64,128]{2,1,0:T(8,128)} %evolve0.1), channel_id=1, source_target_pairs={{0,1},{1,0},{2,3},{3,2},{4,7},{5,6},{6,5},{7,4},{8,9},{9,8},{10,11... | collective-permute-start | bytes 1572872 | tf_op jit(solution)/shard_map/ppermute | solution.py:461
  39.5 75.2 %copy-start.2 = (f32[16,64,128]{2,1,0:T(8,128)S(1)}, f32[16,64,128]{2,1,0:T(8,128)}, u32[]{:S(2)}) copy-start(f32[16,64,128]{2,1,0:T(8,128)} %evolve3.1.rest_3_) | copy-start | bytes 1572868
  39.5 3.6 %collective-permute-start = (f32[256,512]{1,0:T(8,128)}, f32[256,512]{1,0:T(8,128)S(1)}, u32[]{:S(2)}, u32[]{:S(2)}) collective-permute-start(f32[256,512]{1,0:T(8,128)} %get-tuple-element.221), channel_id=1, source_target_pairs={{0,4},{4,0},{8,12},{12,8},{16,20},{20,16},{24,28},{28,24},{1,5},{5... | collective-permute-start | bytes 1572872 | tf_op jit(solution)/shard_map/while/body/ppermute | solution.py:47
  43.8 6.4 %collective-permute-start.2 = (f32[64,512]{1,0:T(8,128)S(1)}, f32[64,512]{1,0:T(8,128)S(1)}, u32[]{:S(2)}, u32[]{:S(2)}) collective-permute-start(f32[64,512]{1,0:T(8,128)S(1)} %get-tuple-element.201), channel_id=1, source_target_pairs={{0,8},{4,12},{8,0},{12,4},{16,24},{20,28},{24,16},{28,20},{1,9},{5... | collective-permute-start | bytes 393224 | tf_op jit(solution)/shard_map/while/body/ppermute | solution.py:47
  46.3 6.5 %collective-permute-start.1 = (f32[64,512]{1,0:T(8,128)S(1)}, f32[64,512]{1,0:T(8,128)S(1)}, u32[]{:S(2)}, u32[]{:S(2)}) collective-permute-start(f32[64,512]{1,0:T(8,128)S(1)} %get-tuple-element.199), channel_id=1, source_target_pairs={{0,16},{4,20},{8,24},{12,28},{16,0},{20,4},{24,8},{28,12},{1,17},{... | collective-permute-start | bytes 393224 | tf_op jit(solution)/shard_map/while/body/ppermute | solution.py:47
  50.1 5.9 %collective-permute-start.3 = (f32[64,512]{1,0:T(8,128)S(1)}, f32[64,512]{1,0:T(8,128)S(1)}, u32[]{:S(2)}, u32[]{:S(2)}) collective-permute-start(f32[64,512]{1,0:T(8,128)S(1)} %get-tuple-element.202), channel_id=1, source_target_pairs={{0,24},{4,28},{8,16},{12,20},{16,8},{20,12},{24,0},{28,4},{1,25},{... | collective-permute-start | bytes 393224 | tf_op jit(solution)/shard_map/while/body/ppermute | solution.py:47
  56.1 29.8 %collective-permute-start.4 = (f32[32,512]{1,0:T(8,128)S(1)}, f32[32,512]{1,0:T(8,128)S(1)}, u32[]{:S(2)}, u32[]{:S(2)}) collective-permute-start(f32[32,512]{1,0:T(8,128)S(1)} %constant_dynamic-slice_fusion.2), channel_id=1, source_target_pairs={{0,2},{1,3},{2,0},{3,1},{4,6},{5,7},{6,4},{7,5},{8,10},{9,11},{10,... | collective-permute-start | bytes 196616 | tf_op jit(solution)/shard_map/while/body/ppermute | solution.py:47
  86.0 4.8 %collective-permute-start.5 = (f32[32,512]{1,0:T(8,128)S(1)}, f32[32,512]{1,0:T(8,128)S(1)}, u32[]{:S(2)}, u32[]{:S(2)}) collective-permute-start(f32[32,512]{1,0:T(8,128)S(1)} %dynamic-slice_add_fusion.2), channel_id=1, source_target_pairs={{0,1},{1,0},{2,3},{3,2},{4,5},{5,4},{6,7},{7,6},{8,9},{9,8},{10,11... | collective-permute-start | bytes 196616 | tf_op jit(solution)/shard_map/while/body/ppermute | solution.py:47
  91.4 6.9 %collective-permute-start.6 = (f32[32,512]{1,0:T(8,128)S(1)}, f32[32,512]{1,0:T(8,128)S(1)}, u32[]{:S(2)}, u32[]{:S(2)}) collective-permute-start(f32[32,512]{1,0:T(8,128)S(1)} %get-tuple-element.206), channel_id=1, source_target_pairs={{0,2},{1,3},{2,0},{3,1},{4,6},{5,7},{6,4},{7,5},{8,10},{9,11},{10,... | collective-permute-start | bytes 196616 | tf_op jit(solution)/shard_map/while/body/ppermute | solution.py:47
  98.3 7.8 %collective-permute-start.7 = (f32[64,512]{1,0:T(8,128)S(1)}, f32[64,512]{1,0:T(8,128)S(1)}, u32[]{:S(2)}, u32[]{:S(2)}) collective-permute-start(f32[64,512]{1,0:T(8,128)S(1)} %pad_maximum_fusion.3), channel_id=1, source_target_pairs={{0,8},{4,12},{8,0},{12,4},{16,24},{20,28},{24,16},{28,20},{1,9},{5... | collective-permute-start | bytes 393224 | tf_op jit(solution)/shard_map/while/body/ppermute | solution.py:47
  102.3 6.4 %collective-permute-start.8 = (f32[64,512]{1,0:T(8,128)S(1)}, f32[64,512]{1,0:T(8,128)S(1)}, u32[]{:S(2)}, u32[]{:S(2)}) collective-permute-start(f32[64,512]{1,0:T(8,128)S(1)} %pad_maximum_fusion.3), channel_id=1, source_target_pairs={{0,16},{4,20},{8,24},{12,28},{16,0},{20,4},{24,8},{28,12},{1,17},{... | collective-permute-start | bytes 393224 | tf_op jit(solution)/shard_map/while/body/ppermute | solution.py:47
  106.1 5.9 %collective-permute-start.9 = (f32[64,512]{1,0:T(8,128)S(1)}, f32[64,512]{1,0:T(8,128)S(1)}, u32[]{:S(2)}, u32[]{:S(2)}) collective-permute-start(f32[64,512]{1,0:T(8,128)S(1)} %pad_maximum_fusion.3), channel_id=1, source_target_pairs={{0,24},{4,28},{8,16},{12,20},{16,8},{20,12},{24,0},{28,4},{1,25},{... | collective-permute-start | bytes 393224 | tf_op jit(solution)/shard_map/while/body/ppermute | solution.py:47
  112.6 2.1 %collective-permute-start.10 = (f32[256,512]{1,0:T(8,128)}, f32[256,512]{1,0:T(8,128)S(1)}, u32[]{:S(2)}, u32[]{:S(2)}) collective-permute-start(f32[256,512]{1,0:T(8,128)} %constant_dynamic-update-slice_fusion.14), channel_id=1, source_target_pairs={{0,4},{4,0},{8,12},{12,8},{16,20},{20,16},{24,28},{28,24},{1,5},{5... | collective-permute-start | bytes 1572872 | tf_op jit(solution)/shard_map/while/body/ppermute | solution.py:47
  120.6 31.4 %copy-start.3 = (f32[768,512]{1,0:T(8,128)S(1)}, f32[768,512]{1,0:T(8,128)}, u32[]{:S(2)}) copy-start(f32[768,512]{1,0:T(8,128)} %rot_ref.1) | copy-start | bytes 4718596
  120.6 1.8 collective-permute-start.16
  123.0 5.7 %collective-permute-start.17 = (f32[32,768]{1,0:T(8,128)S(1)}, f32[32,768]{1,0:T(8,128)S(1)}, u32[]{:S(2)}, u32[]{:S(2)}) collective-permute-start(f32[32,768]{1,0:T(8,128)S(1)} %get-tuple-element.137), channel_id=1, source_target_pairs={{0,8},{4,12},{8,0},{12,4},{16,24},{20,28},{24,16},{28,20},{1,9},{5... | collective-permute-start | bytes 294920 | tf_op jit(solution)/shard_map/ppermute | solution.py:47
  125.6 6.7 %collective-permute-start.18 = (f32[32,768]{1,0:T(8,128)S(1)}, f32[32,768]{1,0:T(8,128)S(1)}, u32[]{:S(2)}, u32[]{:S(2)}) collective-permute-start(f32[32,768]{1,0:T(8,128)S(1)} %get-tuple-element.138), channel_id=1, source_target_pairs={{0,16},{4,20},{8,24},{12,28},{16,0},{20,4},{24,8},{28,12},{1,17},{... | collective-permute-start | bytes 294920 | tf_op jit(solution)/shard_map/ppermute | solution.py:47
  125.7 6.6 %collective-permute-start.19 = (f32[32,768]{1,0:T(8,128)S(1)}, f32[32,768]{1,0:T(8,128)S(1)}, u32[]{:S(2)}, u32[]{:S(2)}) collective-permute-start(f32[32,768]{1,0:T(8,128)S(1)} %get-tuple-element.139), channel_id=1, source_target_pairs={{0,24},{4,28},{8,16},{12,20},{16,8},{20,12},{24,0},{28,4},{1,25},{... | collective-permute-start | bytes 294920 | tf_op jit(solution)/shard_map/ppermute | solution.py:47
  132.3 7.2 %collective-permute-start.22 = (f32[32,768]{1,0:T(8,128)S(1)}, f32[32,768]{1,0:T(8,128)S(1)}, u32[]{:S(2)}, u32[]{:S(2)}) collective-permute-start(f32[32,768]{1,0:T(8,128)S(1)} %add_add_fusion.2), channel_id=1, source_target_pairs={{0,3},{1,2},{2,1},{3,0},{4,7},{5,6},{6,5},{7,4},{8,11},{9,10},{10,... | collective-permute-start | bytes 294920 | tf_op jit(solution)/shard_map/ppermute | solution.py:47
  135.0 7.8 %collective-permute-start.21 = (f32[32,768]{1,0:T(8,128)S(1)}, f32[32,768]{1,0:T(8,128)S(1)}, u32[]{:S(2)}, u32[]{:S(2)}) collective-permute-start(f32[32,768]{1,0:T(8,128)S(1)} %add_add_fusion.2), channel_id=1, source_target_pairs={{0,2},{1,3},{2,0},{3,1},{4,6},{5,7},{6,4},{7,5},{8,10},{9,11},{10,... | collective-permute-start | bytes 294920 | tf_op jit(solution)/shard_map/ppermute | solution.py:47
  135.0 7.8 %collective-permute-start.20 = (f32[32,768]{1,0:T(8,128)S(1)}, f32[32,768]{1,0:T(8,128)S(1)}, u32[]{:S(2)}, u32[]{:S(2)}) collective-permute-start(f32[32,768]{1,0:T(8,128)S(1)} %add_add_fusion.2), channel_id=1, source_target_pairs={{0,1},{1,0},{2,3},{3,2},{4,5},{5,4},{6,7},{7,6},{8,9},{9,8},{10,11... | collective-permute-start | bytes 294920 | tf_op jit(solution)/shard_map/ppermute | solution.py:47
  142.9 6.6 %collective-permute-start.25 = (f32[32,768]{1,0:T(8,128)S(1)}, f32[32,768]{1,0:T(8,128)S(1)}, u32[]{:S(2)}, u32[]{:S(2)}) collective-permute-start(f32[32,768]{1,0:T(8,128)S(1)} %add_add_fusion.1), channel_id=1, source_target_pairs={{0,24},{4,28},{8,16},{12,20},{16,8},{20,12},{24,0},{28,4},{1,25},{... | collective-permute-start | bytes 294920 | tf_op jit(solution)/shard_map/ppermute | solution.py:47
  144.1 6.1 %collective-permute-start.24 = (f32[32,768]{1,0:T(8,128)S(1)}, f32[32,768]{1,0:T(8,128)S(1)}, u32[]{:S(2)}, u32[]{:S(2)}) collective-permute-start(f32[32,768]{1,0:T(8,128)S(1)} %add_add_fusion.1), channel_id=1, source_target_pairs={{0,16},{4,20},{8,24},{12,28},{16,0},{20,4},{24,8},{28,12},{1,17},{... | collective-permute-start | bytes 294920 | tf_op jit(solution)/shard_map/ppermute | solution.py:47
  144.8 5.4 %collective-permute-start.23 = (f32[32,768]{1,0:T(8,128)S(1)}, f32[32,768]{1,0:T(8,128)S(1)}, u32[]{:S(2)}, u32[]{:S(2)}) collective-permute-start(f32[32,768]{1,0:T(8,128)S(1)} %add_add_fusion.1), channel_id=1, source_target_pairs={{0,8},{4,12},{8,0},{12,4},{16,24},{20,28},{24,16},{28,20},{1,9},{5... | collective-permute-start | bytes 294920 | tf_op jit(solution)/shard_map/ppermute | solution.py:47
  150.2 1.8 collective-permute-start.26

commit v4 on v1

--- a/solution.py
+++ b/solution.py
@@ -12,6 +12,7 @@
 EPS = 1e-06
 MIB = 1024 * 1024
 HI = lax.Precision.HIGHEST
+FIRST = 3
 SCALARS = pl.BlockSpec(memory_space=pltpu.SMEM)
 
 
@@ -25,6 +26,20 @@
 
 def params(mib):
     return pltpu.CompilerParams(vmem_limit_bytes=mib * MIB)
+
+
+def in_hbm(value):
+    return pltpu.with_memory_space_constraint(value, pltpu.HBM)
+
+
+def halves(value):
+    high = value.astype(jnp.bfloat16)
+    return high, (value - high.astype(jnp.float32)).astype(jnp.bfloat16)
+
+
+def mm3(left, right, dims):
+    (lh, ll), (rh, rl) = left, right
+    return mm(lh, rh, dims, None) + (mm(lh, rl, dims, None) + mm(ll, rh, dims, None))
 
 
 def xor_permute(value, axis, mask):
@@ -32,46 +47,66 @@
     return lax.ppermute(value, axis, [(i, i ^ mask) for i in range(size)])
 
 
-def to_lines_kernel(disp_ref, vel_ref, stiff_ref, disp_out, vel_out, last_ref, first_ref):
+def edges_kernel(stiff_ref, disp_low, vel_low, disp_high, vel_high, last_ref, first_ref):
+    w = STEPS
+    lines = stiff_ref.shape[0]
+    for ref, disp, vel, at, start in ((last_ref, disp_high, vel_high, 8 - w, lines - w), (first_ref, disp_low, vel_low, 0, 0)):
+        for i in range(w):
+            ref[i] = disp[:, at + i, :]
+            ref[w + i] = vel[:, at + i, :]
+        ref[2 * w] = jnp.zeros_like(ref[2 * w])
+        ref[2 * w, :w, :] = stiff_ref[start:start + w, :]
+
+
+def edges(disp, vel, stiff):
+    members, lines, width = disp.shape
+    w = STEPS
+    low = pl.BlockSpec((members, 8, width), lambda i: (0, 0, 0))
+    high = pl.BlockSpec((members, 8, width), lambda i: (0, lines // 8 - 1, 0))
+    edge = pl.BlockSpec((2 * w + 1, members, width), lambda i: (0, 0, 0))
+    return pl.pallas_call(
+        edges_kernel,
+        grid=(1,),
+        in_specs=[pl.BlockSpec((lines, width), lambda i: (0, 0)), low, low, high, high],
+        out_specs=[edge, edge],
+        out_shape=[pltpu.HBM((2 * w + 1, members, width), jnp.float32)] * 2,
+        compiler_params=params(6),
+        name="edges",
+    )(in_hbm(stiff), in_hbm(disp), in_hbm(vel), in_hbm(disp), in_hbm(vel))
+
+
+def to_lines_kernel(disp_ref, vel_ref, disp_out, vel_out):
     lines, group, _ = disp_out.shape
     for line in range(lines):
         disp_out[line] = disp_ref[pl.ds(line, group, stride=lines), :]
         vel_out[line] = vel_ref[pl.ds(line, group, stride=lines), :]
-    w = STEPS
-    for ref, start in ((last_ref, lines - w), (first_ref, 0)):
-        for i in range(w):
-            ref[i] = disp_ref[pl.ds(start + i, group, stride=lines), :]
-            ref[w + i] = vel_ref[pl.ds(start + i, group, stride=lines), :]
-        ref[2 * w] = jnp.zeros_like(ref[2 * w])
-        ref[2 * w, :w, :] = stiff_ref[start:start + w, :]
-
-
-def to_lines(disp, vel, stiff):
+
+
+def to_lines(disp, vel):
     members, lines, width = disp.shape
     group = 16
-    w = STEPS
     flat = pl.BlockSpec((group * lines, width), lambda i: (i, 0))
     out = pl.BlockSpec((lines, group, width), lambda i: (0, i, 0))
-    edge = pl.BlockSpec((2 * w + 1, group, width), lambda i: (0, i, 0))
     return pl.pallas_call(
         to_lines_kernel,
         grid=(members // group,),
-        in_specs=[flat, flat, pl.BlockSpec((lines, width), lambda i: (0, 0))],
-        out_specs=[out, out, edge, edge],
-        out_shape=[shape(lines, members, width)] * 2 + [shape(2 * w + 1, members, width)] * 2,
-        compiler_params=params(32),
+        in_specs=[flat, flat],
+        out_specs=[out, out],
+        out_shape=[shape(lines, members, width)] * 2,
+        compiler_params=params(8),
         name="to_lines",
-    )(disp.reshape(members * lines, width), vel.reshape(members * lines, width), stiff)
-
-
-def evolve_kernel(index_ref, disp_ref, vel_ref, stiff_ref, before_ref, after_ref, *rest, masks, size):
-    outs, (disp_pad, vel_pad, stiff_pad) = rest[:len(masks)], rest[len(masks):]
+    )(in_hbm(disp.reshape(members * lines, width)), in_hbm(vel.reshape(members * lines, width)))
+
+
+def evolve_kernel(index_ref, disp_ref, vel_ref, stiff_ref, before_ref, after_ref, *rest, slots):
+    outs, (disp_pad, vel_pad, stiff_pad) = rest[:-3], rest[-3:]
+    size = outs[0].shape[0]
     lines, members, width = disp_ref.shape
     w = STEPS
     blocks = lines // size
     lane = lax.broadcasted_iota(jnp.int32, (8, width), 1)
-    for mask, out in zip(masks, outs):
-        block = index_ref[0] ^ mask
+    for slot, out in zip(slots, outs):
+        block = index_ref[0] ^ index_ref[FIRST + slot]
         start = block * size
         disp_pad[w:w + size] = disp_ref[pl.ds(start, size)]
         vel_pad[w:w + size] = vel_ref[pl.ds(start, size)]
@@ -113,10 +148,9 @@
                     u = disp[i]
                     right = jnp.where(lane == width - 1, 0.0, pltpu.roll(u, width - 1, 1))
                     left = jnp.where(lane == 0, 0.0, pltpu.roll(u, 1, 1))
-                    laplace = disp[i + 1] + disp[i - 1] + right + left - 4.0 * u
-                    square = u * u
+                    around = (disp[i + 1] + disp[i - 1]) + (right + left)
                     stiff = jnp.broadcast_to(stiff_pad[8 - w + i:8 - w + i + 1, :], (8, width))
-                    vel[i] = vel[i] + stiff * (laplace - 0.5 * u * (square / (1.0 + square)))
+                    vel[i] = vel[i] + stiff * (around + u * (0.5 * pl.reciprocal(1.0 + u * u) - 4.5))
                     new[i] = u + vel[i]
                 disp = new
             for i in range(size):
@@ -126,18 +160,57 @@
         lax.fori_loop(0, members // 8, group_step, 0)
 
 
-def evolve(index, disp, vel, stiff, before, after, masks, size):
+def evolve(index, disp, vel, stiff, before, after, slots, size):
     lines, members, width = disp.shape
     w = STEPS
     return pl.pallas_call(
-        functools.partial(evolve_kernel, masks=masks, size=size),
+        functools.partial(evolve_kernel, slots=slots),
         in_specs=[SCALARS] + [pl.BlockSpec(memory_space=pltpu.VMEM)] * 5,
-        out_shape=[shape(size, members, width)] * len(masks),
+        out_shape=[pltpu.HBM((size, members, width), jnp.float32)] * len(slots),
+        out_specs=[pl.BlockSpec((size, members, width), lambda: (0, 0, 0))] * len(slots),
         scratch_shapes=[pltpu.VMEM((size + 2 * w, members, width), jnp.float32)] * 2
         + [pltpu.VMEM((size + 16, width), jnp.float32)],
-        compiler_params=params(32),
-        name="evolve" + "".join(str(m) for m in masks),
+        compiler_params=params(10),
+        name="evolve%d" % slots[0],
     )(index, disp, vel, stiff, before, after)
+
+
+def basis_gram_kernel(index_ref, basis_ref, send_ref, keep_ref, sum_ref, mixed_ref):
+    lines, width, rank = basis_ref.shape
+    step = pl.program_id(0)
+
+    @pl.when(step == 0)
+    def _():
+        sum_ref[...] = jnp.zeros_like(sum_ref)
+        mixed_ref[...] = jnp.zeros_like(mixed_ref)
+
+    high, low = halves(basis_ref[...].reshape(lines * width, rank))
+    sum_ref[...] += mm(high, high, ((0,), (0,)), None)
+    mixed_ref[...] += mm(high, low, ((0,), (0,)), None)
+
+    @pl.when(step == pl.num_programs(0) - 1)
+    def _():
+        sum_ref[...] += mixed_ref[...] + mixed_ref[...].T
+        half = keep_ref.shape[0]
+        core = index_ref[1]
+        keep_ref[...] = sum_ref[pl.ds(pl.multiple_of(core * half, half), half), :]
+        send_ref[...] = sum_ref[pl.ds(pl.multiple_of((1 - core) * half, half), half), :]
+
+
+def basis_gram(index, basis):
+    lines, width, rank = basis.shape
+    block = 4
+    half = pl.BlockSpec((rank // 2, rank), lambda i: (0, 0))
+    return pl.pallas_call(
+        basis_gram_kernel,
+        grid=(lines // block,),
+        in_specs=[SCALARS, pl.BlockSpec((block, width, rank), lambda i: (i, 0, 0))],
+        out_specs=[half, half],
+        out_shape=[shape(rank // 2, rank)] * 2,
+        scratch_shapes=[pltpu.VMEM((rank, rank), jnp.float32)] * 2,
+        compiler_params=params(14),
+        name="basis_gram",
+    )(index, in_hbm(basis))
 
 
 def products_kernel(index_ref, basis_ref, *rest):
@@ -146,7 +219,7 @@
     rank = basis_ref.shape[-1]
     step = pl.program_id(0)
     for k, piece in enumerate(pieces):
-        at = pl.multiple_of((index_ref[0] ^ k) * members, members)
+        at = pl.multiple_of((index_ref[0] ^ index_ref[FIRST + k]) * members, members)
         for line in range(lines):
             snap_ref[pl.ds(at, members), line * width:(line + 1) * width] = piece[line]
 
@@ -156,7 +229,7 @@
 
     snap = snap_ref[...]
     rows = basis_ref[...].reshape(lines * width, rank)
-    sum_ref[:, :rank] += mm(snap, rows, ((1,), (0,)))
+    sum_ref[:, :rank] += mm3(halves(snap), halves(rows), ((1,), (0,)))
     sum_ref[:, rank:] += mm(snap, snap, ((1,), (1,)))
 
     @pl.when(step == pl.num_programs(0) - 1)
@@ -171,7 +244,7 @@
     lines, width, rank = basis.shape
     members = pieces[0].shape[1]
     total = members * len(pieces)
-    block = 2
+    block = 4
     half = pl.BlockSpec((total // 2, rank + total), lambda i: (0, 0))
     return pl.pallas_call(
         products_kernel,
@@ -181,9 +254,9 @@
         out_specs=[half, half],
         out_shape=[shape(total // 2, rank + total)] * 2,
         scratch_shapes=[pltpu.VMEM((total, block * width), jnp.float32), pltpu.VMEM((total, rank + total), jnp.float32)],
-        compiler_params=params(32),
+        compiler_params=params(14),
         name="products",
-    )(index, basis, *pieces)
+    )(index, in_hbm(basis), *pieces)
 
 
 def split_kernel(index_ref, keep_ref, got_ref, *outs):
@@ -199,7 +272,7 @@
         split_kernel,
         in_specs=[SCALARS] + [pl.BlockSpec(memory_space=pltpu.VMEM)] * 2,
         out_shape=[shape(rows // chips, cols)] * chips,
-        compiler_params=params(16),
+        compiler_params=params(4),
         name="split",
     )(index, keep, got)
 
@@ -210,21 +283,34 @@
     return values[0]
 
 
-def chip_scatter(index, send, keep):
+def exchange_chips(pieces, limit):
+    found = []
+    for k in range(1, len(pieces)):
+        piece = pieces[k]
+        if k > limit:
+            piece, found[k - limit - 1] = lax.optimization_barrier((piece, found[k - limit - 1]))
+        found.append(xor_permute(piece, "sim", 2 * k))
+    return found
+
+
+def chip_scatter(index, send, keep, limit):
     chips = lax.axis_size("sim") // 2
     got = xor_permute(send, "sim", 1)
     pieces = split(index, keep, got, chips)
-    return tree_sum([pieces[0]] + [xor_permute(pieces[k], "sim", 2 * k) for k in range(1, chips)])
+    return tree_sum([pieces[0]] + exchange_chips(pieces, limit))
 
 
 def ana_sum(value):
     return tree_sum([value] + [xor_permute(value, "ana", k) for k in range(1, lax.axis_size("ana"))])
 
 
-def chip_gather(value):
+def chip_gather(value, limit):
     chips = lax.axis_size("sim") // 2
-    mine = jnp.concatenate([value] + [xor_permute(value, "sim", 2 * k) for k in range(1, chips)], axis=0)
-    return mine, xor_permute(mine, "sim", 1)
+    return jnp.concatenate([value] + exchange_chips([value] * chips, limit), axis=0)
+
+
+def with_other_core(value):
+    return value, xor_permute(value, "sim", 1)
 
 
 PANEL = 32
@@ -279,9 +365,9 @@
         out_ref[pl.ds(pl.multiple_of((1 - index_ref[1]) * half + at, rows), rows), :] = other_ref[piece, :]
 
 
-def solve_kernel(index_ref, sums_ref, sums2_ref, gram_ref, gram2_ref, rot_ref, w_ref, coords_ref,
+def solve_kernel(index_ref, sums_ref, sums2_ref, gram_ref, gram2_ref, rot_ref, high_ref, low_ref, coords_ref,
                  work_ref, all_ref, basis_ref, *, count, chips):
-    members, rank = coords_ref.shape
+    rank, members = coords_ref.shape
     ordered(index_ref, sums_ref, sums2_ref, all_ref, chips)
     ordered(index_ref, gram_ref, gram2_ref, basis_ref, chips)
     row = lax.broadcasted_iota(jnp.int32, (members, members), 0)
@@ -299,9 +385,10 @@
     top, bottom = rot_ref[:rank, :], rot_ref[rank:, :]
     upper = jnp.where(row <= col, work_ref[:, :members], 0.0)
     mix = mm(work_ref[:, members:], bottom, ((0,), (0,)))
-    w_ref[:rank, :] = top - mm(coef, mix, ((0,), (0,)))
-    w_ref[rank:, :] = mix * along
-    coords_ref[...] = (mm(coef, top, ((1,), (0,))) + mm(upper, bottom, ((0,), (0,)))) * math.sqrt(rank)
+    high_ref[:rank, :], low_ref[:rank, :] = halves(top - mm(coef, mix, ((0,), (0,))))
+    high_ref[rank:, :], low_ref[rank:, :] = halves(mix * along)
+    coords = (mm(coef, top, ((1,), (0,))) + mm(upper, bottom, ((0,), (0,)))) * math.sqrt(rank)
+    coords_ref[...] = coords.T
 
 
 def solve(index, sums, gram, rotation, count, chips):
@@ -310,44 +397,45 @@
     return pl.pallas_call(
         functools.partial(solve_kernel, count=float(count), chips=chips),
         in_specs=[SCALARS] + [pl.BlockSpec(memory_space=pltpu.VMEM)] * 5,
-        out_shape=(shape(members + rank, rank), shape(members, rank)),
+        out_shape=[shape(members + rank, rank, dtype=jnp.bfloat16)] * 2 + [shape(rank, members)],
         scratch_shapes=[pltpu.VMEM((members, 2 * members), jnp.float32),
                         pltpu.VMEM((members, rank + members), jnp.float32),
                         pltpu.VMEM((rank, rank), jnp.float32)],
-        compiler_params=params(40),
+        compiler_params=params(20),
         name="solve",
     )(index, *sums, *gram, rotation)
 
 
-def rotate_kernel(index_ref, weights_ref, basis_ref, *rest):
+def rotate_kernel(index_ref, high_ref, low_ref, basis_ref, *rest):
     pieces, (out_ref, snap_ref) = rest[:-2], rest[-2:]
     lines, members, width = pieces[0].shape
     rank = basis_ref.shape[-1]
     for k, piece in enumerate(pieces):
-        at = pl.multiple_of((index_ref[0] ^ k) * members, members)
+        at = pl.multiple_of((index_ref[0] ^ index_ref[FIRST + k]) * members, members)
         for line in range(lines):
             snap_ref[pl.ds(at, members), line * width:(line + 1) * width] = piece[line]
     rows = basis_ref[...].reshape(lines * width, rank)
-    out = mm(rows, weights_ref[:rank, :], ((1,), (0,))) + mm(snap_ref[...], weights_ref[rank:, :], ((0,), (0,)))
+    out = mm3(halves(rows), (high_ref[:rank, :], low_ref[:rank, :]), ((1,), (0,)))
+    out = out + mm3(halves(snap_ref[...].T), (high_ref[rank:, :], low_ref[rank:, :]), ((1,), (0,)))
     out_ref[...] = out.reshape(out_ref.shape)
 
 
-def rotate(index, weights, basis, pieces):
+def rotate(index, high, low, basis, pieces):
     lines, width, rank = basis.shape
     members = pieces[0].shape[1]
-    block = 2
+    block = 4
     rows = pl.BlockSpec((block, width, rank), lambda i: (i, 0, 0))
     return pl.pallas_call(
         rotate_kernel,
         grid=(lines // block,),
-        in_specs=[SCALARS, pl.BlockSpec(weights.shape, lambda i: (0, 0)), rows]
+        in_specs=[SCALARS] + [pl.BlockSpec(high.shape, lambda i: (0, 0))] * 2 + [rows]
         + [pl.BlockSpec((block, members, width), lambda i: (i, 0, 0))] * len(pieces),
         out_specs=rows,
         out_shape=shape(lines, width, rank),
         scratch_shapes=[pltpu.VMEM((members * len(pieces), block * width), jnp.float32)],
-        compiler_params=params(32),
+        compiler_params=params(20),
         name="rotate",
-    )(index, weights, basis, *pieces)
+    )(index, high, low, in_hbm(basis), *pieces)
 
 
 def per_device(initial_disp, initial_vel, stiffness, basis, rotation):
@@ -357,34 +445,53 @@
     count = lines * width * sims * ranks
     chips = sims // 2
     core = sim % 2
-    index = jnp.stack([ana, core, sim // 2]).astype(jnp.int32)
-
-    disp, vel, last, first = to_lines(initial_disp, initial_vel, stiffness)
+    near, far = list(range(1, ranks // 2)), list(range(ranks // 2, ranks))
+    orders = (near + far[::-1] + [0], far[::-1] + near + [0])
+    masks = jnp.where(core == 0, jnp.array(orders[0]), jnp.array(orders[1]))
+    first_index = jnp.stack([ana, core, sim // 2])
+    index = jnp.concatenate([first_index, masks]).astype(jnp.int32)
+
+    last, first = edges(initial_disp, initial_vel, stiffness)
     up = [(i, i + 1) for i in range(sims - 1)]
     before = lax.ppermute(last, "sim", up)
     after = lax.ppermute(first, "sim", [(j, i) for i, j in up])
-
-    rows = basis.reshape(lines * width, rank)
-    gram = mm(rows, rows, ((0,), (0,)))
-    half = rank // 2
-    keep = lax.dynamic_slice_in_dim(gram, core * half, half, axis=0)
-    send = lax.dynamic_slice_in_dim(gram, (1 - core) * half, half, axis=0)
-    gram = chip_scatter(index, send, keep)
-
-    far = tuple(range(ranks // 2, ranks))
-    near = tuple(range(ranks // 2))
-    pieces = {}
-    for masks in (far, near):
-        found = evolve(index, disp, vel, stiffness, before, after, masks, lines)
-        for mask, piece in zip(masks, found):
-            pieces[mask] = xor_permute(piece, "ana", mask) if mask else piece
-    pieces = [pieces[k] for k in range(ranks)]
-
-    send, keep = products(index, basis, pieces)
-    sums = chip_gather(ana_sum(chip_scatter(index, send, keep)))
-    gram = chip_gather(ana_sum(gram))
-    weights, coords = solve(index, sums, gram, rotation, count, chips)
-    return rotate(index, weights, basis, pieces), coords.T
+    late_disp, late_vel, _ = lax.optimization_barrier((initial_disp, initial_vel, last[0, 0, 0]))
+    disp, vel = to_lines(late_disp, late_vel)
+    before, after, disp = lax.optimization_barrier((before, after, disp))
+
+    pieces = list(evolve(index, disp, vel, stiffness, before, after, tuple(range(ranks - 1)), lines))
+    order, pieces = lax.optimization_barrier((index, pieces))
+    for slot in range(ranks - 1):
+        pairs = [(s * ranks + a, s * ranks + (a ^ orders[s % 2][slot])) for s in range(sims) for a in range(ranks)]
+        pieces[slot] = lax.ppermute(pieces[slot], ("sim", "ana"), pairs)
+
+    once = 1 + (ana >> 20)
+
+    def meanwhile(_, carry):
+        at, _, _ = carry
+        own, = evolve(at, disp, vel, stiffness, before, after, (ranks - 1,), lines)
+        send, keep = basis_gram(at, basis)
+        return at + (at >> 20), own, chip_scatter(at, send, keep, 2)
+
+    order, own, gram = lax.fori_loop(0, once, meanwhile, (
+        order, jnp.zeros((lines, disp.shape[1], width), jnp.float32), jnp.zeros((rank // sims, rank), jnp.float32)))
+    pieces = pieces + [own]
+    gram_parts = [xor_permute(gram, "ana", k) for k in range(1, ranks)]
+
+    def first_stages(_, carry):
+        at, _ = carry
+        send, keep = products(at, basis, pieces)
+        return at + (at >> 20), chip_scatter(at, send, keep, 2)
+
+    total = initial_disp.shape[0] * ranks
+    order, sums = lax.fori_loop(0, once, first_stages, (order, jnp.zeros((total // sims, rank + total), jnp.float32)))
+    sums, gram, gram_parts = lax.optimization_barrier((sums, gram, gram_parts))
+    gram = chip_gather(tree_sum([gram] + gram_parts), chips)
+    sums = ana_sum(sums)
+    sums = with_other_core(chip_gather(sums, chips))
+    gram = with_other_core(gram)
+    high, low, coords = solve(index, sums, gram, rotation, count, chips)
+    return rotate(index, high, low, basis, pieces), coords
 
 
 def solution(mesh):

time: 171 us -> 155 us (0.906)
  local copies, waits for them, and re-layouts: 16.7 us -> 2.2 us
  matrix products: 7.03 us -> 0 us
  starting transfers between devices: 48.1 us -> 44.8 us
  Pallas kernels: 59 us -> 62.3 us
  other arithmetic: 0.26 us -> 3.38 us
  waiting for transfers between devices: 38.7 us -> 40.7 us
    unnamed x33 -> x15, local copies, waits for them, and re-layouts: 16.6 us -> 0.04 us
    ppermute x25 -> x22, starting transfers between devices: 44.4 us -> 36.1 us  [xor_permute(): return lax.ppermute(value, axis, [(i, i ^ mask) for i in range(size)])]
    dot_general x1 -> x0, matrix products: 7.03 us -> none  [mm(): lax.dot_general(left, right, (dims, ((), ())), precision=precision, prefe...]
    ppermute x25 -> x22, waiting for transfers between devices: 34.5 us -> 40.7 us  [xor_permute(): return lax.ppermute(value, axis, [(i, i ^ mask) for i in range(size)])]
    ppermute x0 -> x3, starting transfers between devices: none -> 5 us  [per_device(): pieces[slot] = lax.ppermute(pieces[slot], ('sim', 'ana'), pairs)]
    ppermute x1, waiting for transfers between devices: 4.17 us -> 0.01 us  [per_device(): after = lax.ppermute(first, 'sim', [(j, i) for i, j in up])]
    add x4, other arithmetic: 0.13 us -> 3.22 us  [tree_sum(): values = [a + b for a, b in zip(values[::2], values[1::2])]]
    broadcast_in_dim x0 -> x3, local copies, waits for them, and re-layouts: none -> 2.16 us  [the longest x1 0.86 us: per_device(): jnp.zeros((lines, disp.shape[1], width), jnp.float32)]
  transfers between devices with their start and end apart: 27 -> 27, of which waited for: 13 -> 11; matrix products, arithmetic and copies ran while one was open for 4% -> 3% of each run, Pallas kernels for 10% -> 10%
where the time goes in v4:
time: 155 us; the launch traced here: 154 us
  Pallas kernels  62.3 us (40%)
  starting transfers between devices  44.8 us (29%)
  waiting for transfers between devices  40.7 us (26%)
  other arithmetic  3.38 us (2%)
  local copies, waits for them, and re-layouts  2.2 us (1%)
    ppermute x22, waiting for transfers between devices, xor_permute(): return lax.ppermute(value, axis, [(i, i ^ mask) for i in range(size)])  40.7 us
    ppermute x22, starting transfers between devices, xor_permute(): return lax.ppermute(value, axis, [(i, i ^ mask) for i in range(size)])  36.1 us
    pallas_call x1, Pallas kernels, solve(): pl.pallas_call(functools.partial(solve_kernel, count=float(count), chips=...  18.6 us
    pallas_call x2, Pallas kernels, evolve(): pl.pallas_call(functools.partial(evolve_kernel, slots=slots), in_specs=[S...  15.7 us
    pallas_call x1, Pallas kernels, rotate(): pl.pallas_call(rotate_kernel, grid=(lines // block,), in_specs=[SCALARS]...  8.29 us
    pallas_call x1, Pallas kernels, products(): pl.pallas_call(products_kernel, grid=(lines // block,), in_specs=[SCALARS...  6.14 us
    pallas_call x1, Pallas kernels, basis_gram(): pl.pallas_call(basis_gram_kernel, grid=(lines // block,), in_specs=[SCALA...  5.39 us
    ppermute x3, starting transfers between devices, per_device(): pieces[slot] = lax.ppermute(pieces[slot], ('sim', 'ana'), pairs)  5 us
  transfers between devices with their start and end apart: 27, of which 11 were waited for; matrix products, arithmetic and copies ran while one was open for 3% of the time, Pallas kernels for 10%

profile of v4, /device:TPU:0, one launch (start us, length us, event | category | flops | bytes accessed | tf_op | source)
XLA Modules:
  0.0 154.2 jit_solution(12629803316334968826)
XLA Ops:
  0.6 2.3 %edges.1 = (f32[9,64,128]{2,1,0:T(8,128)}, f32[9,64,128]{2,1,0:T(8,128)}) custom-call(f32[64,128]{1,0:T(8,128)} %stiff_ref.3, f32[64,64,128]{2,1,0:T(8,128)} %disp_high.1, f32[64,64,128]{2,1,0:T(8,128)} %vel_high.1, f32[64,64,128]{2,1,0:T(8,128)} %disp_high.1, f32[64,64,128]{2,1,0:T(8,128)} %vel_high.1), custom_call_target="tpu_custom_call" | custom-call | tf_op jit(solution)/shard_map/edges/pallas_call | solution.py:67
  2.9 2.4 %collective-permute-start.8 = (f32[9,64,128]{2,1,0:T(8,128)}, f32[9,64,128]{2,1,0:T(8,128)S(1)}, u32[]{:S(2)}, u32[]{:S(2)}) collective-permute-start(f32[9,64,128]{2,1,0:T(8,128)} %get-tuple-element.147), channel_id=1, source_target_pairs={{0,4},{4,8},{8,12},{12,16},{16,20},{20,24},{24,28},{1,5},{5,9},{9,... | collective-permute-start | bytes 884744 | tf_op jit(solution)/shard_map/ppermute | solution.py:456
  5.3 1.3 collective-permute-start.9
  6.7 4.6 %to_lines.1 = (f32[64,64,128]{2,1,0:T(8,128)S(1)}, f32[64,64,128]{2,1,0:T(8,128)S(1)}) custom-call(f32[4096,128]{1,0:T(8,128)} %bitcast.5, f32[4096,128]{1,0:T(8,128)} %bitcast.6), custom_call_target="tpu_custom_call" | custom-call | tf_op jit(solution)/shard_map/to_lines/pallas_call | solution.py:90
  11.4 10.5 %evolve0.1 = (f32[16,64,128]{2,1,0:T(8,128)}, f32[16,64,128]{2,1,0:T(8,128)}, f32[16,64,128]{2,1,0:T(8,128)}) custom-call(s32[7]{0:T(128)S(1)} %pad_add_fusion.index_ref, f32[64,64,128]{2,1,0:T(8,128)S(1)} %get-tuple-element.370.disp_ref, f32[64,64,128]{2,1,0:T(8,128)S(1)} %get-tuple-element.371.vel_ref, f32[64,128]{1,0:T(8,128)S(1)} %copy-done.3, ...), custom_call_target="tpu_custom_call" | custom-call | tf_op jit(solution)/shard_map/evolve0/pallas_call | solution.py:166
  21.9 2.4 %collective-permute-start.10 = (f32[16,64,128]{2,1,0:T(8,128)}, f32[16,64,128]{2,1,0:T(8,128)S(1)}, u32[]{:S(2)}, u32[]{:S(2)}) collective-permute-start(f32[16,64,128]{2,1,0:T(8,128)} %get-tuple-element.161), channel_id=1, source_target_pairs={{0,1},{1,0},{2,3},{3,2},{4,7},{5,6},{6,5},{7,4},{8,9},{9,8},{10,11... | collective-permute-start | bytes 1572872 | tf_op jit(solution)/shard_map/ppermute | solution.py:466
  24.3 2.5 %collective-permute-start.11 = (f32[16,64,128]{2,1,0:T(8,128)}, f32[16,64,128]{2,1,0:T(8,128)}, u32[]{:S(2)}, u32[]{:S(2)}) collective-permute-start(f32[16,64,128]{2,1,0:T(8,128)} %get-tuple-element.162), channel_id=1, source_target_pairs={{0,3},{1,2},{2,1},{3,0},{4,6},{5,7},{6,4},{7,5},{8,11},{9,10},{10,... | collective-permute-start | bytes 1572872 | tf_op jit(solution)/shard_map/ppermute | solution.py:466
  26.9 0.9 broadcast_in_dim.9
  27.8 0.7 broadcast_in_dim.10
  28.4 28.5 %while.26 = (s32[]{:T(128)}, s32[7]{0:T(128)S(1)}, f32[16,64,128]{2,1,0:T(8,128)}, f32[64,512]{1,0:T(8,128)}, s32[]{:T(128)}, /*index=5*/f32[64,64,128]{2,1,0:T(...) while((s32[]{:T(128)}, s32[7]{0:T(128)S(1)}, ...), condition=%wide.region_1.2_spmd, body=%wide.region_0.1_spmd.sunk | while | flops 98320 | bytes 4325709 | solution.py:476
  28.4 5.4 %basis_gram.1 = (f32[256,512]{1,0:T(8,128)S(1)}, f32[256,512]{1,0:T(8,128)S(1)}) custom-call(s32[7]{0:T(128)S(1)} %get-tuple-element.378.index_ref, f32[16,128,512]{2,1,0:T(8,128)} %get-tuple-element.399.basis_ref), custom_call_target="tpu_custom_call" | custom-call | tf_op jit(solution)/shard_map/while/body/basis_gram/pallas_call | solution.py:204
  33.8 3.8 %collective-permute-start = (f32[256,512]{1,0:T(8,128)S(1)}, f32[256,512]{1,0:T(8,128)S(1)}, u32[]{:S(2)}, u32[]{:S(2)}) collective-permute-start(f32[256,512]{1,0:T(8,128)S(1)} %get-tuple-element.342), channel_id=1, source_target_pairs={{0,4},{4,0},{8,12},{12,8},{16,20},{20,16},{24,28},{28,24},{1,5},{5... | collective-permute-start | bytes 1572872 | tf_op jit(solution)/shard_map/while/body/ppermute | solution.py:47
  37.6 1.5 collective-permute-done.got_ref
  39.2 0.6 split.2
  39.8 2.1 %collective-permute-start.2 = (f32[64,512]{1,0:T(8,128)S(1)}, f32[64,512]{1,0:T(8,128)}, u32[]{:S(2)}, u32[]{:S(2)}) collective-permute-start(f32[64,512]{1,0:T(8,128)S(1)} %get-tuple-element.345), channel_id=1, source_target_pairs={{0,8},{4,12},{8,0},{12,4},{16,24},{20,28},{24,16},{28,20},{1,9},{5... | collective-permute-start | bytes 393224 | tf_op jit(solution)/shard_map/while/body/ppermute | solution.py:47
  41.8 5.2 %evolve3.1 = f32[16,64,128]{2,1,0:T(8,128)} custom-call(s32[7]{0:T(128)S(1)} %get-tuple-element.378.index_ref, f32[64,64,128]{2,1,0:T(8,128)S(1)} %get-tuple-element.394.disp_ref, f32[64,64,128]{2,1,0:T(8,128)} %get-tuple-element.395.vel_ref, f32[64,128]{1,0:T(8,128)S(1)} %get-tuple-element.396.stiff_ref, f32[9,64,128]{2,1,0:T(8,128)S(1)} %get-tuple-element.397.before_ref, ...), custom_call_target="tpu_custom_call" | custom-call | tf_op jit(solution)/shard_map/while/body/evolve3/pallas_call | solution.py:166
  47.2 1.3 collective-permute-start.3
  48.6 6.8 %collective-permute-done.1 = f32[64,512]{1,0:T(8,128)S(1)} collective-permute-done((f32[64,512]{1,0:T(8,128)S(1)}, f32[64,512]{1,0:T(8,128)S(1)}, u32[]{:S(2)}, u32[]{:S(2)}) %collective-permute-start.1) | collective-permute-done | bytes 131104 | tf_op jit(solution)/shard_map/while/body/ppermute | solution.py:47
  55.3 1.6 %add_add_fusion.6 = f32[64,512]{1,0:T(8,128)} fusion(f32[64,512]{1,0:T(8,128)S(1)} %collective-permute-done.1, f32[64,512]{1,0:T(8,128)S(1)} %collective-permute-done.3, f32[64,512]{1,0:T(8,128)S(1)} %get-tuple-element.347, f32[64,512]{1,0:T(8,128)} %collective-permute-done.2), kind=kLoop, calls=%fused_computation.clone.1 | loop fusion | flops 98304 | bytes 655360 | tf_op jit(solution)/shard_map/while/body/add | solution.py:282
  56.9 1.4 collective-permute-start.13
  58.3 2.6 %collective-permute-start.14 = (f32[64,512]{1,0:T(8,128)}, f32[64,512]{1,0:T(8,128)S(1)}, u32[]{:S(2)}, u32[]{:S(2)}) collective-permute-start(f32[64,512]{1,0:T(8,128)} %get-tuple-element.168), channel_id=1, source_target_pairs={{0,2},{1,3},{2,0},{3,1},{4,6},{5,7},{6,4},{7,5},{8,10},{9,11},{10,... | collective-permute-start | bytes 393224 | tf_op jit(solution)/shard_map/ppermute | solution.py:47
  61.0 2.5 %collective-permute-done.13 = f32[64,512]{1,0:T(8,128)S(1)} collective-permute-done((f32[64,512]{1,0:T(8,128)}, f32[64,512]{1,0:T(8,128)S(1)}, u32[]{:S(2)}, u32[]{:S(2)}) %collective-permute-start.13) | collective-permute-done | bytes 131104 | tf_op jit(solution)/shard_map/ppermute | solution.py:47
  63.5 3.2 %collective-permute-start.15 = (f32[64,512]{1,0:T(8,128)}, f32[64,512]{1,0:T(8,128)S(1)}, u32[]{:S(2)}, u32[]{:S(2)}) collective-permute-start(f32[64,512]{1,0:T(8,128)} %get-tuple-element.168), channel_id=1, source_target_pairs={{0,3},{1,2},{2,1},{3,0},{4,7},{5,6},{6,5},{7,4},{8,11},{9,10},{10,... | collective-permute-start | bytes 393224 | tf_op jit(solution)/shard_map/ppermute | solution.py:47
  66.7 13.2 %collective-permute-done.14 = f32[64,512]{1,0:T(8,128)S(1)} collective-permute-done((f32[64,512]{1,0:T(8,128)}, f32[64,512]{1,0:T(8,128)S(1)}, u32[]{:S(2)}, u32[]{:S(2)}) %collective-permute-start.14) | collective-permute-done | bytes 131104 | tf_op jit(solution)/shard_map/ppermute | solution.py:47
  79.9 0.6 broadcast_in_dim.11
  80.5 24.2 %while.27 = (s32[]{:T(128)}, s32[7]{0:T(128)S(1)}, f32[32,768]{1,0:T(8,128)}, s32[]{:T(128)}, f32[16,128,512]{2,1,0:T(8,128)}, /*index=5*/f32[16,64,128]{2,1,0:T...) while((s32[]{:T(128)}, s32[7]{0:T(128)S(1)}, ...), condition=%wide.region_3.4_spmd, body=%wide.region_2.3_spmd.sunk | while | flops 73744 | bytes 3244349 | solution.py:487
  80.5 6.1 %products.1 = (f32[128,768]{1,0:T(8,128)S(1)}, f32[128,768]{1,0:T(8,128)S(1)}) custom-call(s32[7]{0:T(128)S(1)} %get-tuple-element.412.index_ref, f32[16,128,512]{2,1,0:T(8,128)} %get-tuple-element.425.basis_ref, f32[16,64,128]{2,1,0:T(8,128)S(1)} %get-tuple-element.426.rest_0_, f32[16,64,128]{2,1,0:T(8,128)} %get-tuple-element.427.rest_1_, ...), custom_call_target="tpu_custom_call" | custom-call | tf_op jit(solution)/shard_map/while/body/products/pallas_call | solution.py:249
  86.7 3.5 %collective-permute-start.4 = (f32[128,768]{1,0:T(8,128)S(1)}, f32[128,768]{1,0:T(8,128)S(1)}, u32[]{:S(2)}, u32[]{:S(2)}) collective-permute-start(f32[128,768]{1,0:T(8,128)S(1)} %get-tuple-element.358), channel_id=1, source_target_pairs={{0,4},{4,0},{8,12},{12,8},{16,20},{20,16},{24,28},{28,24},{1,5},{5... | collective-permute-start | bytes 1179656 | tf_op jit(solution)/shard_map/while/body/ppermute | solution.py:47
  90.2 1.3 collective-permute-done.4.got_ref
  92.1 3.4 %collective-permute-start.6 = (f32[32,768]{1,0:T(8,128)S(1)}, f32[32,768]{1,0:T(8,128)S(1)}, u32[]{:S(2)}, u32[]{:S(2)}) collective-permute-start(f32[32,768]{1,0:T(8,128)S(1)} %get-tuple-element.361), channel_id=1, source_target_pairs={{0,8},{4,12},{8,0},{12,4},{16,24},{20,28},{24,16},{28,20},{1,9},{5... | collective-permute-start | bytes 294920 | tf_op jit(solution)/shard_map/while/body/ppermute | solution.py:47
  95.6 3.0 %collective-permute-done.6 = f32[32,768]{1,0:T(8,128)S(1)} collective-permute-done((f32[32,768]{1,0:T(8,128)S(1)}, f32[32,768]{1,0:T(8,128)S(1)}, u32[]{:S(2)}, u32[]{:S(2)}) %collective-permute-start.6) | collective-permute-done | bytes 98336 | tf_op jit(solution)/shard_map/while/body/ppermute | solution.py:47
  98.6 1.5 collective-permute-start.7
  100.1 4.0 %collective-permute-done.7 = f32[32,768]{1,0:T(8,128)S(1)} collective-permute-done((f32[32,768]{1,0:T(8,128)S(1)}, f32[32,768]{1,0:T(8,128)S(1)}, u32[]{:S(2)}, u32[]{:S(2)}) %collective-permute-start.7) | collective-permute-done | bytes 98336 | tf_op jit(solution)/shard_map/while/body/ppermute | solution.py:47
  104.1 0.7 add_add_fusion.7
  104.8 3.3 %collective-permute-start.16 = (f32[32,768]{1,0:T(8,128)}, f32[32,768]{1,0:T(8,128)S(1)}, u32[]{:S(2)}, u32[]{:S(2)}) collective-permute-start(f32[32,768]{1,0:T(8,128)} %get-tuple-element.167), channel_id=1, source_target_pairs={{0,1},{1,0},{2,3},{3,2},{4,5},{5,4},{6,7},{7,6},{8,9},{9,8},{10,11... | collective-permute-start | bytes 294920 | tf_op jit(solution)/shard_map/ppermute | solution.py:47
  108.1 1.0 collective-permute-start.17
  109.1 1.5 collective-permute-start.18
  110.6 1.8 %collective-permute-start.23 = (f32[64,512]{1,0:T(8,128)S(1)}, f32[64,512]{1,0:T(8,128)S(1)}, u32[]{:S(2)}, u32[]{:S(2)}) collective-permute-start(f32[64,512]{1,0:T(8,128)S(1)} %add_add_fusion.2), channel_id=1, source_target_pairs={{0,8},{4,12},{8,0},{12,4},{16,24},{20,28},{24,16},{28,20},{1,9},{5... | collective-permute-start | bytes 393224 | tf_op jit(solution)/shard_map/ppermute | solution.py:47
  112.4 1.7 %collective-permute-start.25 = (f32[64,512]{1,0:T(8,128)S(1)}, f32[64,512]{1,0:T(8,128)S(1)}, u32[]{:S(2)}, u32[]{:S(2)}) collective-permute-start(f32[64,512]{1,0:T(8,128)S(1)} %add_add_fusion.2), channel_id=1, source_target_pairs={{0,24},{4,28},{8,16},{12,20},{16,8},{20,12},{24,0},{28,4},{1,25},{... | collective-permute-start | bytes 393224 | tf_op jit(solution)/shard_map/ppermute | solution.py:47
  114.1 3.2 %collective-permute-done.17 = f32[32,768]{1,0:T(8,128)S(1)} collective-permute-done((f32[32,768]{1,0:T(8,128)}, f32[32,768]{1,0:T(8,128)S(1)}, u32[]{:S(2)}, u32[]{:S(2)}) %collective-permute-start.17) | collective-permute-done | bytes 98336 | tf_op jit(solution)/shard_map/ppermute | solution.py:47
  117.3 0.9 add_add_fusion.3
  118.3 1.5 collective-permute-start.19
  119.8 2.1 %collective-permute-start.21 = (f32[32,768]{1,0:T(8,128)S(1)}, f32[32,768]{1,0:T(8,128)S(1)}, u32[]{:S(2)}, u32[]{:S(2)}) collective-permute-start(f32[32,768]{1,0:T(8,128)S(1)} %add_add_fusion.3), channel_id=1, source_target_pairs={{0,24},{4,28},{8,16},{12,20},{16,8},{20,12},{24,0},{28,4},{1,25},{... | collective-permute-start | bytes 294920 | tf_op jit(solution)/shard_map/ppermute | solution.py:47
  122.0 1.0 collective-permute-done.19
  122.9 2.5 %collective-permute-done.20 = f32[32,768]{1,0:T(8,128)S(1)} collective-permute-done((f32[32,768]{1,0:T(8,128)S(1)}, f32[32,768]{1,0:T(8,128)S(1)}, u32[]{:S(2)}, u32[]{:S(2)}) %collective-permute-start.20) | collective-permute-done | bytes 98336 | tf_op jit(solution)/shard_map/ppermute | solution.py:47
  125.5 1.7 %collective-permute-done.22.sums2_ref = f32[128,768]{1,0:T(8,128)S(1)} collective-permute-done((f32[128,768]{1,0:T(8,128)S(1)}, f32[128,768]{1,0:T(8,128)S(1)}, u32[]{:S(2)}, u32[]{:S(2)}) %collective-permute-start.22) | collective-permute-done | bytes 393248 | tf_op jit(solution)/shard_map/ppermute | solution.py:47
  127.3 18.6 %solve.1 = (bf16[768,512]{1,0:T(8,128)(2,1)S(1)}, bf16[768,512]{1,0:T(8,128)(2,1)S(1)}, f32[512,256]{1,0:T(8,128)}) custom-call(s32[7]{0:T(128)S(1)} %pad_add_fusion.index_ref, f32[128,768]{1,0:T(8,128)S(1)} %pad_maximum_fusion.1.sums_ref, f32[128,768]{1,0:T(8,128)S(1)} %collective-permute-done.22.sums2_ref, f32[256,512]{1,0:T(8,128)S(1)} %pad_maximum_fusion.gram_ref, ...), custom_call_target="tpu_custom_call" | custom-call | tf_op jit(solution)/shard_map/solve/pallas_call | solution.py:397
  145.9 8.3 %rotate.1 = f32[16,128,512]{2,1,0:T(8,128)} custom-call(s32[7]{0:T(128)S(1)} %pad_add_fusion.index_ref, bf16[768,512]{1,0:T(8,128)(2,1)S(1)} %get-tuple-element.172.high_ref, bf16[768,512]{1,0:T(8,128)(2,1)S(1)} %get-tuple-element.173.low_ref, f32[16,128,512]{2,1,0:T(8,128)} %get-tuple-element.446, f32[16,64,128]{2,1,0:T(8,128)S(1)} %get-tuple-element.449, ...), custom_call_target="tpu_custom_call" | custom-call | tf_op jit(solution)/shard_map/rotate/pallas_call | solution.py:428
  (46 shorter events, 1.5 us)
Async XLA Ops:
  2.9 8.4 %collective-permute-start.8 = (f32[9,64,128]{2,1,0:T(8,128)}, f32[9,64,128]{2,1,0:T(8,128)S(1)}, u32[]{:S(2)}, u32[]{:S(2)}) collective-permute-start(f32[9,64,128]{2,1,0:T(8,128)} %get-tuple-element.147), channel_id=1, source_target_pairs={{0,4},{4,8},{8,12},{12,16},{16,20},{20,24},{24,28},{1,5},{5,9},{9,... | collective-permute-start | bytes 884744 | tf_op jit(solution)/shard_map/ppermute | solution.py:456
  5.3 6.1 %collective-permute-start.9 = (f32[9,64,128]{2,1,0:T(8,128)}, f32[9,64,128]{2,1,0:T(8,128)}, u32[]{:S(2)}, u32[]{:S(2)}) collective-permute-start(f32[9,64,128]{2,1,0:T(8,128)} %get-tuple-element.148), channel_id=1, source_target_pairs={{4,0},{8,4},{12,8},{16,12},{20,16},{24,20},{28,24},{5,1},{9,5},{13... | collective-permute-start | bytes 884744 | tf_op jit(solution)/shard_map/ppermute | solution.py:457
  6.6 4.6 %copy-start.5 = (s32[4]{0:T(128)S(1)}, s32[4]{0:T(128)}, u32[]{:S(2)}) copy-start(s32[4]{0:T(128)} %constant.53.clone) | copy-start | bytes 52
  6.6 4.6 %copy-start.6 = (s32[4]{0:T(128)S(1)}, s32[4]{0:T(128)}, u32[]{:S(2)}) copy-start(s32[4]{0:T(128)} %constant.54.clone) | copy-start | bytes 52
  6.7 4.7 %copy-start.3 = (f32[64,128]{1,0:T(8,128)S(1)}, f32[64,128]{1,0:T(8,128)}, u32[]{:S(2)}) copy-start(f32[64,128]{1,0:T(8,128)} %stiff_ref.3) | copy-start | bytes 98308
  11.3 10.7 %copy-start.1 = (f32[64,64,128]{2,1,0:T(8,128)}, f32[64,64,128]{2,1,0:T(8,128)S(1)}, u32[]{:S(2)}) copy-start(f32[64,64,128]{2,1,0:T(8,128)S(1)} %get-tuple-element.371.vel_ref) | copy-start | bytes 6291460
  21.9 57.9 %collective-permute-start.10 = (f32[16,64,128]{2,1,0:T(8,128)}, f32[16,64,128]{2,1,0:T(8,128)S(1)}, u32[]{:S(2)}, u32[]{:S(2)}) collective-permute-start(f32[16,64,128]{2,1,0:T(8,128)} %get-tuple-element.161), channel_id=1, source_target_pairs={{0,1},{1,0},{2,3},{3,2},{4,7},{5,6},{6,5},{7,4},{8,9},{9,8},{10,11... | collective-permute-start | bytes 1572872 | tf_op jit(solution)/shard_map/ppermute | solution.py:466
  24.3 55.5 %collective-permute-start.11 = (f32[16,64,128]{2,1,0:T(8,128)}, f32[16,64,128]{2,1,0:T(8,128)}, u32[]{:S(2)}, u32[]{:S(2)}) collective-permute-start(f32[16,64,128]{2,1,0:T(8,128)} %get-tuple-element.162), channel_id=1, source_target_pairs={{0,3},{1,2},{2,1},{3,0},{4,6},{5,7},{6,4},{7,5},{8,11},{9,10},{10,... | collective-permute-start | bytes 1572872 | tf_op jit(solution)/shard_map/ppermute | solution.py:466
  26.8 53.1 %collective-permute-start.12 = (f32[16,64,128]{2,1,0:T(8,128)}, f32[16,64,128]{2,1,0:T(8,128)}, u32[]{:S(2)}, u32[]{:S(2)}) collective-permute-start(f32[16,64,128]{2,1,0:T(8,128)} %get-tuple-element.163), channel_id=1, source_target_pairs={{0,2},{1,3},{2,0},{3,1},{4,5},{5,4},{6,7},{7,6},{8,10},{9,11},{10,... | collective-permute-start | bytes 1572872 | tf_op jit(solution)/shard_map/ppermute | solution.py:466
  33.8 5.3 %collective-permute-start = (f32[256,512]{1,0:T(8,128)S(1)}, f32[256,512]{1,0:T(8,128)S(1)}, u32[]{:S(2)}, u32[]{:S(2)}) collective-permute-start(f32[256,512]{1,0:T(8,128)S(1)} %get-tuple-element.342), channel_id=1, source_target_pairs={{0,4},{4,0},{8,12},{12,8},{16,20},{20,16},{24,28},{28,24},{1,5},{5... | collective-permute-start | bytes 1572872 | tf_op jit(solution)/shard_map/while/body/ppermute | solution.py:47
  39.8 7.4 %collective-permute-start.2 = (f32[64,512]{1,0:T(8,128)S(1)}, f32[64,512]{1,0:T(8,128)}, u32[]{:S(2)}, u32[]{:S(2)}) collective-permute-start(f32[64,512]{1,0:T(8,128)S(1)} %get-tuple-element.345), channel_id=1, source_target_pairs={{0,8},{4,12},{8,0},{12,4},{16,24},{20,28},{24,16},{28,20},{1,9},{5... | collective-permute-start | bytes 393224 | tf_op jit(solution)/shard_map/while/body/ppermute | solution.py:47
  47.0 8.3 %collective-permute-start.1 = (f32[64,512]{1,0:T(8,128)S(1)}, f32[64,512]{1,0:T(8,128)S(1)}, u32[]{:S(2)}, u32[]{:S(2)}) collective-permute-start(f32[64,512]{1,0:T(8,128)S(1)} %get-tuple-element.343), channel_id=1, source_target_pairs={{0,16},{4,20},{8,24},{12,28},{16,0},{20,4},{24,8},{28,12},{1,17},{... | collective-permute-start | bytes 393224 | tf_op jit(solution)/shard_map/while/body/ppermute | solution.py:47
  47.2 8.1 %collective-permute-start.3 = (f32[64,512]{1,0:T(8,128)S(1)}, f32[64,512]{1,0:T(8,128)S(1)}, u32[]{:S(2)}, u32[]{:S(2)}) collective-permute-start(f32[64,512]{1,0:T(8,128)S(1)} %get-tuple-element.346), channel_id=1, source_target_pairs={{0,24},{4,28},{8,16},{12,20},{16,8},{20,12},{24,0},{28,4},{1,25},{... | collective-permute-start | bytes 393224 | tf_op jit(solution)/shard_map/while/body/ppermute | solution.py:47
  56.9 6.6 %collective-permute-start.13 = (f32[64,512]{1,0:T(8,128)}, f32[64,512]{1,0:T(8,128)S(1)}, u32[]{:S(2)}, u32[]{:S(2)}) collective-permute-start(f32[64,512]{1,0:T(8,128)} %get-tuple-element.168), channel_id=1, source_target_pairs={{0,1},{1,0},{2,3},{3,2},{4,5},{5,4},{6,7},{7,6},{8,9},{9,8},{10,11... | collective-permute-start | bytes 393224 | tf_op jit(solution)/shard_map/ppermute | solution.py:47
  58.3 21.5 %collective-permute-start.14 = (f32[64,512]{1,0:T(8,128)}, f32[64,512]{1,0:T(8,128)S(1)}, u32[]{:S(2)}, u32[]{:S(2)}) collective-permute-start(f32[64,512]{1,0:T(8,128)} %get-tuple-element.168), channel_id=1, source_target_pairs={{0,2},{1,3},{2,0},{3,1},{4,6},{5,7},{6,4},{7,5},{8,10},{9,11},{10,... | collective-permute-start | bytes 393224 | tf_op jit(solution)/shard_map/ppermute | solution.py:47
  63.5 16.4 %collective-permute-start.15 = (f32[64,512]{1,0:T(8,128)}, f32[64,512]{1,0:T(8,128)S(1)}, u32[]{:S(2)}, u32[]{:S(2)}) collective-permute-start(f32[64,512]{1,0:T(8,128)} %get-tuple-element.168), channel_id=1, source_target_pairs={{0,3},{1,2},{2,1},{3,0},{4,7},{5,6},{6,5},{7,4},{8,11},{9,10},{10,... | collective-permute-start | bytes 393224 | tf_op jit(solution)/shard_map/ppermute | solution.py:47
  80.5 30.0 %copy-start.4 = (f32[64,512]{1,0:T(8,128)S(1)}, f32[64,512]{1,0:T(8,128)}, u32[]{:S(2)}) copy-start(f32[64,512]{1,0:T(8,128)} %get-tuple-element.168) | copy-start | bytes 393220
  86.7 4.8 %collective-permute-start.4 = (f32[128,768]{1,0:T(8,128)S(1)}, f32[128,768]{1,0:T(8,128)S(1)}, u32[]{:S(2)}, u32[]{:S(2)}) collective-permute-start(f32[128,768]{1,0:T(8,128)S(1)} %get-tuple-element.358), channel_id=1, source_target_pairs={{0,4},{4,0},{8,12},{12,8},{16,20},{20,16},{24,28},{28,24},{1,5},{5... | collective-permute-start | bytes 1179656 | tf_op jit(solution)/shard_map/while/body/ppermute | solution.py:47
  92.1 6.5 %collective-permute-start.6 = (f32[32,768]{1,0:T(8,128)S(1)}, f32[32,768]{1,0:T(8,128)S(1)}, u32[]{:S(2)}, u32[]{:S(2)}) collective-permute-start(f32[32,768]{1,0:T(8,128)S(1)} %get-tuple-element.361), channel_id=1, source_target_pairs={{0,8},{4,12},{8,0},{12,4},{16,24},{20,28},{24,16},{28,20},{1,9},{5... | collective-permute-start | bytes 294920 | tf_op jit(solution)/shard_map/while/body/ppermute | solution.py:47
  95.5 4.6 %collective-permute-start.5 = (f32[32,768]{1,0:T(8,128)S(1)}, f32[32,768]{1,0:T(8,128)S(1)}, u32[]{:S(2)}, u32[]{:S(2)}) collective-permute-start(f32[32,768]{1,0:T(8,128)S(1)} %get-tuple-element.359), channel_id=1, source_target_pairs={{0,16},{4,20},{8,24},{12,28},{16,0},{20,4},{24,8},{28,12},{1,17},{... | collective-permute-start | bytes 294920 | tf_op jit(solution)/shard_map/while/body/ppermute | solution.py:47
  98.6 5.5 %collective-permute-start.7 = (f32[32,768]{1,0:T(8,128)S(1)}, f32[32,768]{1,0:T(8,128)S(1)}, u32[]{:S(2)}, u32[]{:S(2)}) collective-permute-start(f32[32,768]{1,0:T(8,128)S(1)} %get-tuple-element.362), channel_id=1, source_target_pairs={{0,24},{4,28},{8,16},{12,20},{16,8},{20,12},{24,0},{28,4},{1,25},{... | collective-permute-start | bytes 294920 | tf_op jit(solution)/shard_map/while/body/ppermute | solution.py:47
  104.8 22.5 %copy-start = (f32[768,512]{1,0:T(8,128)S(1)}, f32[768,512]{1,0:T(8,128)}, u32[]{:S(2)}) copy-start(f32[768,512]{1,0:T(8,128)} %rot_ref.1) | copy-start | bytes 4718596
  104.8 7.6 %collective-permute-start.16 = (f32[32,768]{1,0:T(8,128)}, f32[32,768]{1,0:T(8,128)S(1)}, u32[]{:S(2)}, u32[]{:S(2)}) collective-permute-start(f32[32,768]{1,0:T(8,128)} %get-tuple-element.167), channel_id=1, source_target_pairs={{0,1},{1,0},{2,3},{3,2},{4,5},{5,4},{6,7},{7,6},{8,9},{9,8},{10,11... | collective-permute-start | bytes 294920 | tf_op jit(solution)/shard_map/ppermute | solution.py:47
  108.1 9.3 %collective-permute-start.17 = (f32[32,768]{1,0:T(8,128)}, f32[32,768]{1,0:T(8,128)S(1)}, u32[]{:S(2)}, u32[]{:S(2)}) collective-permute-start(f32[32,768]{1,0:T(8,128)} %get-tuple-element.167), channel_id=1, source_target_pairs={{0,2},{1,3},{2,0},{3,1},{4,6},{5,7},{6,4},{7,5},{8,10},{9,11},{10,... | collective-permute-start | bytes 294920 | tf_op jit(solution)/shard_map/ppermute | solution.py:47
  109.1 8.3 %collective-permute-start.18 = (f32[32,768]{1,0:T(8,128)}, f32[32,768]{1,0:T(8,128)S(1)}, u32[]{:S(2)}, u32[]{:S(2)}) collective-permute-start(f32[32,768]{1,0:T(8,128)} %get-tuple-element.167), channel_id=1, source_target_pairs={{0,3},{1,2},{2,1},{3,0},{4,7},{5,6},{6,5},{7,4},{8,11},{9,10},{10,... | collective-permute-start | bytes 294920 | tf_op jit(solution)/shard_map/ppermute | solution.py:47
  110.6 9.2 %collective-permute-start.23 = (f32[64,512]{1,0:T(8,128)S(1)}, f32[64,512]{1,0:T(8,128)S(1)}, u32[]{:S(2)}, u32[]{:S(2)}) collective-permute-start(f32[64,512]{1,0:T(8,128)S(1)} %add_add_fusion.2), channel_id=1, source_target_pairs={{0,8},{4,12},{8,0},{12,4},{16,24},{20,28},{24,16},{28,20},{1,9},{5... | collective-permute-start | bytes 393224 | tf_op jit(solution)/shard_map/ppermute | solution.py:47
  112.4 9.4 %collective-permute-start.24 = (f32[64,512]{1,0:T(8,128)S(1)}, f32[64,512]{1,0:T(8,128)S(1)}, u32[]{:S(2)}, u32[]{:S(2)}) collective-permute-start(f32[64,512]{1,0:T(8,128)S(1)} %add_add_fusion.2), channel_id=1, source_target_pairs={{0,16},{4,20},{8,24},{12,28},{16,0},{20,4},{24,8},{28,12},{1,17},{... | collective-permute-start | bytes 393224 | tf_op jit(solution)/shard_map/ppermute | solution.py:47
  112.4 9.4 %collective-permute-start.25 = (f32[64,512]{1,0:T(8,128)S(1)}, f32[64,512]{1,0:T(8,128)S(1)}, u32[]{:S(2)}, u32[]{:S(2)}) collective-permute-start(f32[64,512]{1,0:T(8,128)S(1)} %add_add_fusion.2), channel_id=1, source_target_pairs={{0,24},{4,28},{8,16},{12,20},{16,8},{20,12},{24,0},{28,4},{1,25},{... | collective-permute-start | bytes 393224 | tf_op jit(solution)/shard_map/ppermute | solution.py:47
  118.3 4.7 %collective-permute-start.19 = (f32[32,768]{1,0:T(8,128)S(1)}, f32[32,768]{1,0:T(8,128)S(1)}, u32[]{:S(2)}, u32[]{:S(2)}) collective-permute-start(f32[32,768]{1,0:T(8,128)S(1)} %add_add_fusion.3), channel_id=1, source_target_pairs={{0,8},{4,12},{8,0},{12,4},{16,24},{20,28},{24,16},{28,20},{1,9},{5... | collective-permute-start | bytes 294920 | tf_op jit(solution)/shard_map/ppermute | solution.py:47
  119.8 5.7 %collective-permute-start.20 = (f32[32,768]{1,0:T(8,128)S(1)}, f32[32,768]{1,0:T(8,128)S(1)}, u32[]{:S(2)}, u32[]{:S(2)}) collective-permute-start(f32[32,768]{1,0:T(8,128)S(1)} %add_add_fusion.3), channel_id=1, source_target_pairs={{0,16},{4,20},{8,24},{12,28},{16,0},{20,4},{24,8},{28,12},{1,17},{... | collective-permute-start | bytes 294920 | tf_op jit(solution)/shard_map/ppermute | solution.py:47
  119.8 5.7 %collective-permute-start.21 = (f32[32,768]{1,0:T(8,128)S(1)}, f32[32,768]{1,0:T(8,128)S(1)}, u32[]{:S(2)}, u32[]{:S(2)}) collective-permute-start(f32[32,768]{1,0:T(8,128)S(1)} %add_add_fusion.3), channel_id=1, source_target_pairs={{0,24},{4,28},{8,16},{12,20},{16,8},{20,12},{24,0},{28,4},{1,25},{... | collective-permute-start | bytes 294920 | tf_op jit(solution)/shard_map/ppermute | solution.py:47
  121.9 24.0 %copy-start.2 = (f32[16,64,128]{2,1,0:T(8,128)S(1)}, f32[16,64,128]{2,1,0:T(8,128)}, u32[]{:S(2)}) copy-start(f32[16,64,128]{2,1,0:T(8,128)} %get-tuple-element.447) | copy-start | bytes 1572868
  121.9 5.4 %collective-permute-start.26 = (f32[256,512]{1,0:T(8,128)S(1)}, f32[256,512]{1,0:T(8,128)S(1)}, u32[]{:S(2)}, u32[]{:S(2)}) collective-permute-start(f32[256,512]{1,0:T(8,128)S(1)} %pad_maximum_fusion.gram_ref), channel_id=1, source_target_pairs={{0,4},{4,0},{8,12},{12,8},{16,20},{20,16},{24,28},{28,24},{1,5},{5... | collective-permute-start | bytes 1572872 | tf_op jit(solution)/shard_map/ppermute | solution.py:47
  125.5 1.8 %collective-permute-start.22 = (f32[128,768]{1,0:T(8,128)S(1)}, f32[128,768]{1,0:T(8,128)S(1)}, u32[]{:S(2)}, u32[]{:S(2)}) collective-permute-start(f32[128,768]{1,0:T(8,128)S(1)} %pad_maximum_fusion.1.sums_ref), channel_id=1, source_target_pairs={{0,4},{4,0},{8,12},{12,8},{16,20},{20,16},{24,28},{28,24},{1,5},{5... | collective-permute-start | bytes 1179656 | tf_op jit(solution)/shard_map/ppermute | solution.py:47

commit v5 on v4

--- a/solution.py
+++ b/solution.py
@@ -99,79 +99,61 @@
 
 
 def evolve_kernel(index_ref, disp_ref, vel_ref, stiff_ref, before_ref, after_ref, *rest, slots):
-    outs, (disp_pad, vel_pad, stiff_pad) = rest[:-3], rest[-3:]
-    size = outs[0].shape[0]
+    outs, (even_ref, odd_ref, speed_ref, pad_ref, all_ref, sem) = rest[:slots], rest[slots:]
     lines, members, width = disp_ref.shape
     w = STEPS
-    blocks = lines // size
+    full = lines + 2 * w
+    size = lines // slots
     lane = lax.broadcasted_iota(jnp.int32, (8, width), 1)
-    for slot, out in zip(slots, outs):
-        block = index_ref[0] ^ index_ref[FIRST + slot]
-        start = block * size
-        disp_pad[w:w + size] = disp_ref[pl.ds(start, size)]
-        vel_pad[w:w + size] = vel_ref[pl.ds(start, size)]
-        stiff_pad[8:8 + size, :] = stiff_ref[pl.ds(pl.multiple_of(start, 8), size), :]
-
-        @pl.when(block == 0)
-        def _():
-            disp_pad[:w] = before_ref[:w]
-            vel_pad[:w] = before_ref[w:2 * w]
-            stiff_pad[8 - w:8, :] = before_ref[2 * w, :w, :]
-
-        @pl.when(block > 0)
-        def _():
-            low = jnp.maximum(start - w, 0)
-            disp_pad[:w] = disp_ref[pl.ds(low, w)]
-            vel_pad[:w] = vel_ref[pl.ds(low, w)]
-            stiff_pad[:8, :] = stiff_ref[pl.ds(pl.multiple_of(jnp.maximum(start - 8, 0), 8), 8), :]
-
-        @pl.when(block == blocks - 1)
-        def _():
-            disp_pad[w + size:] = after_ref[:w]
-            vel_pad[w + size:] = after_ref[w:2 * w]
-            stiff_pad[8 + size:8 + size + w, :] = after_ref[2 * w, :w, :]
-
-        @pl.when(block < blocks - 1)
-        def _():
-            high = jnp.minimum(start + size, lines - 8)
-            disp_pad[w + size:] = disp_ref[pl.ds(high, w)]
-            vel_pad[w + size:] = vel_ref[pl.ds(high, w)]
-            stiff_pad[8 + size:, :] = stiff_ref[pl.ds(pl.multiple_of(high, 8), 8), :]
-
-        def group_step(g, carry):
-            at = pl.ds(pl.multiple_of(g * 8, 8), 8)
-            disp = {i: disp_pad[i, at, :] for i in range(size + 2 * w)}
-            vel = {i: vel_pad[i, at, :] for i in range(1, size + 2 * w - 1)}
-            for step in range(1, w + 1):
-                new = {}
-                for i in range(step, size + 2 * w - step):
-                    u = disp[i]
-                    right = jnp.where(lane == width - 1, 0.0, pltpu.roll(u, width - 1, 1))
-                    left = jnp.where(lane == 0, 0.0, pltpu.roll(u, 1, 1))
-                    around = (disp[i + 1] + disp[i - 1]) + (right + left)
-                    stiff = jnp.broadcast_to(stiff_pad[8 - w + i:8 - w + i + 1, :], (8, width))
-                    vel[i] = vel[i] + stiff * (around + u * (0.5 * pl.reciprocal(1.0 + u * u) - 4.5))
-                    new[i] = u + vel[i]
-                disp = new
-            for i in range(size):
-                out[i, at, :] = disp[w + i]
-            return carry
-
-        lax.fori_loop(0, members // 8, group_step, 0)
-
-
-def evolve(index, disp, vel, stiff, before, after, slots, size):
+    pad_ref[w:2 * w, :] = before_ref[2 * w, :w, :]
+    pad_ref[8:8 + lines, :] = stiff_ref[...]
+    pad_ref[8 + lines:8 + lines + w, :] = after_ref[2 * w, :w, :]
+
+    def group_step(g, carry):
+        at = pl.ds(pl.multiple_of(g * 8, 8), 8)
+        for i in range(w):
+            even_ref[i], speed_ref[i] = before_ref[i, at, :], before_ref[w + i, at, :]
+            even_ref[w + lines + i], speed_ref[w + lines + i] = after_ref[i, at, :], after_ref[w + i, at, :]
+        for i in range(lines):
+            even_ref[w + i], speed_ref[w + i] = disp_ref[i, at, :], vel_ref[i, at, :]
+        now, then = even_ref, odd_ref
+        for step in range(1, w + 1):
+            for i in range(step, full - step):
+                u = now[i]
+                right = jnp.where(lane == width - 1, 0.0, pltpu.roll(u, width - 1, 1))
+                left = jnp.where(lane == 0, 0.0, pltpu.roll(u, 1, 1))
+                around = (now[i + 1] + now[i - 1]) + (right + left)
+                stiff = jnp.broadcast_to(pad_ref[8 - w + i:8 - w + i + 1, :], (8, width))
+                speed = speed_ref[i] + stiff * (around + u * (0.5 / (1.0 + u * u) - 4.5))
+                if step < w:
+                    then[i], speed_ref[i] = u + speed, speed
+                else:
+                    all_ref[i - w, at, :] = u + speed
+            now, then = then, now
+        return carry
+
+    lax.fori_loop(0, members // 8, group_step, 0)
+    copies = []
+    for slot, out in enumerate(outs):
+        start = (index_ref[0] ^ index_ref[FIRST + slot]) * size
+        copies.append(pltpu.make_async_copy(all_ref.at[pl.ds(start, size)], out, sem.at[slot]))
+        copies[-1].start()
+    for copy in copies:
+        copy.wait()
+
+
+def evolve(index, disp, vel, stiff, before, after, slots):
     lines, members, width = disp.shape
-    w = STEPS
+    line = pltpu.VMEM((lines + 2 * STEPS, 8, width), jnp.float32)
     return pl.pallas_call(
         functools.partial(evolve_kernel, slots=slots),
         in_specs=[SCALARS] + [pl.BlockSpec(memory_space=pltpu.VMEM)] * 5,
-        out_shape=[pltpu.HBM((size, members, width), jnp.float32)] * len(slots),
-        out_specs=[pl.BlockSpec((size, members, width), lambda: (0, 0, 0))] * len(slots),
-        scratch_shapes=[pltpu.VMEM((size + 2 * w, members, width), jnp.float32)] * 2
-        + [pltpu.VMEM((size + 16, width), jnp.float32)],
-        compiler_params=params(10),
-        name="evolve%d" % slots[0],
+        out_shape=[pltpu.HBM((lines // slots, members, width), jnp.float32)] * slots,
+        out_specs=[pl.BlockSpec(memory_space=pltpu.HBM)] * slots,
+        scratch_shapes=[line, line, line, pltpu.VMEM((lines + 16, width), jnp.float32),
+                        pltpu.VMEM((lines, members, width), jnp.float32), pltpu.SemaphoreType.DMA((slots,))],
+        compiler_params=params(8),
+        name="evolve",
     )(index, disp, vel, stiff, before, after)
 
 
@@ -459,32 +441,22 @@
     disp, vel = to_lines(late_disp, late_vel)
     before, after, disp = lax.optimization_barrier((before, after, disp))
 
-    pieces = list(evolve(index, disp, vel, stiffness, before, after, tuple(range(ranks - 1)), lines))
+    pieces = list(evolve(index, disp, vel, stiffness, before, after, ranks))
     order, pieces = lax.optimization_barrier((index, pieces))
     for slot in range(ranks - 1):
         pairs = [(s * ranks + a, s * ranks + (a ^ orders[s % 2][slot])) for s in range(sims) for a in range(ranks)]
         pieces[slot] = lax.ppermute(pieces[slot], ("sim", "ana"), pairs)
 
-    once = 1 + (ana >> 20)
-
     def meanwhile(_, carry):
-        at, _, _ = carry
-        own, = evolve(at, disp, vel, stiffness, before, after, (ranks - 1,), lines)
+        at, _ = carry
         send, keep = basis_gram(at, basis)
-        return at + (at >> 20), own, chip_scatter(at, send, keep, 2)
-
-    order, own, gram = lax.fori_loop(0, once, meanwhile, (
-        order, jnp.zeros((lines, disp.shape[1], width), jnp.float32), jnp.zeros((rank // sims, rank), jnp.float32)))
-    pieces = pieces + [own]
+        return at + (at >> 20), chip_scatter(at, send, keep, 2)
+
+    order, gram = lax.fori_loop(0, 1 + (ana >> 20), meanwhile, (order, jnp.zeros((rank // sims, rank), jnp.float32)))
     gram_parts = [xor_permute(gram, "ana", k) for k in range(1, ranks)]
 
-    def first_stages(_, carry):
-        at, _ = carry
-        send, keep = products(at, basis, pieces)
-        return at + (at >> 20), chip_scatter(at, send, keep, 2)
-
-    total = initial_disp.shape[0] * ranks
-    order, sums = lax.fori_loop(0, once, first_stages, (order, jnp.zeros((total // sims, rank + total), jnp.float32)))
+    send, keep = products(order, basis, pieces)
+    sums = chip_scatter(order, send, keep, chips)
     sums, gram, gram_parts = lax.optimization_barrier((sums, gram, gram_parts))
     gram = chip_gather(tree_sum([gram] + gram_parts), chips)
     sums = ana_sum(sums)

time: 155 us -> 145 us (0.935)
  Pallas kernels: 62.3 us -> 53.4 us
  waiting for transfers between devices: 40.7 us -> 46.9 us
  starting transfers between devices: 44.8 us -> 41.7 us
  other arithmetic: 3.38 us -> 0.93 us
    ppermute x3, waiting for transfers between devices: 0.01 us -> 19.2 us  [per_device(): pieces[slot] = lax.ppermute(pieces[slot], ('sim', 'ana'), pairs)]
    ppermute x22, waiting for transfers between devices: 40.7 us -> 27.7 us  [xor_permute(): return lax.ppermute(value, axis, [(i, i ^ mask) for i in range(size)])]
    pallas_call x2 -> x1, Pallas kernels: 15.7 us -> 7.28 us  [evolve(): pl.pallas_call(functools.partial(evolve_kernel, slots=slots), in_specs=[S...]
    ppermute x22, starting transfers between devices: 36.1 us -> 33 us  [xor_permute(): return lax.ppermute(value, axis, [(i, i ^ mask) for i in range(size)])]
    add x4, other arithmetic: 3.22 us -> 0.78 us  [tree_sum(): values = [a + b for a, b in zip(values[::2], values[1::2])]]
  transfers between devices with their start and end apart: 27 -> 27, of which waited for: 11 -> 13; matrix products, arithmetic and copies ran while one was open for 3% -> 1% of each run, Pallas kernels for 10% -> 7%
where the time goes in v5:
time: 145 us; the launch traced here: 144 us
  Pallas kernels  53.4 us (37%)
  waiting for transfers between devices  46.9 us (32%)
  starting transfers between devices  41.7 us (29%)
    ppermute x22, starting transfers between devices, xor_permute(): return lax.ppermute(value, axis, [(i, i ^ mask) for i in range(size)])  33 us
    ppermute x22, waiting for transfers between devices, xor_permute(): return lax.ppermute(value, axis, [(i, i ^ mask) for i in range(size)])  27.7 us
    ppermute x3, waiting for transfers between devices, per_device(): pieces[slot] = lax.ppermute(pieces[slot], ('sim', 'ana'), pairs)  19.2 us
    pallas_call x1, Pallas kernels, solve(): pl.pallas_call(functools.partial(solve_kernel, count=float(count), chips=...  18.6 us
    pallas_call x1, Pallas kernels, rotate(): pl.pallas_call(rotate_kernel, grid=(lines // block,), in_specs=[SCALARS]...  8.07 us
    pallas_call x1, Pallas kernels, evolve(): pl.pallas_call(functools.partial(evolve_kernel, slots=slots), in_specs=[S...  7.28 us
    pallas_call x1, Pallas kernels, products(): pl.pallas_call(products_kernel, grid=(lines // block,), in_specs=[SCALARS...  5.91 us
    pallas_call x1, Pallas kernels, basis_gram(): pl.pallas_call(basis_gram_kernel, grid=(lines // block,), in_specs=[SCALA...  5.45 us
  transfers between devices with their start and end apart: 27, of which 13 were waited for; matrix products, arithmetic and copies ran while one was open for 1% of the time, Pallas kernels for 7%

profile of v5, /device:TPU:0, one launch (start us, length us, event | category | flops | bytes accessed | tf_op | source)
XLA Modules:
  0.0 144.4 jit_solution(10399692005031531417)
XLA Ops:
  0.6 2.3 %edges.1 = (f32[9,64,128]{2,1,0:T(8,128)}, f32[9,64,128]{2,1,0:T(8,128)}) custom-call(f32[64,128]{1,0:T(8,128)} %stiff_ref.3, f32[64,64,128]{2,1,0:T(8,128)} %disp_high.1, f32[64,64,128]{2,1,0:T(8,128)} %vel_high.1, f32[64,64,128]{2,1,0:T(8,128)} %disp_high.1, f32[64,64,128]{2,1,0:T(8,128)} %vel_high.1), custom_call_target="tpu_custom_call" | custom-call | tf_op jit(solution)/shard_map/edges/pallas_call | solution.py:67
  2.9 2.4 %collective-permute-start.4 = (f32[9,64,128]{2,1,0:T(8,128)}, f32[9,64,128]{2,1,0:T(8,128)S(1)}, u32[]{:S(2)}, u32[]{:S(2)}) collective-permute-start(f32[9,64,128]{2,1,0:T(8,128)} %get-tuple-element.70), channel_id=1, source_target_pairs={{0,4},{4,8},{8,12},{12,16},{16,20},{20,24},{24,28},{1,5},{5,9},{9,... | collective-permute-start | bytes 884744 | tf_op jit(solution)/shard_map/ppermute | solution.py:438
  5.3 1.3 collective-permute-start.5
  6.7 4.6 %to_lines.1 = (f32[64,64,128]{2,1,0:T(8,128)S(1)}, f32[64,64,128]{2,1,0:T(8,128)S(1)}) custom-call(f32[4096,128]{1,0:T(8,128)} %bitcast.5, f32[4096,128]{1,0:T(8,128)} %bitcast.6), custom_call_target="tpu_custom_call" | custom-call | tf_op jit(solution)/shard_map/to_lines/pallas_call | solution.py:90
  11.3 0.1 pad_add_fusion.index_ref
  11.4 7.3 %evolve.1 = (f32[16,64,128]{2,1,0:T(8,128)}, f32[16,64,128]{2,1,0:T(8,128)}, f32[16,64,128]{2,1,0:T(8,128)}, f32[16,64,128]{2,1,0:T(8,128)}) custom-call(s32[7]{0:T(128)S(1)} %pad_add_fusion.index_ref, f32[64,64,128]{2,1,0:T(8,128)S(1)} %get-tuple-element.75.disp_ref, f32[64,64,128]{2,1,0:T(8,128)S(1)} %get-tuple-element.76.vel_ref, ...), custom_call_target="tpu_custom_call" | custom-call | tf_op jit(solution)/shard_map/evolve/pallas_call | solution.py:148
  18.7 2.5 %collective-permute-start.6 = (f32[16,64,128]{2,1,0:T(8,128)}, f32[16,64,128]{2,1,0:T(8,128)S(1)}, u32[]{:S(2)}, u32[]{:S(2)}) collective-permute-start(f32[16,64,128]{2,1,0:T(8,128)} %get-tuple-element.85), channel_id=1, source_target_pairs={{0,1},{1,0},{2,3},{3,2},{4,7},{5,6},{6,5},{7,4},{8,9},{9,8},{10,11... | collective-permute-start | bytes 1572872 | tf_op jit(solution)/shard_map/ppermute | solution.py:448
  21.1 2.5 %collective-permute-start.7 = (f32[16,64,128]{2,1,0:T(8,128)}, f32[16,64,128]{2,1,0:T(8,128)S(1)}, u32[]{:S(2)}, u32[]{:S(2)}) collective-permute-start(f32[16,64,128]{2,1,0:T(8,128)} %get-tuple-element.86), channel_id=1, source_target_pairs={{0,3},{1,2},{2,1},{3,0},{4,6},{5,7},{6,4},{7,5},{8,11},{9,10},{10,... | collective-permute-start | bytes 1572872 | tf_op jit(solution)/shard_map/ppermute | solution.py:448
  23.6 0.1 collective-permute-start.8
  23.7 0.7 broadcast_in_dim.3
  24.4 24.5 %while.12 = (s32[]{:T(128)}, s32[7]{0:T(128)S(1)}, f32[64,512]{1,0:T(8,128)}, s32[]{:T(128)}, f32[16,128,512]{2,1,0:T(8,128)}, /*index=5*/s32[]{:T(128)}) while((s32[]{:T(128)}, s32[7]{0:T(128)S(1)}, f32[64,512]{1,0:T(8,128)}, s32[]{:T(128)}, f32[16,128,512]{2,1,0:T(8,128)}, /*index=5*/s32[]{:T(128)}) %tuple.34), condition=%wide.region_1.2_spmd, body=%wide.region_0.1_spmd.sunk | while | flops 98320 | bytes 4325661 | solution.py:455
  24.4 5.5 %basis_gram.1 = (f32[256,512]{1,0:T(8,128)S(1)}, f32[256,512]{1,0:T(8,128)S(1)}) custom-call(s32[7]{0:T(128)S(1)} %get-tuple-element.167.index_ref, f32[16,128,512]{2,1,0:T(8,128)} %get-tuple-element.176.basis_ref), custom_call_target="tpu_custom_call" | custom-call | tf_op jit(solution)/shard_map/while/body/basis_gram/pallas_call | solution.py:186
  29.9 3.9 %collective-permute-start = (f32[256,512]{1,0:T(8,128)S(1)}, f32[256,512]{1,0:T(8,128)S(1)}, u32[]{:S(2)}, u32[]{:S(2)}) collective-permute-start(f32[256,512]{1,0:T(8,128)S(1)} %get-tuple-element.153), channel_id=1, source_target_pairs={{0,4},{4,0},{8,12},{12,8},{16,20},{20,16},{24,28},{28,24},{1,5},{5... | collective-permute-start | bytes 1572872 | tf_op jit(solution)/shard_map/while/body/ppermute | solution.py:47
  33.8 1.5 %collective-permute-done.got_ref = f32[256,512]{1,0:T(8,128)S(1)} collective-permute-done((f32[256,512]{1,0:T(8,128)S(1)}, f32[256,512]{1,0:T(8,128)S(1)}, u32[]{:S(2)}, u32[]{:S(2)}) %collective-permute-start) | collective-permute-done | bytes 524320 | tf_op jit(solution)/shard_map/while/body/ppermute | solution.py:47
  35.3 0.6 split.3
  35.9 2.1 %collective-permute-start.2 = (f32[64,512]{1,0:T(8,128)S(1)}, f32[64,512]{1,0:T(8,128)S(1)}, u32[]{:S(2)}, u32[]{:S(2)}) collective-permute-start(f32[64,512]{1,0:T(8,128)S(1)} %get-tuple-element.156), channel_id=1, source_target_pairs={{0,8},{4,12},{8,0},{12,4},{16,24},{20,28},{24,16},{28,20},{1,9},{5... | collective-permute-start | bytes 393224 | tf_op jit(solution)/shard_map/while/body/ppermute | solution.py:47
  38.0 4.0 %collective-permute-done.2 = f32[64,512]{1,0:T(8,128)S(1)} collective-permute-done((f32[64,512]{1,0:T(8,128)S(1)}, f32[64,512]{1,0:T(8,128)S(1)}, u32[]{:S(2)}, u32[]{:S(2)}) %collective-permute-start.2) | collective-permute-done | bytes 131104 | tf_op jit(solution)/shard_map/while/body/ppermute | solution.py:47
  42.0 1.0 collective-permute-start.3
  43.0 0.5 collective-permute-done.1
  43.5 4.7 %collective-permute-done.3 = f32[64,512]{1,0:T(8,128)S(1)} collective-permute-done((f32[64,512]{1,0:T(8,128)S(1)}, f32[64,512]{1,0:T(8,128)S(1)}, u32[]{:S(2)}, u32[]{:S(2)}) %collective-permute-start.3) | collective-permute-done | bytes 131104 | tf_op jit(solution)/shard_map/while/body/ppermute | solution.py:47
  48.2 0.7 add_add_fusion.5
  48.9 19.2 %collective-permute-done.8.rest_2_ = f32[16,64,128]{2,1,0:T(8,128)S(1)} collective-permute-done((f32[16,64,128]{2,1,0:T(8,128)}, f32[16,64,128]{2,1,0:T(8,128)S(1)}, u32[]{:S(2)}, u32[]{:S(2)}) %collective-permute-start.8) | collective-permute-done | bytes 524320 | tf_op jit(solution)/shard_map/ppermute | solution.py:448
  68.1 5.9 %products.1 = (f32[128,768]{1,0:T(8,128)S(1)}, f32[128,768]{1,0:T(8,128)S(1)}) custom-call(s32[7]{0:T(128)S(1)} %get-tuple-element.84.index_ref, f32[16,128,512]{2,1,0:T(8,128)} %get-tuple-element.197, f32[16,64,128]{2,1,0:T(8,128)S(1)} %collective-permute-done.6.rest_0_, f32[16,64,128]{2,1,0:T(8,128)S(1)} %collective-permute-done.7.rest_1_, ...), custom_call_target="tpu_custom_call" | custom-call | tf_op jit(solution)/shard_map/products/pallas_call | solution.py:231
  74.0 2.2 %collective-permute-start.9 = (f32[128,768]{1,0:T(8,128)S(1)}, f32[128,768]{1,0:T(8,128)S(1)}, u32[]{:S(2)}, u32[]{:S(2)}) collective-permute-start(f32[128,768]{1,0:T(8,128)S(1)} %get-tuple-element.90), channel_id=1, source_target_pairs={{0,4},{4,0},{8,12},{12,8},{16,20},{20,16},{24,28},{28,24},{1,5},{5... | collective-permute-start | bytes 1179656 | tf_op jit(solution)/shard_map/ppermute | solution.py:47
  76.3 1.3 collective-permute-done.9.got_ref
  77.6 0.6 split.2
  78.2 4.7 %collective-permute-start.10 = (f32[32,768]{1,0:T(8,128)S(1)}, f32[32,768]{1,0:T(8,128)S(1)}, u32[]{:S(2)}, u32[]{:S(2)}) collective-permute-start(f32[32,768]{1,0:T(8,128)S(1)} %get-tuple-element.92), channel_id=1, source_target_pairs={{0,8},{4,12},{8,0},{12,4},{16,24},{20,28},{24,16},{28,20},{1,9},{5... | collective-permute-start | bytes 294920 | tf_op jit(solution)/shard_map/ppermute | solution.py:47
  82.9 1.5 %collective-permute-start.12 = (f32[32,768]{1,0:T(8,128)S(1)}, f32[32,768]{1,0:T(8,128)S(1)}, u32[]{:S(2)}, u32[]{:S(2)}) collective-permute-start(f32[32,768]{1,0:T(8,128)S(1)} %get-tuple-element.94), channel_id=1, source_target_pairs={{0,24},{4,28},{8,16},{12,20},{16,8},{20,12},{24,0},{28,4},{1,25},{... | collective-permute-start | bytes 294920 | tf_op jit(solution)/shard_map/ppermute | solution.py:47
  84.5 2.6 %collective-permute-start.15 = (f32[64,512]{1,0:T(8,128)S(1)}, f32[64,512]{1,0:T(8,128)S(1)}, u32[]{:S(2)}, u32[]{:S(2)}) collective-permute-start(f32[64,512]{1,0:T(8,128)S(1)} %copy-done.3), channel_id=1, source_target_pairs={{0,3},{1,2},{2,1},{3,0},{4,7},{5,6},{6,5},{7,4},{8,11},{9,10},{10,... | collective-permute-start | bytes 393224 | tf_op jit(solution)/shard_map/ppermute | solution.py:47
  87.1 1.8 %collective-permute-start.13 = (f32[64,512]{1,0:T(8,128)S(1)}, f32[64,512]{1,0:T(8,128)S(1)}, u32[]{:S(2)}, u32[]{:S(2)}) collective-permute-start(f32[64,512]{1,0:T(8,128)S(1)} %copy-done.3), channel_id=1, source_target_pairs={{0,1},{1,0},{2,3},{3,2},{4,5},{5,4},{6,7},{7,6},{8,9},{9,8},{10,11... | collective-permute-start | bytes 393224 | tf_op jit(solution)/shard_map/ppermute | solution.py:47
  88.9 0.7 collective-permute-done.11
  89.6 3.1 %collective-permute-done.15 = f32[64,512]{1,0:T(8,128)S(1)} collective-permute-done((f32[64,512]{1,0:T(8,128)S(1)}, f32[64,512]{1,0:T(8,128)S(1)}, u32[]{:S(2)}, u32[]{:S(2)}) %collective-permute-start.15) | collective-permute-done | bytes 131104 | tf_op jit(solution)/shard_map/ppermute | solution.py:47
  92.8 4.4 %collective-permute-done.14 = f32[64,512]{1,0:T(8,128)S(1)} collective-permute-done((f32[64,512]{1,0:T(8,128)S(1)}, f32[64,512]{1,0:T(8,128)S(1)}, u32[]{:S(2)}, u32[]{:S(2)}) %collective-permute-start.14) | collective-permute-done | bytes 131104 | tf_op jit(solution)/shard_map/ppermute | solution.py:47
  97.2 2.3 %collective-permute-start.18 = (f32[32,768]{1,0:T(8,128)S(1)}, f32[32,768]{1,0:T(8,128)S(1)}, u32[]{:S(2)}, u32[]{:S(2)}) collective-permute-start(f32[32,768]{1,0:T(8,128)S(1)} %add_add_fusion.3), channel_id=1, source_target_pairs={{0,3},{1,2},{2,1},{3,0},{4,7},{5,6},{6,5},{7,4},{8,11},{9,10},{10,... | collective-permute-start | bytes 294920 | tf_op jit(solution)/shard_map/ppermute | solution.py:47
  99.5 2.1 %collective-permute-start.16 = (f32[32,768]{1,0:T(8,128)S(1)}, f32[32,768]{1,0:T(8,128)S(1)}, u32[]{:S(2)}, u32[]{:S(2)}) collective-permute-start(f32[32,768]{1,0:T(8,128)S(1)} %add_add_fusion.3), channel_id=1, source_target_pairs={{0,1},{1,0},{2,3},{3,2},{4,5},{5,4},{6,7},{7,6},{8,9},{9,8},{10,11... | collective-permute-start | bytes 294920 | tf_op jit(solution)/shard_map/ppermute | solution.py:47
  101.6 1.5 %collective-permute-start.25 = (f32[64,512]{1,0:T(8,128)S(1)}, f32[64,512]{1,0:T(8,128)S(1)}, u32[]{:S(2)}, u32[]{:S(2)}) collective-permute-start(f32[64,512]{1,0:T(8,128)S(1)} %add_add_fusion.1), channel_id=1, source_target_pairs={{0,24},{4,28},{8,16},{12,20},{16,8},{20,12},{24,0},{28,4},{1,25},{... | collective-permute-start | bytes 393224 | tf_op jit(solution)/shard_map/ppermute | solution.py:47
  103.1 2.0 %collective-permute-start.24 = (f32[64,512]{1,0:T(8,128)S(1)}, f32[64,512]{1,0:T(8,128)S(1)}, u32[]{:S(2)}, u32[]{:S(2)}) collective-permute-start(f32[64,512]{1,0:T(8,128)S(1)} %add_add_fusion.1), channel_id=1, source_target_pairs={{0,16},{4,20},{8,24},{12,28},{16,0},{20,4},{24,8},{28,12},{1,17},{... | collective-permute-start | bytes 393224 | tf_op jit(solution)/shard_map/ppermute | solution.py:47
  105.1 1.5 %collective-permute-start.23 = (f32[64,512]{1,0:T(8,128)S(1)}, f32[64,512]{1,0:T(8,128)S(1)}, u32[]{:S(2)}, u32[]{:S(2)}) collective-permute-start(f32[64,512]{1,0:T(8,128)S(1)} %add_add_fusion.1), channel_id=1, source_target_pairs={{0,8},{4,12},{8,0},{12,4},{16,24},{20,28},{24,16},{28,20},{1,9},{5... | collective-permute-start | bytes 393224 | tf_op jit(solution)/shard_map/ppermute | solution.py:47
  106.6 1.4 collective-permute-done.17
  108.1 1.5 %collective-permute-start.21 = (f32[32,768]{1,0:T(8,128)S(1)}, f32[32,768]{1,0:T(8,128)S(1)}, u32[]{:S(2)}, u32[]{:S(2)}) collective-permute-start(f32[32,768]{1,0:T(8,128)S(1)} %add_add_fusion.2), channel_id=1, source_target_pairs={{0,24},{4,28},{8,16},{12,20},{16,8},{20,12},{24,0},{28,4},{1,25},{... | collective-permute-start | bytes 294920 | tf_op jit(solution)/shard_map/ppermute | solution.py:47
  109.6 1.7 %collective-permute-start.20 = (f32[32,768]{1,0:T(8,128)S(1)}, f32[32,768]{1,0:T(8,128)S(1)}, u32[]{:S(2)}, u32[]{:S(2)}) collective-permute-start(f32[32,768]{1,0:T(8,128)S(1)} %add_add_fusion.2), channel_id=1, source_target_pairs={{0,16},{4,20},{8,24},{12,28},{16,0},{20,4},{24,8},{28,12},{1,17},{... | collective-permute-start | bytes 294920 | tf_op jit(solution)/shard_map/ppermute | solution.py:47
  111.3 0.4 collective-permute-start.19
  111.8 2.8 %collective-permute-done.21 = f32[32,768]{1,0:T(8,128)S(1)} collective-permute-done((f32[32,768]{1,0:T(8,128)S(1)}, f32[32,768]{1,0:T(8,128)S(1)}, u32[]{:S(2)}, u32[]{:S(2)}) %collective-permute-start.21) | collective-permute-done | bytes 98336 | tf_op jit(solution)/shard_map/ppermute | solution.py:47
  114.6 1.4 collective-permute-done.20
  116.0 0.1 collective-permute-start.22
  116.1 1.7 %collective-permute-done.22.sums2_ref = f32[128,768]{1,0:T(8,128)S(1)} collective-permute-done((f32[128,768]{1,0:T(8,128)S(1)}, f32[128,768]{1,0:T(8,128)S(1)}, u32[]{:S(2)}, u32[]{:S(2)}) %collective-permute-start.22) | collective-permute-done | bytes 393248 | tf_op jit(solution)/shard_map/ppermute | solution.py:47
  117.8 18.6 %solve.1 = (bf16[768,512]{1,0:T(8,128)(2,1)S(1)}, bf16[768,512]{1,0:T(8,128)(2,1)S(1)}, f32[512,256]{1,0:T(8,128)}) custom-call(s32[7]{0:T(128)S(1)} %pad_add_fusion.index_ref, f32[128,768]{1,0:T(8,128)S(1)} %pad_maximum_fusion.1.sums_ref, f32[128,768]{1,0:T(8,128)S(1)} %collective-permute-done.22.sums2_ref, f32[256,512]{1,0:T(8,128)S(1)} %pad_maximum_fusion.gram_ref, ...), custom_call_target="tpu_custom_call" | custom-call | tf_op jit(solution)/shard_map/solve/pallas_call | solution.py:379
  136.4 8.1 %rotate.1 = f32[16,128,512]{2,1,0:T(8,128)} custom-call(s32[7]{0:T(128)S(1)} %pad_add_fusion.index_ref, bf16[768,512]{1,0:T(8,128)(2,1)S(1)} %get-tuple-element.101.high_ref, bf16[768,512]{1,0:T(8,128)(2,1)S(1)} %get-tuple-element.102.low_ref, f32[16,128,512]{2,1,0:T(8,128)} %get-tuple-element.197, f32[16,64,128]{2,1,0:T(8,128)S(1)} %collective-permute-done.6.rest_0_, ...), custom_call_target="tpu_custom_call" | custom-call | tf_op jit(solution)/shard_map/rotate/pallas_call | solution.py:410
  (39 shorter events, 0.3 us)
Async XLA Ops:
  2.9 8.4 %collective-permute-start.4 = (f32[9,64,128]{2,1,0:T(8,128)}, f32[9,64,128]{2,1,0:T(8,128)S(1)}, u32[]{:S(2)}, u32[]{:S(2)}) collective-permute-start(f32[9,64,128]{2,1,0:T(8,128)} %get-tuple-element.70), channel_id=1, source_target_pairs={{0,4},{4,8},{8,12},{12,16},{16,20},{20,24},{24,28},{1,5},{5,9},{9,... | collective-permute-start | bytes 884744 | tf_op jit(solution)/shard_map/ppermute | solution.py:438
  5.3 6.1 %collective-permute-start.5 = (f32[9,64,128]{2,1,0:T(8,128)}, f32[9,64,128]{2,1,0:T(8,128)S(1)}, u32[]{:S(2)}, u32[]{:S(2)}) collective-permute-start(f32[9,64,128]{2,1,0:T(8,128)} %get-tuple-element.71), channel_id=1, source_target_pairs={{4,0},{8,4},{12,8},{16,12},{20,16},{24,20},{28,24},{5,1},{9,5},{13... | collective-permute-start | bytes 884744 | tf_op jit(solution)/shard_map/ppermute | solution.py:439
  6.6 4.6 %copy-start.4 = (s32[4]{0:T(128)S(1)}, s32[4]{0:T(128)}, u32[]{:S(2)}) copy-start(s32[4]{0:T(128)} %constant.48.clone) | copy-start | bytes 52
  6.6 4.6 %copy-start.5 = (s32[4]{0:T(128)S(1)}, s32[4]{0:T(128)}, u32[]{:S(2)}) copy-start(s32[4]{0:T(128)} %constant.47.clone) | copy-start | bytes 52
  6.7 4.7 %copy-start.2 = (f32[64,128]{1,0:T(8,128)S(1)}, f32[64,128]{1,0:T(8,128)}, u32[]{:S(2)}) copy-start(f32[64,128]{1,0:T(8,128)} %stiff_ref.3) | copy-start | bytes 98308
  18.7 30.2 %collective-permute-start.6 = (f32[16,64,128]{2,1,0:T(8,128)}, f32[16,64,128]{2,1,0:T(8,128)S(1)}, u32[]{:S(2)}, u32[]{:S(2)}) collective-permute-start(f32[16,64,128]{2,1,0:T(8,128)} %get-tuple-element.85), channel_id=1, source_target_pairs={{0,1},{1,0},{2,3},{3,2},{4,7},{5,6},{6,5},{7,4},{8,9},{9,8},{10,11... | collective-permute-start | bytes 1572872 | tf_op jit(solution)/shard_map/ppermute | solution.py:448
  21.1 27.7 %collective-permute-start.7 = (f32[16,64,128]{2,1,0:T(8,128)}, f32[16,64,128]{2,1,0:T(8,128)S(1)}, u32[]{:S(2)}, u32[]{:S(2)}) collective-permute-start(f32[16,64,128]{2,1,0:T(8,128)} %get-tuple-element.86), channel_id=1, source_target_pairs={{0,3},{1,2},{2,1},{3,0},{4,6},{5,7},{6,4},{7,5},{8,11},{9,10},{10,... | collective-permute-start | bytes 1572872 | tf_op jit(solution)/shard_map/ppermute | solution.py:448
  23.6 44.5 %collective-permute-start.8 = (f32[16,64,128]{2,1,0:T(8,128)}, f32[16,64,128]{2,1,0:T(8,128)S(1)}, u32[]{:S(2)}, u32[]{:S(2)}) collective-permute-start(f32[16,64,128]{2,1,0:T(8,128)} %get-tuple-element.87), channel_id=1, source_target_pairs={{0,2},{1,3},{2,0},{3,1},{4,5},{5,4},{6,7},{7,6},{8,10},{9,11},{10,... | collective-permute-start | bytes 1572872 | tf_op jit(solution)/shard_map/ppermute | solution.py:448
  24.4 43.7 %copy-start = (f32[16,64,128]{2,1,0:T(8,128)S(1)}, f32[16,64,128]{2,1,0:T(8,128)}, u32[]{:S(2)}) copy-start(f32[16,64,128]{2,1,0:T(8,128)} %get-tuple-element.88.rest_3_) | copy-start | bytes 1572868
  29.9 5.5 %collective-permute-start = (f32[256,512]{1,0:T(8,128)S(1)}, f32[256,512]{1,0:T(8,128)S(1)}, u32[]{:S(2)}, u32[]{:S(2)}) collective-permute-start(f32[256,512]{1,0:T(8,128)S(1)} %get-tuple-element.153), channel_id=1, source_target_pairs={{0,4},{4,0},{8,12},{12,8},{16,20},{20,16},{24,28},{28,24},{1,5},{5... | collective-permute-start | bytes 1572872 | tf_op jit(solution)/shard_map/while/body/ppermute | solution.py:47
  35.9 6.1 %collective-permute-start.2 = (f32[64,512]{1,0:T(8,128)S(1)}, f32[64,512]{1,0:T(8,128)S(1)}, u32[]{:S(2)}, u32[]{:S(2)}) collective-permute-start(f32[64,512]{1,0:T(8,128)S(1)} %get-tuple-element.156), channel_id=1, source_target_pairs={{0,8},{4,12},{8,0},{12,4},{16,24},{20,28},{24,16},{28,20},{1,9},{5... | collective-permute-start | bytes 393224 | tf_op jit(solution)/shard_map/while/body/ppermute | solution.py:47
  38.0 5.5 %collective-permute-start.1 = (f32[64,512]{1,0:T(8,128)S(1)}, f32[64,512]{1,0:T(8,128)S(1)}, u32[]{:S(2)}, u32[]{:S(2)}) collective-permute-start(f32[64,512]{1,0:T(8,128)S(1)} %get-tuple-element.154), channel_id=1, source_target_pairs={{0,16},{4,20},{8,24},{12,28},{16,0},{20,4},{24,8},{28,12},{1,17},{... | collective-permute-start | bytes 393224 | tf_op jit(solution)/shard_map/while/body/ppermute | solution.py:47
  42.0 6.2 %collective-permute-start.3 = (f32[64,512]{1,0:T(8,128)S(1)}, f32[64,512]{1,0:T(8,128)S(1)}, u32[]{:S(2)}, u32[]{:S(2)}) collective-permute-start(f32[64,512]{1,0:T(8,128)S(1)} %get-tuple-element.157), channel_id=1, source_target_pairs={{0,24},{4,28},{8,16},{12,20},{16,8},{20,12},{24,0},{28,4},{1,25},{... | collective-permute-start | bytes 393224 | tf_op jit(solution)/shard_map/while/body/ppermute | solution.py:47
  68.1 16.4 %copy-start.3 = (f32[64,512]{1,0:T(8,128)S(1)}, f32[64,512]{1,0:T(8,128)}, u32[]{:S(2)}) copy-start(f32[64,512]{1,0:T(8,128)} %get-tuple-element.97) | copy-start | bytes 393220
  74.0 3.6 %collective-permute-start.9 = (f32[128,768]{1,0:T(8,128)S(1)}, f32[128,768]{1,0:T(8,128)S(1)}, u32[]{:S(2)}, u32[]{:S(2)}) collective-permute-start(f32[128,768]{1,0:T(8,128)S(1)} %get-tuple-element.90), channel_id=1, source_target_pairs={{0,4},{4,0},{8,12},{12,8},{16,20},{20,16},{24,28},{28,24},{1,5},{5... | collective-permute-start | bytes 1179656 | tf_op jit(solution)/shard_map/ppermute | solution.py:47
  77.6 40.2 %copy-start.1 = (f32[768,512]{1,0:T(8,128)S(1)}, f32[768,512]{1,0:T(8,128)}, u32[]{:S(2)}) copy-start(f32[768,512]{1,0:T(8,128)} %rot_ref.1) | copy-start | bytes 4718596
  78.2 8.9 %collective-permute-start.10 = (f32[32,768]{1,0:T(8,128)S(1)}, f32[32,768]{1,0:T(8,128)S(1)}, u32[]{:S(2)}, u32[]{:S(2)}) collective-permute-start(f32[32,768]{1,0:T(8,128)S(1)} %get-tuple-element.92), channel_id=1, source_target_pairs={{0,8},{4,12},{8,0},{12,4},{16,24},{20,28},{24,16},{28,20},{1,9},{5... | collective-permute-start | bytes 294920 | tf_op jit(solution)/shard_map/ppermute | solution.py:47
  82.9 6.7 %collective-permute-start.11 = (f32[32,768]{1,0:T(8,128)S(1)}, f32[32,768]{1,0:T(8,128)S(1)}, u32[]{:S(2)}, u32[]{:S(2)}) collective-permute-start(f32[32,768]{1,0:T(8,128)S(1)} %get-tuple-element.93), channel_id=1, source_target_pairs={{0,16},{4,20},{8,24},{12,28},{16,0},{20,4},{24,8},{28,12},{1,17},{... | collective-permute-start | bytes 294920 | tf_op jit(solution)/shard_map/ppermute | solution.py:47
  82.9 6.7 %collective-permute-start.12 = (f32[32,768]{1,0:T(8,128)S(1)}, f32[32,768]{1,0:T(8,128)S(1)}, u32[]{:S(2)}, u32[]{:S(2)}) collective-permute-start(f32[32,768]{1,0:T(8,128)S(1)} %get-tuple-element.94), channel_id=1, source_target_pairs={{0,24},{4,28},{8,16},{12,20},{16,8},{20,12},{24,0},{28,4},{1,25},{... | collective-permute-start | bytes 294920 | tf_op jit(solution)/shard_map/ppermute | solution.py:47
  84.5 8.3 %collective-permute-start.15 = (f32[64,512]{1,0:T(8,128)S(1)}, f32[64,512]{1,0:T(8,128)S(1)}, u32[]{:S(2)}, u32[]{:S(2)}) collective-permute-start(f32[64,512]{1,0:T(8,128)S(1)} %copy-done.3), channel_id=1, source_target_pairs={{0,3},{1,2},{2,1},{3,0},{4,7},{5,6},{6,5},{7,4},{8,11},{9,10},{10,... | collective-permute-start | bytes 393224 | tf_op jit(solution)/shard_map/ppermute | solution.py:47
  87.1 10.1 %collective-permute-start.14 = (f32[64,512]{1,0:T(8,128)S(1)}, f32[64,512]{1,0:T(8,128)S(1)}, u32[]{:S(2)}, u32[]{:S(2)}) collective-permute-start(f32[64,512]{1,0:T(8,128)S(1)} %copy-done.3), channel_id=1, source_target_pairs={{0,2},{1,3},{2,0},{3,1},{4,6},{5,7},{6,4},{7,5},{8,10},{9,11},{10,... | collective-permute-start | bytes 393224 | tf_op jit(solution)/shard_map/ppermute | solution.py:47
  87.1 10.1 %collective-permute-start.13 = (f32[64,512]{1,0:T(8,128)S(1)}, f32[64,512]{1,0:T(8,128)S(1)}, u32[]{:S(2)}, u32[]{:S(2)}) collective-permute-start(f32[64,512]{1,0:T(8,128)S(1)} %copy-done.3), channel_id=1, source_target_pairs={{0,1},{1,0},{2,3},{3,2},{4,5},{5,4},{6,7},{7,6},{8,9},{9,8},{10,11... | collective-permute-start | bytes 393224 | tf_op jit(solution)/shard_map/ppermute | solution.py:47
  97.2 7.9 %collective-permute-start.18 = (f32[32,768]{1,0:T(8,128)S(1)}, f32[32,768]{1,0:T(8,128)S(1)}, u32[]{:S(2)}, u32[]{:S(2)}) collective-permute-start(f32[32,768]{1,0:T(8,128)S(1)} %add_add_fusion.3), channel_id=1, source_target_pairs={{0,3},{1,2},{2,1},{3,0},{4,7},{5,6},{6,5},{7,4},{8,11},{9,10},{10,... | collective-permute-start | bytes 294920 | tf_op jit(solution)/shard_map/ppermute | solution.py:47
  99.5 8.6 %collective-permute-start.17 = (f32[32,768]{1,0:T(8,128)S(1)}, f32[32,768]{1,0:T(8,128)S(1)}, u32[]{:S(2)}, u32[]{:S(2)}) collective-permute-start(f32[32,768]{1,0:T(8,128)S(1)} %add_add_fusion.3), channel_id=1, source_target_pairs={{0,2},{1,3},{2,0},{3,1},{4,6},{5,7},{6,4},{7,5},{8,10},{9,11},{10,... | collective-permute-start | bytes 294920 | tf_op jit(solution)/shard_map/ppermute | solution.py:47
  99.5 8.6 %collective-permute-start.16 = (f32[32,768]{1,0:T(8,128)S(1)}, f32[32,768]{1,0:T(8,128)S(1)}, u32[]{:S(2)}, u32[]{:S(2)}) collective-permute-start(f32[32,768]{1,0:T(8,128)S(1)} %add_add_fusion.3), channel_id=1, source_target_pairs={{0,1},{1,0},{2,3},{3,2},{4,5},{5,4},{6,7},{7,6},{8,9},{9,8},{10,11... | collective-permute-start | bytes 294920 | tf_op jit(solution)/shard_map/ppermute | solution.py:47
  101.6 9.7 %collective-permute-start.25 = (f32[64,512]{1,0:T(8,128)S(1)}, f32[64,512]{1,0:T(8,128)S(1)}, u32[]{:S(2)}, u32[]{:S(2)}) collective-permute-start(f32[64,512]{1,0:T(8,128)S(1)} %add_add_fusion.1), channel_id=1, source_target_pairs={{0,24},{4,28},{8,16},{12,20},{16,8},{20,12},{24,0},{28,4},{1,25},{... | collective-permute-start | bytes 393224 | tf_op jit(solution)/shard_map/ppermute | solution.py:47
  103.1 8.6 %collective-permute-start.24 = (f32[64,512]{1,0:T(8,128)S(1)}, f32[64,512]{1,0:T(8,128)S(1)}, u32[]{:S(2)}, u32[]{:S(2)}) collective-permute-start(f32[64,512]{1,0:T(8,128)S(1)} %add_add_fusion.1), channel_id=1, source_target_pairs={{0,16},{4,20},{8,24},{12,28},{16,0},{20,4},{24,8},{28,12},{1,17},{... | collective-permute-start | bytes 393224 | tf_op jit(solution)/shard_map/ppermute | solution.py:47
  105.1 6.6 %collective-permute-start.23 = (f32[64,512]{1,0:T(8,128)S(1)}, f32[64,512]{1,0:T(8,128)S(1)}, u32[]{:S(2)}, u32[]{:S(2)}) collective-permute-start(f32[64,512]{1,0:T(8,128)S(1)} %add_add_fusion.1), channel_id=1, source_target_pairs={{0,8},{4,12},{8,0},{12,4},{16,24},{20,28},{24,16},{28,20},{1,9},{5... | collective-permute-start | bytes 393224 | tf_op jit(solution)/shard_map/ppermute | solution.py:47
  108.1 6.5 %collective-permute-start.21 = (f32[32,768]{1,0:T(8,128)S(1)}, f32[32,768]{1,0:T(8,128)S(1)}, u32[]{:S(2)}, u32[]{:S(2)}) collective-permute-start(f32[32,768]{1,0:T(8,128)S(1)} %add_add_fusion.2), channel_id=1, source_target_pairs={{0,24},{4,28},{8,16},{12,20},{16,8},{20,12},{24,0},{28,4},{1,25},{... | collective-permute-start | bytes 294920 | tf_op jit(solution)/shard_map/ppermute | solution.py:47
  109.6 6.4 %collective-permute-start.20 = (f32[32,768]{1,0:T(8,128)S(1)}, f32[32,768]{1,0:T(8,128)S(1)}, u32[]{:S(2)}, u32[]{:S(2)}) collective-permute-start(f32[32,768]{1,0:T(8,128)S(1)} %add_add_fusion.2), channel_id=1, source_target_pairs={{0,16},{4,20},{8,24},{12,28},{16,0},{20,4},{24,8},{28,12},{1,17},{... | collective-permute-start | bytes 294920 | tf_op jit(solution)/shard_map/ppermute | solution.py:47
  111.3 4.7 %collective-permute-start.19 = (f32[32,768]{1,0:T(8,128)S(1)}, f32[32,768]{1,0:T(8,128)S(1)}, u32[]{:S(2)}, u32[]{:S(2)}) collective-permute-start(f32[32,768]{1,0:T(8,128)S(1)} %add_add_fusion.2), channel_id=1, source_target_pairs={{0,8},{4,12},{8,0},{12,4},{16,24},{20,28},{24,16},{28,20},{1,9},{5... | collective-permute-start | bytes 294920 | tf_op jit(solution)/shard_map/ppermute | solution.py:47
  111.7 6.1 %collective-permute-start.26 = (f32[256,512]{1,0:T(8,128)S(1)}, f32[256,512]{1,0:T(8,128)S(1)}, u32[]{:S(2)}, u32[]{:S(2)}) collective-permute-start(f32[256,512]{1,0:T(8,128)S(1)} %pad_maximum_fusion.gram_ref), channel_id=1, source_target_pairs={{0,4},{4,0},{8,12},{12,8},{16,20},{20,16},{24,28},{28,24},{1,5},{5... | collective-permute-start | bytes 1572872 | tf_op jit(solution)/shard_map/ppermute | solution.py:47
  116.0 1.8 %collective-permute-start.22 = (f32[128,768]{1,0:T(8,128)S(1)}, f32[128,768]{1,0:T(8,128)S(1)}, u32[]{:S(2)}, u32[]{:S(2)}) collective-permute-start(f32[128,768]{1,0:T(8,128)S(1)} %pad_maximum_fusion.1.sums_ref), channel_id=1, source_target_pairs={{0,4},{4,0},{8,12},{12,8},{16,20},{20,16},{24,28},{28,24},{1,5},{5... | collective-permute-start | bytes 1179656 | tf_op jit(solution)/shard_map/ppermute | solution.py:47

commit v6 on v5

--- a/solution.py
+++ b/solution.py
@@ -35,6 +35,12 @@
 def halves(value):
     high = value.astype(jnp.bfloat16)
     return high, (value - high.astype(jnp.float32)).astype(jnp.bfloat16)
+
+
+def thirds(value):
+    high, _ = halves(value)
+    rest = value - high.astype(jnp.float32)
+    return (high,) + halves(rest)
 
 
 def mm3(left, right, dims):
@@ -130,16 +136,16 @@
                 else:
                     all_ref[i - w, at, :] = u + speed
             now, then = then, now
+        for slot, out in enumerate(outs):
+            pltpu.make_async_copy(all_ref.at[block(slot), at], out.at[:, at], sem.at[slot]).start()
         return carry
 
+    def block(slot):
+        return pl.ds((index_ref[0] ^ index_ref[FIRST + slot]) * size, size)
+
     lax.fori_loop(0, members // 8, group_step, 0)
-    copies = []
     for slot, out in enumerate(outs):
-        start = (index_ref[0] ^ index_ref[FIRST + slot]) * size
-        copies.append(pltpu.make_async_copy(all_ref.at[pl.ds(start, size)], out, sem.at[slot]))
-        copies[-1].start()
-    for copy in copies:
-        copy.wait()
+        pltpu.make_async_copy(all_ref.at[block(slot)], out, sem.at[slot]).wait()
 
 
 def evolve(index, disp, vel, stiff, before, after, slots):
@@ -196,7 +202,7 @@
 
 
 def products_kernel(index_ref, basis_ref, *rest):
-    pieces, (send_ref, keep_ref, snap_ref, sum_ref) = rest[:-4], rest[-4:]
+    pieces, (send_ref, keep_ref, snap_ref, sum_ref, mixed_ref) = rest[:-5], rest[-5:]
     lines, members, width = pieces[0].shape
     rank = basis_ref.shape[-1]
     step = pl.program_id(0)
@@ -208,14 +214,17 @@
     @pl.when(step == 0)
     def _():
         sum_ref[...] = jnp.zeros_like(sum_ref)
-
-    snap = snap_ref[...]
+        mixed_ref[...] = jnp.zeros_like(mixed_ref)
+
+    snap = halves(snap_ref[...])
     rows = basis_ref[...].reshape(lines * width, rank)
-    sum_ref[:, :rank] += mm3(halves(snap), halves(rows), ((1,), (0,)))
-    sum_ref[:, rank:] += mm(snap, snap, ((1,), (1,)))
+    sum_ref[:, :rank] += mm3(snap, halves(rows), ((1,), (0,)))
+    sum_ref[:, rank:] += mm(snap[0], snap[0], ((1,), (1,)), None)
+    mixed_ref[...] += mm(snap[0], snap[1], ((1,), (1,)), None)
 
     @pl.when(step == pl.num_programs(0) - 1)
     def _():
+        sum_ref[:, rank:] += mixed_ref[...] + mixed_ref[...].T
         half = keep_ref.shape[0]
         core = index_ref[1]
         keep_ref[...] = sum_ref[pl.ds(pl.multiple_of(core * half, half), half), :]
@@ -235,7 +244,8 @@
         + [pl.BlockSpec((block, members, width), lambda i: (i, 0, 0))] * len(pieces),
         out_specs=[half, half],
         out_shape=[shape(total // 2, rank + total)] * 2,
-        scratch_shapes=[pltpu.VMEM((total, block * width), jnp.float32), pltpu.VMEM((total, rank + total), jnp.float32)],
+        scratch_shapes=[pltpu.VMEM((total, block * width), jnp.float32), pltpu.VMEM((total, rank + total), jnp.float32),
+                        pltpu.VMEM((total, total), jnp.float32)],
         compiler_params=params(14),
         name="products",
     )(index, in_hbm(basis), *pieces)
@@ -263,6 +273,12 @@
     while len(values) > 1:
         values = [a + b for a, b in zip(values[::2], values[1::2])]
     return values[0]
+
+
+def ana_sum_by_pairs(value, bits):
+    for bit in bits:
+        value = value + xor_permute(value, "ana", bit)
+    return value
 
 
 def exchange_chips(pieces, limit):
@@ -330,7 +346,11 @@
         done = jnp.concatenate([jnp.concatenate(v[:tiles], axis=1) for v in x], axis=0)
         lane = lax.broadcasted_iota(jnp.int32, (PANEL, members), 1)
         lower = jnp.where(lane >= start + PANEL, done[:, :members], 0.0)
-        work_ref[...] = work_ref[...] - mm(lower, done, ((0,), (0,)))
+        lh, lm, ll = thirds(lower)
+        dh, dm, dl = thirds(done)
+        left = jnp.concatenate([lh, lh, lm, lh, ll, lm], axis=0)
+        right = jnp.concatenate([dh, dm, dh, dl, dh, dm], axis=0)
+        work_ref[...] = work_ref[...] - mm(left, right, ((0,), (0,)), None)
         work_ref[pl.ds(start, PANEL), :] = done
         return carry
 
@@ -366,10 +386,11 @@
     eliminate(work_ref, members)
     top, bottom = rot_ref[:rank, :], rot_ref[rank:, :]
     upper = jnp.where(row <= col, work_ref[:, :members], 0.0)
-    mix = mm(work_ref[:, members:], bottom, ((0,), (0,)))
-    high_ref[:rank, :], low_ref[:rank, :] = halves(top - mm(coef, mix, ((0,), (0,))))
+    tops, bottoms, coefs = halves(top), halves(bottom), halves(coef)
+    mix = mm3(halves(work_ref[:, members:]), bottoms, ((0,), (0,)))
+    high_ref[:rank, :], low_ref[:rank, :] = halves(top - mm3(coefs, halves(mix), ((0,), (0,))))
     high_ref[rank:, :], low_ref[rank:, :] = halves(mix * along)
-    coords = (mm(coef, top, ((1,), (0,))) + mm(upper, bottom, ((0,), (0,)))) * math.sqrt(rank)
+    coords = (mm3(coefs, tops, ((1,), (0,))) + mm3(halves(upper), bottoms, ((0,), (0,)))) * math.sqrt(rank)
     coords_ref[...] = coords.T
 
 
@@ -450,15 +471,16 @@
     def meanwhile(_, carry):
         at, _ = carry
         send, keep = basis_gram(at, basis)
-        return at + (at >> 20), chip_scatter(at, send, keep, 2)
-
+        return at + (at >> 20), ana_sum_by_pairs(chip_scatter(at, send, keep, 2), bits[:-1])
+
+    bits = [2 ** i for i in range(ranks.bit_length() - 1)]
     order, gram = lax.fori_loop(0, 1 + (ana >> 20), meanwhile, (order, jnp.zeros((rank // sims, rank), jnp.float32)))
-    gram_parts = [xor_permute(gram, "ana", k) for k in range(1, ranks)]
+    gram = ana_sum_by_pairs(gram, bits[-1:])
 
     send, keep = products(order, basis, pieces)
     sums = chip_scatter(order, send, keep, chips)
-    sums, gram, gram_parts = lax.optimization_barrier((sums, gram, gram_parts))
-    gram = chip_gather(tree_sum([gram] + gram_parts), chips)
+    sums, gram = lax.optimization_barrier((sums, gram))
+    gram = chip_gather(gram, chips)
     sums = ana_sum(sums)
     sums = with_other_core(chip_gather(sums, chips))
     gram = with_other_core(gram)

time: 145 us -> 132 us (0.910)
  Pallas kernels: 53.4 us -> 48 us
  starting transfers between devices: 41.7 us -> 37 us
  waiting for transfers between devices: 46.9 us -> 43.7 us
    ppermute x3, waiting for transfers between devices: 19.2 us -> 13.9 us  [per_device(): pieces[slot] = lax.ppermute(pieces[slot], ('sim', 'ana'), pairs)]
    ppermute x22 -> x21, starting transfers between devices: 33 us -> 28.3 us  [xor_permute(): return lax.ppermute(value, axis, [(i, i ^ mask) for i in range(size)])]
    pallas_call x1, Pallas kernels: 18.6 us -> 14.5 us  [solve(): pl.pallas_call(functools.partial(solve_kernel, count=float(count), chips=...]
    ppermute x22 -> x21, waiting for transfers between devices: 27.7 us -> 29.8 us  [xor_permute(): return lax.ppermute(value, axis, [(i, i ^ mask) for i in range(size)])]
  transfers between devices with their start and end apart: 27 -> 26, of which waited for: 13 -> 16; matrix products, arithmetic and copies ran while one was open for 1% -> 1% of each run, Pallas kernels for 7% -> 9%
where the time goes in v6:
time: 132 us; the launch traced here: 131 us
  Pallas kernels  48 us (36%)
  waiting for transfers between devices  43.7 us (33%)
  starting transfers between devices  37 us (28%)
    ppermute x21, waiting for transfers between devices, xor_permute(): return lax.ppermute(value, axis, [(i, i ^ mask) for i in range(size)])  29.8 us
    ppermute x21, starting transfers between devices, xor_permute(): return lax.ppermute(value, axis, [(i, i ^ mask) for i in range(size)])  28.3 us
    pallas_call x1, Pallas kernels, solve(): pl.pallas_call(functools.partial(solve_kernel, count=float(count), chips=...  14.5 us
    ppermute x3, waiting for transfers between devices, per_device(): pieces[slot] = lax.ppermute(pieces[slot], ('sim', 'ana'), pairs)  13.9 us
    pallas_call x1, Pallas kernels, rotate(): pl.pallas_call(rotate_kernel, grid=(lines // block,), in_specs=[SCALARS]...  8.13 us
    pallas_call x1, Pallas kernels, evolve(): pl.pallas_call(functools.partial(evolve_kernel, slots=slots), in_specs=[S...  6.66 us
    pallas_call x1, Pallas kernels, basis_gram(): pl.pallas_call(basis_gram_kernel, grid=(lines // block,), in_specs=[SCALA...  5.44 us
    pallas_call x1, Pallas kernels, products(): pl.pallas_call(products_kernel, grid=(lines // block,), in_specs=[SCALARS...  5.21 us
  transfers between devices with their start and end apart: 26, of which 16 were waited for; matrix products, arithmetic and copies ran while one was open for 1% of the time, Pallas kernels for 9%

profile of v6, /device:TPU:0, one launch (start us, length us, event | category | flops | bytes accessed | tf_op | source)
XLA Modules:
  0.0 131.2 jit_solution(2449881597093077436)
XLA Ops:
  0.6 2.3 %edges.1 = (f32[9,64,128]{2,1,0:T(8,128)}, f32[9,64,128]{2,1,0:T(8,128)}) custom-call(f32[64,128]{1,0:T(8,128)} %stiff_ref.3, f32[64,64,128]{2,1,0:T(8,128)} %disp_high.1, f32[64,64,128]{2,1,0:T(8,128)} %vel_high.1, f32[64,64,128]{2,1,0:T(8,128)} %disp_high.1, f32[64,64,128]{2,1,0:T(8,128)} %vel_high.1), custom_call_target="tpu_custom_call" | custom-call | tf_op jit(solution)/shard_map/edges/pallas_call | solution.py:73
  2.9 2.4 %collective-permute-start.5 = (f32[9,64,128]{2,1,0:T(8,128)}, f32[9,64,128]{2,1,0:T(8,128)S(1)}, u32[]{:S(2)}, u32[]{:S(2)}) collective-permute-start(f32[9,64,128]{2,1,0:T(8,128)} %get-tuple-element.67), channel_id=1, source_target_pairs={{0,4},{4,8},{8,12},{12,16},{16,20},{20,24},{24,28},{1,5},{5,9},{9,... | collective-permute-start | bytes 884744 | tf_op jit(solution)/shard_map/ppermute | solution.py:459
  5.3 1.3 collective-permute-start.6
  6.7 4.6 %to_lines.1 = (f32[64,64,128]{2,1,0:T(8,128)S(1)}, f32[64,64,128]{2,1,0:T(8,128)S(1)}) custom-call(f32[4096,128]{1,0:T(8,128)} %bitcast.5, f32[4096,128]{1,0:T(8,128)} %bitcast.6), custom_call_target="tpu_custom_call" | custom-call | tf_op jit(solution)/shard_map/to_lines/pallas_call | solution.py:96
  11.4 6.7 %evolve.1 = (f32[16,64,128]{2,1,0:T(8,128)}, f32[16,64,128]{2,1,0:T(8,128)}, f32[16,64,128]{2,1,0:T(8,128)}, f32[16,64,128]{2,1,0:T(8,128)}) custom-call(s32[7]{0:T(128)S(1)} %pad_add_fusion.index_ref, f32[64,64,128]{2,1,0:T(8,128)S(1)} %get-tuple-element.72.disp_ref, f32[64,64,128]{2,1,0:T(8,128)S(1)} %get-tuple-element.73.vel_ref, ...), custom_call_target="tpu_custom_call" | custom-call | tf_op jit(solution)/shard_map/evolve/pallas_call | solution.py:154
  18.1 2.5 %collective-permute-start.7 = (f32[16,64,128]{2,1,0:T(8,128)}, f32[16,64,128]{2,1,0:T(8,128)S(1)}, u32[]{:S(2)}, u32[]{:S(2)}) collective-permute-start(f32[16,64,128]{2,1,0:T(8,128)} %get-tuple-element.82), channel_id=1, source_target_pairs={{0,1},{1,0},{2,3},{3,2},{4,7},{5,6},{6,5},{7,4},{8,9},{9,8},{10,11... | collective-permute-start | bytes 1572872 | tf_op jit(solution)/shard_map/ppermute | solution.py:469
  20.5 2.5 %collective-permute-start.8 = (f32[16,64,128]{2,1,0:T(8,128)}, f32[16,64,128]{2,1,0:T(8,128)S(1)}, u32[]{:S(2)}, u32[]{:S(2)}) collective-permute-start(f32[16,64,128]{2,1,0:T(8,128)} %get-tuple-element.83), channel_id=1, source_target_pairs={{0,3},{1,2},{2,1},{3,0},{4,6},{5,7},{6,4},{7,5},{8,11},{9,10},{10,... | collective-permute-start | bytes 1572872 | tf_op jit(solution)/shard_map/ppermute | solution.py:469
  23.0 0.1 collective-permute-start.9
  23.1 0.7 broadcast_in_dim.3
  23.8 29.8 %while.12 = (s32[]{:T(128)}, s32[7]{0:T(128)S(1)}, f32[64,512]{1,0:T(8,128)}, s32[]{:T(128)}, f32[16,128,512]{2,1,0:T(8,128)}, /*index=5*/s32[]{:T(128)}) while((s32[]{:T(128)}, s32[7]{0:T(128)S(1)}, f32[64,512]{1,0:T(8,128)}, s32[]{:T(128)}, f32[16,128,512]{2,1,0:T(8,128)}, /*index=5*/s32[]{:T(128)}) %tuple.34), condition=%wide.region_1.2_spmd, body=%wide.region_0.1_spmd.sunk | while | flops 131088 | bytes 5243205 | solution.py:477
  23.8 5.4 %basis_gram.1 = (f32[256,512]{1,0:T(8,128)S(1)}, f32[256,512]{1,0:T(8,128)S(1)}) custom-call(s32[7]{0:T(128)S(1)} %get-tuple-element.161.index_ref, f32[16,128,512]{2,1,0:T(8,128)} %get-tuple-element.170.basis_ref), custom_call_target="tpu_custom_call" | custom-call | tf_op jit(solution)/shard_map/while/body/basis_gram/pallas_call | solution.py:192
  29.2 3.9 %collective-permute-start = (f32[256,512]{1,0:T(8,128)S(1)}, f32[256,512]{1,0:T(8,128)S(1)}, u32[]{:S(2)}, u32[]{:S(2)}) collective-permute-start(f32[256,512]{1,0:T(8,128)S(1)} %get-tuple-element.147), channel_id=1, source_target_pairs={{0,4},{4,0},{8,12},{12,8},{16,20},{20,16},{24,28},{28,24},{1,5},{5... | collective-permute-start | bytes 1572872 | tf_op jit(solution)/shard_map/while/body/ppermute | solution.py:53
  33.2 1.5 %collective-permute-done.got_ref = f32[256,512]{1,0:T(8,128)S(1)} collective-permute-done((f32[256,512]{1,0:T(8,128)S(1)}, f32[256,512]{1,0:T(8,128)S(1)}, u32[]{:S(2)}, u32[]{:S(2)}) %collective-permute-start) | collective-permute-done | bytes 524320 | tf_op jit(solution)/shard_map/while/body/ppermute | solution.py:53
  34.7 0.6 split.3
  35.3 2.1 %collective-permute-start.2 = (f32[64,512]{1,0:T(8,128)S(1)}, f32[64,512]{1,0:T(8,128)S(1)}, u32[]{:S(2)}, u32[]{:S(2)}) collective-permute-start(f32[64,512]{1,0:T(8,128)S(1)} %get-tuple-element.150), channel_id=1, source_target_pairs={{0,8},{4,12},{8,0},{12,4},{16,24},{20,28},{24,16},{28,20},{1,9},{5... | collective-permute-start | bytes 393224 | tf_op jit(solution)/shard_map/while/body/ppermute | solution.py:53
  37.4 4.0 %collective-permute-done.2 = f32[64,512]{1,0:T(8,128)S(1)} collective-permute-done((f32[64,512]{1,0:T(8,128)S(1)}, f32[64,512]{1,0:T(8,128)S(1)}, u32[]{:S(2)}, u32[]{:S(2)}) %collective-permute-start.2) | collective-permute-done | bytes 131104 | tf_op jit(solution)/shard_map/while/body/ppermute | solution.py:53
  41.4 1.0 collective-permute-start.3
  42.4 0.5 collective-permute-done.1
  42.9 4.7 %collective-permute-done.3 = f32[64,512]{1,0:T(8,128)S(1)} collective-permute-done((f32[64,512]{1,0:T(8,128)S(1)}, f32[64,512]{1,0:T(8,128)S(1)}, u32[]{:S(2)}, u32[]{:S(2)}) %collective-permute-start.3) | collective-permute-done | bytes 131104 | tf_op jit(solution)/shard_map/while/body/ppermute | solution.py:53
  47.6 1.4 %collective-permute-start.4 = (f32[64,512]{1,0:T(8,128)S(1)}, f32[64,512]{1,0:T(8,128)S(1)}, u32[]{:S(2)}, u32[]{:S(2)}) collective-permute-start(f32[64,512]{1,0:T(8,128)S(1)} %add_add_fusion.4), channel_id=1, source_target_pairs={{0,1},{1,0},{2,3},{3,2},{4,5},{5,4},{6,7},{7,6},{8,9},{9,8},{10,11... | collective-permute-start | bytes 393224 | tf_op jit(solution)/shard_map/while/body/ppermute | solution.py:53
  49.0 3.9 %collective-permute-done.4 = f32[64,512]{1,0:T(8,128)S(1)} collective-permute-done((f32[64,512]{1,0:T(8,128)S(1)}, f32[64,512]{1,0:T(8,128)S(1)}, u32[]{:S(2)}, u32[]{:S(2)}) %collective-permute-start.4) | collective-permute-done | bytes 131104 | tf_op jit(solution)/shard_map/while/body/ppermute | solution.py:53
  52.9 0.7 add.83
  53.6 13.9 %collective-permute-done.9.rest_2_ = f32[16,64,128]{2,1,0:T(8,128)S(1)} collective-permute-done((f32[16,64,128]{2,1,0:T(8,128)}, f32[16,64,128]{2,1,0:T(8,128)S(1)}, u32[]{:S(2)}, u32[]{:S(2)}) %collective-permute-start.9) | collective-permute-done | bytes 524320 | tf_op jit(solution)/shard_map/ppermute | solution.py:469
  67.5 5.2 %products.1 = (f32[128,768]{1,0:T(8,128)S(1)}, f32[128,768]{1,0:T(8,128)S(1)}) custom-call(s32[7]{0:T(128)S(1)} %get-tuple-element.81.index_ref, f32[16,128,512]{2,1,0:T(8,128)} %get-tuple-element.191, f32[16,64,128]{2,1,0:T(8,128)S(1)} %collective-permute-done.7.rest_0_, f32[16,64,128]{2,1,0:T(8,128)S(1)} %collective-permute-done.8.rest_1_, ...), custom_call_target="tpu_custom_call" | custom-call | tf_op jit(solution)/shard_map/products/pallas_call | solution.py:240
  72.7 2.2 %collective-permute-start.10 = (f32[128,768]{1,0:T(8,128)S(1)}, f32[128,768]{1,0:T(8,128)S(1)}, u32[]{:S(2)}, u32[]{:S(2)}) collective-permute-start(f32[128,768]{1,0:T(8,128)S(1)} %get-tuple-element.87), channel_id=1, source_target_pairs={{0,4},{4,0},{8,12},{12,8},{16,20},{20,16},{24,28},{28,24},{1,5},{5... | collective-permute-start | bytes 1179656 | tf_op jit(solution)/shard_map/ppermute | solution.py:53
  75.0 1.3 %collective-permute-done.10.got_ref = f32[128,768]{1,0:T(8,128)S(1)} collective-permute-done((f32[128,768]{1,0:T(8,128)S(1)}, f32[128,768]{1,0:T(8,128)S(1)}, u32[]{:S(2)}, u32[]{:S(2)}) %collective-permute-start.10) | collective-permute-done | bytes 393248 | tf_op jit(solution)/shard_map/ppermute | solution.py:53
  76.3 0.6 split.2
  76.9 4.7 %collective-permute-start.11 = (f32[32,768]{1,0:T(8,128)S(1)}, f32[32,768]{1,0:T(8,128)S(1)}, u32[]{:S(2)}, u32[]{:S(2)}) collective-permute-start(f32[32,768]{1,0:T(8,128)S(1)} %get-tuple-element.89), channel_id=1, source_target_pairs={{0,8},{4,12},{8,0},{12,4},{16,24},{20,28},{24,16},{28,20},{1,9},{5... | collective-permute-start | bytes 294920 | tf_op jit(solution)/shard_map/ppermute | solution.py:53
  81.6 1.5 %collective-permute-start.13 = (f32[32,768]{1,0:T(8,128)S(1)}, f32[32,768]{1,0:T(8,128)S(1)}, u32[]{:S(2)}, u32[]{:S(2)}) collective-permute-start(f32[32,768]{1,0:T(8,128)S(1)} %get-tuple-element.91), channel_id=1, source_target_pairs={{0,24},{4,28},{8,16},{12,20},{16,8},{20,12},{24,0},{28,4},{1,25},{... | collective-permute-start | bytes 294920 | tf_op jit(solution)/shard_map/ppermute | solution.py:53
  83.2 1.0 collective-permute-done.14
  84.2 0.6 collective-permute-done.11
  84.8 3.5 %collective-permute-done.12 = f32[32,768]{1,0:T(8,128)S(1)} collective-permute-done((f32[32,768]{1,0:T(8,128)S(1)}, f32[32,768]{1,0:T(8,128)S(1)}, u32[]{:S(2)}, u32[]{:S(2)}) %collective-permute-start.12) | collective-permute-done | bytes 98336 | tf_op jit(solution)/shard_map/ppermute | solution.py:53
  88.3 2.6 %collective-permute-start.17 = (f32[32,768]{1,0:T(8,128)S(1)}, f32[32,768]{1,0:T(8,128)S(1)}, u32[]{:S(2)}, u32[]{:S(2)}) collective-permute-start(f32[32,768]{1,0:T(8,128)S(1)} %add_add_fusion.2), channel_id=1, source_target_pairs={{0,3},{1,2},{2,1},{3,0},{4,7},{5,6},{6,5},{7,4},{8,11},{9,10},{10,... | collective-permute-start | bytes 294920 | tf_op jit(solution)/shard_map/ppermute | solution.py:53
  91.0 0.4 collective-permute-start.16
  91.4 1.4 %collective-permute-start.15 = (f32[32,768]{1,0:T(8,128)S(1)}, f32[32,768]{1,0:T(8,128)S(1)}, u32[]{:S(2)}, u32[]{:S(2)}) collective-permute-start(f32[32,768]{1,0:T(8,128)S(1)} %add_add_fusion.2), channel_id=1, source_target_pairs={{0,1},{1,0},{2,3},{3,2},{4,5},{5,4},{6,7},{7,6},{8,9},{9,8},{10,11... | collective-permute-start | bytes 294920 | tf_op jit(solution)/shard_map/ppermute | solution.py:53
  92.8 1.2 collective-permute-start.24
  94.0 0.8 collective-permute-start.23
  94.8 0.7 collective-permute-done.17
  95.5 1.0 collective-permute-start.22
  96.5 1.9 %collective-permute-done.16 = f32[32,768]{1,0:T(8,128)S(1)} collective-permute-done((f32[32,768]{1,0:T(8,128)S(1)}, f32[32,768]{1,0:T(8,128)S(1)}, u32[]{:S(2)}, u32[]{:S(2)}) %collective-permute-start.16) | collective-permute-done | bytes 98336 | tf_op jit(solution)/shard_map/ppermute | solution.py:53
  98.4 2.6 %collective-permute-start.20 = (f32[32,768]{1,0:T(8,128)S(1)}, f32[32,768]{1,0:T(8,128)S(1)}, u32[]{:S(2)}, u32[]{:S(2)}) collective-permute-start(f32[32,768]{1,0:T(8,128)S(1)} %add_add_fusion.1), channel_id=1, source_target_pairs={{0,24},{4,28},{8,16},{12,20},{16,8},{20,12},{24,0},{28,4},{1,25},{... | collective-permute-start | bytes 294920 | tf_op jit(solution)/shard_map/ppermute | solution.py:53
  101.0 1.2 collective-permute-start.19
  102.4 2.0 %collective-permute-done.20 = f32[32,768]{1,0:T(8,128)S(1)} collective-permute-done((f32[32,768]{1,0:T(8,128)S(1)}, f32[32,768]{1,0:T(8,128)S(1)}, u32[]{:S(2)}, u32[]{:S(2)}) %collective-permute-start.20) | collective-permute-done | bytes 98336 | tf_op jit(solution)/shard_map/ppermute | solution.py:53
  104.4 1.2 collective-permute-done.19
  105.6 1.2 collective-permute-done.18
  106.9 1.7 %collective-permute-done.21.sums2_ref = f32[128,768]{1,0:T(8,128)S(1)} collective-permute-done((f32[128,768]{1,0:T(8,128)S(1)}, f32[128,768]{1,0:T(8,128)S(1)}, u32[]{:S(2)}, u32[]{:S(2)}) %collective-permute-start.21) | collective-permute-done | bytes 393248 | tf_op jit(solution)/shard_map/ppermute | solution.py:53
  108.7 14.5 %solve.1 = (bf16[768,512]{1,0:T(8,128)(2,1)S(1)}, bf16[768,512]{1,0:T(8,128)(2,1)S(1)}, f32[512,256]{1,0:T(8,128)}) custom-call(s32[7]{0:T(128)S(1)} %pad_add_fusion.index_ref, f32[128,768]{1,0:T(8,128)S(1)} %pad_maximum_fusion.sums_ref, f32[128,768]{1,0:T(8,128)S(1)} %collective-permute-done.21.sums2_ref, ...), custom_call_target="tpu_custom_call" | custom-call | tf_op jit(solution)/shard_map/solve/pallas_call | solution.py:400
  123.1 8.1 %rotate.1 = f32[16,128,512]{2,1,0:T(8,128)} custom-call(s32[7]{0:T(128)S(1)} %pad_add_fusion.index_ref, bf16[768,512]{1,0:T(8,128)(2,1)S(1)} %get-tuple-element.95.high_ref, bf16[768,512]{1,0:T(8,128)(2,1)S(1)} %get-tuple-element.96.low_ref, f32[16,128,512]{2,1,0:T(8,128)} %get-tuple-element.191, f32[16,64,128]{2,1,0:T(8,128)S(1)} %collective-permute-done.7.rest_0_, ...), custom_call_target="tpu_custom_call" | custom-call | tf_op jit(solution)/shard_map/rotate/pallas_call | solution.py:431
  (41 shorter events, 0.5 us)
Async XLA Ops:
  2.9 8.4 %collective-permute-start.5 = (f32[9,64,128]{2,1,0:T(8,128)}, f32[9,64,128]{2,1,0:T(8,128)S(1)}, u32[]{:S(2)}, u32[]{:S(2)}) collective-permute-start(f32[9,64,128]{2,1,0:T(8,128)} %get-tuple-element.67), channel_id=1, source_target_pairs={{0,4},{4,8},{8,12},{12,16},{16,20},{20,24},{24,28},{1,5},{5,9},{9,... | collective-permute-start | bytes 884744 | tf_op jit(solution)/shard_map/ppermute | solution.py:459
  5.3 6.1 %collective-permute-start.6 = (f32[9,64,128]{2,1,0:T(8,128)}, f32[9,64,128]{2,1,0:T(8,128)S(1)}, u32[]{:S(2)}, u32[]{:S(2)}) collective-permute-start(f32[9,64,128]{2,1,0:T(8,128)} %get-tuple-element.68), channel_id=1, source_target_pairs={{4,0},{8,4},{12,8},{16,12},{20,16},{24,20},{28,24},{5,1},{9,5},{13... | collective-permute-start | bytes 884744 | tf_op jit(solution)/shard_map/ppermute | solution.py:460
  6.6 4.6 %copy-start.4 = (s32[4]{0:T(128)S(1)}, s32[4]{0:T(128)}, u32[]{:S(2)}) copy-start(s32[4]{0:T(128)} %constant.48.clone) | copy-start | bytes 52
  6.6 4.6 %copy-start.5 = (s32[4]{0:T(128)S(1)}, s32[4]{0:T(128)}, u32[]{:S(2)}) copy-start(s32[4]{0:T(128)} %constant.47.clone) | copy-start | bytes 52
  6.7 4.7 %copy-start.2 = (f32[64,128]{1,0:T(8,128)S(1)}, f32[64,128]{1,0:T(8,128)}, u32[]{:S(2)}) copy-start(f32[64,128]{1,0:T(8,128)} %stiff_ref.3) | copy-start | bytes 98308
  18.1 35.5 %collective-permute-start.7 = (f32[16,64,128]{2,1,0:T(8,128)}, f32[16,64,128]{2,1,0:T(8,128)S(1)}, u32[]{:S(2)}, u32[]{:S(2)}) collective-permute-start(f32[16,64,128]{2,1,0:T(8,128)} %get-tuple-element.82), channel_id=1, source_target_pairs={{0,1},{1,0},{2,3},{3,2},{4,7},{5,6},{6,5},{7,4},{8,9},{9,8},{10,11... | collective-permute-start | bytes 1572872 | tf_op jit(solution)/shard_map/ppermute | solution.py:469
  20.5 33.1 %collective-permute-start.8 = (f32[16,64,128]{2,1,0:T(8,128)}, f32[16,64,128]{2,1,0:T(8,128)S(1)}, u32[]{:S(2)}, u32[]{:S(2)}) collective-permute-start(f32[16,64,128]{2,1,0:T(8,128)} %get-tuple-element.83), channel_id=1, source_target_pairs={{0,3},{1,2},{2,1},{3,0},{4,6},{5,7},{6,4},{7,5},{8,11},{9,10},{10,... | collective-permute-start | bytes 1572872 | tf_op jit(solution)/shard_map/ppermute | solution.py:469
  23.0 44.5 %collective-permute-start.9 = (f32[16,64,128]{2,1,0:T(8,128)}, f32[16,64,128]{2,1,0:T(8,128)S(1)}, u32[]{:S(2)}, u32[]{:S(2)}) collective-permute-start(f32[16,64,128]{2,1,0:T(8,128)} %get-tuple-element.84), channel_id=1, source_target_pairs={{0,2},{1,3},{2,0},{3,1},{4,5},{5,4},{6,7},{7,6},{8,10},{9,11},{10,... | collective-permute-start | bytes 1572872 | tf_op jit(solution)/shard_map/ppermute | solution.py:469
  23.8 43.7 %copy-start = (f32[16,64,128]{2,1,0:T(8,128)S(1)}, f32[16,64,128]{2,1,0:T(8,128)}, u32[]{:S(2)}) copy-start(f32[16,64,128]{2,1,0:T(8,128)} %get-tuple-element.85.rest_3_) | copy-start | bytes 1572868
  29.2 5.5 %collective-permute-start = (f32[256,512]{1,0:T(8,128)S(1)}, f32[256,512]{1,0:T(8,128)S(1)}, u32[]{:S(2)}, u32[]{:S(2)}) collective-permute-start(f32[256,512]{1,0:T(8,128)S(1)} %get-tuple-element.147), channel_id=1, source_target_pairs={{0,4},{4,0},{8,12},{12,8},{16,20},{20,16},{24,28},{28,24},{1,5},{5... | collective-permute-start | bytes 1572872 | tf_op jit(solution)/shard_map/while/body/ppermute | solution.py:53
  35.3 6.1 %collective-permute-start.2 = (f32[64,512]{1,0:T(8,128)S(1)}, f32[64,512]{1,0:T(8,128)S(1)}, u32[]{:S(2)}, u32[]{:S(2)}) collective-permute-start(f32[64,512]{1,0:T(8,128)S(1)} %get-tuple-element.150), channel_id=1, source_target_pairs={{0,8},{4,12},{8,0},{12,4},{16,24},{20,28},{24,16},{28,20},{1,9},{5... | collective-permute-start | bytes 393224 | tf_op jit(solution)/shard_map/while/body/ppermute | solution.py:53
  37.4 5.5 %collective-permute-start.1 = (f32[64,512]{1,0:T(8,128)S(1)}, f32[64,512]{1,0:T(8,128)S(1)}, u32[]{:S(2)}, u32[]{:S(2)}) collective-permute-start(f32[64,512]{1,0:T(8,128)S(1)} %get-tuple-element.148), channel_id=1, source_target_pairs={{0,16},{4,20},{8,24},{12,28},{16,0},{20,4},{24,8},{28,12},{1,17},{... | collective-permute-start | bytes 393224 | tf_op jit(solution)/shard_map/while/body/ppermute | solution.py:53
  41.4 6.2 %collective-permute-start.3 = (f32[64,512]{1,0:T(8,128)S(1)}, f32[64,512]{1,0:T(8,128)S(1)}, u32[]{:S(2)}, u32[]{:S(2)}) collective-permute-start(f32[64,512]{1,0:T(8,128)S(1)} %get-tuple-element.151), channel_id=1, source_target_pairs={{0,24},{4,28},{8,16},{12,20},{16,8},{20,12},{24,0},{28,4},{1,25},{... | collective-permute-start | bytes 393224 | tf_op jit(solution)/shard_map/while/body/ppermute | solution.py:53
  47.6 5.3 %collective-permute-start.4 = (f32[64,512]{1,0:T(8,128)S(1)}, f32[64,512]{1,0:T(8,128)S(1)}, u32[]{:S(2)}, u32[]{:S(2)}) collective-permute-start(f32[64,512]{1,0:T(8,128)S(1)} %add_add_fusion.4), channel_id=1, source_target_pairs={{0,1},{1,0},{2,3},{3,2},{4,5},{5,4},{6,7},{7,6},{8,9},{9,8},{10,11... | collective-permute-start | bytes 393224 | tf_op jit(solution)/shard_map/while/body/ppermute | solution.py:53
  67.5 7.5 %copy-start.3 = (f32[64,512]{1,0:T(8,128)S(1)}, f32[64,512]{1,0:T(8,128)}, u32[]{:S(2)}) copy-start(f32[64,512]{1,0:T(8,128)} %get-tuple-element.92) | copy-start | bytes 393220
  72.7 35.9 %copy-start.1 = (f32[768,512]{1,0:T(8,128)S(1)}, f32[768,512]{1,0:T(8,128)}, u32[]{:S(2)}) copy-start(f32[768,512]{1,0:T(8,128)} %rot_ref.1) | copy-start | bytes 4718596
  72.7 3.6 %collective-permute-start.10 = (f32[128,768]{1,0:T(8,128)S(1)}, f32[128,768]{1,0:T(8,128)S(1)}, u32[]{:S(2)}, u32[]{:S(2)}) collective-permute-start(f32[128,768]{1,0:T(8,128)S(1)} %get-tuple-element.87), channel_id=1, source_target_pairs={{0,4},{4,0},{8,12},{12,8},{16,20},{20,16},{24,28},{28,24},{1,5},{5... | collective-permute-start | bytes 1179656 | tf_op jit(solution)/shard_map/ppermute | solution.py:53
  74.9 9.2 %collective-permute-start.14 = (f32[64,512]{1,0:T(8,128)S(1)}, f32[64,512]{1,0:T(8,128)S(1)}, u32[]{:S(2)}, u32[]{:S(2)}) collective-permute-start(f32[64,512]{1,0:T(8,128)S(1)} %copy-done.3), channel_id=1, source_target_pairs={{0,2},{1,3},{2,0},{3,1},{4,6},{5,7},{6,4},{7,5},{8,10},{9,11},{10,... | collective-permute-start | bytes 393224 | tf_op jit(solution)/shard_map/ppermute | solution.py:53
  76.9 7.9 %collective-permute-start.11 = (f32[32,768]{1,0:T(8,128)S(1)}, f32[32,768]{1,0:T(8,128)S(1)}, u32[]{:S(2)}, u32[]{:S(2)}) collective-permute-start(f32[32,768]{1,0:T(8,128)S(1)} %get-tuple-element.89), channel_id=1, source_target_pairs={{0,8},{4,12},{8,0},{12,4},{16,24},{20,28},{24,16},{28,20},{1,9},{5... | collective-permute-start | bytes 294920 | tf_op jit(solution)/shard_map/ppermute | solution.py:53
  81.6 6.7 %collective-permute-start.12 = (f32[32,768]{1,0:T(8,128)S(1)}, f32[32,768]{1,0:T(8,128)S(1)}, u32[]{:S(2)}, u32[]{:S(2)}) collective-permute-start(f32[32,768]{1,0:T(8,128)S(1)} %get-tuple-element.90), channel_id=1, source_target_pairs={{0,16},{4,20},{8,24},{12,28},{16,0},{20,4},{24,8},{28,12},{1,17},{... | collective-permute-start | bytes 294920 | tf_op jit(solution)/shard_map/ppermute | solution.py:53
  81.6 6.7 %collective-permute-start.13 = (f32[32,768]{1,0:T(8,128)S(1)}, f32[32,768]{1,0:T(8,128)S(1)}, u32[]{:S(2)}, u32[]{:S(2)}) collective-permute-start(f32[32,768]{1,0:T(8,128)S(1)} %get-tuple-element.91), channel_id=1, source_target_pairs={{0,24},{4,28},{8,16},{12,20},{16,8},{20,12},{24,0},{28,4},{1,25},{... | collective-permute-start | bytes 294920 | tf_op jit(solution)/shard_map/ppermute | solution.py:53
  88.3 7.2 %collective-permute-start.17 = (f32[32,768]{1,0:T(8,128)S(1)}, f32[32,768]{1,0:T(8,128)S(1)}, u32[]{:S(2)}, u32[]{:S(2)}) collective-permute-start(f32[32,768]{1,0:T(8,128)S(1)} %add_add_fusion.2), channel_id=1, source_target_pairs={{0,3},{1,2},{2,1},{3,0},{4,7},{5,6},{6,5},{7,4},{8,11},{9,10},{10,... | collective-permute-start | bytes 294920 | tf_op jit(solution)/shard_map/ppermute | solution.py:53
  91.0 7.4 %collective-permute-start.16 = (f32[32,768]{1,0:T(8,128)S(1)}, f32[32,768]{1,0:T(8,128)S(1)}, u32[]{:S(2)}, u32[]{:S(2)}) collective-permute-start(f32[32,768]{1,0:T(8,128)S(1)} %add_add_fusion.2), channel_id=1, source_target_pairs={{0,2},{1,3},{2,0},{3,1},{4,6},{5,7},{6,4},{7,5},{8,10},{9,11},{10,... | collective-permute-start | bytes 294920 | tf_op jit(solution)/shard_map/ppermute | solution.py:53
  91.4 7.0 %collective-permute-start.15 = (f32[32,768]{1,0:T(8,128)S(1)}, f32[32,768]{1,0:T(8,128)S(1)}, u32[]{:S(2)}, u32[]{:S(2)}) collective-permute-start(f32[32,768]{1,0:T(8,128)S(1)} %add_add_fusion.2), channel_id=1, source_target_pairs={{0,1},{1,0},{2,3},{3,2},{4,5},{5,4},{6,7},{7,6},{8,9},{9,8},{10,11... | collective-permute-start | bytes 294920 | tf_op jit(solution)/shard_map/ppermute | solution.py:53
  92.8 9.5 %collective-permute-start.24 = (f32[64,512]{1,0:T(8,128)S(1)}, f32[64,512]{1,0:T(8,128)S(1)}, u32[]{:S(2)}, u32[]{:S(2)}) collective-permute-start(f32[64,512]{1,0:T(8,128)S(1)} %add.52), channel_id=1, source_target_pairs={{0,24},{4,28},{8,16},{12,20},{16,8},{20,12},{24,0},{28,4},{1,25},{... | collective-permute-start | bytes 393224 | tf_op jit(solution)/shard_map/ppermute | solution.py:53
  94.0 8.3 %collective-permute-start.23 = (f32[64,512]{1,0:T(8,128)S(1)}, f32[64,512]{1,0:T(8,128)S(1)}, u32[]{:S(2)}, u32[]{:S(2)}) collective-permute-start(f32[64,512]{1,0:T(8,128)S(1)} %add.52), channel_id=1, source_target_pairs={{0,16},{4,20},{8,24},{12,28},{16,0},{20,4},{24,8},{28,12},{1,17},{... | collective-permute-start | bytes 393224 | tf_op jit(solution)/shard_map/ppermute | solution.py:53
  95.5 6.7 %collective-permute-start.22 = (f32[64,512]{1,0:T(8,128)S(1)}, f32[64,512]{1,0:T(8,128)S(1)}, u32[]{:S(2)}, u32[]{:S(2)}) collective-permute-start(f32[64,512]{1,0:T(8,128)S(1)} %add.52), channel_id=1, source_target_pairs={{0,8},{4,12},{8,0},{12,4},{16,24},{20,28},{24,16},{28,20},{1,9},{5... | collective-permute-start | bytes 393224 | tf_op jit(solution)/shard_map/ppermute | solution.py:53
  98.4 6.0 %collective-permute-start.20 = (f32[32,768]{1,0:T(8,128)S(1)}, f32[32,768]{1,0:T(8,128)S(1)}, u32[]{:S(2)}, u32[]{:S(2)}) collective-permute-start(f32[32,768]{1,0:T(8,128)S(1)} %add_add_fusion.1), channel_id=1, source_target_pairs={{0,24},{4,28},{8,16},{12,20},{16,8},{20,12},{24,0},{28,4},{1,25},{... | collective-permute-start | bytes 294920 | tf_op jit(solution)/shard_map/ppermute | solution.py:53
  101.0 4.6 %collective-permute-start.19 = (f32[32,768]{1,0:T(8,128)S(1)}, f32[32,768]{1,0:T(8,128)S(1)}, u32[]{:S(2)}, u32[]{:S(2)}) collective-permute-start(f32[32,768]{1,0:T(8,128)S(1)} %add_add_fusion.1), channel_id=1, source_target_pairs={{0,16},{4,20},{8,24},{12,28},{16,0},{20,4},{24,8},{28,12},{1,17},{... | collective-permute-start | bytes 294920 | tf_op jit(solution)/shard_map/ppermute | solution.py:53
  102.2 4.6 %collective-permute-start.18 = (f32[32,768]{1,0:T(8,128)S(1)}, f32[32,768]{1,0:T(8,128)S(1)}, u32[]{:S(2)}, u32[]{:S(2)}) collective-permute-start(f32[32,768]{1,0:T(8,128)S(1)} %add_add_fusion.1), channel_id=1, source_target_pairs={{0,8},{4,12},{8,0},{12,4},{16,24},{20,28},{24,16},{28,20},{1,9},{5... | collective-permute-start | bytes 294920 | tf_op jit(solution)/shard_map/ppermute | solution.py:53
  102.3 6.4 %collective-permute-start.25 = (f32[256,512]{1,0:T(8,128)S(1)}, f32[256,512]{1,0:T(8,128)S(1)}, u32[]{:S(2)}, u32[]{:S(2)}) collective-permute-start(f32[256,512]{1,0:T(8,128)S(1)} %constant_dynamic-update-slice_fusion.gram_ref), channel_id=1, source_target_pairs={{0,4},{4,0},{8,12},{12,8},{16,20},{20,16},{24,28},{28,24},{1,5},{5... | collective-permute-start | bytes 1572872 | tf_op jit(solution)/shard_map/ppermute | solution.py:53
  106.9 1.8 %collective-permute-start.21 = (f32[128,768]{1,0:T(8,128)S(1)}, f32[128,768]{1,0:T(8,128)S(1)}, u32[]{:S(2)}, u32[]{:S(2)}) collective-permute-start(f32[128,768]{1,0:T(8,128)S(1)} %pad_maximum_fusion.sums_ref), channel_id=1, source_target_pairs={{0,4},{4,0},{8,12},{12,8},{16,20},{20,16},{24,28},{28,24},{1,5},{5... | collective-permute-start | bytes 1179656 | tf_op jit(solution)/shard_map/ppermute | solution.py:53

commit v7 on v6

--- a/solution.py
+++ b/solution.py
@@ -163,7 +163,7 @@
     )(index, disp, vel, stiff, before, after)
 
 
-def basis_gram_kernel(index_ref, basis_ref, send_ref, keep_ref, sum_ref, mixed_ref):
+def basis_kernel(index_ref, rot_ref, basis_ref, send_ref, keep_ref, high_ref, low_ref, turned_ref, sum_ref, mixed_ref):
     lines, width, rank = basis_ref.shape
     step = pl.program_id(0)
 
@@ -173,8 +173,11 @@
         mixed_ref[...] = jnp.zeros_like(mixed_ref)
 
     high, low = halves(basis_ref[...].reshape(lines * width, rank))
+    high_ref[...] = high
+    low_ref[...] = low
     sum_ref[...] += mm(high, high, ((0,), (0,)), None)
     mixed_ref[...] += mm(high, low, ((0,), (0,)), None)
+    turned_ref[...] = mm3((high, low), halves(rot_ref[...]), ((1,), (0,)))
 
     @pl.when(step == pl.num_programs(0) - 1)
     def _():
@@ -185,26 +188,28 @@
         send_ref[...] = sum_ref[pl.ds(pl.multiple_of((1 - core) * half, half), half), :]
 
 
-def basis_gram(index, basis):
+def basis_parts(index, basis, rotation):
     lines, width, rank = basis.shape
     block = 4
     half = pl.BlockSpec((rank // 2, rank), lambda i: (0, 0))
-    return pl.pallas_call(
-        basis_gram_kernel,
+    rows = pl.BlockSpec((block * width, rank), lambda i: (i, 0))
+    return pl.pallas_call(
+        basis_kernel,
         grid=(lines // block,),
-        in_specs=[SCALARS, pl.BlockSpec((block, width, rank), lambda i: (i, 0, 0))],
-        out_specs=[half, half],
-        out_shape=[shape(rank // 2, rank)] * 2,
+        in_specs=[SCALARS, pl.BlockSpec((rank, rank), lambda i: (0, 0)), pl.BlockSpec((block, width, rank), lambda i: (i, 0, 0))],
+        out_specs=[half, half, rows, rows, rows],
+        out_shape=[shape(rank // 2, rank)] * 2 + [pltpu.HBM((lines * width, rank), jnp.bfloat16)] * 2
+        + [pltpu.HBM((lines * width, rank), jnp.float32)],
         scratch_shapes=[pltpu.VMEM((rank, rank), jnp.float32)] * 2,
-        compiler_params=params(14),
-        name="basis_gram",
-    )(index, in_hbm(basis))
-
-
-def products_kernel(index_ref, basis_ref, *rest):
+        compiler_params=params(24),
+        name="basis_parts",
+    )(index, in_hbm(rotation), in_hbm(basis))
+
+
+def products_kernel(index_ref, high_ref, low_ref, *rest):
     pieces, (send_ref, keep_ref, snap_ref, sum_ref, mixed_ref) = rest[:-5], rest[-5:]
     lines, members, width = pieces[0].shape
-    rank = basis_ref.shape[-1]
+    rank = high_ref.shape[-1]
     step = pl.program_id(0)
     for k, piece in enumerate(pieces):
         at = pl.multiple_of((index_ref[0] ^ index_ref[FIRST + k]) * members, members)
@@ -217,8 +222,7 @@
         mixed_ref[...] = jnp.zeros_like(mixed_ref)
 
     snap = halves(snap_ref[...])
-    rows = basis_ref[...].reshape(lines * width, rank)
-    sum_ref[:, :rank] += mm3(snap, halves(rows), ((1,), (0,)))
+    sum_ref[:, :rank] += mm3(snap, (high_ref[...], low_ref[...]), ((1,), (0,)))
     sum_ref[:, rank:] += mm(snap[0], snap[0], ((1,), (1,)), None)
     mixed_ref[...] += mm(snap[0], snap[1], ((1,), (1,)), None)
 
@@ -231,16 +235,16 @@
         send_ref[...] = sum_ref[pl.ds(pl.multiple_of((1 - core) * half, half), half), :]
 
 
-def products(index, basis, pieces):
-    lines, width, rank = basis.shape
-    members = pieces[0].shape[1]
+def products(index, high, low, pieces):
+    rank = high.shape[1]
+    lines, members, width = pieces[0].shape
     total = members * len(pieces)
     block = 4
     half = pl.BlockSpec((total // 2, rank + total), lambda i: (0, 0))
     return pl.pallas_call(
         products_kernel,
         grid=(lines // block,),
-        in_specs=[SCALARS, pl.BlockSpec((block, width, rank), lambda i: (i, 0, 0))]
+        in_specs=[SCALARS] + [pl.BlockSpec((block * width, rank), lambda i: (i, 0))] * 2
         + [pl.BlockSpec((block, members, width), lambda i: (i, 0, 0))] * len(pieces),
         out_specs=[half, half],
         out_shape=[shape(total // 2, rank + total)] * 2,
@@ -248,7 +252,7 @@
                         pltpu.VMEM((total, total), jnp.float32)],
         compiler_params=params(14),
         name="products",
-    )(index, in_hbm(basis), *pieces)
+    )(index, in_hbm(high), in_hbm(low), *pieces)
 
 
 def split_kernel(index_ref, keep_ref, got_ref, *outs):
@@ -313,12 +317,13 @@
 
 PANEL = 32
 
-def eliminate(work_ref, members):
+def eliminate(work_ref, members, aside):
     tiles = work_ref.shape[1] // 128
     groups = PANEL // 8
     sub = lax.broadcasted_iota(jnp.int32, (8, 128), 0)
 
     def panel_step(k, carry):
+        aside(k)
         start = pl.multiple_of(k * PANEL, PANEL)
         at = pl.multiple_of((k * PANEL) // 128 * 128, 128)
         diag = work_ref[pl.ds(start, PANEL), pl.ds(at, 128)]
@@ -367,9 +372,18 @@
         out_ref[pl.ds(pl.multiple_of((1 - index_ref[1]) * half + at, rows), rows), :] = other_ref[piece, :]
 
 
-def solve_kernel(index_ref, sums_ref, sums2_ref, gram_ref, gram2_ref, rot_ref, high_ref, low_ref, coords_ref,
-                 work_ref, all_ref, basis_ref, *, count, chips):
+def solve_kernel(index_ref, sums_ref, sums2_ref, gram_ref, gram2_ref, rot_ref, high_hbm, low_hbm, *rest, count, chips, ranks):
+    pieces, rest = rest[:ranks], rest[ranks:]
+    mix_high, mix_low, rem_high, rem_low, coords_ref = rest[:5]
+    work_ref, all_ref, basis_ref, high_ref, low_ref, snap_ref, sem = rest[5:]
     rank, members = coords_ref.shape
+    each = members // ranks
+    copies = [pltpu.make_async_copy(high_hbm, high_ref, sem.at[0]), pltpu.make_async_copy(low_hbm, low_ref, sem.at[1])]
+    for k, piece in enumerate(pieces):
+        at = pl.multiple_of((index_ref[0] ^ index_ref[FIRST + k]) * each, each)
+        copies.append(pltpu.make_async_copy(piece, snap_ref.at[:, pl.ds(at, each), :], sem.at[2 + k]))
+    for copy in copies:
+        copy.start()
     ordered(index_ref, sums_ref, sums2_ref, all_ref, chips)
     ordered(index_ref, gram_ref, gram2_ref, basis_ref, chips)
     row = lax.broadcasted_iota(jnp.int32, (members, members), 0)
@@ -383,62 +397,65 @@
     correct = 2.0 * coef - mm(coef, basis_ref[...], ((1,), (0,))) / count
     work_ref[:, :members] = inner * (along / count) * across - mm(correct, coef, ((1,), (1,)))
     work_ref[:, members:] = jnp.where(eye, 1.0, 0.0)
-    eliminate(work_ref, members)
-    top, bottom = rot_ref[:rank, :], rot_ref[rank:, :]
+    all_ref[:, :rank] = coef
+    for copy in copies:
+        copy.wait()
+    lines, _, width = snap_ref.shape
+    block = lines // (members // PANEL)
+
+    def remainder(k):
+        at = pl.ds(pl.multiple_of(k * (block * width), block * width), block * width)
+        taken = mm3((high_ref[at, :], low_ref[at, :]), halves(all_ref[:, :rank]), ((1,), (1,)))
+        panel = jnp.concatenate([snap_ref[k * block + i].T for i in range(block)], axis=0) * across
+        rem_high[at, :], rem_low[at, :] = halves(panel - taken)
+
+    eliminate(work_ref, members, remainder)
+    coefs, tops, bottoms = halves(all_ref[:, :rank]), halves(rot_ref[:rank, :]), halves(rot_ref[rank:, :])
     upper = jnp.where(row <= col, work_ref[:, :members], 0.0)
-    tops, bottoms, coefs = halves(top), halves(bottom), halves(coef)
-    mix = mm3(halves(work_ref[:, members:]), bottoms, ((0,), (0,)))
-    high_ref[:rank, :], low_ref[:rank, :] = halves(top - mm3(coefs, halves(mix), ((0,), (0,))))
-    high_ref[rank:, :], low_ref[rank:, :] = halves(mix * along)
+    mix_high[...], mix_low[...] = halves(mm3(halves(work_ref[:, members:]), bottoms, ((0,), (0,))))
     coords = (mm3(coefs, tops, ((1,), (0,))) + mm3(halves(upper), bottoms, ((0,), (0,)))) * math.sqrt(rank)
     coords_ref[...] = coords.T
 
 
-def solve(index, sums, gram, rotation, count, chips):
-    rank = gram[0].shape[1]
+def solve(index, sums, gram, rotation, high, low, pieces, count, chips):
+    rows, rank = high.shape
     members = rotation.shape[0] - rank
-    return pl.pallas_call(
-        functools.partial(solve_kernel, count=float(count), chips=chips),
-        in_specs=[SCALARS] + [pl.BlockSpec(memory_space=pltpu.VMEM)] * 5,
-        out_shape=[shape(members + rank, rank, dtype=jnp.bfloat16)] * 2 + [shape(rank, members)],
+    ranks = len(pieces)
+    lines, each, width = pieces[0].shape
+    half = jnp.bfloat16
+    return pl.pallas_call(
+        functools.partial(solve_kernel, count=float(count), chips=chips, ranks=ranks),
+        in_specs=[SCALARS] + [pl.BlockSpec(memory_space=pltpu.VMEM)] * 5 + [pl.BlockSpec(memory_space=pl.ANY)] * (2 + ranks),
+        out_shape=[shape(members, rank, dtype=half)] * 2 + [shape(rows, members, dtype=half)] * 2 + [shape(rank, members)],
         scratch_shapes=[pltpu.VMEM((members, 2 * members), jnp.float32),
                         pltpu.VMEM((members, rank + members), jnp.float32),
-                        pltpu.VMEM((rank, rank), jnp.float32)],
-        compiler_params=params(20),
+                        pltpu.VMEM((rank, rank), jnp.float32),
+                        pltpu.VMEM((rows, rank), half), pltpu.VMEM((rows, rank), half),
+                        pltpu.VMEM((lines, members, width), jnp.float32), pltpu.SemaphoreType.DMA((2 + ranks,))],
+        compiler_params=params(28),
         name="solve",
-    )(index, *sums, *gram, rotation)
-
-
-def rotate_kernel(index_ref, high_ref, low_ref, basis_ref, *rest):
-    pieces, (out_ref, snap_ref) = rest[:-2], rest[-2:]
-    lines, members, width = pieces[0].shape
-    rank = basis_ref.shape[-1]
-    for k, piece in enumerate(pieces):
-        at = pl.multiple_of((index_ref[0] ^ index_ref[FIRST + k]) * members, members)
-        for line in range(lines):
-            snap_ref[pl.ds(at, members), line * width:(line + 1) * width] = piece[line]
-    rows = basis_ref[...].reshape(lines * width, rank)
-    out = mm3(halves(rows), (high_ref[:rank, :], low_ref[:rank, :]), ((1,), (0,)))
-    out = out + mm3(halves(snap_ref[...].T), (high_ref[rank:, :], low_ref[rank:, :]), ((1,), (0,)))
+    )(index, *sums, *gram, rotation, high, low, *pieces)
+
+
+def rotate_kernel(mix_high, mix_low, rem_high, rem_low, turned_ref, out_ref):
+    out = turned_ref[...] + mm3((rem_high[...], rem_low[...]), (mix_high[...], mix_low[...]), ((1,), (0,)))
     out_ref[...] = out.reshape(out_ref.shape)
 
 
-def rotate(index, high, low, basis, pieces):
-    lines, width, rank = basis.shape
-    members = pieces[0].shape[1]
+def rotate(mix, rest, turned, dims):
+    lines, width, rank = dims
+    members = mix[0].shape[0]
     block = 4
-    rows = pl.BlockSpec((block, width, rank), lambda i: (i, 0, 0))
     return pl.pallas_call(
         rotate_kernel,
         grid=(lines // block,),
-        in_specs=[SCALARS] + [pl.BlockSpec(high.shape, lambda i: (0, 0))] * 2 + [rows]
-        + [pl.BlockSpec((block, members, width), lambda i: (i, 0, 0))] * len(pieces),
-        out_specs=rows,
+        in_specs=[pl.BlockSpec((members, rank), lambda i: (0, 0))] * 2 + [pl.BlockSpec((block * width, members), lambda i: (i, 0))] * 2
+        + [pl.BlockSpec((block * width, rank), lambda i: (i, 0))],
+        out_specs=pl.BlockSpec((block, width, rank), lambda i: (i, 0, 0)),
         out_shape=shape(lines, width, rank),
-        scratch_shapes=[pltpu.VMEM((members * len(pieces), block * width), jnp.float32)],
-        compiler_params=params(20),
+        compiler_params=params(14),
         name="rotate",
-    )(index, high, low, in_hbm(basis), *pieces)
+    )(*mix, *rest, in_hbm(turned))
 
 
 def per_device(initial_disp, initial_vel, stiffness, basis, rotation):
@@ -469,23 +486,25 @@
         pieces[slot] = lax.ppermute(pieces[slot], ("sim", "ana"), pairs)
 
     def meanwhile(_, carry):
-        at, _ = carry
-        send, keep = basis_gram(at, basis)
-        return at + (at >> 20), ana_sum_by_pairs(chip_scatter(at, send, keep, 2), bits[:-1])
+        at, *_ = carry
+        send, keep, high, low, turned = basis_parts(at, basis, rotation)
+        return at + (at >> 20), ana_sum_by_pairs(chip_scatter(at, send, keep, 2), bits[:-1]), high, low, turned
 
     bits = [2 ** i for i in range(ranks.bit_length() - 1)]
-    order, gram = lax.fori_loop(0, 1 + (ana >> 20), meanwhile, (order, jnp.zeros((rank // sims, rank), jnp.float32)))
+    empty = [jnp.zeros((lines * width, rank), t) for t in (jnp.bfloat16, jnp.bfloat16, jnp.float32)]
+    order, gram, high, low, turned = lax.fori_loop(
+        0, 1 + (ana >> 20), meanwhile, (order, jnp.zeros((rank // sims, rank), jnp.float32), *empty))
     gram = ana_sum_by_pairs(gram, bits[-1:])
 
-    send, keep = products(order, basis, pieces)
+    send, keep = products(order, high, low, pieces)
     sums = chip_scatter(order, send, keep, chips)
     sums, gram = lax.optimization_barrier((sums, gram))
     gram = chip_gather(gram, chips)
     sums = ana_sum(sums)
     sums = with_other_core(chip_gather(sums, chips))
     gram = with_other_core(gram)
-    high, low, coords = solve(index, sums, gram, rotation, count, chips)
-    return rotate(index, high, low, basis, pieces), coords
+    *found, coords = solve(index, sums, gram, rotation, high, low, pieces, count, chips)
+    return rotate(found[:2], found[2:], turned, basis.shape), coords
 
 
 def solution(mesh):

time: 132 us -> 132 us (level)
  waiting for transfers between devices: 43.7 us -> 37.9 us
  local copies, waits for them, and re-layouts: 0.75 us -> 6.23 us
  Pallas kernels: 48 us -> 50.9 us
  starting transfers between devices: 37 us -> 34.6 us
    ppermute x3, waiting for transfers between devices: 13.9 us -> 0.01 us  [per_device(): pieces[slot] = lax.ppermute(pieces[slot], ('sim', 'ana'), pairs)]
    ppermute x21, waiting for transfers between devices: 29.8 us -> 37.9 us  [xor_permute(): return lax.ppermute(value, axis, [(i, i ^ mask) for i in range(size)])]
    another operation x0 -> x2, local copies, waits for them, and re-layouts: none -> 2.97 us
    broadcast_in_dim x0 -> x1, local copies, waits for them, and re-layouts: none -> 2.5 us  [per_device(): jnp.zeros((lines * width, rank), t)]
    pallas_call x2, Pallas kernels: 13.6 us -> 16 us  [the longest x1 10.3 us: basis_parts(): pl.pallas_call(basis_kernel, grid=(lines // block,), in_specs=[SCALARS, p...]
    ppermute x21, starting transfers between devices: 28.3 us -> 25.9 us  [xor_permute(): return lax.ppermute(value, axis, [(i, i ^ mask) for i in range(size)])]
  transfers between devices with their start and end apart: 26 -> 26, of which waited for: 16 -> 14; matrix products, arithmetic and copies ran while one was open for 1% -> 5% of each run, Pallas kernels for 9% -> 12%
where the time goes in v7:
time: 132 us
  Pallas kernels  50.9 us (39%)
  waiting for transfers between devices  37.9 us (29%)
  starting transfers between devices  34.6 us (26%)
  local copies, waits for them, and re-layouts  6.23 us (5%)
    ppermute x21, waiting for transfers between devices, xor_permute(): return lax.ppermute(value, axis, [(i, i ^ mask) for i in range(size)])  37.9 us
    ppermute x21, starting transfers between devices, xor_permute(): return lax.ppermute(value, axis, [(i, i ^ mask) for i in range(size)])  25.9 us
    pallas_call x1, Pallas kernels, solve(): pl.pallas_call(functools.partial(solve_kernel, count=float(count), chips=...  14.9 us
    pallas_call x1, Pallas kernels, basis_parts(): pl.pallas_call(basis_kernel, grid=(lines // block,), in_specs=[SCALARS, p...  10.3 us
    pallas_call x1, Pallas kernels, evolve(): pl.pallas_call(functools.partial(evolve_kernel, slots=slots), in_specs=[S...  6.66 us
    pallas_call x1, Pallas kernels, rotate(): pl.pallas_call(rotate_kernel, grid=(lines // block,), in_specs=[pl.BlockS...  5.79 us
    pallas_call x1, Pallas kernels, products(): pl.pallas_call(products_kernel, grid=(lines // block,), in_specs=[SCALARS...  5.26 us
    ppermute x3, starting transfers between devices, per_device(): pieces[slot] = lax.ppermute(pieces[slot], ('sim', 'ana'), pairs)  5.06 us
  transfers between devices with their start and end apart: 26, of which 14 were waited for; matrix products, arithmetic and copies ran while one was open for 5% of the time, Pallas kernels for 12%

profile of v7, /device:TPU:0, one launch (start us, length us, event | category | flops | bytes accessed | tf_op | source)
XLA Modules:
  0.0 131.6 jit_solution(5354410694693873793)
XLA Ops:
  0.6 2.3 %edges.1 = (f32[9,64,128]{2,1,0:T(8,128)}, f32[9,64,128]{2,1,0:T(8,128)}) custom-call(f32[64,128]{1,0:T(8,128)} %stiff_ref.3, f32[64,64,128]{2,1,0:T(8,128)} %disp_high.1, f32[64,64,128]{2,1,0:T(8,128)} %vel_high.1, f32[64,64,128]{2,1,0:T(8,128)} %disp_high.1, f32[64,64,128]{2,1,0:T(8,128)} %vel_high.1), custom_call_target="tpu_custom_call" | custom-call | tf_op jit(solution)/shard_map/edges/pallas_call | solution.py:73
  2.9 2.4 %collective-permute-start.5 = (f32[9,64,128]{2,1,0:T(8,128)}, f32[9,64,128]{2,1,0:T(8,128)S(1)}, u32[]{:S(2)}, u32[]{:S(2)}) collective-permute-start(f32[9,64,128]{2,1,0:T(8,128)} %get-tuple-element.92), channel_id=1, source_target_pairs={{0,4},{4,8},{8,12},{12,16},{16,20},{20,24},{24,28},{1,5},{5,9},{9,... | collective-permute-start | bytes 884744 | tf_op jit(solution)/shard_map/ppermute | solution.py:476
  5.3 1.3 collective-permute-start.6
  6.7 4.6 %to_lines.1 = (f32[64,64,128]{2,1,0:T(8,128)S(1)}, f32[64,64,128]{2,1,0:T(8,128)S(1)}) custom-call(f32[4096,128]{1,0:T(8,128)} %bitcast.5, f32[4096,128]{1,0:T(8,128)} %bitcast.6), custom_call_target="tpu_custom_call" | custom-call | tf_op jit(solution)/shard_map/to_lines/pallas_call | solution.py:96
  11.4 6.7 %evolve.1 = (f32[16,64,128]{2,1,0:T(8,128)}, f32[16,64,128]{2,1,0:T(8,128)}, f32[16,64,128]{2,1,0:T(8,128)}, f32[16,64,128]{2,1,0:T(8,128)}) custom-call(s32[7]{0:T(128)S(1)} %pad_add_fusion.index_ref, f32[64,64,128]{2,1,0:T(8,128)S(1)} %get-tuple-element.97.disp_ref, f32[64,64,128]{2,1,0:T(8,128)S(1)} %get-tuple-element.98.vel_ref, ...), custom_call_target="tpu_custom_call" | custom-call | tf_op jit(solution)/shard_map/evolve/pallas_call | solution.py:154
  18.1 2.5 %collective-permute-start.7 = (f32[16,64,128]{2,1,0:T(8,128)}, f32[16,64,128]{2,1,0:T(8,128)S(1)}, u32[]{:S(2)}, u32[]{:S(2)}) collective-permute-start(f32[16,64,128]{2,1,0:T(8,128)} %get-tuple-element.109), channel_id=1, source_target_pairs={{0,1},{1,0},{2,3},{3,2},{4,7},{5,6},{6,5},{7,4},{8,9},{9,8},{10,11... | collective-permute-start | bytes 1572872 | tf_op jit(solution)/shard_map/ppermute | solution.py:486
  20.6 2.5 %collective-permute-start.8 = (f32[16,64,128]{2,1,0:T(8,128)}, f32[16,64,128]{2,1,0:T(8,128)S(1)}, u32[]{:S(2)}, u32[]{:S(2)}) collective-permute-start(f32[16,64,128]{2,1,0:T(8,128)} %get-tuple-element.110), channel_id=1, source_target_pairs={{0,3},{1,2},{2,1},{3,0},{4,6},{5,7},{6,4},{7,5},{8,11},{9,10},{10,... | collective-permute-start | bytes 1572872 | tf_op jit(solution)/shard_map/ppermute | solution.py:486
  23.1 0.7 broadcast_in_dim.6
  23.8 1.5 %broadcast.8.clone = bf16[2048,512]{1,0:T(8,128)(2,1)} broadcast(bf16[]{:T(256)} %constant.48.clone.1), dimensions={} | broadcast | bytes 2097154 | tf_op jit(solution)/shard_map/broadcast.3
  25.3 1.5 %broadcast.8 = bf16[2048,512]{1,0:T(8,128)(2,1)} broadcast(bf16[]{:T(256)} %constant.48.clone.1), dimensions={} | broadcast | bytes 2097154 | tf_op jit(solution)/shard_map/broadcast.3
  26.8 2.5 %broadcast_in_dim.7 = f32[2048,512]{1,0:T(8,128)} broadcast(f32[]{:T(128)} %constant.47.clone.1), dimensions={} | broadcast | bytes 4194308 | tf_op jit(solution)/shard_map/broadcast_in_dim | solution.py:494
  29.3 43.3 %while.18 = (s32[]{:T(128)}, s32[7]{0:T(128)S(1)}, f32[64,512]{1,0:T(8,128)}, bf16[2048,512]{1,0:T(8,128)(2,1)}, bf16[2048,512]{1,0:T(8,128)(2,1)}, /*index=5*/f...) while((s32[]{:T(128)}, s32[7]{0:T(128)S(1)}, ...), condition=%wide.region_1.2_spmd, body=%wide.region_0.1_spmd.sunk | while | flops 131088 | bytes 5243237 | solution.py:495
  29.3 10.3 %basis_parts.1 = (f32[256,512]{1,0:T(8,128)S(1)}, f32[256,512]{1,0:T(8,128)S(1)}, bf16[2048,512]{1,0:T(8,128)(2,1)}, bf16[2048,512]{1,0:T(8,128)(2,1)}, f32[2048,512]{1,0:T(8,128)}) custom-call(s32[7]{0:T(128)S(1)} %get-tuple-element.227.index_ref, f32[768,512]{1,0:T(8,128)} %get-tuple-element.243.rot_ref, f32[16,128,512]{2,1,0:T(8,128)} %get-tuple-element.244.basis_ref), custom_call_target="tpu_custom_call" | custom-call | tf_op jit(solution)/shard_map/while/body/basis_parts/pallas_call | solution.py:196
  39.5 3.9 %collective-permute-start = (f32[256,512]{1,0:T(8,128)S(1)}, f32[256,512]{1,0:T(8,128)S(1)}, u32[]{:S(2)}, u32[]{:S(2)}) collective-permute-start(f32[256,512]{1,0:T(8,128)S(1)} %get-tuple-element.206), channel_id=1, source_target_pairs={{0,4},{4,0},{8,12},{12,8},{16,20},{20,16},{24,28},{28,24},{1,5},{5... | collective-permute-start | bytes 1572872 | tf_op jit(solution)/shard_map/while/body/ppermute | solution.py:53
  43.4 1.5 %collective-permute-done.got_ref = f32[256,512]{1,0:T(8,128)S(1)} collective-permute-done((f32[256,512]{1,0:T(8,128)S(1)}, f32[256,512]{1,0:T(8,128)S(1)}, u32[]{:S(2)}, u32[]{:S(2)}) %collective-permute-start) | collective-permute-done | bytes 524320 | tf_op jit(solution)/shard_map/while/body/ppermute | solution.py:53
  44.9 0.6 split.3
  45.5 2.1 %collective-permute-start.2 = (f32[64,512]{1,0:T(8,128)S(1)}, f32[64,512]{1,0:T(8,128)S(1)}, u32[]{:S(2)}, u32[]{:S(2)}) collective-permute-start(f32[64,512]{1,0:T(8,128)S(1)} %get-tuple-element.209), channel_id=1, source_target_pairs={{0,8},{4,12},{8,0},{12,4},{16,24},{20,28},{24,16},{28,20},{1,9},{5... | collective-permute-start | bytes 393224 | tf_op jit(solution)/shard_map/while/body/ppermute | solution.py:53
  47.7 4.0 %collective-permute-done.2 = f32[64,512]{1,0:T(8,128)S(1)} collective-permute-done((f32[64,512]{1,0:T(8,128)S(1)}, f32[64,512]{1,0:T(8,128)S(1)}, u32[]{:S(2)}, u32[]{:S(2)}) %collective-permute-start.2) | collective-permute-done | bytes 131104 | tf_op jit(solution)/shard_map/while/body/ppermute | solution.py:53
  51.6 1.0 collective-permute-start.3
  52.6 0.5 collective-permute-done.1
  53.1 4.7 %collective-permute-done.3 = f32[64,512]{1,0:T(8,128)S(1)} collective-permute-done((f32[64,512]{1,0:T(8,128)S(1)}, f32[64,512]{1,0:T(8,128)S(1)}, u32[]{:S(2)}, u32[]{:S(2)}) %collective-permute-start.3) | collective-permute-done | bytes 131104 | tf_op jit(solution)/shard_map/while/body/ppermute | solution.py:53
  57.8 1.4 %collective-permute-start.4 = (f32[64,512]{1,0:T(8,128)S(1)}, f32[64,512]{1,0:T(8,128)S(1)}, u32[]{:S(2)}, u32[]{:S(2)}) collective-permute-start(f32[64,512]{1,0:T(8,128)S(1)} %add_add_fusion.4), channel_id=1, source_target_pairs={{0,1},{1,0},{2,3},{3,2},{4,5},{5,4},{6,7},{7,6},{8,9},{9,8},{10,11... | collective-permute-start | bytes 393224 | tf_op jit(solution)/shard_map/while/body/ppermute | solution.py:53
  59.3 12.7 %collective-permute-done.4 = f32[64,512]{1,0:T(8,128)S(1)} collective-permute-done((f32[64,512]{1,0:T(8,128)S(1)}, f32[64,512]{1,0:T(8,128)S(1)}, u32[]{:S(2)}, u32[]{:S(2)}) %collective-permute-start.4) | collective-permute-done | bytes 131104 | tf_op jit(solution)/shard_map/while/body/ppermute | solution.py:53
  71.9 0.7 add.83
  72.6 5.3 %products.1 = (f32[128,768]{1,0:T(8,128)S(1)}, f32[128,768]{1,0:T(8,128)S(1)}) custom-call(s32[7]{0:T(128)S(1)} %get-tuple-element.106.index_ref, bf16[2048,512]{1,0:T(8,128)(2,1)} %get-tuple-element.107.high_ref.high_hbm, bf16[2048,512]{1,0:T(8,128)(2,1)} %get-tuple-element.108.low_ref.low_hbm, f32[16,64,128]{2,1,0:T(8,128)S(1)} %collective-permute-done.7.rest_0_, ...), custom_call_target="tpu_custom_call" | custom-call | tf_op jit(solution)/shard_map/products/pallas_call | solution.py:244
  78.0 1.5 %collective-permute-start.14 = (f32[64,512]{1,0:T(8,128)S(1)}, f32[64,512]{1,0:T(8,128)S(1)}, u32[]{:S(2)}, u32[]{:S(2)}) collective-permute-start(f32[64,512]{1,0:T(8,128)S(1)} %copy-done.8), channel_id=1, source_target_pairs={{0,2},{1,3},{2,0},{3,1},{4,6},{5,7},{6,4},{7,5},{8,10},{9,11},{10,... | collective-permute-start | bytes 393224 | tf_op jit(solution)/shard_map/ppermute | solution.py:53
  79.7 0.6 split.2
  80.3 3.6 %collective-permute-start.11 = (f32[32,768]{1,0:T(8,128)S(1)}, f32[32,768]{1,0:T(8,128)S(1)}, u32[]{:S(2)}, u32[]{:S(2)}) collective-permute-start(f32[32,768]{1,0:T(8,128)S(1)} %get-tuple-element.116), channel_id=1, source_target_pairs={{0,8},{4,12},{8,0},{12,4},{16,24},{20,28},{24,16},{28,20},{1,9},{5... | collective-permute-start | bytes 294920 | tf_op jit(solution)/shard_map/ppermute | solution.py:53
  83.9 1.5 %collective-permute-start.13 = (f32[32,768]{1,0:T(8,128)S(1)}, f32[32,768]{1,0:T(8,128)S(1)}, u32[]{:S(2)}, u32[]{:S(2)}) collective-permute-start(f32[32,768]{1,0:T(8,128)S(1)} %get-tuple-element.118), channel_id=1, source_target_pairs={{0,24},{4,28},{8,16},{12,20},{16,8},{20,12},{24,0},{28,4},{1,25},{... | collective-permute-start | bytes 294920 | tf_op jit(solution)/shard_map/ppermute | solution.py:53
  85.4 2.2 %collective-permute-done.14 = f32[64,512]{1,0:T(8,128)S(1)} collective-permute-done((f32[64,512]{1,0:T(8,128)S(1)}, f32[64,512]{1,0:T(8,128)S(1)}, u32[]{:S(2)}, u32[]{:S(2)}) %collective-permute-start.14) | collective-permute-done | bytes 131104 | tf_op jit(solution)/shard_map/ppermute | solution.py:53
  87.7 2.9 %collective-permute-done.12 = f32[32,768]{1,0:T(8,128)S(1)} collective-permute-done((f32[32,768]{1,0:T(8,128)S(1)}, f32[32,768]{1,0:T(8,128)S(1)}, u32[]{:S(2)}, u32[]{:S(2)}) %collective-permute-start.12) | collective-permute-done | bytes 98336 | tf_op jit(solution)/shard_map/ppermute | solution.py:53
  90.6 2.6 %collective-permute-start.17 = (f32[32,768]{1,0:T(8,128)S(1)}, f32[32,768]{1,0:T(8,128)S(1)}, u32[]{:S(2)}, u32[]{:S(2)}) collective-permute-start(f32[32,768]{1,0:T(8,128)S(1)} %add_add_fusion.2), channel_id=1, source_target_pairs={{0,3},{1,2},{2,1},{3,0},{4,7},{5,6},{6,5},{7,4},{8,11},{9,10},{10,... | collective-permute-start | bytes 294920 | tf_op jit(solution)/shard_map/ppermute | solution.py:53
  93.2 0.4 collective-permute-start.16
  93.6 1.4 %collective-permute-start.15 = (f32[32,768]{1,0:T(8,128)S(1)}, f32[32,768]{1,0:T(8,128)S(1)}, u32[]{:S(2)}, u32[]{:S(2)}) collective-permute-start(f32[32,768]{1,0:T(8,128)S(1)} %add_add_fusion.2), channel_id=1, source_target_pairs={{0,1},{1,0},{2,3},{3,2},{4,5},{5,4},{6,7},{7,6},{8,9},{9,8},{10,11... | collective-permute-start | bytes 294920 | tf_op jit(solution)/shard_map/ppermute | solution.py:53
  95.0 1.2 collective-permute-start.24
  96.2 0.8 collective-permute-start.23
  97.0 1.0 collective-permute-done.17
  98.1 0.6 collective-permute-start.22
  98.7 3.0 %collective-permute-done.16 = f32[32,768]{1,0:T(8,128)S(1)} collective-permute-done((f32[32,768]{1,0:T(8,128)S(1)}, f32[32,768]{1,0:T(8,128)S(1)}, u32[]{:S(2)}, u32[]{:S(2)}) %collective-permute-start.16) | collective-permute-done | bytes 98336 | tf_op jit(solution)/shard_map/ppermute | solution.py:53
  101.7 1.5 %collective-permute-start.20 = (f32[32,768]{1,0:T(8,128)S(1)}, f32[32,768]{1,0:T(8,128)S(1)}, u32[]{:S(2)}, u32[]{:S(2)}) collective-permute-start(f32[32,768]{1,0:T(8,128)S(1)} %add_add_fusion.1), channel_id=1, source_target_pairs={{0,24},{4,28},{8,16},{12,20},{16,8},{20,12},{24,0},{28,4},{1,25},{... | collective-permute-start | bytes 294920 | tf_op jit(solution)/shard_map/ppermute | solution.py:53
  103.2 1.2 collective-permute-start.19
  104.4 0.9 collective-permute-start.18
  105.4 2.5 %collective-permute-done.20 = f32[32,768]{1,0:T(8,128)S(1)} collective-permute-done((f32[32,768]{1,0:T(8,128)S(1)}, f32[32,768]{1,0:T(8,128)S(1)}, u32[]{:S(2)}, u32[]{:S(2)}) %collective-permute-start.20) | collective-permute-done | bytes 98336 | tf_op jit(solution)/shard_map/ppermute | solution.py:53
  107.9 0.6 collective-permute-done.19
  108.6 0.5 collective-permute-done.18
  109.2 1.7 %collective-permute-done.21.sums2_ref = f32[128,768]{1,0:T(8,128)S(1)} collective-permute-done((f32[128,768]{1,0:T(8,128)S(1)}, f32[128,768]{1,0:T(8,128)S(1)}, u32[]{:S(2)}, u32[]{:S(2)}) %collective-permute-start.21) | collective-permute-done | bytes 393248 | tf_op jit(solution)/shard_map/ppermute | solution.py:53
  110.9 14.9 %solve.1 = (bf16[256,512]{1,0:T(8,128)(2,1)S(1)}, bf16[256,512]{1,0:T(8,128)(2,1)S(1)}, bf16[2048,256]{1,0:T(8,128)(2,1)S(1)}, bf16[2048,256]{1,0:T(8,128)(2,1)S(1)}, f32[512,256]{1,0:T(8,128)}) custom-call(s32[7]{0:T(128)S(1)} %copy-done.3, f32[128,768]{1,0:T(8,128)S(1)} %pad_maximum_fusion.sums_ref, f32[128,768]{1,0:T(8,128)S(1)} %collective-permute-done.21.sums2_ref, ...), custom_call_target="tpu_custom_call" | custom-call | tf_op jit(solution)/shard_map/solve/pallas_call | solution.py:426
  125.8 5.8 %rotate.1 = f32[16,128,512]{2,1,0:T(8,128)} custom-call(bf16[256,512]{1,0:T(8,128)(2,1)S(1)} %get-tuple-element.122.mix_high, bf16[256,512]{1,0:T(8,128)(2,1)S(1)} %get-tuple-element.123.mix_low, bf16[2048,256]{1,0:T(8,128)(2,1)S(1)} %get-tuple-element.124.rem_high, bf16[2048,256]{1,0:T(8,128)(2,1)S(1)} %get-tuple-element.125.rem_low, ...), custom_call_target="tpu_custom_call" | custom-call | tf_op jit(solution)/shard_map/rotate/pallas_call | solution.py:449
  (53 shorter events, 0.9 us)
Async XLA Ops:
  2.9 8.4 %collective-permute-start.5 = (f32[9,64,128]{2,1,0:T(8,128)}, f32[9,64,128]{2,1,0:T(8,128)S(1)}, u32[]{:S(2)}, u32[]{:S(2)}) collective-permute-start(f32[9,64,128]{2,1,0:T(8,128)} %get-tuple-element.92), channel_id=1, source_target_pairs={{0,4},{4,8},{8,12},{12,16},{16,20},{20,24},{24,28},{1,5},{5,9},{9,... | collective-permute-start | bytes 884744 | tf_op jit(solution)/shard_map/ppermute | solution.py:476
  5.3 6.1 %collective-permute-start.6 = (f32[9,64,128]{2,1,0:T(8,128)}, f32[9,64,128]{2,1,0:T(8,128)S(1)}, u32[]{:S(2)}, u32[]{:S(2)}) collective-permute-start(f32[9,64,128]{2,1,0:T(8,128)} %get-tuple-element.93), channel_id=1, source_target_pairs={{4,0},{8,4},{12,8},{16,12},{20,16},{24,20},{28,24},{5,1},{9,5},{13... | collective-permute-start | bytes 884744 | tf_op jit(solution)/shard_map/ppermute | solution.py:477
  6.6 4.6 %copy-start.9 = (s32[4]{0:T(128)S(1)}, s32[4]{0:T(128)}, u32[]{:S(2)}) copy-start(s32[4]{0:T(128)} %constant.51.clone) | copy-start | bytes 52
  6.7 4.6 %copy-start.10 = (s32[4]{0:T(128)S(1)}, s32[4]{0:T(128)}, u32[]{:S(2)}) copy-start(s32[4]{0:T(128)} %constant.50.clone) | copy-start | bytes 52
  6.7 4.7 %copy-start.1 = (f32[64,128]{1,0:T(8,128)S(1)}, f32[64,128]{1,0:T(8,128)}, u32[]{:S(2)}) copy-start(f32[64,128]{1,0:T(8,128)} %stiff_ref.3) | copy-start | bytes 98308
  11.4 6.7 %copy-start.2 = (s32[7]{0:T(128)}, s32[7]{0:T(128)S(1)}, u32[]{:S(2)}) copy-start(s32[7]{0:T(128)S(1)} %pad_add_fusion.index_ref) | copy-start | bytes 88
  18.1 54.5 %collective-permute-start.7 = (f32[16,64,128]{2,1,0:T(8,128)}, f32[16,64,128]{2,1,0:T(8,128)S(1)}, u32[]{:S(2)}, u32[]{:S(2)}) collective-permute-start(f32[16,64,128]{2,1,0:T(8,128)} %get-tuple-element.109), channel_id=1, source_target_pairs={{0,1},{1,0},{2,3},{3,2},{4,7},{5,6},{6,5},{7,4},{8,9},{9,8},{10,11... | collective-permute-start | bytes 1572872 | tf_op jit(solution)/shard_map/ppermute | solution.py:486
  20.6 52.0 %collective-permute-start.8 = (f32[16,64,128]{2,1,0:T(8,128)}, f32[16,64,128]{2,1,0:T(8,128)S(1)}, u32[]{:S(2)}, u32[]{:S(2)}) collective-permute-start(f32[16,64,128]{2,1,0:T(8,128)} %get-tuple-element.110), channel_id=1, source_target_pairs={{0,3},{1,2},{2,1},{3,0},{4,6},{5,7},{6,4},{7,5},{8,11},{9,10},{10,... | collective-permute-start | bytes 1572872 | tf_op jit(solution)/shard_map/ppermute | solution.py:486
  23.0 49.6 %collective-permute-start.9 = (f32[16,64,128]{2,1,0:T(8,128)}, f32[16,64,128]{2,1,0:T(8,128)S(1)}, u32[]{:S(2)}, u32[]{:S(2)}) collective-permute-start(f32[16,64,128]{2,1,0:T(8,128)} %get-tuple-element.111), channel_id=1, source_target_pairs={{0,2},{1,3},{2,0},{3,1},{4,5},{5,4},{6,7},{7,6},{8,10},{9,11},{10,... | collective-permute-start | bytes 1572872 | tf_op jit(solution)/shard_map/ppermute | solution.py:486
  26.8 2.5 %copy-start.4 = (s32[7]{0:T(128)S(1)}, s32[7]{0:T(128)}, u32[]{:S(2)}) copy-start(s32[7]{0:T(128)} %copy-done.2) | copy-start | bytes 88
  29.3 43.3 %copy-start = (f32[16,64,128]{2,1,0:T(8,128)S(1)}, f32[16,64,128]{2,1,0:T(8,128)}, u32[]{:S(2)}) copy-start(f32[16,64,128]{2,1,0:T(8,128)} %get-tuple-element.112.rest_3_) | copy-start | bytes 1572868
  39.5 5.4 %collective-permute-start = (f32[256,512]{1,0:T(8,128)S(1)}, f32[256,512]{1,0:T(8,128)S(1)}, u32[]{:S(2)}, u32[]{:S(2)}) collective-permute-start(f32[256,512]{1,0:T(8,128)S(1)} %get-tuple-element.206), channel_id=1, source_target_pairs={{0,4},{4,0},{8,12},{12,8},{16,20},{20,16},{24,28},{28,24},{1,5},{5... | collective-permute-start | bytes 1572872 | tf_op jit(solution)/shard_map/while/body/ppermute | solution.py:53
  45.5 6.1 %collective-permute-start.2 = (f32[64,512]{1,0:T(8,128)S(1)}, f32[64,512]{1,0:T(8,128)S(1)}, u32[]{:S(2)}, u32[]{:S(2)}) collective-permute-start(f32[64,512]{1,0:T(8,128)S(1)} %get-tuple-element.209), channel_id=1, source_target_pairs={{0,8},{4,12},{8,0},{12,4},{16,24},{20,28},{24,16},{28,20},{1,9},{5... | collective-permute-start | bytes 393224 | tf_op jit(solution)/shard_map/while/body/ppermute | solution.py:53
  47.6 5.5 %collective-permute-start.1 = (f32[64,512]{1,0:T(8,128)S(1)}, f32[64,512]{1,0:T(8,128)S(1)}, u32[]{:S(2)}, u32[]{:S(2)}) collective-permute-start(f32[64,512]{1,0:T(8,128)S(1)} %get-tuple-element.207), channel_id=1, source_target_pairs={{0,16},{4,20},{8,24},{12,28},{16,0},{20,4},{24,8},{28,12},{1,17},{... | collective-permute-start | bytes 393224 | tf_op jit(solution)/shard_map/while/body/ppermute | solution.py:53
  51.6 6.1 %collective-permute-start.3 = (f32[64,512]{1,0:T(8,128)S(1)}, f32[64,512]{1,0:T(8,128)S(1)}, u32[]{:S(2)}, u32[]{:S(2)}) collective-permute-start(f32[64,512]{1,0:T(8,128)S(1)} %get-tuple-element.210), channel_id=1, source_target_pairs={{0,24},{4,28},{8,16},{12,20},{16,8},{20,12},{24,0},{28,4},{1,25},{... | collective-permute-start | bytes 393224 | tf_op jit(solution)/shard_map/while/body/ppermute | solution.py:53
  57.8 14.1 %collective-permute-start.4 = (f32[64,512]{1,0:T(8,128)S(1)}, f32[64,512]{1,0:T(8,128)S(1)}, u32[]{:S(2)}, u32[]{:S(2)}) collective-permute-start(f32[64,512]{1,0:T(8,128)S(1)} %add_add_fusion.4), channel_id=1, source_target_pairs={{0,1},{1,0},{2,3},{3,2},{4,5},{5,4},{6,7},{7,6},{8,9},{9,8},{10,11... | collective-permute-start | bytes 393224 | tf_op jit(solution)/shard_map/while/body/ppermute | solution.py:53
  72.6 5.4 %copy-start.8 = (f32[64,512]{1,0:T(8,128)S(1)}, f32[64,512]{1,0:T(8,128)}, u32[]{:S(2)}) copy-start(f32[64,512]{1,0:T(8,128)} %get-tuple-element.119) | copy-start | bytes 393220
  72.6 38.2 %copy-start.7 = (bf16[2048,512]{1,0:T(8,128)(2,1)S(1)}, bf16[2048,512]{1,0:T(8,128)(2,1)}, u32[]{:S(2)}) copy-start(bf16[2048,512]{1,0:T(8,128)(2,1)} %get-tuple-element.107.high_ref.high_hbm) | copy-start | bytes 6291460
  77.9 33.0 %copy-start.3 = (s32[7]{0:T(128)S(1)}, s32[7]{0:T(128)}, u32[]{:S(2)}) copy-start(s32[7]{0:T(128)} %copy-done.2) | copy-start | bytes 88
  77.9 33.0 %copy-start.5 = (f32[768,512]{1,0:T(8,128)S(1)}, f32[768,512]{1,0:T(8,128)}, u32[]{:S(2)}) copy-start(f32[768,512]{1,0:T(8,128)} %get-tuple-element.265) | copy-start | bytes 4718596
  77.9 33.0 %copy-start.6 = (bf16[2048,512]{1,0:T(8,128)(2,1)S(1)}, bf16[2048,512]{1,0:T(8,128)(2,1)}, u32[]{:S(2)}) copy-start(bf16[2048,512]{1,0:T(8,128)(2,1)} %get-tuple-element.108.low_ref.low_hbm) | copy-start | bytes 6291460
  77.9 1.8 %collective-permute-start.10 = (f32[128,768]{1,0:T(8,128)S(1)}, f32[128,768]{1,0:T(8,128)S(1)}, u32[]{:S(2)}, u32[]{:S(2)}) collective-permute-start(f32[128,768]{1,0:T(8,128)S(1)} %get-tuple-element.114), channel_id=1, source_target_pairs={{0,4},{4,0},{8,12},{12,8},{16,20},{20,16},{24,28},{28,24},{1,5},{5... | collective-permute-start | bytes 1179656 | tf_op jit(solution)/shard_map/ppermute | solution.py:53
  78.0 9.6 %collective-permute-start.14 = (f32[64,512]{1,0:T(8,128)S(1)}, f32[64,512]{1,0:T(8,128)S(1)}, u32[]{:S(2)}, u32[]{:S(2)}) collective-permute-start(f32[64,512]{1,0:T(8,128)S(1)} %copy-done.8), channel_id=1, source_target_pairs={{0,2},{1,3},{2,0},{3,1},{4,6},{5,7},{6,4},{7,5},{8,10},{9,11},{10,... | collective-permute-start | bytes 393224 | tf_op jit(solution)/shard_map/ppermute | solution.py:53
  80.3 7.3 %collective-permute-start.11 = (f32[32,768]{1,0:T(8,128)S(1)}, f32[32,768]{1,0:T(8,128)S(1)}, u32[]{:S(2)}, u32[]{:S(2)}) collective-permute-start(f32[32,768]{1,0:T(8,128)S(1)} %get-tuple-element.116), channel_id=1, source_target_pairs={{0,8},{4,12},{8,0},{12,4},{16,24},{20,28},{24,16},{28,20},{1,9},{5... | collective-permute-start | bytes 294920 | tf_op jit(solution)/shard_map/ppermute | solution.py:53
  83.9 6.7 %collective-permute-start.12 = (f32[32,768]{1,0:T(8,128)S(1)}, f32[32,768]{1,0:T(8,128)S(1)}, u32[]{:S(2)}, u32[]{:S(2)}) collective-permute-start(f32[32,768]{1,0:T(8,128)S(1)} %get-tuple-element.117), channel_id=1, source_target_pairs={{0,16},{4,20},{8,24},{12,28},{16,0},{20,4},{24,8},{28,12},{1,17},{... | collective-permute-start | bytes 294920 | tf_op jit(solution)/shard_map/ppermute | solution.py:53
  83.9 6.7 %collective-permute-start.13 = (f32[32,768]{1,0:T(8,128)S(1)}, f32[32,768]{1,0:T(8,128)S(1)}, u32[]{:S(2)}, u32[]{:S(2)}) collective-permute-start(f32[32,768]{1,0:T(8,128)S(1)} %get-tuple-element.118), channel_id=1, source_target_pairs={{0,24},{4,28},{8,16},{12,20},{16,8},{20,12},{24,0},{28,4},{1,25},{... | collective-permute-start | bytes 294920 | tf_op jit(solution)/shard_map/ppermute | solution.py:53
  90.6 7.5 %collective-permute-start.17 = (f32[32,768]{1,0:T(8,128)S(1)}, f32[32,768]{1,0:T(8,128)S(1)}, u32[]{:S(2)}, u32[]{:S(2)}) collective-permute-start(f32[32,768]{1,0:T(8,128)S(1)} %add_add_fusion.2), channel_id=1, source_target_pairs={{0,3},{1,2},{2,1},{3,0},{4,7},{5,6},{6,5},{7,4},{8,11},{9,10},{10,... | collective-permute-start | bytes 294920 | tf_op jit(solution)/shard_map/ppermute | solution.py:53
  93.2 8.5 %collective-permute-start.16 = (f32[32,768]{1,0:T(8,128)S(1)}, f32[32,768]{1,0:T(8,128)S(1)}, u32[]{:S(2)}, u32[]{:S(2)}) collective-permute-start(f32[32,768]{1,0:T(8,128)S(1)} %add_add_fusion.2), channel_id=1, source_target_pairs={{0,2},{1,3},{2,0},{3,1},{4,6},{5,7},{6,4},{7,5},{8,10},{9,11},{10,... | collective-permute-start | bytes 294920 | tf_op jit(solution)/shard_map/ppermute | solution.py:53
  93.6 8.1 %collective-permute-start.15 = (f32[32,768]{1,0:T(8,128)S(1)}, f32[32,768]{1,0:T(8,128)S(1)}, u32[]{:S(2)}, u32[]{:S(2)}) collective-permute-start(f32[32,768]{1,0:T(8,128)S(1)} %add_add_fusion.2), channel_id=1, source_target_pairs={{0,1},{1,0},{2,3},{3,2},{4,5},{5,4},{6,7},{7,6},{8,9},{9,8},{10,11... | collective-permute-start | bytes 294920 | tf_op jit(solution)/shard_map/ppermute | solution.py:53
  95.0 10.3 %collective-permute-start.24 = (f32[64,512]{1,0:T(8,128)S(1)}, f32[64,512]{1,0:T(8,128)S(1)}, u32[]{:S(2)}, u32[]{:S(2)}) collective-permute-start(f32[64,512]{1,0:T(8,128)S(1)} %add.52), channel_id=1, source_target_pairs={{0,24},{4,28},{8,16},{12,20},{16,8},{20,12},{24,0},{28,4},{1,25},{... | collective-permute-start | bytes 393224 | tf_op jit(solution)/shard_map/ppermute | solution.py:53
  96.2 9.1 %collective-permute-start.23 = (f32[64,512]{1,0:T(8,128)S(1)}, f32[64,512]{1,0:T(8,128)S(1)}, u32[]{:S(2)}, u32[]{:S(2)}) collective-permute-start(f32[64,512]{1,0:T(8,128)S(1)} %add.52), channel_id=1, source_target_pairs={{0,16},{4,20},{8,24},{12,28},{16,0},{20,4},{24,8},{28,12},{1,17},{... | collective-permute-start | bytes 393224 | tf_op jit(solution)/shard_map/ppermute | solution.py:53
  98.1 6.4 %collective-permute-start.22 = (f32[64,512]{1,0:T(8,128)S(1)}, f32[64,512]{1,0:T(8,128)S(1)}, u32[]{:S(2)}, u32[]{:S(2)}) collective-permute-start(f32[64,512]{1,0:T(8,128)S(1)} %add.52), channel_id=1, source_target_pairs={{0,8},{4,12},{8,0},{12,4},{16,24},{20,28},{24,16},{28,20},{1,9},{5... | collective-permute-start | bytes 393224 | tf_op jit(solution)/shard_map/ppermute | solution.py:53
  101.7 6.2 %collective-permute-start.20 = (f32[32,768]{1,0:T(8,128)S(1)}, f32[32,768]{1,0:T(8,128)S(1)}, u32[]{:S(2)}, u32[]{:S(2)}) collective-permute-start(f32[32,768]{1,0:T(8,128)S(1)} %add_add_fusion.1), channel_id=1, source_target_pairs={{0,24},{4,28},{8,16},{12,20},{16,8},{20,12},{24,0},{28,4},{1,25},{... | collective-permute-start | bytes 294920 | tf_op jit(solution)/shard_map/ppermute | solution.py:53
  103.2 5.4 %collective-permute-start.19 = (f32[32,768]{1,0:T(8,128)S(1)}, f32[32,768]{1,0:T(8,128)S(1)}, u32[]{:S(2)}, u32[]{:S(2)}) collective-permute-start(f32[32,768]{1,0:T(8,128)S(1)} %add_add_fusion.1), channel_id=1, source_target_pairs={{0,16},{4,20},{8,24},{12,28},{16,0},{20,4},{24,8},{28,12},{1,17},{... | collective-permute-start | bytes 294920 | tf_op jit(solution)/shard_map/ppermute | solution.py:53
  104.4 4.6 %collective-permute-start.18 = (f32[32,768]{1,0:T(8,128)S(1)}, f32[32,768]{1,0:T(8,128)S(1)}, u32[]{:S(2)}, u32[]{:S(2)}) collective-permute-start(f32[32,768]{1,0:T(8,128)S(1)} %add_add_fusion.1), channel_id=1, source_target_pairs={{0,8},{4,12},{8,0},{12,4},{16,24},{20,28},{24,16},{28,20},{1,9},{5... | collective-permute-start | bytes 294920 | tf_op jit(solution)/shard_map/ppermute | solution.py:53
  105.3 5.5 %collective-permute-start.25 = (f32[256,512]{1,0:T(8,128)S(1)}, f32[256,512]{1,0:T(8,128)S(1)}, u32[]{:S(2)}, u32[]{:S(2)}) collective-permute-start(f32[256,512]{1,0:T(8,128)S(1)} %constant_dynamic-update-slice_fusion.gram_ref), channel_id=1, source_target_pairs={{0,4},{4,0},{8,12},{12,8},{16,20},{20,16},{24,28},{28,24},{1,5},{5... | collective-permute-start | bytes 1572872 | tf_op jit(solution)/shard_map/ppermute | solution.py:53
  109.1 1.8 %collective-permute-start.21 = (f32[128,768]{1,0:T(8,128)S(1)}, f32[128,768]{1,0:T(8,128)S(1)}, u32[]{:S(2)}, u32[]{:S(2)}) collective-permute-start(f32[128,768]{1,0:T(8,128)S(1)} %pad_maximum_fusion.sums_ref), channel_id=1, source_target_pairs={{0,4},{4,0},{8,12},{12,8},{16,20},{20,16},{24,28},{28,24},{1,5},{5... | collective-permute-start | bytes 1179656 | tf_op jit(solution)/shard_map/ppermute | solution.py:53

commit v8 on v7

--- a/solution.py
+++ b/solution.py
@@ -45,7 +45,8 @@
 
 def mm3(left, right, dims):
     (lh, ll), (rh, rl) = left, right
-    return mm(lh, rh, dims, None) + (mm(lh, rl, dims, None) + mm(ll, rh, dims, None))
+    (over,), (under,) = dims
+    return mm(jnp.concatenate([ll, lh, lh], axis=over), jnp.concatenate([rh, rl, rh], axis=under), dims, None)
 
 
 def xor_permute(value, axis, mask):
@@ -161,6 +162,15 @@
         compiler_params=params(8),
         name="evolve",
     )(index, disp, vel, stiff, before, after)
+
+
+def room(*arrays):
+    return pl.pallas_call(
+        lambda *refs: None,
+        out_specs=[pl.BlockSpec(memory_space=pl.ANY)] * len(arrays),
+        out_shape=[pltpu.HBM(a.shape, a.dtype) for a in arrays],
+        name="room",
+    )()
 
 
 def basis_kernel(index_ref, rot_ref, basis_ref, send_ref, keep_ref, high_ref, low_ref, turned_ref, sum_ref, mixed_ref):
@@ -491,7 +501,7 @@
         return at + (at >> 20), ana_sum_by_pairs(chip_scatter(at, send, keep, 2), bits[:-1]), high, low, turned
 
     bits = [2 ** i for i in range(ranks.bit_length() - 1)]
-    empty = [jnp.zeros((lines * width, rank), t) for t in (jnp.bfloat16, jnp.bfloat16, jnp.float32)]
+    empty = room(*[shape(lines * width, rank, dtype=t) for t in (jnp.bfloat16, jnp.bfloat16, jnp.float32)])
     order, gram, high, low, turned = lax.fori_loop(
         0, 1 + (ana >> 20), meanwhile, (order, jnp.zeros((rank // sims, rank), jnp.float32), *empty))
     gram = ana_sum_by_pairs(gram, bits[-1:])

time: 132 us -> 130 us (0.985)
  local copies, waits for them, and re-layouts: 6.23 us -> 0.75 us
  starting transfers between devices: 34.6 us -> 37 us
    ppermute x3, waiting for transfers between devices: 0.01 us -> 8.48 us  [per_device(): pieces[slot] = lax.ppermute(pieces[slot], ('sim', 'ana'), pairs)]
    ppermute x21, waiting for transfers between devices: 37.9 us -> 30.5 us  [xor_permute(): return lax.ppermute(value, axis, [(i, i ^ mask) for i in range(size)])]
    another operation x2 -> x0, local copies, waits for them, and re-layouts: 2.97 us -> none
    broadcast_in_dim x1 -> x0, local copies, waits for them, and re-layouts: 2.5 us -> none  [per_device(): jnp.zeros((lines * width, rank), t)]
    ppermute x21, starting transfers between devices: 25.9 us -> 28.2 us  [xor_permute(): return lax.ppermute(value, axis, [(i, i ^ mask) for i in range(size)])]
  transfers between devices with their start and end apart: 26 -> 26, of which waited for: 14 -> 16; matrix products, arithmetic and copies ran while one was open for 5% -> 1% of each run, Pallas kernels for 12% -> 12%
where the time goes in v8:
time: 130 us; the launch traced here: 129 us
  Pallas kernels  50.9 us (39%)
  waiting for transfers between devices  39 us (30%)
  starting transfers between devices  37 us (28%)
    ppermute x21, waiting for transfers between devices, xor_permute(): return lax.ppermute(value, axis, [(i, i ^ mask) for i in range(size)])  30.5 us
    ppermute x21, starting transfers between devices, xor_permute(): return lax.ppermute(value, axis, [(i, i ^ mask) for i in range(size)])  28.2 us
    pallas_call x1, Pallas kernels, solve(): pl.pallas_call(functools.partial(solve_kernel, count=float(count), chips=...  14.8 us
    pallas_call x1, Pallas kernels, basis_parts(): pl.pallas_call(basis_kernel, grid=(lines // block,), in_specs=[SCALARS, p...  10.3 us
    ppermute x3, waiting for transfers between devices, per_device(): pieces[slot] = lax.ppermute(pieces[slot], ('sim', 'ana'), pairs)  8.48 us
    pallas_call x1, Pallas kernels, evolve(): pl.pallas_call(functools.partial(evolve_kernel, slots=slots), in_specs=[S...  6.67 us
    pallas_call x1, Pallas kernels, rotate(): pl.pallas_call(rotate_kernel, grid=(lines // block,), in_specs=[pl.BlockS...  5.79 us
    pallas_call x1, Pallas kernels, products(): pl.pallas_call(products_kernel, grid=(lines // block,), in_specs=[SCALARS...  5.26 us
  transfers between devices with their start and end apart: 26, of which 16 were waited for; matrix products, arithmetic and copies ran while one was open for 1% of the time, Pallas kernels for 12%

profile of v8, /device:TPU:0, one launch (start us, length us, event | category | flops | bytes accessed | tf_op | source)
XLA Modules:
  0.0 129.4 jit_solution(2312853708588660074)
XLA Ops:
  0.6 2.3 %edges.1 = (f32[9,64,128]{2,1,0:T(8,128)}, f32[9,64,128]{2,1,0:T(8,128)}) custom-call(f32[64,128]{1,0:T(8,128)} %stiff_ref.3, f32[64,64,128]{2,1,0:T(8,128)} %disp_high.1, f32[64,64,128]{2,1,0:T(8,128)} %vel_high.1, f32[64,64,128]{2,1,0:T(8,128)} %disp_high.1, f32[64,64,128]{2,1,0:T(8,128)} %vel_high.1), custom_call_target="tpu_custom_call" | custom-call | tf_op jit(solution)/shard_map/edges/pallas_call | solution.py:74
  3.0 2.4 %collective-permute-start.5 = (f32[9,64,128]{2,1,0:T(8,128)}, f32[9,64,128]{2,1,0:T(8,128)S(1)}, u32[]{:S(2)}, u32[]{:S(2)}) collective-permute-start(f32[9,64,128]{2,1,0:T(8,128)} %get-tuple-element.95), channel_id=1, source_target_pairs={{0,4},{4,8},{8,12},{12,16},{16,20},{20,24},{24,28},{1,5},{5,9},{9,... | collective-permute-start | bytes 884744 | tf_op jit(solution)/shard_map/ppermute | solution.py:486
  5.3 1.3 collective-permute-start.6
  6.7 4.6 %to_lines.1 = (f32[64,64,128]{2,1,0:T(8,128)S(1)}, f32[64,64,128]{2,1,0:T(8,128)S(1)}) custom-call(f32[4096,128]{1,0:T(8,128)} %bitcast.5, f32[4096,128]{1,0:T(8,128)} %bitcast.6), custom_call_target="tpu_custom_call" | custom-call | tf_op jit(solution)/shard_map/to_lines/pallas_call | solution.py:97
  11.4 6.7 %evolve.1 = (f32[16,64,128]{2,1,0:T(8,128)}, f32[16,64,128]{2,1,0:T(8,128)}, f32[16,64,128]{2,1,0:T(8,128)}, f32[16,64,128]{2,1,0:T(8,128)}) custom-call(s32[7]{0:T(128)S(1)} %pad_add_fusion.index_ref, f32[64,64,128]{2,1,0:T(8,128)S(1)} %get-tuple-element.100.disp_ref, f32[64,64,128]{2,1,0:T(8,128)S(1)} %get-tuple-element.101.vel_ref, ...), custom_call_target="tpu_custom_call" | custom-call | tf_op jit(solution)/shard_map/evolve/pallas_call | solution.py:155
  18.1 2.5 %collective-permute-start.7 = (f32[16,64,128]{2,1,0:T(8,128)}, f32[16,64,128]{2,1,0:T(8,128)S(1)}, u32[]{:S(2)}, u32[]{:S(2)}) collective-permute-start(f32[16,64,128]{2,1,0:T(8,128)} %get-tuple-element.115), channel_id=1, source_target_pairs={{0,1},{1,0},{2,3},{3,2},{4,7},{5,6},{6,5},{7,4},{8,9},{9,8},{10,11... | collective-permute-start | bytes 1572872 | tf_op jit(solution)/shard_map/ppermute | solution.py:496
  20.6 2.5 %collective-permute-start.8 = (f32[16,64,128]{2,1,0:T(8,128)}, f32[16,64,128]{2,1,0:T(8,128)S(1)}, u32[]{:S(2)}, u32[]{:S(2)}) collective-permute-start(f32[16,64,128]{2,1,0:T(8,128)} %get-tuple-element.116), channel_id=1, source_target_pairs={{0,3},{1,2},{2,1},{3,0},{4,6},{5,7},{6,4},{7,5},{8,11},{9,10},{10,... | collective-permute-start | bytes 1572872 | tf_op jit(solution)/shard_map/ppermute | solution.py:496
  23.1 0.1 collective-permute-start.9
  23.2 0.7 broadcast_in_dim.3
  23.8 35.3 %while.18 = (s32[]{:T(128)}, s32[7]{0:T(128)S(1)}, f32[64,512]{1,0:T(8,128)}, bf16[2048,512]{1,0:T(8,128)(2,1)}, bf16[2048,512]{1,0:T(8,128)(2,1)}, /*index=5*/f...) while((s32[]{:T(128)}, s32[7]{0:T(128)S(1)}, ...), condition=%wide.region_1.2_spmd, body=%wide.region_0.1_spmd.sunk | while | flops 131088 | bytes 5243237 | solution.py:505
  23.8 10.3 %basis_parts.1 = (f32[256,512]{1,0:T(8,128)S(1)}, f32[256,512]{1,0:T(8,128)S(1)}, bf16[2048,512]{1,0:T(8,128)(2,1)}, bf16[2048,512]{1,0:T(8,128)(2,1)}, f32[2048,512]{1,0:T(8,128)}) custom-call(s32[7]{0:T(128)S(1)} %get-tuple-element.233.index_ref, f32[768,512]{1,0:T(8,128)} %get-tuple-element.249.rot_ref, f32[16,128,512]{2,1,0:T(8,128)} %get-tuple-element.250.basis_ref), custom_call_target="tpu_custom_call" | custom-call | tf_op jit(solution)/shard_map/while/body/basis_parts/pallas_call | solution.py:206
  34.1 3.8 %collective-permute-start = (f32[256,512]{1,0:T(8,128)S(1)}, f32[256,512]{1,0:T(8,128)S(1)}, u32[]{:S(2)}, u32[]{:S(2)}) collective-permute-start(f32[256,512]{1,0:T(8,128)S(1)} %get-tuple-element.212), channel_id=1, source_target_pairs={{0,4},{4,0},{8,12},{12,8},{16,20},{20,16},{24,28},{28,24},{1,5},{5... | collective-permute-start | bytes 1572872 | tf_op jit(solution)/shard_map/while/body/ppermute | solution.py:54
  37.9 1.5 %collective-permute-done.got_ref = f32[256,512]{1,0:T(8,128)S(1)} collective-permute-done((f32[256,512]{1,0:T(8,128)S(1)}, f32[256,512]{1,0:T(8,128)S(1)}, u32[]{:S(2)}, u32[]{:S(2)}) %collective-permute-start) | collective-permute-done | bytes 524320 | tf_op jit(solution)/shard_map/while/body/ppermute | solution.py:54
  39.5 0.6 split.3
  40.1 2.1 %collective-permute-start.2 = (f32[64,512]{1,0:T(8,128)S(1)}, f32[64,512]{1,0:T(8,128)S(1)}, u32[]{:S(2)}, u32[]{:S(2)}) collective-permute-start(f32[64,512]{1,0:T(8,128)S(1)} %get-tuple-element.215), channel_id=1, source_target_pairs={{0,8},{4,12},{8,0},{12,4},{16,24},{20,28},{24,16},{28,20},{1,9},{5... | collective-permute-start | bytes 393224 | tf_op jit(solution)/shard_map/while/body/ppermute | solution.py:54
  42.2 4.0 %collective-permute-done.2 = f32[64,512]{1,0:T(8,128)S(1)} collective-permute-done((f32[64,512]{1,0:T(8,128)S(1)}, f32[64,512]{1,0:T(8,128)S(1)}, u32[]{:S(2)}, u32[]{:S(2)}) %collective-permute-start.2) | collective-permute-done | bytes 131104 | tf_op jit(solution)/shard_map/while/body/ppermute | solution.py:54
  46.2 1.0 collective-permute-start.3
  47.2 0.5 collective-permute-done.1
  47.6 4.7 %collective-permute-done.3 = f32[64,512]{1,0:T(8,128)S(1)} collective-permute-done((f32[64,512]{1,0:T(8,128)S(1)}, f32[64,512]{1,0:T(8,128)S(1)}, u32[]{:S(2)}, u32[]{:S(2)}) %collective-permute-start.3) | collective-permute-done | bytes 131104 | tf_op jit(solution)/shard_map/while/body/ppermute | solution.py:54
  52.4 1.4 %collective-permute-start.4 = (f32[64,512]{1,0:T(8,128)S(1)}, f32[64,512]{1,0:T(8,128)S(1)}, u32[]{:S(2)}, u32[]{:S(2)}) collective-permute-start(f32[64,512]{1,0:T(8,128)S(1)} %add_add_fusion.4), channel_id=1, source_target_pairs={{0,1},{1,0},{2,3},{3,2},{4,5},{5,4},{6,7},{7,6},{8,9},{9,8},{10,11... | collective-permute-start | bytes 393224 | tf_op jit(solution)/shard_map/while/body/ppermute | solution.py:54
  53.8 4.6 %collective-permute-done.4 = f32[64,512]{1,0:T(8,128)S(1)} collective-permute-done((f32[64,512]{1,0:T(8,128)S(1)}, f32[64,512]{1,0:T(8,128)S(1)}, u32[]{:S(2)}, u32[]{:S(2)}) %collective-permute-start.4) | collective-permute-done | bytes 131104 | tf_op jit(solution)/shard_map/while/body/ppermute | solution.py:54
  58.4 0.7 add.83
  59.1 8.5 %collective-permute-done.9.rest_2_ = f32[16,64,128]{2,1,0:T(8,128)S(1)} collective-permute-done((f32[16,64,128]{2,1,0:T(8,128)}, f32[16,64,128]{2,1,0:T(8,128)S(1)}, u32[]{:S(2)}, u32[]{:S(2)}) %collective-permute-start.9) | collective-permute-done | bytes 524320 | tf_op jit(solution)/shard_map/ppermute | solution.py:496
  67.6 5.3 %products.1 = (f32[128,768]{1,0:T(8,128)S(1)}, f32[128,768]{1,0:T(8,128)S(1)}) custom-call(s32[7]{0:T(128)S(1)} %get-tuple-element.112.index_ref, bf16[2048,512]{1,0:T(8,128)(2,1)} %get-tuple-element.113.high_ref.high_hbm, bf16[2048,512]{1,0:T(8,128)(2,1)} %get-tuple-element.114.low_ref.low_hbm, f32[16,64,128]{2,1,0:T(8,128)S(1)} %collective-permute-done.7.rest_0_, ...), custom_call_target="tpu_custom_call" | custom-call | tf_op jit(solution)/shard_map/products/pallas_call | solution.py:254
  72.9 2.2 %collective-permute-start.10 = (f32[128,768]{1,0:T(8,128)S(1)}, f32[128,768]{1,0:T(8,128)S(1)}, u32[]{:S(2)}, u32[]{:S(2)}) collective-permute-start(f32[128,768]{1,0:T(8,128)S(1)} %get-tuple-element.120), channel_id=1, source_target_pairs={{0,4},{4,0},{8,12},{12,8},{16,20},{20,16},{24,28},{28,24},{1,5},{5... | collective-permute-start | bytes 1179656 | tf_op jit(solution)/shard_map/ppermute | solution.py:54
  75.1 1.3 %collective-permute-done.10.got_ref = f32[128,768]{1,0:T(8,128)S(1)} collective-permute-done((f32[128,768]{1,0:T(8,128)S(1)}, f32[128,768]{1,0:T(8,128)S(1)}, u32[]{:S(2)}, u32[]{:S(2)}) %collective-permute-start.10) | collective-permute-done | bytes 393248 | tf_op jit(solution)/shard_map/ppermute | solution.py:54
  76.4 0.6 split.2
  77.0 4.7 %collective-permute-start.11 = (f32[32,768]{1,0:T(8,128)S(1)}, f32[32,768]{1,0:T(8,128)S(1)}, u32[]{:S(2)}, u32[]{:S(2)}) collective-permute-start(f32[32,768]{1,0:T(8,128)S(1)} %get-tuple-element.122), channel_id=1, source_target_pairs={{0,8},{4,12},{8,0},{12,4},{16,24},{20,28},{24,16},{28,20},{1,9},{5... | collective-permute-start | bytes 294920 | tf_op jit(solution)/shard_map/ppermute | solution.py:54
  81.7 1.5 %collective-permute-start.13 = (f32[32,768]{1,0:T(8,128)S(1)}, f32[32,768]{1,0:T(8,128)S(1)}, u32[]{:S(2)}, u32[]{:S(2)}) collective-permute-start(f32[32,768]{1,0:T(8,128)S(1)} %get-tuple-element.124), channel_id=1, source_target_pairs={{0,24},{4,28},{8,16},{12,20},{16,8},{20,12},{24,0},{28,4},{1,25},{... | collective-permute-start | bytes 294920 | tf_op jit(solution)/shard_map/ppermute | solution.py:54
  83.3 1.0 collective-permute-done.14
  84.3 0.6 collective-permute-done.11
  84.9 3.5 %collective-permute-done.12 = f32[32,768]{1,0:T(8,128)S(1)} collective-permute-done((f32[32,768]{1,0:T(8,128)S(1)}, f32[32,768]{1,0:T(8,128)S(1)}, u32[]{:S(2)}, u32[]{:S(2)}) %collective-permute-start.12) | collective-permute-done | bytes 98336 | tf_op jit(solution)/shard_map/ppermute | solution.py:54
  88.4 2.6 %collective-permute-start.17 = (f32[32,768]{1,0:T(8,128)S(1)}, f32[32,768]{1,0:T(8,128)S(1)}, u32[]{:S(2)}, u32[]{:S(2)}) collective-permute-start(f32[32,768]{1,0:T(8,128)S(1)} %add_add_fusion.2), channel_id=1, source_target_pairs={{0,3},{1,2},{2,1},{3,0},{4,7},{5,6},{6,5},{7,4},{8,11},{9,10},{10,... | collective-permute-start | bytes 294920 | tf_op jit(solution)/shard_map/ppermute | solution.py:54
  91.1 0.4 collective-permute-start.16
  91.5 1.4 %collective-permute-start.15 = (f32[32,768]{1,0:T(8,128)S(1)}, f32[32,768]{1,0:T(8,128)S(1)}, u32[]{:S(2)}, u32[]{:S(2)}) collective-permute-start(f32[32,768]{1,0:T(8,128)S(1)} %add_add_fusion.2), channel_id=1, source_target_pairs={{0,1},{1,0},{2,3},{3,2},{4,5},{5,4},{6,7},{7,6},{8,9},{9,8},{10,11... | collective-permute-start | bytes 294920 | tf_op jit(solution)/shard_map/ppermute | solution.py:54
  92.9 1.2 collective-permute-start.24
  94.1 0.8 collective-permute-start.23
  94.9 0.7 collective-permute-done.17
  95.6 1.0 collective-permute-start.22
  96.6 1.9 %collective-permute-done.16 = f32[32,768]{1,0:T(8,128)S(1)} collective-permute-done((f32[32,768]{1,0:T(8,128)S(1)}, f32[32,768]{1,0:T(8,128)S(1)}, u32[]{:S(2)}, u32[]{:S(2)}) %collective-permute-start.16) | collective-permute-done | bytes 98336 | tf_op jit(solution)/shard_map/ppermute | solution.py:54
  98.5 2.6 %collective-permute-start.20 = (f32[32,768]{1,0:T(8,128)S(1)}, f32[32,768]{1,0:T(8,128)S(1)}, u32[]{:S(2)}, u32[]{:S(2)}) collective-permute-start(f32[32,768]{1,0:T(8,128)S(1)} %add_add_fusion.1), channel_id=1, source_target_pairs={{0,24},{4,28},{8,16},{12,20},{16,8},{20,12},{24,0},{28,4},{1,25},{... | collective-permute-start | bytes 294920 | tf_op jit(solution)/shard_map/ppermute | solution.py:54
  101.1 1.2 collective-permute-start.19
  102.5 2.0 %collective-permute-done.20 = f32[32,768]{1,0:T(8,128)S(1)} collective-permute-done((f32[32,768]{1,0:T(8,128)S(1)}, f32[32,768]{1,0:T(8,128)S(1)}, u32[]{:S(2)}, u32[]{:S(2)}) %collective-permute-start.20) | collective-permute-done | bytes 98336 | tf_op jit(solution)/shard_map/ppermute | solution.py:54
  104.5 1.2 collective-permute-done.19
  105.7 1.2 collective-permute-done.18
  107.0 1.7 %collective-permute-done.21.sums2_ref = f32[128,768]{1,0:T(8,128)S(1)} collective-permute-done((f32[128,768]{1,0:T(8,128)S(1)}, f32[128,768]{1,0:T(8,128)S(1)}, u32[]{:S(2)}, u32[]{:S(2)}) %collective-permute-start.21) | collective-permute-done | bytes 393248 | tf_op jit(solution)/shard_map/ppermute | solution.py:54
  108.8 14.8 %solve.1 = (bf16[256,512]{1,0:T(8,128)(2,1)S(1)}, bf16[256,512]{1,0:T(8,128)(2,1)S(1)}, bf16[2048,256]{1,0:T(8,128)(2,1)S(1)}, bf16[2048,256]{1,0:T(8,128)(2,1)S(1)}, f32[512,256]{1,0:T(8,128)}) custom-call(s32[7]{0:T(128)S(1)} %pad_add_fusion.index_ref, f32[128,768]{1,0:T(8,128)S(1)} %pad_maximum_fusion.sums_ref, ...), custom_call_target="tpu_custom_call" | custom-call | tf_op jit(solution)/shard_map/solve/pallas_call | solution.py:436
  123.6 5.8 %rotate.1 = f32[16,128,512]{2,1,0:T(8,128)} custom-call(bf16[256,512]{1,0:T(8,128)(2,1)S(1)} %get-tuple-element.128.mix_high, bf16[256,512]{1,0:T(8,128)(2,1)S(1)} %get-tuple-element.129.mix_low, bf16[2048,256]{1,0:T(8,128)(2,1)S(1)} %get-tuple-element.130.rem_high, bf16[2048,256]{1,0:T(8,128)(2,1)S(1)} %get-tuple-element.131.rem_low, ...), custom_call_target="tpu_custom_call" | custom-call | tf_op jit(solution)/shard_map/rotate/pallas_call | solution.py:459
  (46 shorter events, 0.6 us)
Async XLA Ops:
  3.0 8.5 %collective-permute-start.5 = (f32[9,64,128]{2,1,0:T(8,128)}, f32[9,64,128]{2,1,0:T(8,128)S(1)}, u32[]{:S(2)}, u32[]{:S(2)}) collective-permute-start(f32[9,64,128]{2,1,0:T(8,128)} %get-tuple-element.95), channel_id=1, source_target_pairs={{0,4},{4,8},{8,12},{12,16},{16,20},{20,24},{24,28},{1,5},{5,9},{9,... | collective-permute-start | bytes 884744 | tf_op jit(solution)/shard_map/ppermute | solution.py:486
  5.3 6.1 %collective-permute-start.6 = (f32[9,64,128]{2,1,0:T(8,128)}, f32[9,64,128]{2,1,0:T(8,128)S(1)}, u32[]{:S(2)}, u32[]{:S(2)}) collective-permute-start(f32[9,64,128]{2,1,0:T(8,128)} %get-tuple-element.96), channel_id=1, source_target_pairs={{4,0},{8,4},{12,8},{16,12},{20,16},{24,20},{28,24},{5,1},{9,5},{13... | collective-permute-start | bytes 884744 | tf_op jit(solution)/shard_map/ppermute | solution.py:487
  6.7 4.6 %copy-start.6 = (s32[4]{0:T(128)S(1)}, s32[4]{0:T(128)}, u32[]{:S(2)}) copy-start(s32[4]{0:T(128)} %constant.48.clone) | copy-start | bytes 52
  6.7 4.6 %copy-start.7 = (s32[4]{0:T(128)S(1)}, s32[4]{0:T(128)}, u32[]{:S(2)}) copy-start(s32[4]{0:T(128)} %constant.47.clone) | copy-start | bytes 52
  6.7 4.7 %copy-start.1 = (f32[64,128]{1,0:T(8,128)S(1)}, f32[64,128]{1,0:T(8,128)}, u32[]{:S(2)}) copy-start(f32[64,128]{1,0:T(8,128)} %stiff_ref.3) | copy-start | bytes 98308
  18.1 41.0 %collective-permute-start.7 = (f32[16,64,128]{2,1,0:T(8,128)}, f32[16,64,128]{2,1,0:T(8,128)S(1)}, u32[]{:S(2)}, u32[]{:S(2)}) collective-permute-start(f32[16,64,128]{2,1,0:T(8,128)} %get-tuple-element.115), channel_id=1, source_target_pairs={{0,1},{1,0},{2,3},{3,2},{4,7},{5,6},{6,5},{7,4},{8,9},{9,8},{10,11... | collective-permute-start | bytes 1572872 | tf_op jit(solution)/shard_map/ppermute | solution.py:496
  20.6 38.5 %collective-permute-start.8 = (f32[16,64,128]{2,1,0:T(8,128)}, f32[16,64,128]{2,1,0:T(8,128)S(1)}, u32[]{:S(2)}, u32[]{:S(2)}) collective-permute-start(f32[16,64,128]{2,1,0:T(8,128)} %get-tuple-element.116), channel_id=1, source_target_pairs={{0,3},{1,2},{2,1},{3,0},{4,6},{5,7},{6,4},{7,5},{8,11},{9,10},{10,... | collective-permute-start | bytes 1572872 | tf_op jit(solution)/shard_map/ppermute | solution.py:496
  23.1 44.5 %collective-permute-start.9 = (f32[16,64,128]{2,1,0:T(8,128)}, f32[16,64,128]{2,1,0:T(8,128)S(1)}, u32[]{:S(2)}, u32[]{:S(2)}) collective-permute-start(f32[16,64,128]{2,1,0:T(8,128)} %get-tuple-element.117), channel_id=1, source_target_pairs={{0,2},{1,3},{2,0},{3,1},{4,5},{5,4},{6,7},{7,6},{8,10},{9,11},{10,... | collective-permute-start | bytes 1572872 | tf_op jit(solution)/shard_map/ppermute | solution.py:496
  23.8 43.7 %copy-start = (f32[16,64,128]{2,1,0:T(8,128)S(1)}, f32[16,64,128]{2,1,0:T(8,128)}, u32[]{:S(2)}) copy-start(f32[16,64,128]{2,1,0:T(8,128)} %get-tuple-element.118.rest_3_) | copy-start | bytes 1572868
  34.1 5.4 %collective-permute-start = (f32[256,512]{1,0:T(8,128)S(1)}, f32[256,512]{1,0:T(8,128)S(1)}, u32[]{:S(2)}, u32[]{:S(2)}) collective-permute-start(f32[256,512]{1,0:T(8,128)S(1)} %get-tuple-element.212), channel_id=1, source_target_pairs={{0,4},{4,0},{8,12},{12,8},{16,20},{20,16},{24,28},{28,24},{1,5},{5... | collective-permute-start | bytes 1572872 | tf_op jit(solution)/shard_map/while/body/ppermute | solution.py:54
  40.1 6.1 %collective-permute-start.2 = (f32[64,512]{1,0:T(8,128)S(1)}, f32[64,512]{1,0:T(8,128)S(1)}, u32[]{:S(2)}, u32[]{:S(2)}) collective-permute-start(f32[64,512]{1,0:T(8,128)S(1)} %get-tuple-element.215), channel_id=1, source_target_pairs={{0,8},{4,12},{8,0},{12,4},{16,24},{20,28},{24,16},{28,20},{1,9},{5... | collective-permute-start | bytes 393224 | tf_op jit(solution)/shard_map/while/body/ppermute | solution.py:54
  42.2 5.5 %collective-permute-start.1 = (f32[64,512]{1,0:T(8,128)S(1)}, f32[64,512]{1,0:T(8,128)S(1)}, u32[]{:S(2)}, u32[]{:S(2)}) collective-permute-start(f32[64,512]{1,0:T(8,128)S(1)} %get-tuple-element.213), channel_id=1, source_target_pairs={{0,16},{4,20},{8,24},{12,28},{16,0},{20,4},{24,8},{28,12},{1,17},{... | collective-permute-start | bytes 393224 | tf_op jit(solution)/shard_map/while/body/ppermute | solution.py:54
  46.2 6.1 %collective-permute-start.3 = (f32[64,512]{1,0:T(8,128)S(1)}, f32[64,512]{1,0:T(8,128)S(1)}, u32[]{:S(2)}, u32[]{:S(2)}) collective-permute-start(f32[64,512]{1,0:T(8,128)S(1)} %get-tuple-element.216), channel_id=1, source_target_pairs={{0,24},{4,28},{8,16},{12,20},{16,8},{20,12},{24,0},{28,4},{1,25},{... | collective-permute-start | bytes 393224 | tf_op jit(solution)/shard_map/while/body/ppermute | solution.py:54
  52.4 6.1 %collective-permute-start.4 = (f32[64,512]{1,0:T(8,128)S(1)}, f32[64,512]{1,0:T(8,128)S(1)}, u32[]{:S(2)}, u32[]{:S(2)}) collective-permute-start(f32[64,512]{1,0:T(8,128)S(1)} %add_add_fusion.4), channel_id=1, source_target_pairs={{0,1},{1,0},{2,3},{3,2},{4,5},{5,4},{6,7},{7,6},{8,9},{9,8},{10,11... | collective-permute-start | bytes 393224 | tf_op jit(solution)/shard_map/while/body/ppermute | solution.py:54
  67.6 7.5 %copy-start.5 = (f32[64,512]{1,0:T(8,128)S(1)}, f32[64,512]{1,0:T(8,128)}, u32[]{:S(2)}) copy-start(f32[64,512]{1,0:T(8,128)} %get-tuple-element.125) | copy-start | bytes 393220
  67.6 41.2 %copy-start.4 = (bf16[2048,512]{1,0:T(8,128)(2,1)S(1)}, bf16[2048,512]{1,0:T(8,128)(2,1)}, u32[]{:S(2)}) copy-start(bf16[2048,512]{1,0:T(8,128)(2,1)} %get-tuple-element.114.low_ref.low_hbm) | copy-start | bytes 6291460
  72.9 35.9 %copy-start.2 = (f32[768,512]{1,0:T(8,128)S(1)}, f32[768,512]{1,0:T(8,128)}, u32[]{:S(2)}) copy-start(f32[768,512]{1,0:T(8,128)} %get-tuple-element.271) | copy-start | bytes 4718596
  72.9 35.9 %copy-start.3 = (bf16[2048,512]{1,0:T(8,128)(2,1)S(1)}, bf16[2048,512]{1,0:T(8,128)(2,1)}, u32[]{:S(2)}) copy-start(bf16[2048,512]{1,0:T(8,128)(2,1)} %get-tuple-element.113.high_ref.high_hbm) | copy-start | bytes 6291460
  72.9 3.6 %collective-permute-start.10 = (f32[128,768]{1,0:T(8,128)S(1)}, f32[128,768]{1,0:T(8,128)S(1)}, u32[]{:S(2)}, u32[]{:S(2)}) collective-permute-start(f32[128,768]{1,0:T(8,128)S(1)} %get-tuple-element.120), channel_id=1, source_target_pairs={{0,4},{4,0},{8,12},{12,8},{16,20},{20,16},{24,28},{28,24},{1,5},{5... | collective-permute-start | bytes 1179656 | tf_op jit(solution)/shard_map/ppermute | solution.py:54
  75.1 9.2 %collective-permute-start.14 = (f32[64,512]{1,0:T(8,128)S(1)}, f32[64,512]{1,0:T(8,128)S(1)}, u32[]{:S(2)}, u32[]{:S(2)}) collective-permute-start(f32[64,512]{1,0:T(8,128)S(1)} %copy-done.5), channel_id=1, source_target_pairs={{0,2},{1,3},{2,0},{3,1},{4,6},{5,7},{6,4},{7,5},{8,10},{9,11},{10,... | collective-permute-start | bytes 393224 | tf_op jit(solution)/shard_map/ppermute | solution.py:54
  77.0 7.8 %collective-permute-start.11 = (f32[32,768]{1,0:T(8,128)S(1)}, f32[32,768]{1,0:T(8,128)S(1)}, u32[]{:S(2)}, u32[]{:S(2)}) collective-permute-start(f32[32,768]{1,0:T(8,128)S(1)} %get-tuple-element.122), channel_id=1, source_target_pairs={{0,8},{4,12},{8,0},{12,4},{16,24},{20,28},{24,16},{28,20},{1,9},{5... | collective-permute-start | bytes 294920 | tf_op jit(solution)/shard_map/ppermute | solution.py:54
  81.7 6.7 %collective-permute-start.12 = (f32[32,768]{1,0:T(8,128)S(1)}, f32[32,768]{1,0:T(8,128)S(1)}, u32[]{:S(2)}, u32[]{:S(2)}) collective-permute-start(f32[32,768]{1,0:T(8,128)S(1)} %get-tuple-element.123), channel_id=1, source_target_pairs={{0,16},{4,20},{8,24},{12,28},{16,0},{20,4},{24,8},{28,12},{1,17},{... | collective-permute-start | bytes 294920 | tf_op jit(solution)/shard_map/ppermute | solution.py:54
  81.7 6.7 %collective-permute-start.13 = (f32[32,768]{1,0:T(8,128)S(1)}, f32[32,768]{1,0:T(8,128)S(1)}, u32[]{:S(2)}, u32[]{:S(2)}) collective-permute-start(f32[32,768]{1,0:T(8,128)S(1)} %get-tuple-element.124), channel_id=1, source_target_pairs={{0,24},{4,28},{8,16},{12,20},{16,8},{20,12},{24,0},{28,4},{1,25},{... | collective-permute-start | bytes 294920 | tf_op jit(solution)/shard_map/ppermute | solution.py:54
  88.4 7.2 %collective-permute-start.17 = (f32[32,768]{1,0:T(8,128)S(1)}, f32[32,768]{1,0:T(8,128)S(1)}, u32[]{:S(2)}, u32[]{:S(2)}) collective-permute-start(f32[32,768]{1,0:T(8,128)S(1)} %add_add_fusion.2), channel_id=1, source_target_pairs={{0,3},{1,2},{2,1},{3,0},{4,7},{5,6},{6,5},{7,4},{8,11},{9,10},{10,... | collective-permute-start | bytes 294920 | tf_op jit(solution)/shard_map/ppermute | solution.py:54
  91.1 7.4 %collective-permute-start.16 = (f32[32,768]{1,0:T(8,128)S(1)}, f32[32,768]{1,0:T(8,128)S(1)}, u32[]{:S(2)}, u32[]{:S(2)}) collective-permute-start(f32[32,768]{1,0:T(8,128)S(1)} %add_add_fusion.2), channel_id=1, source_target_pairs={{0,2},{1,3},{2,0},{3,1},{4,6},{5,7},{6,4},{7,5},{8,10},{9,11},{10,... | collective-permute-start | bytes 294920 | tf_op jit(solution)/shard_map/ppermute | solution.py:54
  91.5 7.0 %collective-permute-start.15 = (f32[32,768]{1,0:T(8,128)S(1)}, f32[32,768]{1,0:T(8,128)S(1)}, u32[]{:S(2)}, u32[]{:S(2)}) collective-permute-start(f32[32,768]{1,0:T(8,128)S(1)} %add_add_fusion.2), channel_id=1, source_target_pairs={{0,1},{1,0},{2,3},{3,2},{4,5},{5,4},{6,7},{7,6},{8,9},{9,8},{10,11... | collective-permute-start | bytes 294920 | tf_op jit(solution)/shard_map/ppermute | solution.py:54
  92.9 9.5 %collective-permute-start.24 = (f32[64,512]{1,0:T(8,128)S(1)}, f32[64,512]{1,0:T(8,128)S(1)}, u32[]{:S(2)}, u32[]{:S(2)}) collective-permute-start(f32[64,512]{1,0:T(8,128)S(1)} %add.52), channel_id=1, source_target_pairs={{0,24},{4,28},{8,16},{12,20},{16,8},{20,12},{24,0},{28,4},{1,25},{... | collective-permute-start | bytes 393224 | tf_op jit(solution)/shard_map/ppermute | solution.py:54
  94.1 8.3 %collective-permute-start.23 = (f32[64,512]{1,0:T(8,128)S(1)}, f32[64,512]{1,0:T(8,128)S(1)}, u32[]{:S(2)}, u32[]{:S(2)}) collective-permute-start(f32[64,512]{1,0:T(8,128)S(1)} %add.52), channel_id=1, source_target_pairs={{0,16},{4,20},{8,24},{12,28},{16,0},{20,4},{24,8},{28,12},{1,17},{... | collective-permute-start | bytes 393224 | tf_op jit(solution)/shard_map/ppermute | solution.py:54
  95.6 6.7 %collective-permute-start.22 = (f32[64,512]{1,0:T(8,128)S(1)}, f32[64,512]{1,0:T(8,128)S(1)}, u32[]{:S(2)}, u32[]{:S(2)}) collective-permute-start(f32[64,512]{1,0:T(8,128)S(1)} %add.52), channel_id=1, source_target_pairs={{0,8},{4,12},{8,0},{12,4},{16,24},{20,28},{24,16},{28,20},{1,9},{5... | collective-permute-start | bytes 393224 | tf_op jit(solution)/shard_map/ppermute | solution.py:54
  98.5 6.0 %collective-permute-start.20 = (f32[32,768]{1,0:T(8,128)S(1)}, f32[32,768]{1,0:T(8,128)S(1)}, u32[]{:S(2)}, u32[]{:S(2)}) collective-permute-start(f32[32,768]{1,0:T(8,128)S(1)} %add_add_fusion.1), channel_id=1, source_target_pairs={{0,24},{4,28},{8,16},{12,20},{16,8},{20,12},{24,0},{28,4},{1,25},{... | collective-permute-start | bytes 294920 | tf_op jit(solution)/shard_map/ppermute | solution.py:54
  101.1 4.6 %collective-permute-start.19 = (f32[32,768]{1,0:T(8,128)S(1)}, f32[32,768]{1,0:T(8,128)S(1)}, u32[]{:S(2)}, u32[]{:S(2)}) collective-permute-start(f32[32,768]{1,0:T(8,128)S(1)} %add_add_fusion.1), channel_id=1, source_target_pairs={{0,16},{4,20},{8,24},{12,28},{16,0},{20,4},{24,8},{28,12},{1,17},{... | collective-permute-start | bytes 294920 | tf_op jit(solution)/shard_map/ppermute | solution.py:54
  102.3 4.6 %collective-permute-start.18 = (f32[32,768]{1,0:T(8,128)S(1)}, f32[32,768]{1,0:T(8,128)S(1)}, u32[]{:S(2)}, u32[]{:S(2)}) collective-permute-start(f32[32,768]{1,0:T(8,128)S(1)} %add_add_fusion.1), channel_id=1, source_target_pairs={{0,8},{4,12},{8,0},{12,4},{16,24},{20,28},{24,16},{28,20},{1,9},{5... | collective-permute-start | bytes 294920 | tf_op jit(solution)/shard_map/ppermute | solution.py:54
  102.4 6.4 %collective-permute-start.25 = (f32[256,512]{1,0:T(8,128)S(1)}, f32[256,512]{1,0:T(8,128)S(1)}, u32[]{:S(2)}, u32[]{:S(2)}) collective-permute-start(f32[256,512]{1,0:T(8,128)S(1)} %constant_dynamic-update-slice_fusion.gram_ref), channel_id=1, source_target_pairs={{0,4},{4,0},{8,12},{12,8},{16,20},{20,16},{24,28},{28,24},{1,5},{5... | collective-permute-start | bytes 1572872 | tf_op jit(solution)/shard_map/ppermute | solution.py:54
  107.0 1.8 %collective-permute-start.21 = (f32[128,768]{1,0:T(8,128)S(1)}, f32[128,768]{1,0:T(8,128)S(1)}, u32[]{:S(2)}, u32[]{:S(2)}) collective-permute-start(f32[128,768]{1,0:T(8,128)S(1)} %pad_maximum_fusion.sums_ref), channel_id=1, source_target_pairs={{0,4},{4,0},{8,12},{12,8},{16,20},{20,16},{24,28},{28,24},{1,5},{5... | collective-permute-start | bytes 1179656 | tf_op jit(solution)/shard_map/ppermute | solution.py:54

commit v9 on v8

--- a/solution.py
+++ b/solution.py
@@ -382,17 +382,17 @@
         out_ref[pl.ds(pl.multiple_of((1 - index_ref[1]) * half + at, rows), rows), :] = other_ref[piece, :]
 
 
-def solve_kernel(index_ref, sums_ref, sums2_ref, gram_ref, gram2_ref, rot_ref, high_hbm, low_hbm, *rest, count, chips, ranks):
+def solve_kernel(index_ref, sums_ref, sums2_ref, gram_ref, gram2_ref, rot_ref, high_hbm, low_hbm, turned_hbm, *rest, count, chips, ranks):
     pieces, rest = rest[:ranks], rest[ranks:]
-    mix_high, mix_low, rem_high, rem_low, coords_ref = rest[:5]
-    work_ref, all_ref, basis_ref, high_ref, low_ref, snap_ref, sem = rest[5:]
+    out_hbm, coords_ref, work_ref, all_ref, basis_ref, high_ref, low_ref, snap_ref, rem_high, rem_low, out_ref, sem, out_sem = rest
     rank, members = coords_ref.shape
     each = members // ranks
     copies = [pltpu.make_async_copy(high_hbm, high_ref, sem.at[0]), pltpu.make_async_copy(low_hbm, low_ref, sem.at[1])]
     for k, piece in enumerate(pieces):
         at = pl.multiple_of((index_ref[0] ^ index_ref[FIRST + k]) * each, each)
         copies.append(pltpu.make_async_copy(piece, snap_ref.at[:, pl.ds(at, each), :], sem.at[2 + k]))
-    for copy in copies:
+    turned = pltpu.make_async_copy(turned_hbm, out_ref, out_sem)
+    for copy in copies + [turned]:
         copy.start()
     ordered(index_ref, sums_ref, sums2_ref, all_ref, chips)
     ordered(index_ref, gram_ref, gram2_ref, basis_ref, chips)
@@ -421,13 +421,21 @@
 
     eliminate(work_ref, members, remainder)
     coefs, tops, bottoms = halves(all_ref[:, :rank]), halves(rot_ref[:rank, :]), halves(rot_ref[rank:, :])
+    mix_high, mix_low = halves(mm3(halves(work_ref[:, members:]), bottoms, ((0,), (0,))))
+    turned.wait()
+    step = 2 * block
+    for first in range(0, lines, step):
+        at = slice(first * width, (first + step) * width)
+        done = mm3((rem_high[at, :], rem_low[at, :]), (mix_high, mix_low), ((1,), (0,)))
+        out_ref[first:first + step] += done.reshape(step, width, rank)
+        pltpu.make_async_copy(out_ref.at[pl.ds(first, step)], out_hbm.at[pl.ds(first, step)], out_sem).start()
     upper = jnp.where(row <= col, work_ref[:, :members], 0.0)
-    mix_high[...], mix_low[...] = halves(mm3(halves(work_ref[:, members:]), bottoms, ((0,), (0,))))
     coords = (mm3(coefs, tops, ((1,), (0,))) + mm3(halves(upper), bottoms, ((0,), (0,)))) * math.sqrt(rank)
     coords_ref[...] = coords.T
-
-
-def solve(index, sums, gram, rotation, high, low, pieces, count, chips):
+    pltpu.make_async_copy(out_ref, out_hbm, out_sem).wait()
+
+
+def solve(index, sums, gram, rotation, high, low, turned, pieces, count, chips):
     rows, rank = high.shape
     members = rotation.shape[0] - rank
     ranks = len(pieces)
@@ -435,37 +443,20 @@
     half = jnp.bfloat16
     return pl.pallas_call(
         functools.partial(solve_kernel, count=float(count), chips=chips, ranks=ranks),
-        in_specs=[SCALARS] + [pl.BlockSpec(memory_space=pltpu.VMEM)] * 5 + [pl.BlockSpec(memory_space=pl.ANY)] * (2 + ranks),
-        out_shape=[shape(members, rank, dtype=half)] * 2 + [shape(rows, members, dtype=half)] * 2 + [shape(rank, members)],
+        in_specs=[SCALARS] + [pl.BlockSpec(memory_space=pltpu.VMEM)] * 5 + [pl.BlockSpec(memory_space=pl.ANY)] * (3 + ranks),
+        out_specs=[pl.BlockSpec(memory_space=pltpu.HBM), pl.BlockSpec(memory_space=pltpu.VMEM)],
+        out_shape=[pltpu.HBM((lines, width, rank), jnp.float32), shape(rank, members)],
         scratch_shapes=[pltpu.VMEM((members, 2 * members), jnp.float32),
                         pltpu.VMEM((members, rank + members), jnp.float32),
                         pltpu.VMEM((rank, rank), jnp.float32),
                         pltpu.VMEM((rows, rank), half), pltpu.VMEM((rows, rank), half),
-                        pltpu.VMEM((lines, members, width), jnp.float32), pltpu.SemaphoreType.DMA((2 + ranks,))],
-        compiler_params=params(28),
+                        pltpu.VMEM((lines, members, width), jnp.float32),
+                        pltpu.VMEM((rows, members), half), pltpu.VMEM((rows, members), half),
+                        pltpu.VMEM((lines, width, rank), jnp.float32),
+                        pltpu.SemaphoreType.DMA((2 + ranks,)), pltpu.SemaphoreType.DMA],
+        compiler_params=params(36),
         name="solve",
-    )(index, *sums, *gram, rotation, high, low, *pieces)
-
-
-def rotate_kernel(mix_high, mix_low, rem_high, rem_low, turned_ref, out_ref):
-    out = turned_ref[...] + mm3((rem_high[...], rem_low[...]), (mix_high[...], mix_low[...]), ((1,), (0,)))
-    out_ref[...] = out.reshape(out_ref.shape)
-
-
-def rotate(mix, rest, turned, dims):
-    lines, width, rank = dims
-    members = mix[0].shape[0]
-    block = 4
-    return pl.pallas_call(
-        rotate_kernel,
-        grid=(lines // block,),
-        in_specs=[pl.BlockSpec((members, rank), lambda i: (0, 0))] * 2 + [pl.BlockSpec((block * width, members), lambda i: (i, 0))] * 2
-        + [pl.BlockSpec((block * width, rank), lambda i: (i, 0))],
-        out_specs=pl.BlockSpec((block, width, rank), lambda i: (i, 0, 0)),
-        out_shape=shape(lines, width, rank),
-        compiler_params=params(14),
-        name="rotate",
-    )(*mix, *rest, in_hbm(turned))
+    )(index, *sums, *gram, rotation, high, low, in_hbm(turned.reshape(lines, width, rank)), *pieces)
 
 
 def per_device(initial_disp, initial_vel, stiffness, basis, rotation):
@@ -513,8 +504,7 @@
     sums = ana_sum(sums)
     sums = with_other_core(chip_gather(sums, chips))
     gram = with_other_core(gram)
-    *found, coords = solve(index, sums, gram, rotation, high, low, pieces, count, chips)
-    return rotate(found[:2], found[2:], turned, basis.shape), coords
+    return tuple(solve(index, sums, gram, rotation, high, low, turned, pieces, count, chips))
 
 
 def solution(mesh):

time: 130 us -> 126 us (0.969)
  Pallas kernels: 50.9 us -> 47.4 us
    pallas_call x1 -> x0, Pallas kernels: 5.79 us -> none  [rotate(): pl.pallas_call(rotate_kernel, grid=(lines // block,), in_specs=[pl.BlockS...]
    pallas_call x1, Pallas kernels: 14.8 us -> 17.1 us  [solve(): pl.pallas_call(functools.partial(solve_kernel, count=float(count), chips=...]
  transfers between devices with their start and end apart: 26 -> 26, of which waited for: 16 -> 16; matrix products, arithmetic and copies ran while one was open for 1% -> 1% of each run, Pallas kernels for 12% -> 13%
where the time goes in v9:
time: 126 us
  Pallas kernels  47.4 us (38%)
  waiting for transfers between devices  38.9 us (31%)
  starting transfers between devices  37 us (29%)
    ppermute x21, waiting for transfers between devices, xor_permute(): return lax.ppermute(value, axis, [(i, i ^ mask) for i in range(size)])  30.5 us
    ppermute x21, starting transfers between devices, xor_permute(): return lax.ppermute(value, axis, [(i, i ^ mask) for i in range(size)])  28.3 us
    pallas_call x1, Pallas kernels, solve(): pl.pallas_call(functools.partial(solve_kernel, count=float(count), chips=...  17.1 us
    pallas_call x1, Pallas kernels, basis_parts(): pl.pallas_call(basis_kernel, grid=(lines // block,), in_specs=[SCALARS, p...  10.3 us
    ppermute x3, waiting for transfers between devices, per_device(): pieces[slot] = lax.ppermute(pieces[slot], ('sim', 'ana'), pairs)  8.43 us
    pallas_call x1, Pallas kernels, evolve(): pl.pallas_call(functools.partial(evolve_kernel, slots=slots), in_specs=[S...  6.69 us
    pallas_call x1, Pallas kernels, products(): pl.pallas_call(products_kernel, grid=(lines // block,), in_specs=[SCALARS...  5.26 us
    ppermute x3, starting transfers between devices, per_device(): pieces[slot] = lax.ppermute(pieces[slot], ('sim', 'ana'), pairs)  5.06 us
  transfers between devices with their start and end apart: 26, of which 16 were waited for; matrix products, arithmetic and copies ran while one was open for 1% of the time, Pallas kernels for 13%

profile of v9, /device:TPU:0, one launch (start us, length us, event | category | flops | bytes accessed | tf_op | source)
XLA Modules:
  0.0 125.9 jit_solution(15232678604250876066)
XLA Ops:
  0.6 2.3 %edges.1 = (f32[9,64,128]{2,1,0:T(8,128)}, f32[9,64,128]{2,1,0:T(8,128)}) custom-call(f32[64,128]{1,0:T(8,128)} %stiff_ref.3, f32[64,64,128]{2,1,0:T(8,128)} %disp_high.1, f32[64,64,128]{2,1,0:T(8,128)} %vel_high.1, f32[64,64,128]{2,1,0:T(8,128)} %disp_high.1, f32[64,64,128]{2,1,0:T(8,128)} %vel_high.1), custom_call_target="tpu_custom_call" | custom-call | tf_op jit(solution)/shard_map/edges/pallas_call | solution.py:74
  3.0 2.4 %collective-permute-start.5 = (f32[9,64,128]{2,1,0:T(8,128)}, f32[9,64,128]{2,1,0:T(8,128)S(1)}, u32[]{:S(2)}, u32[]{:S(2)}) collective-permute-start(f32[9,64,128]{2,1,0:T(8,128)} %get-tuple-element.90), channel_id=1, source_target_pairs={{0,4},{4,8},{8,12},{12,16},{16,20},{20,24},{24,28},{1,5},{5,9},{9,... | collective-permute-start | bytes 884744 | tf_op jit(solution)/shard_map/ppermute | solution.py:477
  5.3 1.3 %collective-permute-start.6 = (f32[9,64,128]{2,1,0:T(8,128)}, f32[9,64,128]{2,1,0:T(8,128)S(1)}, u32[]{:S(2)}, u32[]{:S(2)}) collective-permute-start(f32[9,64,128]{2,1,0:T(8,128)} %get-tuple-element.91), channel_id=1, source_target_pairs={{4,0},{8,4},{12,8},{16,12},{20,16},{24,20},{28,24},{5,1},{9,5},{13... | collective-permute-start | bytes 884744 | tf_op jit(solution)/shard_map/ppermute | solution.py:478
  6.7 4.6 %to_lines.1 = (f32[64,64,128]{2,1,0:T(8,128)S(1)}, f32[64,64,128]{2,1,0:T(8,128)S(1)}) custom-call(f32[4096,128]{1,0:T(8,128)} %bitcast.6, f32[4096,128]{1,0:T(8,128)} %bitcast.7), custom_call_target="tpu_custom_call" | custom-call | tf_op jit(solution)/shard_map/to_lines/pallas_call | solution.py:97
  11.3 0.1 pad_add_fusion.index_ref
  11.4 6.7 %evolve.1 = (f32[16,64,128]{2,1,0:T(8,128)}, f32[16,64,128]{2,1,0:T(8,128)}, f32[16,64,128]{2,1,0:T(8,128)}, f32[16,64,128]{2,1,0:T(8,128)}) custom-call(s32[7]{0:T(128)S(1)} %pad_add_fusion.index_ref, f32[64,64,128]{2,1,0:T(8,128)S(1)} %get-tuple-element.95.disp_ref, f32[64,64,128]{2,1,0:T(8,128)S(1)} %get-tuple-element.96.vel_ref, ...), custom_call_target="tpu_custom_call" | custom-call | tf_op jit(solution)/shard_map/evolve/pallas_call | solution.py:155
  18.1 2.5 %collective-permute-start.7 = (f32[16,64,128]{2,1,0:T(8,128)}, f32[16,64,128]{2,1,0:T(8,128)S(1)}, u32[]{:S(2)}, u32[]{:S(2)}) collective-permute-start(f32[16,64,128]{2,1,0:T(8,128)} %get-tuple-element.110), channel_id=1, source_target_pairs={{0,1},{1,0},{2,3},{3,2},{4,7},{5,6},{6,5},{7,4},{8,9},{9,8},{10,11... | collective-permute-start | bytes 1572872 | tf_op jit(solution)/shard_map/ppermute | solution.py:487
  20.6 2.5 %collective-permute-start.8 = (f32[16,64,128]{2,1,0:T(8,128)}, f32[16,64,128]{2,1,0:T(8,128)S(1)}, u32[]{:S(2)}, u32[]{:S(2)}) collective-permute-start(f32[16,64,128]{2,1,0:T(8,128)} %get-tuple-element.111), channel_id=1, source_target_pairs={{0,3},{1,2},{2,1},{3,0},{4,6},{5,7},{6,4},{7,5},{8,11},{9,10},{10,... | collective-permute-start | bytes 1572872 | tf_op jit(solution)/shard_map/ppermute | solution.py:487
  23.1 0.1 collective-permute-start.9
  23.2 0.7 broadcast_in_dim.3
  23.9 35.3 %while.18 = (s32[]{:T(128)}, s32[7]{0:T(128)S(1)}, f32[64,512]{1,0:T(8,128)}, bf16[2048,512]{1,0:T(8,128)(2,1)}, bf16[2048,512]{1,0:T(8,128)(2,1)}, /*index=5*/f...) while((s32[]{:T(128)}, s32[7]{0:T(128)S(1)}, ...), condition=%wide.region_1.2_spmd, body=%wide.region_0.1_spmd.sunk | while | flops 131088 | bytes 5243237 | solution.py:496
  23.9 10.3 %basis_parts.1 = (f32[256,512]{1,0:T(8,128)S(1)}, f32[256,512]{1,0:T(8,128)S(1)}, bf16[2048,512]{1,0:T(8,128)(2,1)}, bf16[2048,512]{1,0:T(8,128)(2,1)}, f32[2048,512]{1,0:T(8,128)}) custom-call(s32[7]{0:T(128)S(1)} %get-tuple-element.223.index_ref, f32[768,512]{1,0:T(8,128)} %get-tuple-element.239.rot_ref, f32[16,128,512]{2,1,0:T(8,128)} %get-tuple-element.240.basis_ref), custom_call_target="tpu_custom_call" | custom-call | tf_op jit(solution)/shard_map/while/body/basis_parts/pallas_call | solution.py:206
  34.1 3.8 %collective-permute-start = (f32[256,512]{1,0:T(8,128)S(1)}, f32[256,512]{1,0:T(8,128)S(1)}, u32[]{:S(2)}, u32[]{:S(2)}) collective-permute-start(f32[256,512]{1,0:T(8,128)S(1)} %get-tuple-element.202), channel_id=1, source_target_pairs={{0,4},{4,0},{8,12},{12,8},{16,20},{20,16},{24,28},{28,24},{1,5},{5... | collective-permute-start | bytes 1572872 | tf_op jit(solution)/shard_map/while/body/ppermute | solution.py:54
  38.0 1.5 %collective-permute-done.got_ref = f32[256,512]{1,0:T(8,128)S(1)} collective-permute-done((f32[256,512]{1,0:T(8,128)S(1)}, f32[256,512]{1,0:T(8,128)S(1)}, u32[]{:S(2)}, u32[]{:S(2)}) %collective-permute-start) | collective-permute-done | bytes 524320 | tf_op jit(solution)/shard_map/while/body/ppermute | solution.py:54
  39.5 0.6 split.3
  40.1 2.1 %collective-permute-start.2 = (f32[64,512]{1,0:T(8,128)S(1)}, f32[64,512]{1,0:T(8,128)S(1)}, u32[]{:S(2)}, u32[]{:S(2)}) collective-permute-start(f32[64,512]{1,0:T(8,128)S(1)} %get-tuple-element.205), channel_id=1, source_target_pairs={{0,8},{4,12},{8,0},{12,4},{16,24},{20,28},{24,16},{28,20},{1,9},{5... | collective-permute-start | bytes 393224 | tf_op jit(solution)/shard_map/while/body/ppermute | solution.py:54
  42.3 4.0 %collective-permute-done.2 = f32[64,512]{1,0:T(8,128)S(1)} collective-permute-done((f32[64,512]{1,0:T(8,128)S(1)}, f32[64,512]{1,0:T(8,128)S(1)}, u32[]{:S(2)}, u32[]{:S(2)}) %collective-permute-start.2) | collective-permute-done | bytes 131104 | tf_op jit(solution)/shard_map/while/body/ppermute | solution.py:54
  46.2 1.0 collective-permute-start.3
  47.2 0.5 collective-permute-done.1
  47.7 4.7 %collective-permute-done.3 = f32[64,512]{1,0:T(8,128)S(1)} collective-permute-done((f32[64,512]{1,0:T(8,128)S(1)}, f32[64,512]{1,0:T(8,128)S(1)}, u32[]{:S(2)}, u32[]{:S(2)}) %collective-permute-start.3) | collective-permute-done | bytes 131104 | tf_op jit(solution)/shard_map/while/body/ppermute | solution.py:54
  52.4 1.4 %collective-permute-start.4 = (f32[64,512]{1,0:T(8,128)S(1)}, f32[64,512]{1,0:T(8,128)S(1)}, u32[]{:S(2)}, u32[]{:S(2)}) collective-permute-start(f32[64,512]{1,0:T(8,128)S(1)} %add_add_fusion.4), channel_id=1, source_target_pairs={{0,1},{1,0},{2,3},{3,2},{4,5},{5,4},{6,7},{7,6},{8,9},{9,8},{10,11... | collective-permute-start | bytes 393224 | tf_op jit(solution)/shard_map/while/body/ppermute | solution.py:54
  53.8 4.7 %collective-permute-done.4 = f32[64,512]{1,0:T(8,128)S(1)} collective-permute-done((f32[64,512]{1,0:T(8,128)S(1)}, f32[64,512]{1,0:T(8,128)S(1)}, u32[]{:S(2)}, u32[]{:S(2)}) %collective-permute-start.4) | collective-permute-done | bytes 131104 | tf_op jit(solution)/shard_map/while/body/ppermute | solution.py:54
  58.5 0.7 add.83
  59.2 8.4 %collective-permute-done.9.rest_2_ = f32[16,64,128]{2,1,0:T(8,128)S(1)} collective-permute-done((f32[16,64,128]{2,1,0:T(8,128)}, f32[16,64,128]{2,1,0:T(8,128)S(1)}, u32[]{:S(2)}, u32[]{:S(2)}) %collective-permute-start.9) | collective-permute-done | bytes 524320 | tf_op jit(solution)/shard_map/ppermute | solution.py:487
  67.6 5.3 %products.1 = (f32[128,768]{1,0:T(8,128)S(1)}, f32[128,768]{1,0:T(8,128)S(1)}) custom-call(s32[7]{0:T(128)S(1)} %get-tuple-element.107.index_ref, bf16[2048,512]{1,0:T(8,128)(2,1)} %get-tuple-element.108.high_ref.high_hbm, bf16[2048,512]{1,0:T(8,128)(2,1)} %get-tuple-element.109.low_ref.low_hbm, f32[16,64,128]{2,1,0:T(8,128)S(1)} %collective-permute-done.7.rest_0_, ...), custom_call_target="tpu_custom_call" | custom-call | tf_op jit(solution)/shard_map/products/pallas_call | solution.py:254
  72.9 2.2 %collective-permute-start.10 = (f32[128,768]{1,0:T(8,128)S(1)}, f32[128,768]{1,0:T(8,128)S(1)}, u32[]{:S(2)}, u32[]{:S(2)}) collective-permute-start(f32[128,768]{1,0:T(8,128)S(1)} %get-tuple-element.115), channel_id=1, source_target_pairs={{0,4},{4,0},{8,12},{12,8},{16,20},{20,16},{24,28},{28,24},{1,5},{5... | collective-permute-start | bytes 1179656 | tf_op jit(solution)/shard_map/ppermute | solution.py:54
  75.1 1.3 %collective-permute-done.10.got_ref = f32[128,768]{1,0:T(8,128)S(1)} collective-permute-done((f32[128,768]{1,0:T(8,128)S(1)}, f32[128,768]{1,0:T(8,128)S(1)}, u32[]{:S(2)}, u32[]{:S(2)}) %collective-permute-start.10) | collective-permute-done | bytes 393248 | tf_op jit(solution)/shard_map/ppermute | solution.py:54
  76.5 0.6 split.2
  77.1 4.7 %collective-permute-start.11 = (f32[32,768]{1,0:T(8,128)S(1)}, f32[32,768]{1,0:T(8,128)S(1)}, u32[]{:S(2)}, u32[]{:S(2)}) collective-permute-start(f32[32,768]{1,0:T(8,128)S(1)} %get-tuple-element.117), channel_id=1, source_target_pairs={{0,8},{4,12},{8,0},{12,4},{16,24},{20,28},{24,16},{28,20},{1,9},{5... | collective-permute-start | bytes 294920 | tf_op jit(solution)/shard_map/ppermute | solution.py:54
  81.8 1.5 %collective-permute-start.13 = (f32[32,768]{1,0:T(8,128)S(1)}, f32[32,768]{1,0:T(8,128)S(1)}, u32[]{:S(2)}, u32[]{:S(2)}) collective-permute-start(f32[32,768]{1,0:T(8,128)S(1)} %get-tuple-element.119), channel_id=1, source_target_pairs={{0,24},{4,28},{8,16},{12,20},{16,8},{20,12},{24,0},{28,4},{1,25},{... | collective-permute-start | bytes 294920 | tf_op jit(solution)/shard_map/ppermute | solution.py:54
  83.3 1.0 collective-permute-done.14
  84.3 0.6 collective-permute-done.11
  84.9 3.5 %collective-permute-done.12 = f32[32,768]{1,0:T(8,128)S(1)} collective-permute-done((f32[32,768]{1,0:T(8,128)S(1)}, f32[32,768]{1,0:T(8,128)S(1)}, u32[]{:S(2)}, u32[]{:S(2)}) %collective-permute-start.12) | collective-permute-done | bytes 98336 | tf_op jit(solution)/shard_map/ppermute | solution.py:54
  88.4 2.6 %collective-permute-start.17 = (f32[32,768]{1,0:T(8,128)S(1)}, f32[32,768]{1,0:T(8,128)S(1)}, u32[]{:S(2)}, u32[]{:S(2)}) collective-permute-start(f32[32,768]{1,0:T(8,128)S(1)} %add_add_fusion.2), channel_id=1, source_target_pairs={{0,3},{1,2},{2,1},{3,0},{4,7},{5,6},{6,5},{7,4},{8,11},{9,10},{10,... | collective-permute-start | bytes 294920 | tf_op jit(solution)/shard_map/ppermute | solution.py:54
  91.1 0.4 collective-permute-start.16
  91.5 1.4 %collective-permute-start.15 = (f32[32,768]{1,0:T(8,128)S(1)}, f32[32,768]{1,0:T(8,128)S(1)}, u32[]{:S(2)}, u32[]{:S(2)}) collective-permute-start(f32[32,768]{1,0:T(8,128)S(1)} %add_add_fusion.2), channel_id=1, source_target_pairs={{0,1},{1,0},{2,3},{3,2},{4,5},{5,4},{6,7},{7,6},{8,9},{9,8},{10,11... | collective-permute-start | bytes 294920 | tf_op jit(solution)/shard_map/ppermute | solution.py:54
  92.9 1.2 collective-permute-start.24
  94.1 0.8 collective-permute-start.23
  94.9 0.7 collective-permute-done.17
  95.6 1.0 collective-permute-start.22
  96.6 1.9 %collective-permute-done.16 = f32[32,768]{1,0:T(8,128)S(1)} collective-permute-done((f32[32,768]{1,0:T(8,128)S(1)}, f32[32,768]{1,0:T(8,128)S(1)}, u32[]{:S(2)}, u32[]{:S(2)}) %collective-permute-start.16) | collective-permute-done | bytes 98336 | tf_op jit(solution)/shard_map/ppermute | solution.py:54
  98.5 2.6 %collective-permute-start.20 = (f32[32,768]{1,0:T(8,128)S(1)}, f32[32,768]{1,0:T(8,128)S(1)}, u32[]{:S(2)}, u32[]{:S(2)}) collective-permute-start(f32[32,768]{1,0:T(8,128)S(1)} %add_add_fusion.1), channel_id=1, source_target_pairs={{0,24},{4,28},{8,16},{12,20},{16,8},{20,12},{24,0},{28,4},{1,25},{... | collective-permute-start | bytes 294920 | tf_op jit(solution)/shard_map/ppermute | solution.py:54
  101.1 1.2 collective-permute-start.19
  102.5 2.0 %collective-permute-done.20 = f32[32,768]{1,0:T(8,128)S(1)} collective-permute-done((f32[32,768]{1,0:T(8,128)S(1)}, f32[32,768]{1,0:T(8,128)S(1)}, u32[]{:S(2)}, u32[]{:S(2)}) %collective-permute-start.20) | collective-permute-done | bytes 98336 | tf_op jit(solution)/shard_map/ppermute | solution.py:54
  104.5 1.2 collective-permute-done.19
  105.7 1.2 collective-permute-done.18
  107.1 1.7 %collective-permute-done.21.sums2_ref = f32[128,768]{1,0:T(8,128)S(1)} collective-permute-done((f32[128,768]{1,0:T(8,128)S(1)}, f32[128,768]{1,0:T(8,128)S(1)}, u32[]{:S(2)}, u32[]{:S(2)}) %collective-permute-start.21) | collective-permute-done | bytes 393248 | tf_op jit(solution)/shard_map/ppermute | solution.py:54
  108.8 17.1 %solve.1 = (f32[16,128,512]{2,1,0:T(8,128)}, f32[512,256]{1,0:T(8,128)}) custom-call(s32[7]{0:T(128)S(1)} %pad_add_fusion.index_ref, f32[128,768]{1,0:T(8,128)S(1)} %pad_maximum_fusion.sums_ref, f32[128,768]{1,0:T(8,128)S(1)} %collective-permute-done.21.sums2_ref, f32[256,512]{1,0:T(8,128)S(1)} %constant_dynamic-update-slice_fusion.gram_ref, ...), custom_call_target="tpu_custom_call" | custom-call | tf_op jit(solution)/shard_map/solve/pallas_call | solution.py:444
  (45 shorter events, 0.5 us)
Async XLA Ops:
  3.0 8.5 %collective-permute-start.5 = (f32[9,64,128]{2,1,0:T(8,128)}, f32[9,64,128]{2,1,0:T(8,128)S(1)}, u32[]{:S(2)}, u32[]{:S(2)}) collective-permute-start(f32[9,64,128]{2,1,0:T(8,128)} %get-tuple-element.90), channel_id=1, source_target_pairs={{0,4},{4,8},{8,12},{12,16},{16,20},{20,24},{24,28},{1,5},{5,9},{9,... | collective-permute-start | bytes 884744 | tf_op jit(solution)/shard_map/ppermute | solution.py:477
  5.3 6.1 %collective-permute-start.6 = (f32[9,64,128]{2,1,0:T(8,128)}, f32[9,64,128]{2,1,0:T(8,128)S(1)}, u32[]{:S(2)}, u32[]{:S(2)}) collective-permute-start(f32[9,64,128]{2,1,0:T(8,128)} %get-tuple-element.91), channel_id=1, source_target_pairs={{4,0},{8,4},{12,8},{16,12},{20,16},{24,20},{28,24},{5,1},{9,5},{13... | collective-permute-start | bytes 884744 | tf_op jit(solution)/shard_map/ppermute | solution.py:478
  6.7 4.6 %copy-start.6 = (s32[4]{0:T(128)S(1)}, s32[4]{0:T(128)}, u32[]{:S(2)}) copy-start(s32[4]{0:T(128)} %constant.48.clone) | copy-start | bytes 52
  6.7 4.6 %copy-start.7 = (s32[4]{0:T(128)S(1)}, s32[4]{0:T(128)}, u32[]{:S(2)}) copy-start(s32[4]{0:T(128)} %constant.47.clone) | copy-start | bytes 52
  6.7 4.7 %copy-start.1 = (f32[64,128]{1,0:T(8,128)S(1)}, f32[64,128]{1,0:T(8,128)}, u32[]{:S(2)}) copy-start(f32[64,128]{1,0:T(8,128)} %stiff_ref.3) | copy-start | bytes 98308
  18.1 41.0 %collective-permute-start.7 = (f32[16,64,128]{2,1,0:T(8,128)}, f32[16,64,128]{2,1,0:T(8,128)S(1)}, u32[]{:S(2)}, u32[]{:S(2)}) collective-permute-start(f32[16,64,128]{2,1,0:T(8,128)} %get-tuple-element.110), channel_id=1, source_target_pairs={{0,1},{1,0},{2,3},{3,2},{4,7},{5,6},{6,5},{7,4},{8,9},{9,8},{10,11... | collective-permute-start | bytes 1572872 | tf_op jit(solution)/shard_map/ppermute | solution.py:487
  20.6 38.6 %collective-permute-start.8 = (f32[16,64,128]{2,1,0:T(8,128)}, f32[16,64,128]{2,1,0:T(8,128)S(1)}, u32[]{:S(2)}, u32[]{:S(2)}) collective-permute-start(f32[16,64,128]{2,1,0:T(8,128)} %get-tuple-element.111), channel_id=1, source_target_pairs={{0,3},{1,2},{2,1},{3,0},{4,6},{5,7},{6,4},{7,5},{8,11},{9,10},{10,... | collective-permute-start | bytes 1572872 | tf_op jit(solution)/shard_map/ppermute | solution.py:487
  23.1 44.5 %collective-permute-start.9 = (f32[16,64,128]{2,1,0:T(8,128)}, f32[16,64,128]{2,1,0:T(8,128)S(1)}, u32[]{:S(2)}, u32[]{:S(2)}) collective-permute-start(f32[16,64,128]{2,1,0:T(8,128)} %get-tuple-element.112), channel_id=1, source_target_pairs={{0,2},{1,3},{2,0},{3,1},{4,5},{5,4},{6,7},{7,6},{8,10},{9,11},{10,... | collective-permute-start | bytes 1572872 | tf_op jit(solution)/shard_map/ppermute | solution.py:487
  23.9 43.7 %copy-start = (f32[16,64,128]{2,1,0:T(8,128)S(1)}, f32[16,64,128]{2,1,0:T(8,128)}, u32[]{:S(2)}) copy-start(f32[16,64,128]{2,1,0:T(8,128)} %get-tuple-element.113.rest_3_) | copy-start | bytes 1572868
  34.1 5.4 %collective-permute-start = (f32[256,512]{1,0:T(8,128)S(1)}, f32[256,512]{1,0:T(8,128)S(1)}, u32[]{:S(2)}, u32[]{:S(2)}) collective-permute-start(f32[256,512]{1,0:T(8,128)S(1)} %get-tuple-element.202), channel_id=1, source_target_pairs={{0,4},{4,0},{8,12},{12,8},{16,20},{20,16},{24,28},{28,24},{1,5},{5... | collective-permute-start | bytes 1572872 | tf_op jit(solution)/shard_map/while/body/ppermute | solution.py:54
  40.1 6.1 %collective-permute-start.2 = (f32[64,512]{1,0:T(8,128)S(1)}, f32[64,512]{1,0:T(8,128)S(1)}, u32[]{:S(2)}, u32[]{:S(2)}) collective-permute-start(f32[64,512]{1,0:T(8,128)S(1)} %get-tuple-element.205), channel_id=1, source_target_pairs={{0,8},{4,12},{8,0},{12,4},{16,24},{20,28},{24,16},{28,20},{1,9},{5... | collective-permute-start | bytes 393224 | tf_op jit(solution)/shard_map/while/body/ppermute | solution.py:54
  42.2 5.5 %collective-permute-start.1 = (f32[64,512]{1,0:T(8,128)S(1)}, f32[64,512]{1,0:T(8,128)S(1)}, u32[]{:S(2)}, u32[]{:S(2)}) collective-permute-start(f32[64,512]{1,0:T(8,128)S(1)} %get-tuple-element.203), channel_id=1, source_target_pairs={{0,16},{4,20},{8,24},{12,28},{16,0},{20,4},{24,8},{28,12},{1,17},{... | collective-permute-start | bytes 393224 | tf_op jit(solution)/shard_map/while/body/ppermute | solution.py:54
  46.2 6.1 %collective-permute-start.3 = (f32[64,512]{1,0:T(8,128)S(1)}, f32[64,512]{1,0:T(8,128)S(1)}, u32[]{:S(2)}, u32[]{:S(2)}) collective-permute-start(f32[64,512]{1,0:T(8,128)S(1)} %get-tuple-element.206), channel_id=1, source_target_pairs={{0,24},{4,28},{8,16},{12,20},{16,8},{20,12},{24,0},{28,4},{1,25},{... | collective-permute-start | bytes 393224 | tf_op jit(solution)/shard_map/while/body/ppermute | solution.py:54
  52.4 6.1 %collective-permute-start.4 = (f32[64,512]{1,0:T(8,128)S(1)}, f32[64,512]{1,0:T(8,128)S(1)}, u32[]{:S(2)}, u32[]{:S(2)}) collective-permute-start(f32[64,512]{1,0:T(8,128)S(1)} %add_add_fusion.4), channel_id=1, source_target_pairs={{0,1},{1,0},{2,3},{3,2},{4,5},{5,4},{6,7},{7,6},{8,9},{9,8},{10,11... | collective-permute-start | bytes 393224 | tf_op jit(solution)/shard_map/while/body/ppermute | solution.py:54
  67.6 7.5 %copy-start.5 = (f32[64,512]{1,0:T(8,128)S(1)}, f32[64,512]{1,0:T(8,128)}, u32[]{:S(2)}) copy-start(f32[64,512]{1,0:T(8,128)} %get-tuple-element.120) | copy-start | bytes 393220
  67.6 41.2 %copy-start.4 = (bf16[2048,512]{1,0:T(8,128)(2,1)S(1)}, bf16[2048,512]{1,0:T(8,128)(2,1)}, u32[]{:S(2)}) copy-start(bf16[2048,512]{1,0:T(8,128)(2,1)} %get-tuple-element.109.low_ref.low_hbm) | copy-start | bytes 6291460
  72.9 35.9 %copy-start.2 = (f32[768,512]{1,0:T(8,128)S(1)}, f32[768,512]{1,0:T(8,128)}, u32[]{:S(2)}) copy-start(f32[768,512]{1,0:T(8,128)} %get-tuple-element.261) | copy-start | bytes 4718596
  72.9 35.9 %copy-start.3 = (bf16[2048,512]{1,0:T(8,128)(2,1)S(1)}, bf16[2048,512]{1,0:T(8,128)(2,1)}, u32[]{:S(2)}) copy-start(bf16[2048,512]{1,0:T(8,128)(2,1)} %get-tuple-element.108.high_ref.high_hbm) | copy-start | bytes 6291460
  72.9 3.6 %collective-permute-start.10 = (f32[128,768]{1,0:T(8,128)S(1)}, f32[128,768]{1,0:T(8,128)S(1)}, u32[]{:S(2)}, u32[]{:S(2)}) collective-permute-start(f32[128,768]{1,0:T(8,128)S(1)} %get-tuple-element.115), channel_id=1, source_target_pairs={{0,4},{4,0},{8,12},{12,8},{16,20},{20,16},{24,28},{28,24},{1,5},{5... | collective-permute-start | bytes 1179656 | tf_op jit(solution)/shard_map/ppermute | solution.py:54
  75.1 9.2 %collective-permute-start.14 = (f32[64,512]{1,0:T(8,128)S(1)}, f32[64,512]{1,0:T(8,128)S(1)}, u32[]{:S(2)}, u32[]{:S(2)}) collective-permute-start(f32[64,512]{1,0:T(8,128)S(1)} %copy-done.5), channel_id=1, source_target_pairs={{0,2},{1,3},{2,0},{3,1},{4,6},{5,7},{6,4},{7,5},{8,10},{9,11},{10,... | collective-permute-start | bytes 393224 | tf_op jit(solution)/shard_map/ppermute | solution.py:54
  77.1 7.8 %collective-permute-start.11 = (f32[32,768]{1,0:T(8,128)S(1)}, f32[32,768]{1,0:T(8,128)S(1)}, u32[]{:S(2)}, u32[]{:S(2)}) collective-permute-start(f32[32,768]{1,0:T(8,128)S(1)} %get-tuple-element.117), channel_id=1, source_target_pairs={{0,8},{4,12},{8,0},{12,4},{16,24},{20,28},{24,16},{28,20},{1,9},{5... | collective-permute-start | bytes 294920 | tf_op jit(solution)/shard_map/ppermute | solution.py:54
  81.8 6.7 %collective-permute-start.12 = (f32[32,768]{1,0:T(8,128)S(1)}, f32[32,768]{1,0:T(8,128)S(1)}, u32[]{:S(2)}, u32[]{:S(2)}) collective-permute-start(f32[32,768]{1,0:T(8,128)S(1)} %get-tuple-element.118), channel_id=1, source_target_pairs={{0,16},{4,20},{8,24},{12,28},{16,0},{20,4},{24,8},{28,12},{1,17},{... | collective-permute-start | bytes 294920 | tf_op jit(solution)/shard_map/ppermute | solution.py:54
  81.8 6.7 %collective-permute-start.13 = (f32[32,768]{1,0:T(8,128)S(1)}, f32[32,768]{1,0:T(8,128)S(1)}, u32[]{:S(2)}, u32[]{:S(2)}) collective-permute-start(f32[32,768]{1,0:T(8,128)S(1)} %get-tuple-element.119), channel_id=1, source_target_pairs={{0,24},{4,28},{8,16},{12,20},{16,8},{20,12},{24,0},{28,4},{1,25},{... | collective-permute-start | bytes 294920 | tf_op jit(solution)/shard_map/ppermute | solution.py:54
  88.4 7.2 %collective-permute-start.17 = (f32[32,768]{1,0:T(8,128)S(1)}, f32[32,768]{1,0:T(8,128)S(1)}, u32[]{:S(2)}, u32[]{:S(2)}) collective-permute-start(f32[32,768]{1,0:T(8,128)S(1)} %add_add_fusion.2), channel_id=1, source_target_pairs={{0,3},{1,2},{2,1},{3,0},{4,7},{5,6},{6,5},{7,4},{8,11},{9,10},{10,... | collective-permute-start | bytes 294920 | tf_op jit(solution)/shard_map/ppermute | solution.py:54
  91.1 7.4 %collective-permute-start.16 = (f32[32,768]{1,0:T(8,128)S(1)}, f32[32,768]{1,0:T(8,128)S(1)}, u32[]{:S(2)}, u32[]{:S(2)}) collective-permute-start(f32[32,768]{1,0:T(8,128)S(1)} %add_add_fusion.2), channel_id=1, source_target_pairs={{0,2},{1,3},{2,0},{3,1},{4,6},{5,7},{6,4},{7,5},{8,10},{9,11},{10,... | collective-permute-start | bytes 294920 | tf_op jit(solution)/shard_map/ppermute | solution.py:54
  91.5 7.0 %collective-permute-start.15 = (f32[32,768]{1,0:T(8,128)S(1)}, f32[32,768]{1,0:T(8,128)S(1)}, u32[]{:S(2)}, u32[]{:S(2)}) collective-permute-start(f32[32,768]{1,0:T(8,128)S(1)} %add_add_fusion.2), channel_id=1, source_target_pairs={{0,1},{1,0},{2,3},{3,2},{4,5},{5,4},{6,7},{7,6},{8,9},{9,8},{10,11... | collective-permute-start | bytes 294920 | tf_op jit(solution)/shard_map/ppermute | solution.py:54
  92.9 9.5 %collective-permute-start.24 = (f32[64,512]{1,0:T(8,128)S(1)}, f32[64,512]{1,0:T(8,128)S(1)}, u32[]{:S(2)}, u32[]{:S(2)}) collective-permute-start(f32[64,512]{1,0:T(8,128)S(1)} %add.52), channel_id=1, source_target_pairs={{0,24},{4,28},{8,16},{12,20},{16,8},{20,12},{24,0},{28,4},{1,25},{... | collective-permute-start | bytes 393224 | tf_op jit(solution)/shard_map/ppermute | solution.py:54
  94.1 8.3 %collective-permute-start.23 = (f32[64,512]{1,0:T(8,128)S(1)}, f32[64,512]{1,0:T(8,128)S(1)}, u32[]{:S(2)}, u32[]{:S(2)}) collective-permute-start(f32[64,512]{1,0:T(8,128)S(1)} %add.52), channel_id=1, source_target_pairs={{0,16},{4,20},{8,24},{12,28},{16,0},{20,4},{24,8},{28,12},{1,17},{... | collective-permute-start | bytes 393224 | tf_op jit(solution)/shard_map/ppermute | solution.py:54
  95.6 6.7 %collective-permute-start.22 = (f32[64,512]{1,0:T(8,128)S(1)}, f32[64,512]{1,0:T(8,128)S(1)}, u32[]{:S(2)}, u32[]{:S(2)}) collective-permute-start(f32[64,512]{1,0:T(8,128)S(1)} %add.52), channel_id=1, source_target_pairs={{0,8},{4,12},{8,0},{12,4},{16,24},{20,28},{24,16},{28,20},{1,9},{5... | collective-permute-start | bytes 393224 | tf_op jit(solution)/shard_map/ppermute | solution.py:54
  98.5 6.0 %collective-permute-start.20 = (f32[32,768]{1,0:T(8,128)S(1)}, f32[32,768]{1,0:T(8,128)S(1)}, u32[]{:S(2)}, u32[]{:S(2)}) collective-permute-start(f32[32,768]{1,0:T(8,128)S(1)} %add_add_fusion.1), channel_id=1, source_target_pairs={{0,24},{4,28},{8,16},{12,20},{16,8},{20,12},{24,0},{28,4},{1,25},{... | collective-permute-start | bytes 294920 | tf_op jit(solution)/shard_map/ppermute | solution.py:54
  101.1 4.6 %collective-permute-start.19 = (f32[32,768]{1,0:T(8,128)S(1)}, f32[32,768]{1,0:T(8,128)S(1)}, u32[]{:S(2)}, u32[]{:S(2)}) collective-permute-start(f32[32,768]{1,0:T(8,128)S(1)} %add_add_fusion.1), channel_id=1, source_target_pairs={{0,16},{4,20},{8,24},{12,28},{16,0},{20,4},{24,8},{28,12},{1,17},{... | collective-permute-start | bytes 294920 | tf_op jit(solution)/shard_map/ppermute | solution.py:54
  102.3 4.6 %collective-permute-start.18 = (f32[32,768]{1,0:T(8,128)S(1)}, f32[32,768]{1,0:T(8,128)S(1)}, u32[]{:S(2)}, u32[]{:S(2)}) collective-permute-start(f32[32,768]{1,0:T(8,128)S(1)} %add_add_fusion.1), channel_id=1, source_target_pairs={{0,8},{4,12},{8,0},{12,4},{16,24},{20,28},{24,16},{28,20},{1,9},{5... | collective-permute-start | bytes 294920 | tf_op jit(solution)/shard_map/ppermute | solution.py:54
  102.4 6.4 %collective-permute-start.25 = (f32[256,512]{1,0:T(8,128)S(1)}, f32[256,512]{1,0:T(8,128)S(1)}, u32[]{:S(2)}, u32[]{:S(2)}) collective-permute-start(f32[256,512]{1,0:T(8,128)S(1)} %constant_dynamic-update-slice_fusion.gram_ref), channel_id=1, source_target_pairs={{0,4},{4,0},{8,12},{12,8},{16,20},{20,16},{24,28},{28,24},{1,5},{5... | collective-permute-start | bytes 1572872 | tf_op jit(solution)/shard_map/ppermute | solution.py:54
  107.0 1.8 %collective-permute-start.21 = (f32[128,768]{1,0:T(8,128)S(1)}, f32[128,768]{1,0:T(8,128)S(1)}, u32[]{:S(2)}, u32[]{:S(2)}) collective-permute-start(f32[128,768]{1,0:T(8,128)S(1)} %pad_maximum_fusion.sums_ref), channel_id=1, source_target_pairs={{0,4},{4,0},{8,12},{12,8},{16,20},{20,16},{24,28},{28,24},{1,5},{5... | collective-permute-start | bytes 1179656 | tf_op jit(solution)/shard_map/ppermute | solution.py:54

commit v10 on v9

--- a/solution.py
+++ b/solution.py
@@ -216,53 +216,75 @@
     )(index, in_hbm(rotation), in_hbm(basis))
 
 
-def products_kernel(index_ref, high_ref, low_ref, *rest):
-    pieces, (send_ref, keep_ref, snap_ref, sum_ref, mixed_ref) = rest[:-5], rest[-5:]
+CHUNKS = 4
+
+
+def products_of(high_ref, low_ref, snap_high, snap_low, start, out_ref, waits):
+    rows, rank = out_ref.shape[0], high_ref.shape[1]
+    at = pl.ds(pl.multiple_of(start, rows), rows)
+    high, low = snap_high[at, :], snap_low[at, :]
+    across = ((1,), (1,))
+    mixed = mm(high, snap_low[...], across, None) + mm(low, snap_high[...], across, None)
+    out_ref[:, rank:] = mm(high, snap_high[...], across, None) + mixed
+    along = ((1,), (0,))
+    size = high_ref.shape[0] // CHUNKS
+    for c in range(CHUNKS):
+        cells = slice(c * size, (c + 1) * size)
+        for wait in waits:
+            wait(c)
+        mixed = mm(high[:, cells], low_ref[cells, :], along, None) + mm(low[:, cells], high_ref[cells, :], along, None)
+        part = mm(high[:, cells], high_ref[cells, :], along, None) + mixed
+        out_ref[:, :rank] = part if c == 0 else out_ref[:, :rank] + part
+
+
+def send_products_kernel(index_ref, high_hbm, low_hbm, *rest):
+    pieces, (send_ref, snap_high, snap_low, high_ref, low_ref, sem) = rest[:-6], rest[-6:]
     lines, members, width = pieces[0].shape
-    rank = high_ref.shape[-1]
-    step = pl.program_id(0)
+    size = high_ref.shape[0] // CHUNKS
+
+    def fetch(which, c):
+        source, target = ((high_hbm, high_ref), (low_hbm, low_ref))[which]
+        cells = pl.ds(c * size, size)
+        return pltpu.make_async_copy(source.at[cells], target.at[cells], sem.at[which, c])
+
+    for c in range(CHUNKS):
+        fetch(0, c).start()
+        fetch(1, c).start()
     for k, piece in enumerate(pieces):
-        at = pl.multiple_of((index_ref[0] ^ index_ref[FIRST + k]) * members, members)
+        at = pl.ds(pl.multiple_of((index_ref[0] ^ index_ref[FIRST + k]) * members, members), members)
         for line in range(lines):
-            snap_ref[pl.ds(at, members), line * width:(line + 1) * width] = piece[line]
-
-    @pl.when(step == 0)
-    def _():
-        sum_ref[...] = jnp.zeros_like(sum_ref)
-        mixed_ref[...] = jnp.zeros_like(mixed_ref)
-
-    snap = halves(snap_ref[...])
-    sum_ref[:, :rank] += mm3(snap, (high_ref[...], low_ref[...]), ((1,), (0,)))
-    sum_ref[:, rank:] += mm(snap[0], snap[0], ((1,), (1,)), None)
-    mixed_ref[...] += mm(snap[0], snap[1], ((1,), (1,)), None)
-
-    @pl.when(step == pl.num_programs(0) - 1)
-    def _():
-        sum_ref[:, rank:] += mixed_ref[...] + mixed_ref[...].T
-        half = keep_ref.shape[0]
-        core = index_ref[1]
-        keep_ref[...] = sum_ref[pl.ds(pl.multiple_of(core * half, half), half), :]
-        send_ref[...] = sum_ref[pl.ds(pl.multiple_of((1 - core) * half, half), half), :]
+            cols = slice(line * width, (line + 1) * width)
+            snap_high[at, cols], snap_low[at, cols] = halves(piece[line])
+    start = (1 - index_ref[1]) * send_ref.shape[0]
+    waits = [lambda c: fetch(0, c).wait(), lambda c: fetch(1, c).wait()]
+    products_of(high_ref, low_ref, snap_high, snap_low, start, send_ref, waits)
+
+
+def keep_products_kernel(index_ref, high_ref, low_ref, snap_high, snap_low, keep_ref):
+    products_of(high_ref, low_ref, snap_high, snap_low, index_ref[1] * keep_ref.shape[0], keep_ref, [])
 
 
 def products(index, high, low, pieces):
-    rank = high.shape[1]
-    lines, members, width = pieces[0].shape
-    total = members * len(pieces)
-    block = 4
-    half = pl.BlockSpec((total // 2, rank + total), lambda i: (0, 0))
-    return pl.pallas_call(
-        products_kernel,
-        grid=(lines // block,),
-        in_specs=[SCALARS] + [pl.BlockSpec((block * width, rank), lambda i: (i, 0))] * 2
-        + [pl.BlockSpec((block, members, width), lambda i: (i, 0, 0))] * len(pieces),
-        out_specs=[half, half],
-        out_shape=[shape(total // 2, rank + total)] * 2,
-        scratch_shapes=[pltpu.VMEM((total, block * width), jnp.float32), pltpu.VMEM((total, rank + total), jnp.float32),
-                        pltpu.VMEM((total, total), jnp.float32)],
-        compiler_params=params(14),
-        name="products",
+    rows, rank = high.shape
+    total = pieces[0].shape[1] * len(pieces)
+    vmem = pl.BlockSpec(memory_space=pltpu.VMEM)
+    half = shape(total // 2, rank + total)
+    send, *snap = pl.pallas_call(
+        send_products_kernel,
+        in_specs=[SCALARS] + [pl.BlockSpec(memory_space=pl.ANY)] * 2 + [vmem] * len(pieces),
+        out_shape=[half] + [shape(total, rows, dtype=jnp.bfloat16)] * 2,
+        scratch_shapes=[pltpu.VMEM(high.shape, jnp.bfloat16)] * 2 + [pltpu.SemaphoreType.DMA((2, CHUNKS))],
+        compiler_params=params(16),
+        name="send_products",
     )(index, in_hbm(high), in_hbm(low), *pieces)
+    keep = pl.pallas_call(
+        keep_products_kernel,
+        in_specs=[SCALARS] + [vmem] * 4,
+        out_shape=half,
+        compiler_params=params(12),
+        name="keep_products",
+    )(index, high, low, *snap)
+    return send, keep
 
 
 def split_kernel(index_ref, keep_ref, got_ref, *outs):

time: 126 us -> 128 us (1.016)
  Pallas kernels: 47.4 us -> 50.1 us
    pallas_call x1 -> x2, Pallas kernels: 5.26 us -> 7.69 us  [the longest x1 5.31 us: products(): pl.pallas_call(send_products_kernel, in_specs=[SCALARS] + [pl.BlockSpec(m...]
  transfers between devices with their start and end apart: 26 -> 26, of which waited for: 16 -> 14; matrix products, arithmetic and copies ran while one was open for 1% -> 1% of each run, Pallas kernels for 13% -> 14%
where the time goes in v10:
time: 128 us
  Pallas kernels  50.1 us (39%)
  waiting for transfers between devices  39.3 us (31%)
  starting transfers between devices  35.9 us (28%)
    ppermute x21, waiting for transfers between devices, xor_permute(): return lax.ppermute(value, axis, [(i, i ^ mask) for i in range(size)])  30.8 us
    ppermute x21, starting transfers between devices, xor_permute(): return lax.ppermute(value, axis, [(i, i ^ mask) for i in range(size)])  27.1 us
    pallas_call x1, Pallas kernels, solve(): pl.pallas_call(functools.partial(solve_kernel, count=float(count), chips=...  17.4 us
    pallas_call x1, Pallas kernels, basis_parts(): pl.pallas_call(basis_kernel, grid=(lines // block,), in_specs=[SCALARS, p...  10.3 us
    ppermute x3, waiting for transfers between devices, per_device(): pieces[slot] = lax.ppermute(pieces[slot], ('sim', 'ana'), pairs)  8.42 us
    pallas_call x1, Pallas kernels, evolve(): pl.pallas_call(functools.partial(evolve_kernel, slots=slots), in_specs=[S...  6.69 us
    pallas_call x1, Pallas kernels, products(): pl.pallas_call(send_products_kernel, in_specs=[SCALARS] + [pl.BlockSpec(m...  5.31 us
    ppermute x3, starting transfers between devices, per_device(): pieces[slot] = lax.ppermute(pieces[slot], ('sim', 'ana'), pairs)  5.06 us
  transfers between devices with their start and end apart: 26, of which 14 were waited for; matrix products, arithmetic and copies ran while one was open for 1% of the time, Pallas kernels for 14%

profile of v10, /device:TPU:0, one launch (start us, length us, event | category | flops | bytes accessed | tf_op | source)
XLA Modules:
  0.0 128.0 jit_solution(3418475406225422959)
XLA Ops:
  0.6 2.3 %edges.1 = (f32[9,64,128]{2,1,0:T(8,128)}, f32[9,64,128]{2,1,0:T(8,128)}) custom-call(f32[64,128]{1,0:T(8,128)} %stiff_ref.3, f32[64,64,128]{2,1,0:T(8,128)} %disp_high.1, f32[64,64,128]{2,1,0:T(8,128)} %vel_high.1, f32[64,64,128]{2,1,0:T(8,128)} %disp_high.1, f32[64,64,128]{2,1,0:T(8,128)} %vel_high.1), custom_call_target="tpu_custom_call" | custom-call | tf_op jit(solution)/shard_map/edges/pallas_call | solution.py:74
  3.0 2.4 %collective-permute-start.5 = (f32[9,64,128]{2,1,0:T(8,128)}, f32[9,64,128]{2,1,0:T(8,128)S(1)}, u32[]{:S(2)}, u32[]{:S(2)}) collective-permute-start(f32[9,64,128]{2,1,0:T(8,128)} %get-tuple-element.91), channel_id=1, source_target_pairs={{0,4},{4,8},{8,12},{12,16},{16,20},{20,24},{24,28},{1,5},{5,9},{9,... | collective-permute-start | bytes 884744 | tf_op jit(solution)/shard_map/ppermute | solution.py:499
  5.3 1.3 %collective-permute-start.6 = (f32[9,64,128]{2,1,0:T(8,128)}, f32[9,64,128]{2,1,0:T(8,128)S(1)}, u32[]{:S(2)}, u32[]{:S(2)}) collective-permute-start(f32[9,64,128]{2,1,0:T(8,128)} %get-tuple-element.92), channel_id=1, source_target_pairs={{4,0},{8,4},{12,8},{16,12},{20,16},{24,20},{28,24},{5,1},{9,5},{13... | collective-permute-start | bytes 884744 | tf_op jit(solution)/shard_map/ppermute | solution.py:500
  6.7 4.6 %to_lines.1 = (f32[64,64,128]{2,1,0:T(8,128)S(1)}, f32[64,64,128]{2,1,0:T(8,128)S(1)}) custom-call(f32[4096,128]{1,0:T(8,128)} %bitcast.6, f32[4096,128]{1,0:T(8,128)} %bitcast.7), custom_call_target="tpu_custom_call" | custom-call | tf_op jit(solution)/shard_map/to_lines/pallas_call | solution.py:97
  11.3 0.1 pad_add_fusion.index_ref
  11.4 6.7 %evolve.1 = (f32[16,64,128]{2,1,0:T(8,128)}, f32[16,64,128]{2,1,0:T(8,128)}, f32[16,64,128]{2,1,0:T(8,128)}, f32[16,64,128]{2,1,0:T(8,128)}) custom-call(s32[7]{0:T(128)S(1)} %pad_add_fusion.index_ref, f32[64,64,128]{2,1,0:T(8,128)S(1)} %get-tuple-element.96.disp_ref, f32[64,64,128]{2,1,0:T(8,128)S(1)} %get-tuple-element.97.vel_ref, ...), custom_call_target="tpu_custom_call" | custom-call | tf_op jit(solution)/shard_map/evolve/pallas_call | solution.py:155
  18.1 2.5 %collective-permute-start.7 = (f32[16,64,128]{2,1,0:T(8,128)}, f32[16,64,128]{2,1,0:T(8,128)S(1)}, u32[]{:S(2)}, u32[]{:S(2)}) collective-permute-start(f32[16,64,128]{2,1,0:T(8,128)} %get-tuple-element.111), channel_id=1, source_target_pairs={{0,1},{1,0},{2,3},{3,2},{4,7},{5,6},{6,5},{7,4},{8,9},{9,8},{10,11... | collective-permute-start | bytes 1572872 | tf_op jit(solution)/shard_map/ppermute | solution.py:509
  20.6 2.5 %collective-permute-start.8 = (f32[16,64,128]{2,1,0:T(8,128)}, f32[16,64,128]{2,1,0:T(8,128)S(1)}, u32[]{:S(2)}, u32[]{:S(2)}) collective-permute-start(f32[16,64,128]{2,1,0:T(8,128)} %get-tuple-element.112), channel_id=1, source_target_pairs={{0,3},{1,2},{2,1},{3,0},{4,6},{5,7},{6,4},{7,5},{8,11},{9,10},{10,... | collective-permute-start | bytes 1572872 | tf_op jit(solution)/shard_map/ppermute | solution.py:509
  23.1 0.1 collective-permute-start.9
  23.2 0.7 broadcast_in_dim.3
  23.9 35.3 %while.18 = (s32[]{:T(128)}, s32[7]{0:T(128)S(1)}, f32[64,512]{1,0:T(8,128)}, bf16[2048,512]{1,0:T(8,128)(2,1)}, bf16[2048,512]{1,0:T(8,128)(2,1)}, /*index=5*/f...) while((s32[]{:T(128)}, s32[7]{0:T(128)S(1)}, ...), condition=%wide.region_1.2_spmd, body=%wide.region_0.1_spmd.sunk | while | flops 131088 | bytes 5243237 | solution.py:518
  23.9 10.3 %basis_parts.1 = (f32[256,512]{1,0:T(8,128)S(1)}, f32[256,512]{1,0:T(8,128)S(1)}, bf16[2048,512]{1,0:T(8,128)(2,1)}, bf16[2048,512]{1,0:T(8,128)(2,1)}, f32[2048,512]{1,0:T(8,128)}) custom-call(s32[7]{0:T(128)S(1)} %get-tuple-element.225.index_ref, f32[768,512]{1,0:T(8,128)} %get-tuple-element.241.rot_ref, f32[16,128,512]{2,1,0:T(8,128)} %get-tuple-element.242.basis_ref), custom_call_target="tpu_custom_call" | custom-call | tf_op jit(solution)/shard_map/while/body/basis_parts/pallas_call | solution.py:206
  34.1 3.8 %collective-permute-start = (f32[256,512]{1,0:T(8,128)S(1)}, f32[256,512]{1,0:T(8,128)S(1)}, u32[]{:S(2)}, u32[]{:S(2)}) collective-permute-start(f32[256,512]{1,0:T(8,128)S(1)} %get-tuple-element.204), channel_id=1, source_target_pairs={{0,4},{4,0},{8,12},{12,8},{16,20},{20,16},{24,28},{28,24},{1,5},{5... | collective-permute-start | bytes 1572872 | tf_op jit(solution)/shard_map/while/body/ppermute | solution.py:54
  38.0 1.5 %collective-permute-done.got_ref = f32[256,512]{1,0:T(8,128)S(1)} collective-permute-done((f32[256,512]{1,0:T(8,128)S(1)}, f32[256,512]{1,0:T(8,128)S(1)}, u32[]{:S(2)}, u32[]{:S(2)}) %collective-permute-start) | collective-permute-done | bytes 524320 | tf_op jit(solution)/shard_map/while/body/ppermute | solution.py:54
  39.5 0.6 split.3
  40.1 2.1 %collective-permute-start.2 = (f32[64,512]{1,0:T(8,128)S(1)}, f32[64,512]{1,0:T(8,128)S(1)}, u32[]{:S(2)}, u32[]{:S(2)}) collective-permute-start(f32[64,512]{1,0:T(8,128)S(1)} %get-tuple-element.207), channel_id=1, source_target_pairs={{0,8},{4,12},{8,0},{12,4},{16,24},{20,28},{24,16},{28,20},{1,9},{5... | collective-permute-start | bytes 393224 | tf_op jit(solution)/shard_map/while/body/ppermute | solution.py:54
  42.3 4.0 %collective-permute-done.2 = f32[64,512]{1,0:T(8,128)S(1)} collective-permute-done((f32[64,512]{1,0:T(8,128)S(1)}, f32[64,512]{1,0:T(8,128)S(1)}, u32[]{:S(2)}, u32[]{:S(2)}) %collective-permute-start.2) | collective-permute-done | bytes 131104 | tf_op jit(solution)/shard_map/while/body/ppermute | solution.py:54
  46.2 1.0 collective-permute-start.3
  47.2 0.4 collective-permute-done.1
  47.7 4.7 %collective-permute-done.3 = f32[64,512]{1,0:T(8,128)S(1)} collective-permute-done((f32[64,512]{1,0:T(8,128)S(1)}, f32[64,512]{1,0:T(8,128)S(1)}, u32[]{:S(2)}, u32[]{:S(2)}) %collective-permute-start.3) | collective-permute-done | bytes 131104 | tf_op jit(solution)/shard_map/while/body/ppermute | solution.py:54
  52.4 1.4 %collective-permute-start.4 = (f32[64,512]{1,0:T(8,128)S(1)}, f32[64,512]{1,0:T(8,128)S(1)}, u32[]{:S(2)}, u32[]{:S(2)}) collective-permute-start(f32[64,512]{1,0:T(8,128)S(1)} %add_add_fusion.4), channel_id=1, source_target_pairs={{0,1},{1,0},{2,3},{3,2},{4,5},{5,4},{6,7},{7,6},{8,9},{9,8},{10,11... | collective-permute-start | bytes 393224 | tf_op jit(solution)/shard_map/while/body/ppermute | solution.py:54
  53.8 4.7 %collective-permute-done.4 = f32[64,512]{1,0:T(8,128)S(1)} collective-permute-done((f32[64,512]{1,0:T(8,128)S(1)}, f32[64,512]{1,0:T(8,128)S(1)}, u32[]{:S(2)}, u32[]{:S(2)}) %collective-permute-start.4) | collective-permute-done | bytes 131104 | tf_op jit(solution)/shard_map/while/body/ppermute | solution.py:54
  58.5 0.7 add.83
  59.2 8.4 %collective-permute-done.9.rest_2_ = f32[16,64,128]{2,1,0:T(8,128)S(1)} collective-permute-done((f32[16,64,128]{2,1,0:T(8,128)}, f32[16,64,128]{2,1,0:T(8,128)S(1)}, u32[]{:S(2)}, u32[]{:S(2)}) %collective-permute-start.9) | collective-permute-done | bytes 524320 | tf_op jit(solution)/shard_map/ppermute | solution.py:509
  67.6 5.3 %send_products.1 = (f32[128,768]{1,0:T(8,128)S(1)}, bf16[256,2048]{1,0:T(8,128)(2,1)S(1)}, bf16[256,2048]{1,0:T(8,128)(2,1)S(1)}) custom-call(s32[7]{0:T(128)S(1)} %get-tuple-element.108.index_ref, bf16[2048,512]{1,0:T(8,128)(2,1)} %get-tuple-element.109.high_hbm.high_ref, bf16[2048,512]{1,0:T(8,128)(2,1)} %get-tuple-element.110.low_hbm.low_ref, ...), custom_call_target="tpu_custom_call" | custom-call | tf_op jit(solution)/shard_map/send_products/pallas_call | solution.py:272
  72.9 2.2 %collective-permute-start.10 = (f32[128,768]{1,0:T(8,128)S(1)}, f32[128,768]{1,0:T(8,128)S(1)}, u32[]{:S(2)}, u32[]{:S(2)}) collective-permute-start(f32[128,768]{1,0:T(8,128)S(1)} %get-tuple-element.117), channel_id=1, source_target_pairs={{0,4},{4,0},{8,12},{12,8},{16,20},{20,16},{24,28},{28,24},{1,5},{5... | collective-permute-start | bytes 1179656 | tf_op jit(solution)/shard_map/ppermute | solution.py:54
  75.1 2.4 %keep_products.1.keep_ref = f32[128,768]{1,0:T(8,128)S(1)} custom-call(s32[7]{0:T(128)S(1)} %get-tuple-element.108.index_ref, bf16[2048,512]{1,0:T(8,128)(2,1)S(1)} %copy-done.3, bf16[2048,512]{1,0:T(8,128)(2,1)S(1)} %copy-done.4, bf16[256,2048]{1,0:T(8,128)(2,1)S(1)} %get-tuple-element.115.snap_high, bf16[256,2048]{1,0:T(8,128)(2,1)S(1)} %get-tuple-element.116.snap_low), custom_call_target="tpu_custom_call" | custom-call | tf_op jit(solution)/shard_map/keep_products/pallas_call | solution.py:280
  77.6 0.6 split.2
  78.2 4.5 %collective-permute-start.11 = (f32[32,768]{1,0:T(8,128)S(1)}, f32[32,768]{1,0:T(8,128)S(1)}, u32[]{:S(2)}, u32[]{:S(2)}) collective-permute-start(f32[32,768]{1,0:T(8,128)S(1)} %get-tuple-element.119), channel_id=1, source_target_pairs={{0,8},{4,12},{8,0},{12,4},{16,24},{20,28},{24,16},{28,20},{1,9},{5... | collective-permute-start | bytes 294920 | tf_op jit(solution)/shard_map/ppermute | solution.py:54
  82.6 1.5 %collective-permute-start.13 = (f32[32,768]{1,0:T(8,128)S(1)}, f32[32,768]{1,0:T(8,128)S(1)}, u32[]{:S(2)}, u32[]{:S(2)}) collective-permute-start(f32[32,768]{1,0:T(8,128)S(1)} %get-tuple-element.121), channel_id=1, source_target_pairs={{0,24},{4,28},{8,16},{12,20},{16,8},{20,12},{24,0},{28,4},{1,25},{... | collective-permute-start | bytes 294920 | tf_op jit(solution)/shard_map/ppermute | solution.py:54
  84.2 0.1 collective-permute-done.14
  84.3 1.6 %collective-permute-done.11 = f32[32,768]{1,0:T(8,128)S(1)} collective-permute-done((f32[32,768]{1,0:T(8,128)S(1)}, f32[32,768]{1,0:T(8,128)S(1)}, u32[]{:S(2)}, u32[]{:S(2)}) %collective-permute-start.11) | collective-permute-done | bytes 98336 | tf_op jit(solution)/shard_map/ppermute | solution.py:54
  86.0 3.6 %collective-permute-done.12 = f32[32,768]{1,0:T(8,128)S(1)} collective-permute-done((f32[32,768]{1,0:T(8,128)S(1)}, f32[32,768]{1,0:T(8,128)S(1)}, u32[]{:S(2)}, u32[]{:S(2)}) %collective-permute-start.12) | collective-permute-done | bytes 98336 | tf_op jit(solution)/shard_map/ppermute | solution.py:54
  89.6 2.7 %collective-permute-start.17 = (f32[32,768]{1,0:T(8,128)S(1)}, f32[32,768]{1,0:T(8,128)S(1)}, u32[]{:S(2)}, u32[]{:S(2)}) collective-permute-start(f32[32,768]{1,0:T(8,128)S(1)} %add_add_fusion.2), channel_id=1, source_target_pairs={{0,3},{1,2},{2,1},{3,0},{4,7},{5,6},{6,5},{7,4},{8,11},{9,10},{10,... | collective-permute-start | bytes 294920 | tf_op jit(solution)/shard_map/ppermute | solution.py:54
  92.2 1.7 %collective-permute-start.16 = (f32[32,768]{1,0:T(8,128)S(1)}, f32[32,768]{1,0:T(8,128)S(1)}, u32[]{:S(2)}, u32[]{:S(2)}) collective-permute-start(f32[32,768]{1,0:T(8,128)S(1)} %add_add_fusion.2), channel_id=1, source_target_pairs={{0,2},{1,3},{2,0},{3,1},{4,6},{5,7},{6,4},{7,5},{8,10},{9,11},{10,... | collective-permute-start | bytes 294920 | tf_op jit(solution)/shard_map/ppermute | solution.py:54
  93.9 0.1 collective-permute-start.15
  94.0 1.2 collective-permute-start.24
  95.2 0.6 collective-permute-start.23
  95.8 1.2 collective-permute-done.17
  97.0 0.6 collective-permute-start.22
  97.6 3.3 %collective-permute-done.16 = f32[32,768]{1,0:T(8,128)S(1)} collective-permute-done((f32[32,768]{1,0:T(8,128)S(1)}, f32[32,768]{1,0:T(8,128)S(1)}, u32[]{:S(2)}, u32[]{:S(2)}) %collective-permute-start.16) | collective-permute-done | bytes 98336 | tf_op jit(solution)/shard_map/ppermute | solution.py:54
  101.0 2.3 %collective-permute-start.20 = (f32[32,768]{1,0:T(8,128)S(1)}, f32[32,768]{1,0:T(8,128)S(1)}, u32[]{:S(2)}, u32[]{:S(2)}) collective-permute-start(f32[32,768]{1,0:T(8,128)S(1)} %add_add_fusion.1), channel_id=1, source_target_pairs={{0,24},{4,28},{8,16},{12,20},{16,8},{20,12},{24,0},{28,4},{1,25},{... | collective-permute-start | bytes 294920 | tf_op jit(solution)/shard_map/ppermute | solution.py:54
  103.3 1.2 collective-permute-start.18
  104.6 0.1 collective-permute-start.25
  104.7 2.0 %collective-permute-done.20 = f32[32,768]{1,0:T(8,128)S(1)} collective-permute-done((f32[32,768]{1,0:T(8,128)S(1)}, f32[32,768]{1,0:T(8,128)S(1)}, u32[]{:S(2)}, u32[]{:S(2)}) %collective-permute-start.20) | collective-permute-done | bytes 98336 | tf_op jit(solution)/shard_map/ppermute | solution.py:54
  106.6 2.0 %collective-permute-done.19 = f32[32,768]{1,0:T(8,128)S(1)} collective-permute-done((f32[32,768]{1,0:T(8,128)S(1)}, f32[32,768]{1,0:T(8,128)S(1)}, u32[]{:S(2)}, u32[]{:S(2)}) %collective-permute-start.19) | collective-permute-done | bytes 98336 | tf_op jit(solution)/shard_map/ppermute | solution.py:54
  108.7 1.7 %collective-permute-done.21.sums2_ref = f32[128,768]{1,0:T(8,128)S(1)} collective-permute-done((f32[128,768]{1,0:T(8,128)S(1)}, f32[128,768]{1,0:T(8,128)S(1)}, u32[]{:S(2)}, u32[]{:S(2)}) %collective-permute-start.21) | collective-permute-done | bytes 393248 | tf_op jit(solution)/shard_map/ppermute | solution.py:54
  110.4 17.4 %solve.1 = (f32[16,128,512]{2,1,0:T(8,128)}, f32[512,256]{1,0:T(8,128)}) custom-call(s32[7]{0:T(128)S(1)} %pad_add_fusion.index_ref, f32[128,768]{1,0:T(8,128)S(1)} %pad_maximum_fusion.sums_ref, f32[128,768]{1,0:T(8,128)S(1)} %collective-permute-done.21.sums2_ref, f32[256,512]{1,0:T(8,128)S(1)} %constant_dynamic-update-slice_fusion.gram_ref, ...), custom_call_target="tpu_custom_call" | custom-call | tf_op jit(solution)/shard_map/solve/pallas_call | solution.py:466
  (46 shorter events, 0.4 us)
Async XLA Ops:
  3.0 8.5 %collective-permute-start.5 = (f32[9,64,128]{2,1,0:T(8,128)}, f32[9,64,128]{2,1,0:T(8,128)S(1)}, u32[]{:S(2)}, u32[]{:S(2)}) collective-permute-start(f32[9,64,128]{2,1,0:T(8,128)} %get-tuple-element.91), channel_id=1, source_target_pairs={{0,4},{4,8},{8,12},{12,16},{16,20},{20,24},{24,28},{1,5},{5,9},{9,... | collective-permute-start | bytes 884744 | tf_op jit(solution)/shard_map/ppermute | solution.py:499
  5.3 6.1 %collective-permute-start.6 = (f32[9,64,128]{2,1,0:T(8,128)}, f32[9,64,128]{2,1,0:T(8,128)S(1)}, u32[]{:S(2)}, u32[]{:S(2)}) collective-permute-start(f32[9,64,128]{2,1,0:T(8,128)} %get-tuple-element.92), channel_id=1, source_target_pairs={{4,0},{8,4},{12,8},{16,12},{20,16},{24,20},{28,24},{5,1},{9,5},{13... | collective-permute-start | bytes 884744 | tf_op jit(solution)/shard_map/ppermute | solution.py:500
  6.7 4.6 %copy-start.6 = (s32[4]{0:T(128)S(1)}, s32[4]{0:T(128)}, u32[]{:S(2)}) copy-start(s32[4]{0:T(128)} %constant.48.clone) | copy-start | bytes 52
  6.7 4.6 %copy-start.7 = (s32[4]{0:T(128)S(1)}, s32[4]{0:T(128)}, u32[]{:S(2)}) copy-start(s32[4]{0:T(128)} %constant.47.clone) | copy-start | bytes 52
  6.7 4.7 %copy-start.1 = (f32[64,128]{1,0:T(8,128)S(1)}, f32[64,128]{1,0:T(8,128)}, u32[]{:S(2)}) copy-start(f32[64,128]{1,0:T(8,128)} %stiff_ref.3) | copy-start | bytes 98308
  18.1 41.1 %collective-permute-start.7 = (f32[16,64,128]{2,1,0:T(8,128)}, f32[16,64,128]{2,1,0:T(8,128)S(1)}, u32[]{:S(2)}, u32[]{:S(2)}) collective-permute-start(f32[16,64,128]{2,1,0:T(8,128)} %get-tuple-element.111), channel_id=1, source_target_pairs={{0,1},{1,0},{2,3},{3,2},{4,7},{5,6},{6,5},{7,4},{8,9},{9,8},{10,11... | collective-permute-start | bytes 1572872 | tf_op jit(solution)/shard_map/ppermute | solution.py:509
  20.6 38.6 %collective-permute-start.8 = (f32[16,64,128]{2,1,0:T(8,128)}, f32[16,64,128]{2,1,0:T(8,128)S(1)}, u32[]{:S(2)}, u32[]{:S(2)}) collective-permute-start(f32[16,64,128]{2,1,0:T(8,128)} %get-tuple-element.112), channel_id=1, source_target_pairs={{0,3},{1,2},{2,1},{3,0},{4,6},{5,7},{6,4},{7,5},{8,11},{9,10},{10,... | collective-permute-start | bytes 1572872 | tf_op jit(solution)/shard_map/ppermute | solution.py:509
  23.1 44.5 %collective-permute-start.9 = (f32[16,64,128]{2,1,0:T(8,128)}, f32[16,64,128]{2,1,0:T(8,128)S(1)}, u32[]{:S(2)}, u32[]{:S(2)}) collective-permute-start(f32[16,64,128]{2,1,0:T(8,128)} %get-tuple-element.113), channel_id=1, source_target_pairs={{0,2},{1,3},{2,0},{3,1},{4,5},{5,4},{6,7},{7,6},{8,10},{9,11},{10,... | collective-permute-start | bytes 1572872 | tf_op jit(solution)/shard_map/ppermute | solution.py:509
  23.9 43.7 %copy-start = (f32[16,64,128]{2,1,0:T(8,128)S(1)}, f32[16,64,128]{2,1,0:T(8,128)}, u32[]{:S(2)}) copy-start(f32[16,64,128]{2,1,0:T(8,128)} %get-tuple-element.114.rest_3_) | copy-start | bytes 1572868
  34.1 5.4 %collective-permute-start = (f32[256,512]{1,0:T(8,128)S(1)}, f32[256,512]{1,0:T(8,128)S(1)}, u32[]{:S(2)}, u32[]{:S(2)}) collective-permute-start(f32[256,512]{1,0:T(8,128)S(1)} %get-tuple-element.204), channel_id=1, source_target_pairs={{0,4},{4,0},{8,12},{12,8},{16,20},{20,16},{24,28},{28,24},{1,5},{5... | collective-permute-start | bytes 1572872 | tf_op jit(solution)/shard_map/while/body/ppermute | solution.py:54
  40.1 6.1 %collective-permute-start.2 = (f32[64,512]{1,0:T(8,128)S(1)}, f32[64,512]{1,0:T(8,128)S(1)}, u32[]{:S(2)}, u32[]{:S(2)}) collective-permute-start(f32[64,512]{1,0:T(8,128)S(1)} %get-tuple-element.207), channel_id=1, source_target_pairs={{0,8},{4,12},{8,0},{12,4},{16,24},{20,28},{24,16},{28,20},{1,9},{5... | collective-permute-start | bytes 393224 | tf_op jit(solution)/shard_map/while/body/ppermute | solution.py:54
  42.2 5.5 %collective-permute-start.1 = (f32[64,512]{1,0:T(8,128)S(1)}, f32[64,512]{1,0:T(8,128)S(1)}, u32[]{:S(2)}, u32[]{:S(2)}) collective-permute-start(f32[64,512]{1,0:T(8,128)S(1)} %get-tuple-element.205), channel_id=1, source_target_pairs={{0,16},{4,20},{8,24},{12,28},{16,0},{20,4},{24,8},{28,12},{1,17},{... | collective-permute-start | bytes 393224 | tf_op jit(solution)/shard_map/while/body/ppermute | solution.py:54
  46.2 6.2 %collective-permute-start.3 = (f32[64,512]{1,0:T(8,128)S(1)}, f32[64,512]{1,0:T(8,128)S(1)}, u32[]{:S(2)}, u32[]{:S(2)}) collective-permute-start(f32[64,512]{1,0:T(8,128)S(1)} %get-tuple-element.208), channel_id=1, source_target_pairs={{0,24},{4,28},{8,16},{12,20},{16,8},{20,12},{24,0},{28,4},{1,25},{... | collective-permute-start | bytes 393224 | tf_op jit(solution)/shard_map/while/body/ppermute | solution.py:54
  52.4 6.1 %collective-permute-start.4 = (f32[64,512]{1,0:T(8,128)S(1)}, f32[64,512]{1,0:T(8,128)S(1)}, u32[]{:S(2)}, u32[]{:S(2)}) collective-permute-start(f32[64,512]{1,0:T(8,128)S(1)} %add_add_fusion.4), channel_id=1, source_target_pairs={{0,1},{1,0},{2,3},{3,2},{4,5},{5,4},{6,7},{7,6},{8,9},{9,8},{10,11... | collective-permute-start | bytes 393224 | tf_op jit(solution)/shard_map/while/body/ppermute | solution.py:54
  67.6 7.5 %copy-start.5 = (f32[64,512]{1,0:T(8,128)S(1)}, f32[64,512]{1,0:T(8,128)}, u32[]{:S(2)}) copy-start(f32[64,512]{1,0:T(8,128)} %get-tuple-element.122) | copy-start | bytes 393220
  67.6 7.5 %copy-start.3 = (bf16[2048,512]{1,0:T(8,128)(2,1)S(1)}, bf16[2048,512]{1,0:T(8,128)(2,1)}, u32[]{:S(2)}) copy-start(bf16[2048,512]{1,0:T(8,128)(2,1)} %get-tuple-element.109.high_hbm.high_ref) | copy-start | bytes 6291460
  67.6 7.5 %copy-start.4 = (bf16[2048,512]{1,0:T(8,128)(2,1)S(1)}, bf16[2048,512]{1,0:T(8,128)(2,1)}, u32[]{:S(2)}) copy-start(bf16[2048,512]{1,0:T(8,128)(2,1)} %get-tuple-element.110.low_hbm.low_ref) | copy-start | bytes 6291460
  72.9 4.6 %collective-permute-start.10 = (f32[128,768]{1,0:T(8,128)S(1)}, f32[128,768]{1,0:T(8,128)S(1)}, u32[]{:S(2)}, u32[]{:S(2)}) collective-permute-start(f32[128,768]{1,0:T(8,128)S(1)} %get-tuple-element.117), channel_id=1, source_target_pairs={{0,4},{4,0},{8,12},{12,8},{16,20},{20,16},{24,28},{28,24},{1,5},{5... | collective-permute-start | bytes 1179656 | tf_op jit(solution)/shard_map/ppermute | solution.py:54
  75.1 9.2 %collective-permute-start.14 = (f32[64,512]{1,0:T(8,128)S(1)}, f32[64,512]{1,0:T(8,128)S(1)}, u32[]{:S(2)}, u32[]{:S(2)}) collective-permute-start(f32[64,512]{1,0:T(8,128)S(1)} %copy-done.5), channel_id=1, source_target_pairs={{0,2},{1,3},{2,0},{3,1},{4,6},{5,7},{6,4},{7,5},{8,10},{9,11},{10,... | collective-permute-start | bytes 393224 | tf_op jit(solution)/shard_map/ppermute | solution.py:54
  77.5 32.9 %copy-start.2 = (f32[768,512]{1,0:T(8,128)S(1)}, f32[768,512]{1,0:T(8,128)}, u32[]{:S(2)}) copy-start(f32[768,512]{1,0:T(8,128)} %get-tuple-element.263) | copy-start | bytes 4718596
  78.2 7.8 %collective-permute-start.11 = (f32[32,768]{1,0:T(8,128)S(1)}, f32[32,768]{1,0:T(8,128)S(1)}, u32[]{:S(2)}, u32[]{:S(2)}) collective-permute-start(f32[32,768]{1,0:T(8,128)S(1)} %get-tuple-element.119), channel_id=1, source_target_pairs={{0,8},{4,12},{8,0},{12,4},{16,24},{20,28},{24,16},{28,20},{1,9},{5... | collective-permute-start | bytes 294920 | tf_op jit(solution)/shard_map/ppermute | solution.py:54
  82.6 6.9 %collective-permute-start.12 = (f32[32,768]{1,0:T(8,128)S(1)}, f32[32,768]{1,0:T(8,128)S(1)}, u32[]{:S(2)}, u32[]{:S(2)}) collective-permute-start(f32[32,768]{1,0:T(8,128)S(1)} %get-tuple-element.120), channel_id=1, source_target_pairs={{0,16},{4,20},{8,24},{12,28},{16,0},{20,4},{24,8},{28,12},{1,17},{... | collective-permute-start | bytes 294920 | tf_op jit(solution)/shard_map/ppermute | solution.py:54
  82.6 6.9 %collective-permute-start.13 = (f32[32,768]{1,0:T(8,128)S(1)}, f32[32,768]{1,0:T(8,128)S(1)}, u32[]{:S(2)}, u32[]{:S(2)}) collective-permute-start(f32[32,768]{1,0:T(8,128)S(1)} %get-tuple-element.121), channel_id=1, source_target_pairs={{0,24},{4,28},{8,16},{12,20},{16,8},{20,12},{24,0},{28,4},{1,25},{... | collective-permute-start | bytes 294920 | tf_op jit(solution)/shard_map/ppermute | solution.py:54
  89.6 7.4 %collective-permute-start.17 = (f32[32,768]{1,0:T(8,128)S(1)}, f32[32,768]{1,0:T(8,128)S(1)}, u32[]{:S(2)}, u32[]{:S(2)}) collective-permute-start(f32[32,768]{1,0:T(8,128)S(1)} %add_add_fusion.2), channel_id=1, source_target_pairs={{0,3},{1,2},{2,1},{3,0},{4,7},{5,6},{6,5},{7,4},{8,11},{9,10},{10,... | collective-permute-start | bytes 294920 | tf_op jit(solution)/shard_map/ppermute | solution.py:54
  92.2 8.7 %collective-permute-start.16 = (f32[32,768]{1,0:T(8,128)S(1)}, f32[32,768]{1,0:T(8,128)S(1)}, u32[]{:S(2)}, u32[]{:S(2)}) collective-permute-start(f32[32,768]{1,0:T(8,128)S(1)} %add_add_fusion.2), channel_id=1, source_target_pairs={{0,2},{1,3},{2,0},{3,1},{4,6},{5,7},{6,4},{7,5},{8,10},{9,11},{10,... | collective-permute-start | bytes 294920 | tf_op jit(solution)/shard_map/ppermute | solution.py:54
  93.9 7.0 %collective-permute-start.15 = (f32[32,768]{1,0:T(8,128)S(1)}, f32[32,768]{1,0:T(8,128)S(1)}, u32[]{:S(2)}, u32[]{:S(2)}) collective-permute-start(f32[32,768]{1,0:T(8,128)S(1)} %add_add_fusion.2), channel_id=1, source_target_pairs={{0,1},{1,0},{2,3},{3,2},{4,5},{5,4},{6,7},{7,6},{8,9},{9,8},{10,11... | collective-permute-start | bytes 294920 | tf_op jit(solution)/shard_map/ppermute | solution.py:54
  94.0 10.5 %collective-permute-start.24 = (f32[64,512]{1,0:T(8,128)S(1)}, f32[64,512]{1,0:T(8,128)S(1)}, u32[]{:S(2)}, u32[]{:S(2)}) collective-permute-start(f32[64,512]{1,0:T(8,128)S(1)} %add.52), channel_id=1, source_target_pairs={{0,24},{4,28},{8,16},{12,20},{16,8},{20,12},{24,0},{28,4},{1,25},{... | collective-permute-start | bytes 393224 | tf_op jit(solution)/shard_map/ppermute | solution.py:54
  95.2 9.3 %collective-permute-start.23 = (f32[64,512]{1,0:T(8,128)S(1)}, f32[64,512]{1,0:T(8,128)S(1)}, u32[]{:S(2)}, u32[]{:S(2)}) collective-permute-start(f32[64,512]{1,0:T(8,128)S(1)} %add.52), channel_id=1, source_target_pairs={{0,16},{4,20},{8,24},{12,28},{16,0},{20,4},{24,8},{28,12},{1,17},{... | collective-permute-start | bytes 393224 | tf_op jit(solution)/shard_map/ppermute | solution.py:54
  97.0 6.3 %collective-permute-start.22 = (f32[64,512]{1,0:T(8,128)S(1)}, f32[64,512]{1,0:T(8,128)S(1)}, u32[]{:S(2)}, u32[]{:S(2)}) collective-permute-start(f32[64,512]{1,0:T(8,128)S(1)} %add.52), channel_id=1, source_target_pairs={{0,8},{4,12},{8,0},{12,4},{16,24},{20,28},{24,16},{28,20},{1,9},{5... | collective-permute-start | bytes 393224 | tf_op jit(solution)/shard_map/ppermute | solution.py:54
  101.0 5.7 %collective-permute-start.20 = (f32[32,768]{1,0:T(8,128)S(1)}, f32[32,768]{1,0:T(8,128)S(1)}, u32[]{:S(2)}, u32[]{:S(2)}) collective-permute-start(f32[32,768]{1,0:T(8,128)S(1)} %add_add_fusion.1), channel_id=1, source_target_pairs={{0,24},{4,28},{8,16},{12,20},{16,8},{20,12},{24,0},{28,4},{1,25},{... | collective-permute-start | bytes 294920 | tf_op jit(solution)/shard_map/ppermute | solution.py:54
  103.3 5.4 %collective-permute-start.19 = (f32[32,768]{1,0:T(8,128)S(1)}, f32[32,768]{1,0:T(8,128)S(1)}, u32[]{:S(2)}, u32[]{:S(2)}) collective-permute-start(f32[32,768]{1,0:T(8,128)S(1)} %add_add_fusion.1), channel_id=1, source_target_pairs={{0,16},{4,20},{8,24},{12,28},{16,0},{20,4},{24,8},{28,12},{1,17},{... | collective-permute-start | bytes 294920 | tf_op jit(solution)/shard_map/ppermute | solution.py:54
  103.3 5.3 %collective-permute-start.18 = (f32[32,768]{1,0:T(8,128)S(1)}, f32[32,768]{1,0:T(8,128)S(1)}, u32[]{:S(2)}, u32[]{:S(2)}) collective-permute-start(f32[32,768]{1,0:T(8,128)S(1)} %add_add_fusion.1), channel_id=1, source_target_pairs={{0,8},{4,12},{8,0},{12,4},{16,24},{20,28},{24,16},{28,20},{1,9},{5... | collective-permute-start | bytes 294920 | tf_op jit(solution)/shard_map/ppermute | solution.py:54
  104.6 5.9 %collective-permute-start.25 = (f32[256,512]{1,0:T(8,128)S(1)}, f32[256,512]{1,0:T(8,128)S(1)}, u32[]{:S(2)}, u32[]{:S(2)}) collective-permute-start(f32[256,512]{1,0:T(8,128)S(1)} %constant_dynamic-update-slice_fusion.gram_ref), channel_id=1, source_target_pairs={{0,4},{4,0},{8,12},{12,8},{16,20},{20,16},{24,28},{28,24},{1,5},{5... | collective-permute-start | bytes 1572872 | tf_op jit(solution)/shard_map/ppermute | solution.py:54
  108.7 1.8 %collective-permute-start.21 = (f32[128,768]{1,0:T(8,128)S(1)}, f32[128,768]{1,0:T(8,128)S(1)}, u32[]{:S(2)}, u32[]{:S(2)}) collective-permute-start(f32[128,768]{1,0:T(8,128)S(1)} %pad_maximum_fusion.sums_ref), channel_id=1, source_target_pairs={{0,4},{4,0},{8,12},{12,8},{16,20},{20,16},{24,28},{28,24},{1,5},{5... | collective-permute-start | bytes 1179656 | tf_op jit(solution)/shard_map/ppermute | solution.py:54

commit v11 on v9

--- a/solution.py
+++ b/solution.py
@@ -76,7 +76,7 @@
         grid=(1,),
         in_specs=[pl.BlockSpec((lines, width), lambda i: (0, 0)), low, low, high, high],
         out_specs=[edge, edge],
-        out_shape=[pltpu.HBM((2 * w + 1, members, width), jnp.float32)] * 2,
+        out_shape=[shape(2 * w + 1, members, width)] * 2,
         compiler_params=params(6),
         name="edges",
     )(in_hbm(stiff), in_hbm(disp), in_hbm(vel), in_hbm(disp), in_hbm(vel))
@@ -173,7 +173,18 @@
     )()
 
 
-def basis_kernel(index_ref, rot_ref, basis_ref, send_ref, keep_ref, high_ref, low_ref, turned_ref, sum_ref, mixed_ref):
+def tiles_of(rank):
+    pairs = [(i, j) for i in range(rank // 128) for j in range(i, rank // 128)]
+    return [(slice(128 * i, 128 * i + 128), slice(128 * j, 128 * j + 128),
+             slice(128 * (t // 2), 128 * (t // 2) + 128), slice(128 * (t % 2), 128 * (t % 2) + 128))
+            for t, (i, j) in enumerate(pairs)]
+
+
+def packed_rows(rank):
+    return len(tiles_of(rank)) * 64
+
+
+def basis_kernel(index_ref, rot_ref, basis_ref, send_ref, keep_ref, high_ref, low_ref, turned_ref, sum_ref, mixed_ref, pack_ref):
     lines, width, rank = basis_ref.shape
     step = pl.program_id(0)
 
@@ -194,23 +205,26 @@
         sum_ref[...] += mixed_ref[...] + mixed_ref[...].T
         half = keep_ref.shape[0]
         core = index_ref[1]
-        keep_ref[...] = sum_ref[pl.ds(pl.multiple_of(core * half, half), half), :]
-        send_ref[...] = sum_ref[pl.ds(pl.multiple_of((1 - core) * half, half), half), :]
+        for row, col, to_row, to_col in tiles_of(rank):
+            pack_ref[to_row, to_col] = sum_ref[row, col]
+        keep_ref[...] = pack_ref[pl.ds(pl.multiple_of(core * half, 8), half), :]
+        send_ref[...] = pack_ref[pl.ds(pl.multiple_of((1 - core) * half, 8), half), :]
 
 
 def basis_parts(index, basis, rotation):
     lines, width, rank = basis.shape
     block = 4
-    half = pl.BlockSpec((rank // 2, rank), lambda i: (0, 0))
+    packed = packed_rows(rank)
+    half = pl.BlockSpec((packed // 2, 256), lambda i: (0, 0))
     rows = pl.BlockSpec((block * width, rank), lambda i: (i, 0))
     return pl.pallas_call(
         basis_kernel,
         grid=(lines // block,),
         in_specs=[SCALARS, pl.BlockSpec((rank, rank), lambda i: (0, 0)), pl.BlockSpec((block, width, rank), lambda i: (i, 0, 0))],
         out_specs=[half, half, rows, rows, rows],
-        out_shape=[shape(rank // 2, rank)] * 2 + [pltpu.HBM((lines * width, rank), jnp.bfloat16)] * 2
+        out_shape=[shape(packed // 2, 256)] * 2 + [pltpu.HBM((lines * width, rank), jnp.bfloat16)] * 2
         + [pltpu.HBM((lines * width, rank), jnp.float32)],
-        scratch_shapes=[pltpu.VMEM((rank, rank), jnp.float32)] * 2,
+        scratch_shapes=[pltpu.VMEM((rank, rank), jnp.float32)] * 2 + [pltpu.VMEM((packed, 256), jnp.float32)],
         compiler_params=params(24),
         name="basis_parts",
     )(index, in_hbm(rotation), in_hbm(basis))
@@ -268,7 +282,7 @@
 def split_kernel(index_ref, keep_ref, got_ref, *outs):
     rows = outs[0].shape[0]
     for k, out in enumerate(outs):
-        at = pl.ds(pl.multiple_of((index_ref[2] ^ k) * rows, rows), rows)
+        at = pl.ds(pl.multiple_of((index_ref[2] ^ k) * rows, 8), rows)
         out[...] = keep_ref[at, :] + got_ref[at, :]
 
 
@@ -378,13 +392,13 @@
     for k in range(chips):
         at = (index_ref[2] ^ k) * rows
         piece = slice(k * rows, (k + 1) * rows)
-        out_ref[pl.ds(pl.multiple_of(index_ref[1] * half + at, rows), rows), :] = mine_ref[piece, :]
-        out_ref[pl.ds(pl.multiple_of((1 - index_ref[1]) * half + at, rows), rows), :] = other_ref[piece, :]
+        out_ref[pl.ds(pl.multiple_of(index_ref[1] * half + at, 8), rows), :] = mine_ref[piece, :]
+        out_ref[pl.ds(pl.multiple_of((1 - index_ref[1]) * half + at, 8), rows), :] = other_ref[piece, :]
 
 
 def solve_kernel(index_ref, sums_ref, sums2_ref, gram_ref, gram2_ref, rot_ref, high_hbm, low_hbm, turned_hbm, *rest, count, chips, ranks):
     pieces, rest = rest[:ranks], rest[ranks:]
-    out_hbm, coords_ref, work_ref, all_ref, basis_ref, high_ref, low_ref, snap_ref, rem_high, rem_low, out_ref, sem, out_sem = rest
+    out_hbm, coords_ref, work_ref, all_ref, basis_ref, high_ref, low_ref, snap_ref, rem_high, rem_low, out_ref, pack_ref, sem, out_sem = rest
     rank, members = coords_ref.shape
     each = members // ranks
     copies = [pltpu.make_async_copy(high_hbm, high_ref, sem.at[0]), pltpu.make_async_copy(low_hbm, low_ref, sem.at[1])]
@@ -395,7 +409,12 @@
     for copy in copies + [turned]:
         copy.start()
     ordered(index_ref, sums_ref, sums2_ref, all_ref, chips)
-    ordered(index_ref, gram_ref, gram2_ref, basis_ref, chips)
+    ordered(index_ref, gram_ref, gram2_ref, pack_ref, chips)
+    for from_row, from_col, at_row, at_col in tiles_of(rank):
+        tile = pack_ref[at_row, at_col]
+        basis_ref[from_row, from_col] = tile
+        if from_row != from_col:
+            basis_ref[from_col, from_row] = tile.T
     row = lax.broadcasted_iota(jnp.int32, (members, members), 0)
     col = lax.broadcasted_iota(jnp.int32, (members, members), 1)
     eye = row == col
@@ -453,6 +472,7 @@
                         pltpu.VMEM((lines, members, width), jnp.float32),
                         pltpu.VMEM((rows, members), half), pltpu.VMEM((rows, members), half),
                         pltpu.VMEM((lines, width, rank), jnp.float32),
+                        pltpu.VMEM((packed_rows(rank), 256), jnp.float32),
                         pltpu.SemaphoreType.DMA((2 + ranks,)), pltpu.SemaphoreType.DMA],
         compiler_params=params(36),
         name="solve",
@@ -494,7 +514,7 @@
     bits = [2 ** i for i in range(ranks.bit_length() - 1)]
     empty = room(*[shape(lines * width, rank, dtype=t) for t in (jnp.bfloat16, jnp.bfloat16, jnp.float32)])
     order, gram, high, low, turned = lax.fori_loop(
-        0, 1 + (ana >> 20), meanwhile, (order, jnp.zeros((rank // sims, rank), jnp.float32), *empty))
+        0, 1 + (ana >> 20), meanwhile, (order, jnp.zeros((packed_rows(rank) // sims, 256), jnp.float32), *empty))
     gram = ana_sum_by_pairs(gram, bits[-1:])
 
     send, keep = products(order, high, low, pieces)

time: 126 us -> 130 us (1.032)
  waiting for transfers between devices: 38.9 us -> 45.2 us
  starting transfers between devices: 37 us -> 35.2 us
    ppermute x3, waiting for transfers between devices: 8.43 us -> 12.7 us  [per_device(): pieces[slot] = lax.ppermute(pieces[slot], ('sim', 'ana'), pairs)]
    ppermute x21, waiting for transfers between devices: 30.5 us -> 32.4 us  [xor_permute(): return lax.ppermute(value, axis, [(i, i ^ mask) for i in range(size)])]
    ppermute x21, starting transfers between devices: 28.3 us -> 26.5 us  [xor_permute(): return lax.ppermute(value, axis, [(i, i ^ mask) for i in range(size)])]
  transfers between devices with their start and end apart: 26 -> 26, of which waited for: 16 -> 16; matrix products, arithmetic and copies ran while one was open for 1% -> 1% of each run, Pallas kernels for 13% -> 12%
where the time goes in v11:
time: 130 us; the launch traced here: 129 us
  Pallas kernels  46.5 us (36%)
  waiting for transfers between devices  45.2 us (35%)
  starting transfers between devices  35.2 us (27%)
    ppermute x21, waiting for transfers between devices, xor_permute(): return lax.ppermute(value, axis, [(i, i ^ mask) for i in range(size)])  32.4 us
    ppermute x21, starting transfers between devices, xor_permute(): return lax.ppermute(value, axis, [(i, i ^ mask) for i in range(size)])  26.5 us
    pallas_call x1, Pallas kernels, solve(): pl.pallas_call(functools.partial(solve_kernel, count=float(count), chips=...  17 us
    ppermute x3, waiting for transfers between devices, per_device(): pieces[slot] = lax.ppermute(pieces[slot], ('sim', 'ana'), pairs)  12.7 us
    pallas_call x1, Pallas kernels, basis_parts(): pl.pallas_call(basis_kernel, grid=(lines // block,), in_specs=[SCALARS, p...  10.2 us
    pallas_call x1, Pallas kernels, evolve(): pl.pallas_call(functools.partial(evolve_kernel, slots=slots), in_specs=[S...  6.69 us
    pallas_call x1, Pallas kernels, products(): pl.pallas_call(products_kernel, grid=(lines // block,), in_specs=[SCALARS...  5.27 us
    ppermute x3, starting transfers between devices, per_device(): pieces[slot] = lax.ppermute(pieces[slot], ('sim', 'ana'), pairs)  5.06 us
  transfers between devices with their start and end apart: 26, of which 16 were waited for; matrix products, arithmetic and copies ran while one was open for 1% of the time, Pallas kernels for 12%

profile of v11, /device:TPU:0, one launch (start us, length us, event | category | flops | bytes accessed | tf_op | source)
XLA Modules:
  0.0 129.3 jit_solution(3736272331253176488)
XLA Ops:
  0.6 1.5 %edges.1 = (f32[9,64,128]{2,1,0:T(8,128)S(1)}, f32[9,64,128]{2,1,0:T(8,128)S(1)}) custom-call(f32[64,128]{1,0:T(8,128)} %stiff_ref.3, f32[64,64,128]{2,1,0:T(8,128)} %disp_high.1, f32[64,64,128]{2,1,0:T(8,128)} %vel_high.1, f32[64,64,128]{2,1,0:T(8,128)} %disp_high.1, f32[64,64,128]{2,1,0:T(8,128)} %vel_high.1), custom_call_target="tpu_custom_call" | custom-call | tf_op jit(solution)/shard_map/edges/pallas_call | solution.py:74
  2.1 2.4 %collective-permute-start.5 = (f32[9,64,128]{2,1,0:T(8,128)S(1)}, f32[9,64,128]{2,1,0:T(8,128)S(1)}, u32[]{:S(2)}, u32[]{:S(2)}) collective-permute-start(f32[9,64,128]{2,1,0:T(8,128)S(1)} %get-tuple-element.90), channel_id=1, source_target_pairs={{0,4},{4,8},{8,12},{12,16},{16,20},{20,24},{24,28},{1,5},{5,9},{9,... | collective-permute-start | bytes 884744 | tf_op jit(solution)/shard_map/ppermute | solution.py:497
  4.5 1.3 collective-permute-start.6
  5.9 4.6 %to_lines.1 = (f32[64,64,128]{2,1,0:T(8,128)S(1)}, f32[64,64,128]{2,1,0:T(8,128)S(1)}) custom-call(f32[4096,128]{1,0:T(8,128)} %bitcast.6, f32[4096,128]{1,0:T(8,128)} %bitcast.7), custom_call_target="tpu_custom_call" | custom-call | tf_op jit(solution)/shard_map/to_lines/pallas_call | solution.py:97
  10.6 6.7 %evolve.1 = (f32[16,64,128]{2,1,0:T(8,128)}, f32[16,64,128]{2,1,0:T(8,128)}, f32[16,64,128]{2,1,0:T(8,128)}, f32[16,64,128]{2,1,0:T(8,128)}) custom-call(s32[7]{0:T(128)S(1)} %pad_add_fusion.index_ref, f32[64,64,128]{2,1,0:T(8,128)S(1)} %get-tuple-element.95.disp_ref, f32[64,64,128]{2,1,0:T(8,128)S(1)} %get-tuple-element.96.vel_ref, ...), custom_call_target="tpu_custom_call" | custom-call | tf_op jit(solution)/shard_map/evolve/pallas_call | solution.py:155
  17.3 2.5 %collective-permute-start.7 = (f32[16,64,128]{2,1,0:T(8,128)}, f32[16,64,128]{2,1,0:T(8,128)S(1)}, u32[]{:S(2)}, u32[]{:S(2)}) collective-permute-start(f32[16,64,128]{2,1,0:T(8,128)} %get-tuple-element.110), channel_id=1, source_target_pairs={{0,1},{1,0},{2,3},{3,2},{4,7},{5,6},{6,5},{7,4},{8,9},{9,8},{10,11... | collective-permute-start | bytes 1572872 | tf_op jit(solution)/shard_map/ppermute | solution.py:507
  19.8 2.5 %collective-permute-start.8 = (f32[16,64,128]{2,1,0:T(8,128)}, f32[16,64,128]{2,1,0:T(8,128)S(1)}, u32[]{:S(2)}, u32[]{:S(2)}) collective-permute-start(f32[16,64,128]{2,1,0:T(8,128)} %get-tuple-element.111), channel_id=1, source_target_pairs={{0,3},{1,2},{2,1},{3,0},{4,6},{5,7},{6,4},{7,5},{8,11},{9,10},{10,... | collective-permute-start | bytes 1572872 | tf_op jit(solution)/shard_map/ppermute | solution.py:507
  22.3 0.1 collective-permute-start.9
  22.4 0.6 broadcast_in_dim.3
  23.0 31.3 %while.18 = (s32[]{:T(128)}, s32[7]{0:T(128)S(1)}, f32[80,256]{1,0:T(8,128)}, bf16[2048,512]{1,0:T(8,128)(2,1)}, bf16[2048,512]{1,0:T(8,128)(2,1)}, /*index=5*/f...) while((s32[]{:T(128)}, s32[7]{0:T(128)S(1)}, ...), condition=%wide.region_1.2_spmd, body=%wide.region_0.1_spmd.sunk | while | flops 81936 | bytes 3277157 | solution.py:516
  23.0 10.2 %basis_parts.1 = (f32[320,256]{1,0:T(8,128)S(1)}, f32[320,256]{1,0:T(8,128)S(1)}, bf16[2048,512]{1,0:T(8,128)(2,1)}, bf16[2048,512]{1,0:T(8,128)(2,1)}, f32[2048,512]{1,0:T(8,128)}) custom-call(s32[7]{0:T(128)S(1)} %get-tuple-element.223.index_ref, f32[768,512]{1,0:T(8,128)} %get-tuple-element.239.rot_ref, f32[16,128,512]{2,1,0:T(8,128)} %get-tuple-element.240.basis_ref), custom_call_target="tpu_custom_call" | custom-call | tf_op jit(solution)/shard_map/while/body/basis_parts/pallas_call | solution.py:220
  33.3 3.6 %collective-permute-start = (f32[320,256]{1,0:T(8,128)S(1)}, f32[320,256]{1,0:T(8,128)S(1)}, u32[]{:S(2)}, u32[]{:S(2)}) collective-permute-start(f32[320,256]{1,0:T(8,128)S(1)} %get-tuple-element.202), channel_id=1, source_target_pairs={{0,4},{4,0},{8,12},{12,8},{16,20},{20,16},{24,28},{28,24},{1,5},{5... | collective-permute-start | bytes 983048 | tf_op jit(solution)/shard_map/while/body/ppermute | solution.py:54
  36.9 1.3 collective-permute-done.got_ref
  38.2 0.6 split.3
  38.8 2.1 %collective-permute-start.2 = (f32[80,256]{1,0:T(8,128)S(1)}, f32[80,256]{1,0:T(8,128)S(1)}, u32[]{:S(2)}, u32[]{:S(2)}) collective-permute-start(f32[80,256]{1,0:T(8,128)S(1)} %get-tuple-element.205), channel_id=1, source_target_pairs={{0,8},{4,12},{8,0},{12,4},{16,24},{20,28},{24,16},{28,20},{1,9},{5... | collective-permute-start | bytes 245768 | tf_op jit(solution)/shard_map/while/body/ppermute | solution.py:54
  40.8 0.3 collective-permute-start.1
  41.1 2.7 %collective-permute-done.2 = f32[80,256]{1,0:T(8,128)S(1)} collective-permute-done((f32[80,256]{1,0:T(8,128)S(1)}, f32[80,256]{1,0:T(8,128)S(1)}, u32[]{:S(2)}, u32[]{:S(2)}) %collective-permute-start.2) | collective-permute-done | bytes 81952 | tf_op jit(solution)/shard_map/while/body/ppermute | solution.py:54
  43.8 1.2 collective-permute-start.3
  45.0 0.2 collective-permute-done.1
  45.3 3.9 %collective-permute-done.3 = f32[80,256]{1,0:T(8,128)S(1)} collective-permute-done((f32[80,256]{1,0:T(8,128)S(1)}, f32[80,256]{1,0:T(8,128)S(1)}, u32[]{:S(2)}, u32[]{:S(2)}) %collective-permute-start.3) | collective-permute-done | bytes 81952 | tf_op jit(solution)/shard_map/while/body/ppermute | solution.py:54
  49.1 1.5 %collective-permute-start.4 = (f32[80,256]{1,0:T(8,128)S(1)}, f32[80,256]{1,0:T(8,128)S(1)}, u32[]{:S(2)}, u32[]{:S(2)}) collective-permute-start(f32[80,256]{1,0:T(8,128)S(1)} %add_add_fusion.4), channel_id=1, source_target_pairs={{0,1},{1,0},{2,3},{3,2},{4,5},{5,4},{6,7},{7,6},{8,9},{9,8},{10,11... | collective-permute-start | bytes 245768 | tf_op jit(solution)/shard_map/while/body/ppermute | solution.py:54
  50.6 3.0 %collective-permute-done.4 = f32[80,256]{1,0:T(8,128)S(1)} collective-permute-done((f32[80,256]{1,0:T(8,128)S(1)}, f32[80,256]{1,0:T(8,128)S(1)}, u32[]{:S(2)}, u32[]{:S(2)}) %collective-permute-start.4) | collective-permute-done | bytes 81952 | tf_op jit(solution)/shard_map/while/body/ppermute | solution.py:54
  53.7 0.6 add.83
  54.3 12.7 %collective-permute-done.9.rest_2_ = f32[16,64,128]{2,1,0:T(8,128)S(1)} collective-permute-done((f32[16,64,128]{2,1,0:T(8,128)}, f32[16,64,128]{2,1,0:T(8,128)S(1)}, u32[]{:S(2)}, u32[]{:S(2)}) %collective-permute-start.9) | collective-permute-done | bytes 524320 | tf_op jit(solution)/shard_map/ppermute | solution.py:507
  67.0 5.3 %products.1 = (f32[128,768]{1,0:T(8,128)S(1)}, f32[128,768]{1,0:T(8,128)S(1)}) custom-call(s32[7]{0:T(128)S(1)} %get-tuple-element.107.index_ref, bf16[2048,512]{1,0:T(8,128)(2,1)} %get-tuple-element.108.high_ref.high_hbm, bf16[2048,512]{1,0:T(8,128)(2,1)} %get-tuple-element.109.low_ref.low_hbm, f32[16,64,128]{2,1,0:T(8,128)S(1)} %collective-permute-done.7.rest_0_, ...), custom_call_target="tpu_custom_call" | custom-call | tf_op jit(solution)/shard_map/products/pallas_call | solution.py:268
  72.3 2.0 %collective-permute-start.10 = (f32[128,768]{1,0:T(8,128)S(1)}, f32[128,768]{1,0:T(8,128)S(1)}, u32[]{:S(2)}, u32[]{:S(2)}) collective-permute-start(f32[128,768]{1,0:T(8,128)S(1)} %get-tuple-element.115), channel_id=1, source_target_pairs={{0,4},{4,0},{8,12},{12,8},{16,20},{20,16},{24,28},{28,24},{1,5},{5... | collective-permute-start | bytes 1179656 | tf_op jit(solution)/shard_map/ppermute | solution.py:54
  74.3 1.3 %collective-permute-done.10.got_ref = f32[128,768]{1,0:T(8,128)S(1)} collective-permute-done((f32[128,768]{1,0:T(8,128)S(1)}, f32[128,768]{1,0:T(8,128)S(1)}, u32[]{:S(2)}, u32[]{:S(2)}) %collective-permute-start.10) | collective-permute-done | bytes 393248 | tf_op jit(solution)/shard_map/ppermute | solution.py:54
  75.7 0.6 split.2
  76.3 4.6 %collective-permute-start.11 = (f32[32,768]{1,0:T(8,128)S(1)}, f32[32,768]{1,0:T(8,128)S(1)}, u32[]{:S(2)}, u32[]{:S(2)}) collective-permute-start(f32[32,768]{1,0:T(8,128)S(1)} %get-tuple-element.117), channel_id=1, source_target_pairs={{0,8},{4,12},{8,0},{12,4},{16,24},{20,28},{24,16},{28,20},{1,9},{5... | collective-permute-start | bytes 294920 | tf_op jit(solution)/shard_map/ppermute | solution.py:54
  80.8 1.5 %collective-permute-start.13 = (f32[32,768]{1,0:T(8,128)S(1)}, f32[32,768]{1,0:T(8,128)S(1)}, u32[]{:S(2)}, u32[]{:S(2)}) collective-permute-start(f32[32,768]{1,0:T(8,128)S(1)} %get-tuple-element.119), channel_id=1, source_target_pairs={{0,24},{4,28},{8,16},{12,20},{16,8},{20,12},{24,0},{28,4},{1,25},{... | collective-permute-start | bytes 294920 | tf_op jit(solution)/shard_map/ppermute | solution.py:54
  82.4 6.4 %collective-permute-done.14 = f32[80,256]{1,0:T(8,128)S(1)} collective-permute-done((f32[80,256]{1,0:T(8,128)S(1)}, f32[80,256]{1,0:T(8,128)S(1)}, u32[]{:S(2)}, u32[]{:S(2)}) %collective-permute-start.14) | collective-permute-done | bytes 81952 | tf_op jit(solution)/shard_map/ppermute | solution.py:54
  88.9 1.5 %collective-permute-start.24 = (f32[80,256]{1,0:T(8,128)S(1)}, f32[80,256]{1,0:T(8,128)S(1)}, u32[]{:S(2)}, u32[]{:S(2)}) collective-permute-start(f32[80,256]{1,0:T(8,128)S(1)} %add.52), channel_id=1, source_target_pairs={{0,24},{4,28},{8,16},{12,20},{16,8},{20,12},{24,0},{28,4},{1,25},{... | collective-permute-start | bytes 245768 | tf_op jit(solution)/shard_map/ppermute | solution.py:54
  90.3 1.7 %collective-permute-start.23 = (f32[80,256]{1,0:T(8,128)S(1)}, f32[80,256]{1,0:T(8,128)S(1)}, u32[]{:S(2)}, u32[]{:S(2)}) collective-permute-start(f32[80,256]{1,0:T(8,128)S(1)} %add.52), channel_id=1, source_target_pairs={{0,16},{4,20},{8,24},{12,28},{16,0},{20,4},{24,8},{28,12},{1,17},{... | collective-permute-start | bytes 245768 | tf_op jit(solution)/shard_map/ppermute | solution.py:54
  92.1 0.4 collective-permute-start.22
  92.4 1.6 %collective-permute-start.17 = (f32[32,768]{1,0:T(8,128)S(1)}, f32[32,768]{1,0:T(8,128)S(1)}, u32[]{:S(2)}, u32[]{:S(2)}) collective-permute-start(f32[32,768]{1,0:T(8,128)S(1)} %add_add_fusion.2), channel_id=1, source_target_pairs={{0,3},{1,2},{2,1},{3,0},{4,7},{5,6},{6,5},{7,4},{8,11},{9,10},{10,... | collective-permute-start | bytes 294920 | tf_op jit(solution)/shard_map/ppermute | solution.py:54
  94.0 2.5 %collective-permute-done.22 = f32[80,256]{1,0:T(8,128)S(1)} collective-permute-done((f32[80,256]{1,0:T(8,128)S(1)}, f32[80,256]{1,0:T(8,128)S(1)}, u32[]{:S(2)}, u32[]{:S(2)}) %collective-permute-start.22) | collective-permute-done | bytes 81952 | tf_op jit(solution)/shard_map/ppermute | solution.py:54
  96.5 0.4 collective-permute-start.15
  96.9 3.1 %collective-permute-done.17 = f32[32,768]{1,0:T(8,128)S(1)} collective-permute-done((f32[32,768]{1,0:T(8,128)S(1)}, f32[32,768]{1,0:T(8,128)S(1)}, u32[]{:S(2)}, u32[]{:S(2)}) %collective-permute-start.17) | collective-permute-done | bytes 98336 | tf_op jit(solution)/shard_map/ppermute | solution.py:54
  100.0 2.2 %collective-permute-done.16 = f32[32,768]{1,0:T(8,128)S(1)} collective-permute-done((f32[32,768]{1,0:T(8,128)S(1)}, f32[32,768]{1,0:T(8,128)S(1)}, u32[]{:S(2)}, u32[]{:S(2)}) %collective-permute-start.16) | collective-permute-done | bytes 98336 | tf_op jit(solution)/shard_map/ppermute | solution.py:54
  102.3 1.3 %collective-permute-start.20 = (f32[32,768]{1,0:T(8,128)S(1)}, f32[32,768]{1,0:T(8,128)S(1)}, u32[]{:S(2)}, u32[]{:S(2)}) collective-permute-start(f32[32,768]{1,0:T(8,128)S(1)} %add_add_fusion.1), channel_id=1, source_target_pairs={{0,24},{4,28},{8,16},{12,20},{16,8},{20,12},{24,0},{28,4},{1,25},{... | collective-permute-start | bytes 294920 | tf_op jit(solution)/shard_map/ppermute | solution.py:54
  103.6 1.7 %collective-permute-start.19 = (f32[32,768]{1,0:T(8,128)S(1)}, f32[32,768]{1,0:T(8,128)S(1)}, u32[]{:S(2)}, u32[]{:S(2)}) collective-permute-start(f32[32,768]{1,0:T(8,128)S(1)} %add_add_fusion.1), channel_id=1, source_target_pairs={{0,16},{4,20},{8,24},{12,28},{16,0},{20,4},{24,8},{28,12},{1,17},{... | collective-permute-start | bytes 294920 | tf_op jit(solution)/shard_map/ppermute | solution.py:54
  105.4 0.5 collective-permute-start.18
  105.9 2.9 %collective-permute-done.20 = f32[32,768]{1,0:T(8,128)S(1)} collective-permute-done((f32[32,768]{1,0:T(8,128)S(1)}, f32[32,768]{1,0:T(8,128)S(1)}, u32[]{:S(2)}, u32[]{:S(2)}) %collective-permute-start.20) | collective-permute-done | bytes 98336 | tf_op jit(solution)/shard_map/ppermute | solution.py:54
  108.8 0.9 collective-permute-done.19
  109.7 0.2 collective-permute-done.18
  110.1 0.5 collective-permute-start.25
  110.7 1.6 %collective-permute-done.25.gram2_ref = f32[320,256]{1,0:T(8,128)S(1)} collective-permute-done((f32[320,256]{1,0:T(8,128)S(1)}, f32[320,256]{1,0:T(8,128)S(1)}, u32[]{:S(2)}, u32[]{:S(2)}) %collective-permute-start.25) | collective-permute-done | bytes 327712 | tf_op jit(solution)/shard_map/ppermute | solution.py:54
  112.3 17.0 %solve.1 = (f32[16,128,512]{2,1,0:T(8,128)}, f32[512,256]{1,0:T(8,128)}) custom-call(s32[7]{0:T(128)S(1)} %pad_add_fusion.index_ref, f32[128,768]{1,0:T(8,128)S(1)} %pad_maximum_fusion.sums_ref, f32[128,768]{1,0:T(8,128)S(1)} %collective-permute-done.21.sums2_ref, f32[320,256]{1,0:T(8,128)S(1)} %constant_dynamic-update-slice_fusion.gram_ref, ...), custom_call_target="tpu_custom_call" | custom-call | tf_op jit(solution)/shard_map/solve/pallas_call | solution.py:463
  (45 shorter events, 0.4 us)
Async XLA Ops:
  2.1 8.5 %collective-permute-start.5 = (f32[9,64,128]{2,1,0:T(8,128)S(1)}, f32[9,64,128]{2,1,0:T(8,128)S(1)}, u32[]{:S(2)}, u32[]{:S(2)}) collective-permute-start(f32[9,64,128]{2,1,0:T(8,128)S(1)} %get-tuple-element.90), channel_id=1, source_target_pairs={{0,4},{4,8},{8,12},{12,16},{16,20},{20,24},{24,28},{1,5},{5,9},{9,... | collective-permute-start | bytes 884744 | tf_op jit(solution)/shard_map/ppermute | solution.py:497
  4.5 6.1 %collective-permute-start.6 = (f32[9,64,128]{2,1,0:T(8,128)S(1)}, f32[9,64,128]{2,1,0:T(8,128)S(1)}, u32[]{:S(2)}, u32[]{:S(2)}) collective-permute-start(f32[9,64,128]{2,1,0:T(8,128)S(1)} %get-tuple-element.91), channel_id=1, source_target_pairs={{4,0},{8,4},{12,8},{16,12},{20,16},{24,20},{28,24},{5,1},{9,5},{13... | collective-permute-start | bytes 884744 | tf_op jit(solution)/shard_map/ppermute | solution.py:498
  5.9 4.6 %copy-start.6 = (s32[4]{0:T(128)S(1)}, s32[4]{0:T(128)}, u32[]{:S(2)}) copy-start(s32[4]{0:T(128)} %constant.48.clone) | copy-start | bytes 52
  5.9 4.6 %copy-start.7 = (s32[4]{0:T(128)S(1)}, s32[4]{0:T(128)}, u32[]{:S(2)}) copy-start(s32[4]{0:T(128)} %constant.47.clone) | copy-start | bytes 52
  5.9 4.7 %copy-start.1 = (f32[64,128]{1,0:T(8,128)S(1)}, f32[64,128]{1,0:T(8,128)}, u32[]{:S(2)}) copy-start(f32[64,128]{1,0:T(8,128)} %stiff_ref.3) | copy-start | bytes 98308
  17.3 37.0 %collective-permute-start.7 = (f32[16,64,128]{2,1,0:T(8,128)}, f32[16,64,128]{2,1,0:T(8,128)S(1)}, u32[]{:S(2)}, u32[]{:S(2)}) collective-permute-start(f32[16,64,128]{2,1,0:T(8,128)} %get-tuple-element.110), channel_id=1, source_target_pairs={{0,1},{1,0},{2,3},{3,2},{4,7},{5,6},{6,5},{7,4},{8,9},{9,8},{10,11... | collective-permute-start | bytes 1572872 | tf_op jit(solution)/shard_map/ppermute | solution.py:507
  19.8 34.5 %collective-permute-start.8 = (f32[16,64,128]{2,1,0:T(8,128)}, f32[16,64,128]{2,1,0:T(8,128)S(1)}, u32[]{:S(2)}, u32[]{:S(2)}) collective-permute-start(f32[16,64,128]{2,1,0:T(8,128)} %get-tuple-element.111), channel_id=1, source_target_pairs={{0,3},{1,2},{2,1},{3,0},{4,6},{5,7},{6,4},{7,5},{8,11},{9,10},{10,... | collective-permute-start | bytes 1572872 | tf_op jit(solution)/shard_map/ppermute | solution.py:507
  22.3 44.7 %collective-permute-start.9 = (f32[16,64,128]{2,1,0:T(8,128)}, f32[16,64,128]{2,1,0:T(8,128)S(1)}, u32[]{:S(2)}, u32[]{:S(2)}) collective-permute-start(f32[16,64,128]{2,1,0:T(8,128)} %get-tuple-element.112), channel_id=1, source_target_pairs={{0,2},{1,3},{2,0},{3,1},{4,5},{5,4},{6,7},{7,6},{8,10},{9,11},{10,... | collective-permute-start | bytes 1572872 | tf_op jit(solution)/shard_map/ppermute | solution.py:507
  23.0 44.0 %copy-start = (f32[16,64,128]{2,1,0:T(8,128)S(1)}, f32[16,64,128]{2,1,0:T(8,128)}, u32[]{:S(2)}) copy-start(f32[16,64,128]{2,1,0:T(8,128)} %get-tuple-element.113.rest_3_) | copy-start | bytes 1572868
  33.3 4.9 %collective-permute-start = (f32[320,256]{1,0:T(8,128)S(1)}, f32[320,256]{1,0:T(8,128)S(1)}, u32[]{:S(2)}, u32[]{:S(2)}) collective-permute-start(f32[320,256]{1,0:T(8,128)S(1)} %get-tuple-element.202), channel_id=1, source_target_pairs={{0,4},{4,0},{8,12},{12,8},{16,20},{20,16},{24,28},{28,24},{1,5},{5... | collective-permute-start | bytes 983048 | tf_op jit(solution)/shard_map/while/body/ppermute | solution.py:54
  38.8 5.0 %collective-permute-start.2 = (f32[80,256]{1,0:T(8,128)S(1)}, f32[80,256]{1,0:T(8,128)S(1)}, u32[]{:S(2)}, u32[]{:S(2)}) collective-permute-start(f32[80,256]{1,0:T(8,128)S(1)} %get-tuple-element.205), channel_id=1, source_target_pairs={{0,8},{4,12},{8,0},{12,4},{16,24},{20,28},{24,16},{28,20},{1,9},{5... | collective-permute-start | bytes 245768 | tf_op jit(solution)/shard_map/while/body/ppermute | solution.py:54
  40.8 4.4 %collective-permute-start.1 = (f32[80,256]{1,0:T(8,128)S(1)}, f32[80,256]{1,0:T(8,128)S(1)}, u32[]{:S(2)}, u32[]{:S(2)}) collective-permute-start(f32[80,256]{1,0:T(8,128)S(1)} %get-tuple-element.203), channel_id=1, source_target_pairs={{0,16},{4,20},{8,24},{12,28},{16,0},{20,4},{24,8},{28,12},{1,17},{... | collective-permute-start | bytes 245768 | tf_op jit(solution)/shard_map/while/body/ppermute | solution.py:54
  43.8 5.3 %collective-permute-start.3 = (f32[80,256]{1,0:T(8,128)S(1)}, f32[80,256]{1,0:T(8,128)S(1)}, u32[]{:S(2)}, u32[]{:S(2)}) collective-permute-start(f32[80,256]{1,0:T(8,128)S(1)} %get-tuple-element.206), channel_id=1, source_target_pairs={{0,24},{4,28},{8,16},{12,20},{16,8},{20,12},{24,0},{28,4},{1,25},{... | collective-permute-start | bytes 245768 | tf_op jit(solution)/shard_map/while/body/ppermute | solution.py:54
  49.1 4.5 %collective-permute-start.4 = (f32[80,256]{1,0:T(8,128)S(1)}, f32[80,256]{1,0:T(8,128)S(1)}, u32[]{:S(2)}, u32[]{:S(2)}) collective-permute-start(f32[80,256]{1,0:T(8,128)S(1)} %add_add_fusion.4), channel_id=1, source_target_pairs={{0,1},{1,0},{2,3},{3,2},{4,5},{5,4},{6,7},{7,6},{8,9},{9,8},{10,11... | collective-permute-start | bytes 245768 | tf_op jit(solution)/shard_map/while/body/ppermute | solution.py:54
  67.0 15.4 %copy-start.5 = (f32[80,256]{1,0:T(8,128)S(1)}, f32[80,256]{1,0:T(8,128)}, u32[]{:S(2)}) copy-start(f32[80,256]{1,0:T(8,128)} %get-tuple-element.120) | copy-start | bytes 245764
  67.0 45.2 %copy-start.3 = (bf16[2048,512]{1,0:T(8,128)(2,1)S(1)}, bf16[2048,512]{1,0:T(8,128)(2,1)}, u32[]{:S(2)}) copy-start(bf16[2048,512]{1,0:T(8,128)(2,1)} %get-tuple-element.108.high_ref.high_hbm) | copy-start | bytes 6291460
  67.0 45.2 %copy-start.4 = (bf16[2048,512]{1,0:T(8,128)(2,1)S(1)}, bf16[2048,512]{1,0:T(8,128)(2,1)}, u32[]{:S(2)}) copy-start(bf16[2048,512]{1,0:T(8,128)(2,1)} %get-tuple-element.109.low_ref.low_hbm) | copy-start | bytes 6291460
  72.3 40.0 %copy-start.2 = (f32[768,512]{1,0:T(8,128)S(1)}, f32[768,512]{1,0:T(8,128)}, u32[]{:S(2)}) copy-start(f32[768,512]{1,0:T(8,128)} %get-tuple-element.263) | copy-start | bytes 4718596
  72.3 3.3 %collective-permute-start.10 = (f32[128,768]{1,0:T(8,128)S(1)}, f32[128,768]{1,0:T(8,128)S(1)}, u32[]{:S(2)}, u32[]{:S(2)}) collective-permute-start(f32[128,768]{1,0:T(8,128)S(1)} %get-tuple-element.115), channel_id=1, source_target_pairs={{0,4},{4,0},{8,12},{12,8},{16,20},{20,16},{24,28},{28,24},{1,5},{5... | collective-permute-start | bytes 1179656 | tf_op jit(solution)/shard_map/ppermute | solution.py:54
  76.3 12.6 %collective-permute-start.11 = (f32[32,768]{1,0:T(8,128)S(1)}, f32[32,768]{1,0:T(8,128)S(1)}, u32[]{:S(2)}, u32[]{:S(2)}) collective-permute-start(f32[32,768]{1,0:T(8,128)S(1)} %get-tuple-element.117), channel_id=1, source_target_pairs={{0,8},{4,12},{8,0},{12,4},{16,24},{20,28},{24,16},{28,20},{1,9},{5... | collective-permute-start | bytes 294920 | tf_op jit(solution)/shard_map/ppermute | solution.py:54
  80.8 8.0 %collective-permute-start.12 = (f32[32,768]{1,0:T(8,128)S(1)}, f32[32,768]{1,0:T(8,128)S(1)}, u32[]{:S(2)}, u32[]{:S(2)}) collective-permute-start(f32[32,768]{1,0:T(8,128)S(1)} %get-tuple-element.118), channel_id=1, source_target_pairs={{0,16},{4,20},{8,24},{12,28},{16,0},{20,4},{24,8},{28,12},{1,17},{... | collective-permute-start | bytes 294920 | tf_op jit(solution)/shard_map/ppermute | solution.py:54
  80.8 8.0 %collective-permute-start.13 = (f32[32,768]{1,0:T(8,128)S(1)}, f32[32,768]{1,0:T(8,128)S(1)}, u32[]{:S(2)}, u32[]{:S(2)}) collective-permute-start(f32[32,768]{1,0:T(8,128)S(1)} %get-tuple-element.119), channel_id=1, source_target_pairs={{0,24},{4,28},{8,16},{12,20},{16,8},{20,12},{24,0},{28,4},{1,25},{... | collective-permute-start | bytes 294920 | tf_op jit(solution)/shard_map/ppermute | solution.py:54
  82.4 6.4 %collective-permute-start.14 = (f32[80,256]{1,0:T(8,128)S(1)}, f32[80,256]{1,0:T(8,128)S(1)}, u32[]{:S(2)}, u32[]{:S(2)}) collective-permute-start(f32[80,256]{1,0:T(8,128)S(1)} %copy-done.5), channel_id=1, source_target_pairs={{0,2},{1,3},{2,0},{3,1},{4,6},{5,7},{6,4},{7,5},{8,10},{9,11},{10,... | collective-permute-start | bytes 245768 | tf_op jit(solution)/shard_map/ppermute | solution.py:54
  88.9 21.2 %collective-permute-start.24 = (f32[80,256]{1,0:T(8,128)S(1)}, f32[80,256]{1,0:T(8,128)S(1)}, u32[]{:S(2)}, u32[]{:S(2)}) collective-permute-start(f32[80,256]{1,0:T(8,128)S(1)} %add.52), channel_id=1, source_target_pairs={{0,24},{4,28},{8,16},{12,20},{16,8},{20,12},{24,0},{28,4},{1,25},{... | collective-permute-start | bytes 245768 | tf_op jit(solution)/shard_map/ppermute | solution.py:54
  90.3 15.5 %collective-permute-start.23 = (f32[80,256]{1,0:T(8,128)S(1)}, f32[80,256]{1,0:T(8,128)S(1)}, u32[]{:S(2)}, u32[]{:S(2)}) collective-permute-start(f32[80,256]{1,0:T(8,128)S(1)} %add.52), channel_id=1, source_target_pairs={{0,16},{4,20},{8,24},{12,28},{16,0},{20,4},{24,8},{28,12},{1,17},{... | collective-permute-start | bytes 245768 | tf_op jit(solution)/shard_map/ppermute | solution.py:54
  92.1 4.4 %collective-permute-start.22 = (f32[80,256]{1,0:T(8,128)S(1)}, f32[80,256]{1,0:T(8,128)S(1)}, u32[]{:S(2)}, u32[]{:S(2)}) collective-permute-start(f32[80,256]{1,0:T(8,128)S(1)} %add.52), channel_id=1, source_target_pairs={{0,8},{4,12},{8,0},{12,4},{16,24},{20,28},{24,16},{28,20},{1,9},{5... | collective-permute-start | bytes 245768 | tf_op jit(solution)/shard_map/ppermute | solution.py:54
  92.4 7.6 %collective-permute-start.17 = (f32[32,768]{1,0:T(8,128)S(1)}, f32[32,768]{1,0:T(8,128)S(1)}, u32[]{:S(2)}, u32[]{:S(2)}) collective-permute-start(f32[32,768]{1,0:T(8,128)S(1)} %add_add_fusion.2), channel_id=1, source_target_pairs={{0,3},{1,2},{2,1},{3,0},{4,7},{5,6},{6,5},{7,4},{8,11},{9,10},{10,... | collective-permute-start | bytes 294920 | tf_op jit(solution)/shard_map/ppermute | solution.py:54
  94.0 8.2 %collective-permute-start.16 = (f32[32,768]{1,0:T(8,128)S(1)}, f32[32,768]{1,0:T(8,128)S(1)}, u32[]{:S(2)}, u32[]{:S(2)}) collective-permute-start(f32[32,768]{1,0:T(8,128)S(1)} %add_add_fusion.2), channel_id=1, source_target_pairs={{0,2},{1,3},{2,0},{3,1},{4,6},{5,7},{6,4},{7,5},{8,10},{9,11},{10,... | collective-permute-start | bytes 294920 | tf_op jit(solution)/shard_map/ppermute | solution.py:54
  96.5 5.8 %collective-permute-start.15 = (f32[32,768]{1,0:T(8,128)S(1)}, f32[32,768]{1,0:T(8,128)S(1)}, u32[]{:S(2)}, u32[]{:S(2)}) collective-permute-start(f32[32,768]{1,0:T(8,128)S(1)} %add_add_fusion.2), channel_id=1, source_target_pairs={{0,1},{1,0},{2,3},{3,2},{4,5},{5,4},{6,7},{7,6},{8,9},{9,8},{10,11... | collective-permute-start | bytes 294920 | tf_op jit(solution)/shard_map/ppermute | solution.py:54
  102.3 6.5 %collective-permute-start.20 = (f32[32,768]{1,0:T(8,128)S(1)}, f32[32,768]{1,0:T(8,128)S(1)}, u32[]{:S(2)}, u32[]{:S(2)}) collective-permute-start(f32[32,768]{1,0:T(8,128)S(1)} %add_add_fusion.1), channel_id=1, source_target_pairs={{0,24},{4,28},{8,16},{12,20},{16,8},{20,12},{24,0},{28,4},{1,25},{... | collective-permute-start | bytes 294920 | tf_op jit(solution)/shard_map/ppermute | solution.py:54
  103.6 6.1 %collective-permute-start.19 = (f32[32,768]{1,0:T(8,128)S(1)}, f32[32,768]{1,0:T(8,128)S(1)}, u32[]{:S(2)}, u32[]{:S(2)}) collective-permute-start(f32[32,768]{1,0:T(8,128)S(1)} %add_add_fusion.1), channel_id=1, source_target_pairs={{0,16},{4,20},{8,24},{12,28},{16,0},{20,4},{24,8},{28,12},{1,17},{... | collective-permute-start | bytes 294920 | tf_op jit(solution)/shard_map/ppermute | solution.py:54
  105.4 4.6 %collective-permute-start.18 = (f32[32,768]{1,0:T(8,128)S(1)}, f32[32,768]{1,0:T(8,128)S(1)}, u32[]{:S(2)}, u32[]{:S(2)}) collective-permute-start(f32[32,768]{1,0:T(8,128)S(1)} %add_add_fusion.1), channel_id=1, source_target_pairs={{0,8},{4,12},{8,0},{12,4},{16,24},{20,28},{24,16},{28,20},{1,9},{5... | collective-permute-start | bytes 294920 | tf_op jit(solution)/shard_map/ppermute | solution.py:54
  110.0 2.3 %collective-permute-start.21 = (f32[128,768]{1,0:T(8,128)S(1)}, f32[128,768]{1,0:T(8,128)S(1)}, u32[]{:S(2)}, u32[]{:S(2)}) collective-permute-start(f32[128,768]{1,0:T(8,128)S(1)} %pad_maximum_fusion.sums_ref), channel_id=1, source_target_pairs={{0,4},{4,0},{8,12},{12,8},{16,20},{20,16},{24,28},{28,24},{1,5},{5... | collective-permute-start | bytes 1179656 | tf_op jit(solution)/shard_map/ppermute | solution.py:54
  110.1 2.2 %collective-permute-start.25 = (f32[320,256]{1,0:T(8,128)S(1)}, f32[320,256]{1,0:T(8,128)S(1)}, u32[]{:S(2)}, u32[]{:S(2)}) collective-permute-start(f32[320,256]{1,0:T(8,128)S(1)} %constant_dynamic-update-slice_fusion.gram_ref), channel_id=1, source_target_pairs={{0,4},{4,0},{8,12},{12,8},{16,20},{20,16},{24,28},{28,24},{1,5},{5... | collective-permute-start | bytes 983048 | tf_op jit(solution)/shard_map/ppermute | solution.py:54

commit v12 on v9

--- a/solution.py
+++ b/solution.py
@@ -76,7 +76,7 @@
         grid=(1,),
         in_specs=[pl.BlockSpec((lines, width), lambda i: (0, 0)), low, low, high, high],
         out_specs=[edge, edge],
-        out_shape=[pltpu.HBM((2 * w + 1, members, width), jnp.float32)] * 2,
+        out_shape=[shape(2 * w + 1, members, width)] * 2,
         compiler_params=params(6),
         name="edges",
     )(in_hbm(stiff), in_hbm(disp), in_hbm(vel), in_hbm(disp), in_hbm(vel))
@@ -466,9 +466,8 @@
     count = lines * width * sims * ranks
     chips = sims // 2
     core = sim % 2
-    near, far = list(range(1, ranks // 2)), list(range(ranks // 2, ranks))
-    orders = (near + far[::-1] + [0], far[::-1] + near + [0])
-    masks = jnp.where(core == 0, jnp.array(orders[0]), jnp.array(orders[1]))
+    slots = list(range(1, ranks)) + [0]
+    masks = jnp.array(slots)
     first_index = jnp.stack([ana, core, sim // 2])
     index = jnp.concatenate([first_index, masks]).astype(jnp.int32)
 
@@ -483,8 +482,7 @@
     pieces = list(evolve(index, disp, vel, stiffness, before, after, ranks))
     order, pieces = lax.optimization_barrier((index, pieces))
     for slot in range(ranks - 1):
-        pairs = [(s * ranks + a, s * ranks + (a ^ orders[s % 2][slot])) for s in range(sims) for a in range(ranks)]
-        pieces[slot] = lax.ppermute(pieces[slot], ("sim", "ana"), pairs)
+        pieces[slot] = xor_permute(pieces[slot], "ana", slots[slot])
 
     def meanwhile(_, carry):
         at, *_ = carry

time: 126 us -> 125 us (level)
  waiting for transfers between devices: 38.9 us -> 33.1 us
  starting transfers between devices: 37 us -> 42.2 us
    ppermute x21 -> x24, starting transfers between devices: 28.3 us -> 38.5 us  [xor_permute(): return lax.ppermute(value, axis, [(i, i ^ mask) for i in range(size)])]
    ppermute x3 -> x0, waiting for transfers between devices: 8.43 us -> none  [per_device(): pieces[slot] = lax.ppermute(pieces[slot], ('sim', 'ana'), pairs)]
    ppermute x3 -> x0, starting transfers between devices: 5.06 us -> none  [per_device(): pieces[slot] = lax.ppermute(pieces[slot], ('sim', 'ana'), pairs)]
    ppermute x21 -> x24, waiting for transfers between devices: 30.5 us -> 33 us  [xor_permute(): return lax.ppermute(value, axis, [(i, i ^ mask) for i in range(size)])]
  transfers between devices with their start and end apart: 26 -> 26, of which waited for: 16 -> 13; matrix products, arithmetic and copies ran while one was open for 1% -> 1% of each run, Pallas kernels for 13% -> 13%
where the time goes in v12:
time: 125 us
  Pallas kernels  46.7 us (37%)
  starting transfers between devices  42.2 us (34%)
  waiting for transfers between devices  33.1 us (26%)
    ppermute x24, starting transfers between devices, xor_permute(): return lax.ppermute(value, axis, [(i, i ^ mask) for i in range(size)])  38.5 us
    ppermute x24, waiting for transfers between devices, xor_permute(): return lax.ppermute(value, axis, [(i, i ^ mask) for i in range(size)])  33 us
    pallas_call x1, Pallas kernels, solve(): pl.pallas_call(functools.partial(solve_kernel, count=float(count), chips=...  17.2 us
    pallas_call x1, Pallas kernels, basis_parts(): pl.pallas_call(basis_kernel, grid=(lines // block,), in_specs=[SCALARS, p...  10.3 us
    pallas_call x1, Pallas kernels, evolve(): pl.pallas_call(functools.partial(evolve_kernel, slots=slots), in_specs=[S...  6.67 us
    pallas_call x1, Pallas kernels, products(): pl.pallas_call(products_kernel, grid=(lines // block,), in_specs=[SCALARS...  5.27 us
    pallas_call x1, Pallas kernels, to_lines(): pl.pallas_call(to_lines_kernel, grid=(members // group,), in_specs=[flat,...  4.58 us
  transfers between devices with their start and end apart: 26, of which 13 were waited for; matrix products, arithmetic and copies ran while one was open for 1% of the time, Pallas kernels for 13%

profile of v12, /device:TPU:0, one launch (start us, length us, event | category | flops | bytes accessed | tf_op | source)
XLA Modules:
  0.0 124.5 jit_solution(3319540545779744771)
XLA Ops:
  0.6 1.5 %edges.1 = (f32[9,64,128]{2,1,0:T(8,128)S(1)}, f32[9,64,128]{2,1,0:T(8,128)S(1)}) custom-call(f32[64,128]{1,0:T(8,128)} %stiff_ref.3, f32[64,64,128]{2,1,0:T(8,128)} %disp_high.1, f32[64,64,128]{2,1,0:T(8,128)} %vel_high.1, f32[64,64,128]{2,1,0:T(8,128)} %disp_high.1, f32[64,64,128]{2,1,0:T(8,128)} %vel_high.1), custom_call_target="tpu_custom_call" | custom-call | tf_op jit(solution)/shard_map/edges/pallas_call | solution.py:74
  2.1 2.4 %collective-permute-start.5 = (f32[9,64,128]{2,1,0:T(8,128)S(1)}, f32[9,64,128]{2,1,0:T(8,128)S(1)}, u32[]{:S(2)}, u32[]{:S(2)}) collective-permute-start(f32[9,64,128]{2,1,0:T(8,128)S(1)} %get-tuple-element.90), channel_id=1, source_target_pairs={{0,4},{4,8},{8,12},{12,16},{16,20},{20,24},{24,28},{1,5},{5,9},{9,... | collective-permute-start | bytes 884744 | tf_op jit(solution)/shard_map/ppermute | solution.py:476
  4.5 1.3 %collective-permute-start.6 = (f32[9,64,128]{2,1,0:T(8,128)S(1)}, f32[9,64,128]{2,1,0:T(8,128)S(1)}, u32[]{:S(2)}, u32[]{:S(2)}) collective-permute-start(f32[9,64,128]{2,1,0:T(8,128)S(1)} %get-tuple-element.91), channel_id=1, source_target_pairs={{4,0},{8,4},{12,8},{16,12},{20,16},{24,20},{28,24},{5,1},{9,5},{13... | collective-permute-start | bytes 884744 | tf_op jit(solution)/shard_map/ppermute | solution.py:477
  5.9 4.6 %to_lines.1 = (f32[64,64,128]{2,1,0:T(8,128)S(1)}, f32[64,64,128]{2,1,0:T(8,128)S(1)}) custom-call(f32[4096,128]{1,0:T(8,128)} %bitcast.6, f32[4096,128]{1,0:T(8,128)} %bitcast.7), custom_call_target="tpu_custom_call" | custom-call | tf_op jit(solution)/shard_map/to_lines/pallas_call | solution.py:97
  10.5 0.1 pad_add_fusion.index_ref
  10.6 6.7 %evolve.1 = (f32[16,64,128]{2,1,0:T(8,128)}, f32[16,64,128]{2,1,0:T(8,128)}, f32[16,64,128]{2,1,0:T(8,128)}, f32[16,64,128]{2,1,0:T(8,128)}) custom-call(s32[7]{0:T(128)S(1)} %pad_add_fusion.index_ref, f32[64,64,128]{2,1,0:T(8,128)S(1)} %get-tuple-element.95.disp_ref, f32[64,64,128]{2,1,0:T(8,128)S(1)} %get-tuple-element.96.vel_ref, ...), custom_call_target="tpu_custom_call" | custom-call | tf_op jit(solution)/shard_map/evolve/pallas_call | solution.py:155
  17.3 2.5 %collective-permute-start.7 = (f32[16,64,128]{2,1,0:T(8,128)}, f32[16,64,128]{2,1,0:T(8,128)S(1)}, u32[]{:S(2)}, u32[]{:S(2)}) collective-permute-start(f32[16,64,128]{2,1,0:T(8,128)} %get-tuple-element.110), channel_id=1, source_target_pairs={{0,1},{1,0},{2,3},{3,2},{4,5},{5,4},{6,7},{7,6},{8,9},{9,8},{10,11... | collective-permute-start | bytes 1572872 | tf_op jit(solution)/shard_map/ppermute | solution.py:54
  19.8 2.6 %collective-permute-start.8 = (f32[16,64,128]{2,1,0:T(8,128)}, f32[16,64,128]{2,1,0:T(8,128)S(1)}, u32[]{:S(2)}, u32[]{:S(2)}) collective-permute-start(f32[16,64,128]{2,1,0:T(8,128)} %get-tuple-element.111), channel_id=1, source_target_pairs={{0,2},{1,3},{2,0},{3,1},{4,6},{5,7},{6,4},{7,5},{8,10},{9,11},{10,... | collective-permute-start | bytes 1572872 | tf_op jit(solution)/shard_map/ppermute | solution.py:54
  22.3 0.7 broadcast_in_dim.3
  23.0 39.9 %while.18 = (s32[]{:T(128)}, s32[7]{0:T(128)S(1)}, f32[64,512]{1,0:T(8,128)}, bf16[2048,512]{1,0:T(8,128)(2,1)}, bf16[2048,512]{1,0:T(8,128)(2,1)}, /*index=5*/f...) while((s32[]{:T(128)}, s32[7]{0:T(128)S(1)}, ...), condition=%wide.region_1.2_spmd, body=%wide.region_0.1_spmd.sunk | while | flops 131088 | bytes 5243237 | solution.py:494
  23.0 10.3 %basis_parts.1 = (f32[256,512]{1,0:T(8,128)S(1)}, f32[256,512]{1,0:T(8,128)S(1)}, bf16[2048,512]{1,0:T(8,128)(2,1)}, bf16[2048,512]{1,0:T(8,128)(2,1)}, f32[2048,512]{1,0:T(8,128)}) custom-call(s32[7]{0:T(128)S(1)} %get-tuple-element.223.index_ref, f32[768,512]{1,0:T(8,128)} %get-tuple-element.239.rot_ref, f32[16,128,512]{2,1,0:T(8,128)} %get-tuple-element.240.basis_ref), custom_call_target="tpu_custom_call" | custom-call | tf_op jit(solution)/shard_map/while/body/basis_parts/pallas_call | solution.py:206
  33.3 3.6 %collective-permute-start = (f32[256,512]{1,0:T(8,128)S(1)}, f32[256,512]{1,0:T(8,128)S(1)}, u32[]{:S(2)}, u32[]{:S(2)}) collective-permute-start(f32[256,512]{1,0:T(8,128)S(1)} %get-tuple-element.202), channel_id=1, source_target_pairs={{0,4},{4,0},{8,12},{12,8},{16,20},{20,16},{24,28},{28,24},{1,5},{5... | collective-permute-start | bytes 1572872 | tf_op jit(solution)/shard_map/while/body/ppermute | solution.py:54
  36.9 1.5 %collective-permute-done.got_ref = f32[256,512]{1,0:T(8,128)S(1)} collective-permute-done((f32[256,512]{1,0:T(8,128)S(1)}, f32[256,512]{1,0:T(8,128)S(1)}, u32[]{:S(2)}, u32[]{:S(2)}) %collective-permute-start) | collective-permute-done | bytes 524320 | tf_op jit(solution)/shard_map/while/body/ppermute | solution.py:54
  38.4 0.6 split.3
  39.0 2.1 %collective-permute-start.2 = (f32[64,512]{1,0:T(8,128)S(1)}, f32[64,512]{1,0:T(8,128)S(1)}, u32[]{:S(2)}, u32[]{:S(2)}) collective-permute-start(f32[64,512]{1,0:T(8,128)S(1)} %get-tuple-element.205), channel_id=1, source_target_pairs={{0,8},{4,12},{8,0},{12,4},{16,24},{20,28},{24,16},{28,20},{1,9},{5... | collective-permute-start | bytes 393224 | tf_op jit(solution)/shard_map/while/body/ppermute | solution.py:54
  41.1 0.5 collective-permute-start.1
  41.6 3.5 %collective-permute-done.2 = f32[64,512]{1,0:T(8,128)S(1)} collective-permute-done((f32[64,512]{1,0:T(8,128)S(1)}, f32[64,512]{1,0:T(8,128)S(1)}, u32[]{:S(2)}, u32[]{:S(2)}) %collective-permute-start.2) | collective-permute-done | bytes 131104 | tf_op jit(solution)/shard_map/while/body/ppermute | solution.py:54
  45.1 1.5 %collective-permute-start.3 = (f32[64,512]{1,0:T(8,128)S(1)}, f32[64,512]{1,0:T(8,128)S(1)}, u32[]{:S(2)}, u32[]{:S(2)}) collective-permute-start(f32[64,512]{1,0:T(8,128)S(1)} %get-tuple-element.206), channel_id=1, source_target_pairs={{0,24},{4,28},{8,16},{12,20},{16,8},{20,12},{24,0},{28,4},{1,25},{... | collective-permute-start | bytes 393224 | tf_op jit(solution)/shard_map/while/body/ppermute | solution.py:54
  46.6 4.6 %collective-permute-done.3 = f32[64,512]{1,0:T(8,128)S(1)} collective-permute-done((f32[64,512]{1,0:T(8,128)S(1)}, f32[64,512]{1,0:T(8,128)S(1)}, u32[]{:S(2)}, u32[]{:S(2)}) %collective-permute-start.3) | collective-permute-done | bytes 131104 | tf_op jit(solution)/shard_map/while/body/ppermute | solution.py:54
  51.3 0.7 collective-permute-start.4
  52.0 10.3 %collective-permute-done.4 = f32[64,512]{1,0:T(8,128)S(1)} collective-permute-done((f32[64,512]{1,0:T(8,128)S(1)}, f32[64,512]{1,0:T(8,128)S(1)}, u32[]{:S(2)}, u32[]{:S(2)}) %collective-permute-start.4) | collective-permute-done | bytes 131104 | tf_op jit(solution)/shard_map/while/body/ppermute | solution.py:54
  62.3 0.7 add.83
  63.0 5.3 %products.1 = (f32[128,768]{1,0:T(8,128)S(1)}, f32[128,768]{1,0:T(8,128)S(1)}) custom-call(s32[7]{0:T(128)S(1)} %get-tuple-element.107.index_ref, bf16[2048,512]{1,0:T(8,128)(2,1)} %get-tuple-element.108.high_ref.high_hbm, bf16[2048,512]{1,0:T(8,128)(2,1)} %get-tuple-element.109.low_ref.low_hbm, f32[16,64,128]{2,1,0:T(8,128)S(1)} %collective-permute-done.7.rest_0_, ...), custom_call_target="tpu_custom_call" | custom-call | tf_op jit(solution)/shard_map/products/pallas_call | solution.py:254
  68.3 0.1 collective-permute-start.10
  68.4 7.8 %collective-permute-start.14 = (f32[64,512]{1,0:T(8,128)S(1)}, f32[64,512]{1,0:T(8,128)S(1)}, u32[]{:S(2)}, u32[]{:S(2)}) collective-permute-start(f32[64,512]{1,0:T(8,128)S(1)} %copy-done.5), channel_id=1, source_target_pairs={{0,2},{1,3},{2,0},{3,1},{4,6},{5,7},{6,4},{7,5},{8,10},{9,11},{10,... | collective-permute-start | bytes 393224 | tf_op jit(solution)/shard_map/ppermute | solution.py:54
  76.2 0.6 split.2
  76.8 4.1 %collective-permute-start.11 = (f32[32,768]{1,0:T(8,128)S(1)}, f32[32,768]{1,0:T(8,128)S(1)}, u32[]{:S(2)}, u32[]{:S(2)}) collective-permute-start(f32[32,768]{1,0:T(8,128)S(1)} %get-tuple-element.117), channel_id=1, source_target_pairs={{0,8},{4,12},{8,0},{12,4},{16,24},{20,28},{24,16},{28,20},{1,9},{5... | collective-permute-start | bytes 294920 | tf_op jit(solution)/shard_map/ppermute | solution.py:54
  80.9 0.3 collective-permute-start.12
  81.2 1.4 %collective-permute-start.13 = (f32[32,768]{1,0:T(8,128)S(1)}, f32[32,768]{1,0:T(8,128)S(1)}, u32[]{:S(2)}, u32[]{:S(2)}) collective-permute-start(f32[32,768]{1,0:T(8,128)S(1)} %get-tuple-element.119), channel_id=1, source_target_pairs={{0,24},{4,28},{8,16},{12,20},{16,8},{20,12},{24,0},{28,4},{1,25},{... | collective-permute-start | bytes 294920 | tf_op jit(solution)/shard_map/ppermute | solution.py:54
  82.6 0.1 collective-permute-done.14
  82.8 0.9 collective-permute-done.11
  83.7 2.6 %collective-permute-done.12 = f32[32,768]{1,0:T(8,128)S(1)} collective-permute-done((f32[32,768]{1,0:T(8,128)S(1)}, f32[32,768]{1,0:T(8,128)S(1)}, u32[]{:S(2)}, u32[]{:S(2)}) %collective-permute-start.12) | collective-permute-done | bytes 98336 | tf_op jit(solution)/shard_map/ppermute | solution.py:54
  86.3 1.3 %collective-permute-done.13 = f32[32,768]{1,0:T(8,128)S(1)} collective-permute-done((f32[32,768]{1,0:T(8,128)S(1)}, f32[32,768]{1,0:T(8,128)S(1)}, u32[]{:S(2)}, u32[]{:S(2)}) %collective-permute-start.13) | collective-permute-done | bytes 98336 | tf_op jit(solution)/shard_map/ppermute | solution.py:54
  87.7 1.4 %collective-permute-start.17 = (f32[32,768]{1,0:T(8,128)S(1)}, f32[32,768]{1,0:T(8,128)S(1)}, u32[]{:S(2)}, u32[]{:S(2)}) collective-permute-start(f32[32,768]{1,0:T(8,128)S(1)} %add_add_fusion.2), channel_id=1, source_target_pairs={{0,3},{1,2},{2,1},{3,0},{4,7},{5,6},{6,5},{7,4},{8,11},{9,10},{10,... | collective-permute-start | bytes 294920 | tf_op jit(solution)/shard_map/ppermute | solution.py:54
  89.1 0.7 collective-permute-start.16
  89.7 2.4 %collective-permute-start.15 = (f32[32,768]{1,0:T(8,128)S(1)}, f32[32,768]{1,0:T(8,128)S(1)}, u32[]{:S(2)}, u32[]{:S(2)}) collective-permute-start(f32[32,768]{1,0:T(8,128)S(1)} %add_add_fusion.2), channel_id=1, source_target_pairs={{0,1},{1,0},{2,3},{3,2},{4,5},{5,4},{6,7},{7,6},{8,9},{9,8},{10,11... | collective-permute-start | bytes 294920 | tf_op jit(solution)/shard_map/ppermute | solution.py:54
  92.1 1.7 %collective-permute-start.24 = (f32[64,512]{1,0:T(8,128)S(1)}, f32[64,512]{1,0:T(8,128)S(1)}, u32[]{:S(2)}, u32[]{:S(2)}) collective-permute-start(f32[64,512]{1,0:T(8,128)S(1)} %add.52), channel_id=1, source_target_pairs={{0,24},{4,28},{8,16},{12,20},{16,8},{20,12},{24,0},{28,4},{1,25},{... | collective-permute-start | bytes 393224 | tf_op jit(solution)/shard_map/ppermute | solution.py:54
  93.8 0.9 collective-permute-start.23
  94.7 0.6 collective-permute-done.17
  95.3 0.7 collective-permute-start.22
  95.9 2.7 %collective-permute-done.16 = f32[32,768]{1,0:T(8,128)S(1)} collective-permute-done((f32[32,768]{1,0:T(8,128)S(1)}, f32[32,768]{1,0:T(8,128)S(1)}, u32[]{:S(2)}, u32[]{:S(2)}) %collective-permute-start.16) | collective-permute-done | bytes 98336 | tf_op jit(solution)/shard_map/ppermute | solution.py:54
  98.7 1.2 collective-permute-start.20
  99.9 0.7 collective-permute-start.19
  100.6 1.7 %collective-permute-start.18 = (f32[32,768]{1,0:T(8,128)S(1)}, f32[32,768]{1,0:T(8,128)S(1)}, u32[]{:S(2)}, u32[]{:S(2)}) collective-permute-start(f32[32,768]{1,0:T(8,128)S(1)} %add_add_fusion.1), channel_id=1, source_target_pairs={{0,8},{4,12},{8,0},{12,4},{16,24},{20,28},{24,16},{28,20},{1,9},{5... | collective-permute-start | bytes 294920 | tf_op jit(solution)/shard_map/ppermute | solution.py:54
  102.4 2.4 %collective-permute-done.20 = f32[32,768]{1,0:T(8,128)S(1)} collective-permute-done((f32[32,768]{1,0:T(8,128)S(1)}, f32[32,768]{1,0:T(8,128)S(1)}, u32[]{:S(2)}, u32[]{:S(2)}) %collective-permute-start.20) | collective-permute-done | bytes 98336 | tf_op jit(solution)/shard_map/ppermute | solution.py:54
  104.8 0.7 collective-permute-done.19
  105.6 1.7 %collective-permute-done.21.sums2_ref = f32[128,768]{1,0:T(8,128)S(1)} collective-permute-done((f32[128,768]{1,0:T(8,128)S(1)}, f32[128,768]{1,0:T(8,128)S(1)}, u32[]{:S(2)}, u32[]{:S(2)}) %collective-permute-start.21) | collective-permute-done | bytes 393248 | tf_op jit(solution)/shard_map/ppermute | solution.py:54
  107.3 17.2 %solve.1 = (f32[16,128,512]{2,1,0:T(8,128)}, f32[512,256]{1,0:T(8,128)}) custom-call(s32[7]{0:T(128)S(1)} %pad_add_fusion.index_ref, f32[128,768]{1,0:T(8,128)S(1)} %pad_maximum_fusion.sums_ref, f32[128,768]{1,0:T(8,128)S(1)} %collective-permute-done.21.sums2_ref, f32[256,512]{1,0:T(8,128)S(1)} %constant_dynamic-update-slice_fusion.gram_ref, ...), custom_call_target="tpu_custom_call" | custom-call | tf_op jit(solution)/shard_map/solve/pallas_call | solution.py:444
  (42 shorter events, 0.4 us)
Async XLA Ops:
  2.1 8.4 %collective-permute-start.5 = (f32[9,64,128]{2,1,0:T(8,128)S(1)}, f32[9,64,128]{2,1,0:T(8,128)S(1)}, u32[]{:S(2)}, u32[]{:S(2)}) collective-permute-start(f32[9,64,128]{2,1,0:T(8,128)S(1)} %get-tuple-element.90), channel_id=1, source_target_pairs={{0,4},{4,8},{8,12},{12,16},{16,20},{20,24},{24,28},{1,5},{5,9},{9,... | collective-permute-start | bytes 884744 | tf_op jit(solution)/shard_map/ppermute | solution.py:476
  4.5 6.1 %collective-permute-start.6 = (f32[9,64,128]{2,1,0:T(8,128)S(1)}, f32[9,64,128]{2,1,0:T(8,128)S(1)}, u32[]{:S(2)}, u32[]{:S(2)}) collective-permute-start(f32[9,64,128]{2,1,0:T(8,128)S(1)} %get-tuple-element.91), channel_id=1, source_target_pairs={{4,0},{8,4},{12,8},{16,12},{20,16},{24,20},{28,24},{5,1},{9,5},{13... | collective-permute-start | bytes 884744 | tf_op jit(solution)/shard_map/ppermute | solution.py:477
  5.9 4.6 %copy-start.6 = (s32[4]{0:T(128)S(1)}, s32[4]{0:T(128)}, u32[]{:S(2)}) copy-start(s32[4]{0:T(128)} %constant.45.clone) | copy-start | bytes 52
  5.9 4.7 %copy-start.1 = (f32[64,128]{1,0:T(8,128)S(1)}, f32[64,128]{1,0:T(8,128)}, u32[]{:S(2)}) copy-start(f32[64,128]{1,0:T(8,128)} %stiff_ref.3) | copy-start | bytes 98308
  17.3 45.7 %collective-permute-start.7 = (f32[16,64,128]{2,1,0:T(8,128)}, f32[16,64,128]{2,1,0:T(8,128)S(1)}, u32[]{:S(2)}, u32[]{:S(2)}) collective-permute-start(f32[16,64,128]{2,1,0:T(8,128)} %get-tuple-element.110), channel_id=1, source_target_pairs={{0,1},{1,0},{2,3},{3,2},{4,5},{5,4},{6,7},{7,6},{8,9},{9,8},{10,11... | collective-permute-start | bytes 1572872 | tf_op jit(solution)/shard_map/ppermute | solution.py:54
  19.8 43.2 %collective-permute-start.8 = (f32[16,64,128]{2,1,0:T(8,128)}, f32[16,64,128]{2,1,0:T(8,128)S(1)}, u32[]{:S(2)}, u32[]{:S(2)}) collective-permute-start(f32[16,64,128]{2,1,0:T(8,128)} %get-tuple-element.111), channel_id=1, source_target_pairs={{0,2},{1,3},{2,0},{3,1},{4,6},{5,7},{6,4},{7,5},{8,10},{9,11},{10,... | collective-permute-start | bytes 1572872 | tf_op jit(solution)/shard_map/ppermute | solution.py:54
  22.3 40.6 %collective-permute-start.9 = (f32[16,64,128]{2,1,0:T(8,128)}, f32[16,64,128]{2,1,0:T(8,128)S(1)}, u32[]{:S(2)}, u32[]{:S(2)}) collective-permute-start(f32[16,64,128]{2,1,0:T(8,128)} %get-tuple-element.112), channel_id=1, source_target_pairs={{0,3},{1,2},{2,1},{3,0},{4,7},{5,6},{6,5},{7,4},{8,11},{9,10},{10,... | collective-permute-start | bytes 1572872 | tf_op jit(solution)/shard_map/ppermute | solution.py:54
  23.0 39.9 %copy-start = (f32[16,64,128]{2,1,0:T(8,128)S(1)}, f32[16,64,128]{2,1,0:T(8,128)}, u32[]{:S(2)}) copy-start(f32[16,64,128]{2,1,0:T(8,128)} %get-tuple-element.113.rest_3_) | copy-start | bytes 1572868
  33.3 5.1 %collective-permute-start = (f32[256,512]{1,0:T(8,128)S(1)}, f32[256,512]{1,0:T(8,128)S(1)}, u32[]{:S(2)}, u32[]{:S(2)}) collective-permute-start(f32[256,512]{1,0:T(8,128)S(1)} %get-tuple-element.202), channel_id=1, source_target_pairs={{0,4},{4,0},{8,12},{12,8},{16,20},{20,16},{24,28},{28,24},{1,5},{5... | collective-permute-start | bytes 1572872 | tf_op jit(solution)/shard_map/while/body/ppermute | solution.py:54
  39.0 6.1 %collective-permute-start.2 = (f32[64,512]{1,0:T(8,128)S(1)}, f32[64,512]{1,0:T(8,128)S(1)}, u32[]{:S(2)}, u32[]{:S(2)}) collective-permute-start(f32[64,512]{1,0:T(8,128)S(1)} %get-tuple-element.205), channel_id=1, source_target_pairs={{0,8},{4,12},{8,0},{12,4},{16,24},{20,28},{24,16},{28,20},{1,9},{5... | collective-permute-start | bytes 393224 | tf_op jit(solution)/shard_map/while/body/ppermute | solution.py:54
  41.1 5.5 %collective-permute-start.1 = (f32[64,512]{1,0:T(8,128)S(1)}, f32[64,512]{1,0:T(8,128)S(1)}, u32[]{:S(2)}, u32[]{:S(2)}) collective-permute-start(f32[64,512]{1,0:T(8,128)S(1)} %get-tuple-element.203), channel_id=1, source_target_pairs={{0,16},{4,20},{8,24},{12,28},{16,0},{20,4},{24,8},{28,12},{1,17},{... | collective-permute-start | bytes 393224 | tf_op jit(solution)/shard_map/while/body/ppermute | solution.py:54
  45.1 6.1 %collective-permute-start.3 = (f32[64,512]{1,0:T(8,128)S(1)}, f32[64,512]{1,0:T(8,128)S(1)}, u32[]{:S(2)}, u32[]{:S(2)}) collective-permute-start(f32[64,512]{1,0:T(8,128)S(1)} %get-tuple-element.206), channel_id=1, source_target_pairs={{0,24},{4,28},{8,16},{12,20},{16,8},{20,12},{24,0},{28,4},{1,25},{... | collective-permute-start | bytes 393224 | tf_op jit(solution)/shard_map/while/body/ppermute | solution.py:54
  51.3 11.0 %collective-permute-start.4 = (f32[64,512]{1,0:T(8,128)S(1)}, f32[64,512]{1,0:T(8,128)S(1)}, u32[]{:S(2)}, u32[]{:S(2)}) collective-permute-start(f32[64,512]{1,0:T(8,128)S(1)} %add_add_fusion.4), channel_id=1, source_target_pairs={{0,1},{1,0},{2,3},{3,2},{4,5},{5,4},{6,7},{7,6},{8,9},{9,8},{10,11... | collective-permute-start | bytes 393224 | tf_op jit(solution)/shard_map/while/body/ppermute | solution.py:54
  63.0 5.4 %copy-start.5 = (f32[64,512]{1,0:T(8,128)S(1)}, f32[64,512]{1,0:T(8,128)}, u32[]{:S(2)}) copy-start(f32[64,512]{1,0:T(8,128)} %get-tuple-element.120) | copy-start | bytes 393220
  63.0 44.3 %copy-start.4 = (bf16[2048,512]{1,0:T(8,128)(2,1)S(1)}, bf16[2048,512]{1,0:T(8,128)(2,1)}, u32[]{:S(2)}) copy-start(bf16[2048,512]{1,0:T(8,128)(2,1)} %get-tuple-element.109.low_ref.low_hbm) | copy-start | bytes 6291460
  68.3 39.1 %copy-start.2 = (f32[768,512]{1,0:T(8,128)S(1)}, f32[768,512]{1,0:T(8,128)}, u32[]{:S(2)}) copy-start(f32[768,512]{1,0:T(8,128)} %get-tuple-element.263) | copy-start | bytes 4718596
  68.3 39.1 %copy-start.3 = (bf16[2048,512]{1,0:T(8,128)(2,1)S(1)}, bf16[2048,512]{1,0:T(8,128)(2,1)}, u32[]{:S(2)}) copy-start(bf16[2048,512]{1,0:T(8,128)(2,1)} %get-tuple-element.108.high_ref.high_hbm) | copy-start | bytes 6291460
  68.3 7.9 %collective-permute-start.10 = (f32[128,768]{1,0:T(8,128)S(1)}, f32[128,768]{1,0:T(8,128)S(1)}, u32[]{:S(2)}, u32[]{:S(2)}) collective-permute-start(f32[128,768]{1,0:T(8,128)S(1)} %get-tuple-element.115), channel_id=1, source_target_pairs={{0,4},{4,0},{8,12},{12,8},{16,20},{20,16},{24,28},{28,24},{1,5},{5... | collective-permute-start | bytes 1179656 | tf_op jit(solution)/shard_map/ppermute | solution.py:54
  68.4 14.4 %collective-permute-start.14 = (f32[64,512]{1,0:T(8,128)S(1)}, f32[64,512]{1,0:T(8,128)S(1)}, u32[]{:S(2)}, u32[]{:S(2)}) collective-permute-start(f32[64,512]{1,0:T(8,128)S(1)} %copy-done.5), channel_id=1, source_target_pairs={{0,2},{1,3},{2,0},{3,1},{4,6},{5,7},{6,4},{7,5},{8,10},{9,11},{10,... | collective-permute-start | bytes 393224 | tf_op jit(solution)/shard_map/ppermute | solution.py:54
  76.8 6.9 %collective-permute-start.11 = (f32[32,768]{1,0:T(8,128)S(1)}, f32[32,768]{1,0:T(8,128)S(1)}, u32[]{:S(2)}, u32[]{:S(2)}) collective-permute-start(f32[32,768]{1,0:T(8,128)S(1)} %get-tuple-element.117), channel_id=1, source_target_pairs={{0,8},{4,12},{8,0},{12,4},{16,24},{20,28},{24,16},{28,20},{1,9},{5... | collective-permute-start | bytes 294920 | tf_op jit(solution)/shard_map/ppermute | solution.py:54
  80.9 5.4 %collective-permute-start.12 = (f32[32,768]{1,0:T(8,128)S(1)}, f32[32,768]{1,0:T(8,128)S(1)}, u32[]{:S(2)}, u32[]{:S(2)}) collective-permute-start(f32[32,768]{1,0:T(8,128)S(1)} %get-tuple-element.118), channel_id=1, source_target_pairs={{0,16},{4,20},{8,24},{12,28},{16,0},{20,4},{24,8},{28,12},{1,17},{... | collective-permute-start | bytes 294920 | tf_op jit(solution)/shard_map/ppermute | solution.py:54
  81.2 6.4 %collective-permute-start.13 = (f32[32,768]{1,0:T(8,128)S(1)}, f32[32,768]{1,0:T(8,128)S(1)}, u32[]{:S(2)}, u32[]{:S(2)}) collective-permute-start(f32[32,768]{1,0:T(8,128)S(1)} %get-tuple-element.119), channel_id=1, source_target_pairs={{0,24},{4,28},{8,16},{12,20},{16,8},{20,12},{24,0},{28,4},{1,25},{... | collective-permute-start | bytes 294920 | tf_op jit(solution)/shard_map/ppermute | solution.py:54
  87.7 7.6 %collective-permute-start.17 = (f32[32,768]{1,0:T(8,128)S(1)}, f32[32,768]{1,0:T(8,128)S(1)}, u32[]{:S(2)}, u32[]{:S(2)}) collective-permute-start(f32[32,768]{1,0:T(8,128)S(1)} %add_add_fusion.2), channel_id=1, source_target_pairs={{0,3},{1,2},{2,1},{3,0},{4,7},{5,6},{6,5},{7,4},{8,11},{9,10},{10,... | collective-permute-start | bytes 294920 | tf_op jit(solution)/shard_map/ppermute | solution.py:54
  89.1 9.6 %collective-permute-start.16 = (f32[32,768]{1,0:T(8,128)S(1)}, f32[32,768]{1,0:T(8,128)S(1)}, u32[]{:S(2)}, u32[]{:S(2)}) collective-permute-start(f32[32,768]{1,0:T(8,128)S(1)} %add_add_fusion.2), channel_id=1, source_target_pairs={{0,2},{1,3},{2,0},{3,1},{4,6},{5,7},{6,4},{7,5},{8,10},{9,11},{10,... | collective-permute-start | bytes 294920 | tf_op jit(solution)/shard_map/ppermute | solution.py:54
  89.7 8.9 %collective-permute-start.15 = (f32[32,768]{1,0:T(8,128)S(1)}, f32[32,768]{1,0:T(8,128)S(1)}, u32[]{:S(2)}, u32[]{:S(2)}) collective-permute-start(f32[32,768]{1,0:T(8,128)S(1)} %add_add_fusion.2), channel_id=1, source_target_pairs={{0,1},{1,0},{2,3},{3,2},{4,5},{5,4},{6,7},{7,6},{8,9},{9,8},{10,11... | collective-permute-start | bytes 294920 | tf_op jit(solution)/shard_map/ppermute | solution.py:54
  92.1 10.2 %collective-permute-start.24 = (f32[64,512]{1,0:T(8,128)S(1)}, f32[64,512]{1,0:T(8,128)S(1)}, u32[]{:S(2)}, u32[]{:S(2)}) collective-permute-start(f32[64,512]{1,0:T(8,128)S(1)} %add.52), channel_id=1, source_target_pairs={{0,24},{4,28},{8,16},{12,20},{16,8},{20,12},{24,0},{28,4},{1,25},{... | collective-permute-start | bytes 393224 | tf_op jit(solution)/shard_map/ppermute | solution.py:54
  93.8 8.5 %collective-permute-start.23 = (f32[64,512]{1,0:T(8,128)S(1)}, f32[64,512]{1,0:T(8,128)S(1)}, u32[]{:S(2)}, u32[]{:S(2)}) collective-permute-start(f32[64,512]{1,0:T(8,128)S(1)} %add.52), channel_id=1, source_target_pairs={{0,16},{4,20},{8,24},{12,28},{16,0},{20,4},{24,8},{28,12},{1,17},{... | collective-permute-start | bytes 393224 | tf_op jit(solution)/shard_map/ppermute | solution.py:54
  95.3 5.3 %collective-permute-start.22 = (f32[64,512]{1,0:T(8,128)S(1)}, f32[64,512]{1,0:T(8,128)S(1)}, u32[]{:S(2)}, u32[]{:S(2)}) collective-permute-start(f32[64,512]{1,0:T(8,128)S(1)} %add.52), channel_id=1, source_target_pairs={{0,8},{4,12},{8,0},{12,4},{16,24},{20,28},{24,16},{28,20},{1,9},{5... | collective-permute-start | bytes 393224 | tf_op jit(solution)/shard_map/ppermute | solution.py:54
  98.7 6.1 %collective-permute-start.20 = (f32[32,768]{1,0:T(8,128)S(1)}, f32[32,768]{1,0:T(8,128)S(1)}, u32[]{:S(2)}, u32[]{:S(2)}) collective-permute-start(f32[32,768]{1,0:T(8,128)S(1)} %add_add_fusion.1), channel_id=1, source_target_pairs={{0,24},{4,28},{8,16},{12,20},{16,8},{20,12},{24,0},{28,4},{1,25},{... | collective-permute-start | bytes 294920 | tf_op jit(solution)/shard_map/ppermute | solution.py:54
  99.9 5.6 %collective-permute-start.19 = (f32[32,768]{1,0:T(8,128)S(1)}, f32[32,768]{1,0:T(8,128)S(1)}, u32[]{:S(2)}, u32[]{:S(2)}) collective-permute-start(f32[32,768]{1,0:T(8,128)S(1)} %add_add_fusion.1), channel_id=1, source_target_pairs={{0,16},{4,20},{8,24},{12,28},{16,0},{20,4},{24,8},{28,12},{1,17},{... | collective-permute-start | bytes 294920 | tf_op jit(solution)/shard_map/ppermute | solution.py:54
  100.6 4.9 %collective-permute-start.18 = (f32[32,768]{1,0:T(8,128)S(1)}, f32[32,768]{1,0:T(8,128)S(1)}, u32[]{:S(2)}, u32[]{:S(2)}) collective-permute-start(f32[32,768]{1,0:T(8,128)S(1)} %add_add_fusion.1), channel_id=1, source_target_pairs={{0,8},{4,12},{8,0},{12,4},{16,24},{20,28},{24,16},{28,20},{1,9},{5... | collective-permute-start | bytes 294920 | tf_op jit(solution)/shard_map/ppermute | solution.py:54
  102.3 5.0 %collective-permute-start.25 = (f32[256,512]{1,0:T(8,128)S(1)}, f32[256,512]{1,0:T(8,128)S(1)}, u32[]{:S(2)}, u32[]{:S(2)}) collective-permute-start(f32[256,512]{1,0:T(8,128)S(1)} %constant_dynamic-update-slice_fusion.gram_ref), channel_id=1, source_target_pairs={{0,4},{4,0},{8,12},{12,8},{16,20},{20,16},{24,28},{28,24},{1,5},{5... | collective-permute-start | bytes 1572872 | tf_op jit(solution)/shard_map/ppermute | solution.py:54
  105.5 1.8 %collective-permute-start.21 = (f32[128,768]{1,0:T(8,128)S(1)}, f32[128,768]{1,0:T(8,128)S(1)}, u32[]{:S(2)}, u32[]{:S(2)}) collective-permute-start(f32[128,768]{1,0:T(8,128)S(1)} %pad_maximum_fusion.sums_ref), channel_id=1, source_target_pairs={{0,4},{4,0},{8,12},{12,8},{16,20},{20,16},{24,28},{28,24},{1,5},{5... | collective-permute-start | bytes 1179656 | tf_op jit(solution)/shard_map/ppermute | solution.py:54

commit v13 on v12

--- a/solution.py
+++ b/solution.py
@@ -58,11 +58,13 @@
     w = STEPS
     lines = stiff_ref.shape[0]
     for ref, disp, vel, at, start in ((last_ref, disp_high, vel_high, 8 - w, lines - w), (first_ref, disp_low, vel_low, 0, 0)):
+        skip = 1 if ref is last_ref else 0
         for i in range(w):
             ref[i] = disp[:, at + i, :]
-            ref[w + i] = vel[:, at + i, :]
-        ref[2 * w] = jnp.zeros_like(ref[2 * w])
-        ref[2 * w, :w, :] = stiff_ref[start:start + w, :]
+        for i in range(w - 1):
+            ref[w + i] = vel[:, at + skip + i, :]
+        ref[2 * w - 1] = jnp.zeros_like(ref[2 * w - 1])
+        ref[2 * w - 1, :w, :] = stiff_ref[start:start + w, :]
 
 
 def edges(disp, vel, stiff):
@@ -70,13 +72,13 @@
     w = STEPS
     low = pl.BlockSpec((members, 8, width), lambda i: (0, 0, 0))
     high = pl.BlockSpec((members, 8, width), lambda i: (0, lines // 8 - 1, 0))
-    edge = pl.BlockSpec((2 * w + 1, members, width), lambda i: (0, 0, 0))
+    edge = pl.BlockSpec((2 * w, members, width), lambda i: (0, 0, 0))
     return pl.pallas_call(
         edges_kernel,
         grid=(1,),
         in_specs=[pl.BlockSpec((lines, width), lambda i: (0, 0)), low, low, high, high],
         out_specs=[edge, edge],
-        out_shape=[shape(2 * w + 1, members, width)] * 2,
+        out_shape=[shape(2 * w, members, width)] * 2,
         compiler_params=params(6),
         name="edges",
     )(in_hbm(stiff), in_hbm(disp), in_hbm(vel), in_hbm(disp), in_hbm(vel))
@@ -112,15 +114,16 @@
     full = lines + 2 * w
     size = lines // slots
     lane = lax.broadcasted_iota(jnp.int32, (8, width), 1)
-    pad_ref[w:2 * w, :] = before_ref[2 * w, :w, :]
+    pad_ref[w:2 * w, :] = before_ref[2 * w - 1, :w, :]
     pad_ref[8:8 + lines, :] = stiff_ref[...]
-    pad_ref[8 + lines:8 + lines + w, :] = after_ref[2 * w, :w, :]
+    pad_ref[8 + lines:8 + lines + w, :] = after_ref[2 * w - 1, :w, :]
 
     def group_step(g, carry):
         at = pl.ds(pl.multiple_of(g * 8, 8), 8)
         for i in range(w):
-            even_ref[i], speed_ref[i] = before_ref[i, at, :], before_ref[w + i, at, :]
-            even_ref[w + lines + i], speed_ref[w + lines + i] = after_ref[i, at, :], after_ref[w + i, at, :]
+            even_ref[i], even_ref[w + lines + i] = before_ref[i, at, :], after_ref[i, at, :]
+        for i in range(w - 1):
+            speed_ref[1 + i], speed_ref[w + lines + i] = before_ref[w + i, at, :], after_ref[w + i, at, :]
         for i in range(lines):
             even_ref[w + i], speed_ref[w + i] = disp_ref[i, at, :], vel_ref[i, at, :]
         now, then = even_ref, odd_ref
@@ -249,7 +252,7 @@
     rank = high.shape[1]
     lines, members, width = pieces[0].shape
     total = members * len(pieces)
-    block = 4
+    block = 8
     half = pl.BlockSpec((total // 2, rank + total), lambda i: (0, 0))
     return pl.pallas_call(
         products_kernel,
@@ -260,7 +263,7 @@
         out_shape=[shape(total // 2, rank + total)] * 2,
         scratch_shapes=[pltpu.VMEM((total, block * width), jnp.float32), pltpu.VMEM((total, rank + total), jnp.float32),
                         pltpu.VMEM((total, total), jnp.float32)],
-        compiler_params=params(14),
+        compiler_params=params(22),
         name="products",
     )(index, in_hbm(high), in_hbm(low), *pieces)
 

time: 125 us -> 124 us (level)
  transfers between devices with their start and end apart: 26 -> 26, of which waited for: 13 -> 12; matrix products, arithmetic and copies ran while one was open for 1% -> 1% of each run, Pallas kernels for 13% -> 13%
where the time goes in v13:
time: 124 us
  Pallas kernels  46.2 us (37%)
  starting transfers between devices  42.2 us (34%)
  waiting for transfers between devices  32.6 us (26%)
    ppermute x24, starting transfers between devices, xor_permute(): return lax.ppermute(value, axis, [(i, i ^ mask) for i in range(size)])  38.5 us
    ppermute x24, waiting for transfers between devices, xor_permute(): return lax.ppermute(value, axis, [(i, i ^ mask) for i in range(size)])  32.6 us
    pallas_call x1, Pallas kernels, solve(): pl.pallas_call(functools.partial(solve_kernel, count=float(count), chips=...  17.2 us
    pallas_call x1, Pallas kernels, basis_parts(): pl.pallas_call(basis_kernel, grid=(lines // block,), in_specs=[SCALARS, p...  10.3 us
    pallas_call x1, Pallas kernels, evolve(): pl.pallas_call(functools.partial(evolve_kernel, slots=slots), in_specs=[S...  6.67 us
    pallas_call x1, Pallas kernels, products(): pl.pallas_call(products_kernel, grid=(lines // block,), in_specs=[SCALARS...  4.85 us
    pallas_call x1, Pallas kernels, to_lines(): pl.pallas_call(to_lines_kernel, grid=(members // group,), in_specs=[flat,...  4.58 us
  transfers between devices with their start and end apart: 26, of which 12 were waited for; matrix products, arithmetic and copies ran while one was open for 1% of the time, Pallas kernels for 13%

profile of v13, /device:TPU:0, one launch (start us, length us, event | category | flops | bytes accessed | tf_op | source)
XLA Modules:
  0.0 123.7 jit_solution(3258293866826209048)
XLA Ops:
  0.6 1.5 %edges.1 = (f32[8,64,128]{2,1,0:T(8,128)S(1)}, f32[8,64,128]{2,1,0:T(8,128)S(1)}) custom-call(f32[64,128]{1,0:T(8,128)} %stiff_ref.3, f32[64,64,128]{2,1,0:T(8,128)} %disp_high.1, f32[64,64,128]{2,1,0:T(8,128)} %vel_high.1, f32[64,64,128]{2,1,0:T(8,128)} %disp_high.1, f32[64,64,128]{2,1,0:T(8,128)} %vel_high.1), custom_call_target="tpu_custom_call" | custom-call | tf_op jit(solution)/shard_map/edges/pallas_call | solution.py:76
  2.1 2.4 %collective-permute-start.5 = (f32[8,64,128]{2,1,0:T(8,128)S(1)}, f32[8,64,128]{2,1,0:T(8,128)S(1)}, u32[]{:S(2)}, u32[]{:S(2)}) collective-permute-start(f32[8,64,128]{2,1,0:T(8,128)S(1)} %get-tuple-element.90), channel_id=1, source_target_pairs={{0,4},{4,8},{8,12},{12,16},{16,20},{20,24},{24,28},{1,5},{5,9},{9,... | collective-permute-start | bytes 786440 | tf_op jit(solution)/shard_map/ppermute | solution.py:479
  4.5 1.3 %collective-permute-start.6 = (f32[8,64,128]{2,1,0:T(8,128)S(1)}, f32[8,64,128]{2,1,0:T(8,128)S(1)}, u32[]{:S(2)}, u32[]{:S(2)}) collective-permute-start(f32[8,64,128]{2,1,0:T(8,128)S(1)} %get-tuple-element.91), channel_id=1, source_target_pairs={{4,0},{8,4},{12,8},{16,12},{20,16},{24,20},{28,24},{5,1},{9,5},{13... | collective-permute-start | bytes 786440 | tf_op jit(solution)/shard_map/ppermute | solution.py:480
  5.9 4.6 %to_lines.1 = (f32[64,64,128]{2,1,0:T(8,128)S(1)}, f32[64,64,128]{2,1,0:T(8,128)S(1)}) custom-call(f32[4096,128]{1,0:T(8,128)} %bitcast.6, f32[4096,128]{1,0:T(8,128)} %bitcast.7), custom_call_target="tpu_custom_call" | custom-call | tf_op jit(solution)/shard_map/to_lines/pallas_call | solution.py:99
  10.5 0.1 pad_add_fusion.index_ref
  10.6 6.7 %evolve.1 = (f32[16,64,128]{2,1,0:T(8,128)}, f32[16,64,128]{2,1,0:T(8,128)}, f32[16,64,128]{2,1,0:T(8,128)}, f32[16,64,128]{2,1,0:T(8,128)}) custom-call(s32[7]{0:T(128)S(1)} %pad_add_fusion.index_ref, f32[64,64,128]{2,1,0:T(8,128)S(1)} %get-tuple-element.95.disp_ref, f32[64,64,128]{2,1,0:T(8,128)S(1)} %get-tuple-element.96.vel_ref, ...), custom_call_target="tpu_custom_call" | custom-call | tf_op jit(solution)/shard_map/evolve/pallas_call | solution.py:158
  17.2 2.5 %collective-permute-start.7 = (f32[16,64,128]{2,1,0:T(8,128)}, f32[16,64,128]{2,1,0:T(8,128)S(1)}, u32[]{:S(2)}, u32[]{:S(2)}) collective-permute-start(f32[16,64,128]{2,1,0:T(8,128)} %get-tuple-element.110), channel_id=1, source_target_pairs={{0,1},{1,0},{2,3},{3,2},{4,5},{5,4},{6,7},{7,6},{8,9},{9,8},{10,11... | collective-permute-start | bytes 1572872 | tf_op jit(solution)/shard_map/ppermute | solution.py:54
  19.7 2.6 %collective-permute-start.8 = (f32[16,64,128]{2,1,0:T(8,128)}, f32[16,64,128]{2,1,0:T(8,128)S(1)}, u32[]{:S(2)}, u32[]{:S(2)}) collective-permute-start(f32[16,64,128]{2,1,0:T(8,128)} %get-tuple-element.111), channel_id=1, source_target_pairs={{0,2},{1,3},{2,0},{3,1},{4,6},{5,7},{6,4},{7,5},{8,10},{9,11},{10,... | collective-permute-start | bytes 1572872 | tf_op jit(solution)/shard_map/ppermute | solution.py:54
  22.3 0.7 broadcast_in_dim.3
  23.0 39.6 %while.18 = (s32[]{:T(128)}, s32[7]{0:T(128)S(1)}, f32[64,512]{1,0:T(8,128)}, bf16[2048,512]{1,0:T(8,128)(2,1)}, bf16[2048,512]{1,0:T(8,128)(2,1)}, /*index=5*/f...) while((s32[]{:T(128)}, s32[7]{0:T(128)S(1)}, ...), condition=%wide.region_1.2_spmd, body=%wide.region_0.1_spmd.sunk | while | flops 131088 | bytes 5243237 | solution.py:497
  23.0 10.3 %basis_parts.1 = (f32[256,512]{1,0:T(8,128)S(1)}, f32[256,512]{1,0:T(8,128)S(1)}, bf16[2048,512]{1,0:T(8,128)(2,1)}, bf16[2048,512]{1,0:T(8,128)(2,1)}, f32[2048,512]{1,0:T(8,128)}) custom-call(s32[7]{0:T(128)S(1)} %get-tuple-element.223.index_ref, f32[768,512]{1,0:T(8,128)} %get-tuple-element.239.rot_ref, f32[16,128,512]{2,1,0:T(8,128)} %get-tuple-element.240.basis_ref), custom_call_target="tpu_custom_call" | custom-call | tf_op jit(solution)/shard_map/while/body/basis_parts/pallas_call | solution.py:209
  33.3 2.9 %collective-permute-start = (f32[256,512]{1,0:T(8,128)S(1)}, f32[256,512]{1,0:T(8,128)S(1)}, u32[]{:S(2)}, u32[]{:S(2)}) collective-permute-start(f32[256,512]{1,0:T(8,128)S(1)} %get-tuple-element.202), channel_id=1, source_target_pairs={{0,4},{4,0},{8,12},{12,8},{16,20},{20,16},{24,28},{28,24},{1,5},{5... | collective-permute-start | bytes 1572872 | tf_op jit(solution)/shard_map/while/body/ppermute | solution.py:54
  36.2 1.5 %collective-permute-done.got_ref = f32[256,512]{1,0:T(8,128)S(1)} collective-permute-done((f32[256,512]{1,0:T(8,128)S(1)}, f32[256,512]{1,0:T(8,128)S(1)}, u32[]{:S(2)}, u32[]{:S(2)}) %collective-permute-start) | collective-permute-done | bytes 524320 | tf_op jit(solution)/shard_map/while/body/ppermute | solution.py:54
  37.7 0.6 split.3
  38.3 2.4 %collective-permute-start.2 = (f32[64,512]{1,0:T(8,128)S(1)}, f32[64,512]{1,0:T(8,128)S(1)}, u32[]{:S(2)}, u32[]{:S(2)}) collective-permute-start(f32[64,512]{1,0:T(8,128)S(1)} %get-tuple-element.205), channel_id=1, source_target_pairs={{0,8},{4,12},{8,0},{12,4},{16,24},{20,28},{24,16},{28,20},{1,9},{5... | collective-permute-start | bytes 393224 | tf_op jit(solution)/shard_map/while/body/ppermute | solution.py:54
  40.7 0.9 collective-permute-start.1
  41.6 3.1 %collective-permute-done.2 = f32[64,512]{1,0:T(8,128)S(1)} collective-permute-done((f32[64,512]{1,0:T(8,128)S(1)}, f32[64,512]{1,0:T(8,128)S(1)}, u32[]{:S(2)}, u32[]{:S(2)}) %collective-permute-start.2) | collective-permute-done | bytes 131104 | tf_op jit(solution)/shard_map/while/body/ppermute | solution.py:54
  44.7 1.8 %collective-permute-start.3 = (f32[64,512]{1,0:T(8,128)S(1)}, f32[64,512]{1,0:T(8,128)S(1)}, u32[]{:S(2)}, u32[]{:S(2)}) collective-permute-start(f32[64,512]{1,0:T(8,128)S(1)} %get-tuple-element.206), channel_id=1, source_target_pairs={{0,24},{4,28},{8,16},{12,20},{16,8},{20,12},{24,0},{28,4},{1,25},{... | collective-permute-start | bytes 393224 | tf_op jit(solution)/shard_map/while/body/ppermute | solution.py:54
  46.6 4.3 %collective-permute-done.3 = f32[64,512]{1,0:T(8,128)S(1)} collective-permute-done((f32[64,512]{1,0:T(8,128)S(1)}, f32[64,512]{1,0:T(8,128)S(1)}, u32[]{:S(2)}, u32[]{:S(2)}) %collective-permute-start.3) | collective-permute-done | bytes 131104 | tf_op jit(solution)/shard_map/while/body/ppermute | solution.py:54
  50.9 0.7 collective-permute-start.4
  51.6 10.3 %collective-permute-done.4 = f32[64,512]{1,0:T(8,128)S(1)} collective-permute-done((f32[64,512]{1,0:T(8,128)S(1)}, f32[64,512]{1,0:T(8,128)S(1)}, u32[]{:S(2)}, u32[]{:S(2)}) %collective-permute-start.4) | collective-permute-done | bytes 131104 | tf_op jit(solution)/shard_map/while/body/ppermute | solution.py:54
  61.9 0.7 add.83
  62.6 4.8 %products.1 = (f32[128,768]{1,0:T(8,128)S(1)}, f32[128,768]{1,0:T(8,128)S(1)}) custom-call(s32[7]{0:T(128)S(1)} %get-tuple-element.107.index_ref, bf16[2048,512]{1,0:T(8,128)(2,1)} %get-tuple-element.108.high_ref.high_hbm, bf16[2048,512]{1,0:T(8,128)(2,1)} %get-tuple-element.109.low_ref.low_hbm, f32[16,64,128]{2,1,0:T(8,128)S(1)} %collective-permute-done.7.rest_0_, ...), custom_call_target="tpu_custom_call" | custom-call | tf_op jit(solution)/shard_map/products/pallas_call | solution.py:257
  67.5 0.1 collective-permute-start.10
  67.6 8.0 %collective-permute-start.14 = (f32[64,512]{1,0:T(8,128)S(1)}, f32[64,512]{1,0:T(8,128)S(1)}, u32[]{:S(2)}, u32[]{:S(2)}) collective-permute-start(f32[64,512]{1,0:T(8,128)S(1)} %copy-done.5), channel_id=1, source_target_pairs={{0,2},{1,3},{2,0},{3,1},{4,6},{5,7},{6,4},{7,5},{8,10},{9,11},{10,... | collective-permute-start | bytes 393224 | tf_op jit(solution)/shard_map/ppermute | solution.py:54
  75.6 0.6 split.2
  76.2 4.1 %collective-permute-start.11 = (f32[32,768]{1,0:T(8,128)S(1)}, f32[32,768]{1,0:T(8,128)S(1)}, u32[]{:S(2)}, u32[]{:S(2)}) collective-permute-start(f32[32,768]{1,0:T(8,128)S(1)} %get-tuple-element.117), channel_id=1, source_target_pairs={{0,8},{4,12},{8,0},{12,4},{16,24},{20,28},{24,16},{28,20},{1,9},{5... | collective-permute-start | bytes 294920 | tf_op jit(solution)/shard_map/ppermute | solution.py:54
  80.3 1.5 %collective-permute-start.13 = (f32[32,768]{1,0:T(8,128)S(1)}, f32[32,768]{1,0:T(8,128)S(1)}, u32[]{:S(2)}, u32[]{:S(2)}) collective-permute-start(f32[32,768]{1,0:T(8,128)S(1)} %get-tuple-element.119), channel_id=1, source_target_pairs={{0,24},{4,28},{8,16},{12,20},{16,8},{20,12},{24,0},{28,4},{1,25},{... | collective-permute-start | bytes 294920 | tf_op jit(solution)/shard_map/ppermute | solution.py:54
  81.8 0.3 collective-permute-done.14
  82.1 1.1 collective-permute-done.11
  83.3 3.6 %collective-permute-done.12 = f32[32,768]{1,0:T(8,128)S(1)} collective-permute-done((f32[32,768]{1,0:T(8,128)S(1)}, f32[32,768]{1,0:T(8,128)S(1)}, u32[]{:S(2)}, u32[]{:S(2)}) %collective-permute-start.12) | collective-permute-done | bytes 98336 | tf_op jit(solution)/shard_map/ppermute | solution.py:54
  87.0 1.4 %collective-permute-start.17 = (f32[32,768]{1,0:T(8,128)S(1)}, f32[32,768]{1,0:T(8,128)S(1)}, u32[]{:S(2)}, u32[]{:S(2)}) collective-permute-start(f32[32,768]{1,0:T(8,128)S(1)} %add_add_fusion.2), channel_id=1, source_target_pairs={{0,3},{1,2},{2,1},{3,0},{4,7},{5,6},{6,5},{7,4},{8,11},{9,10},{10,... | collective-permute-start | bytes 294920 | tf_op jit(solution)/shard_map/ppermute | solution.py:54
  88.4 0.7 collective-permute-start.16
  89.1 2.3 %collective-permute-start.15 = (f32[32,768]{1,0:T(8,128)S(1)}, f32[32,768]{1,0:T(8,128)S(1)}, u32[]{:S(2)}, u32[]{:S(2)}) collective-permute-start(f32[32,768]{1,0:T(8,128)S(1)} %add_add_fusion.2), channel_id=1, source_target_pairs={{0,1},{1,0},{2,3},{3,2},{4,5},{5,4},{6,7},{7,6},{8,9},{9,8},{10,11... | collective-permute-start | bytes 294920 | tf_op jit(solution)/shard_map/ppermute | solution.py:54
  91.4 1.4 %collective-permute-start.24 = (f32[64,512]{1,0:T(8,128)S(1)}, f32[64,512]{1,0:T(8,128)S(1)}, u32[]{:S(2)}, u32[]{:S(2)}) collective-permute-start(f32[64,512]{1,0:T(8,128)S(1)} %add.52), channel_id=1, source_target_pairs={{0,24},{4,28},{8,16},{12,20},{16,8},{20,12},{24,0},{28,4},{1,25},{... | collective-permute-start | bytes 393224 | tf_op jit(solution)/shard_map/ppermute | solution.py:54
  92.8 0.9 collective-permute-start.23
  93.7 0.9 collective-permute-done.17
  94.6 0.6 collective-permute-start.22
  95.2 2.6 %collective-permute-done.16 = f32[32,768]{1,0:T(8,128)S(1)} collective-permute-done((f32[32,768]{1,0:T(8,128)S(1)}, f32[32,768]{1,0:T(8,128)S(1)}, u32[]{:S(2)}, u32[]{:S(2)}) %collective-permute-start.16) | collective-permute-done | bytes 98336 | tf_op jit(solution)/shard_map/ppermute | solution.py:54
  97.8 1.4 %collective-permute-start.20 = (f32[32,768]{1,0:T(8,128)S(1)}, f32[32,768]{1,0:T(8,128)S(1)}, u32[]{:S(2)}, u32[]{:S(2)}) collective-permute-start(f32[32,768]{1,0:T(8,128)S(1)} %add_add_fusion.1), channel_id=1, source_target_pairs={{0,24},{4,28},{8,16},{12,20},{16,8},{20,12},{24,0},{28,4},{1,25},{... | collective-permute-start | bytes 294920 | tf_op jit(solution)/shard_map/ppermute | solution.py:54
  99.2 0.7 collective-permute-start.19
  99.9 1.5 %collective-permute-start.18 = (f32[32,768]{1,0:T(8,128)S(1)}, f32[32,768]{1,0:T(8,128)S(1)}, u32[]{:S(2)}, u32[]{:S(2)}) collective-permute-start(f32[32,768]{1,0:T(8,128)S(1)} %add_add_fusion.1), channel_id=1, source_target_pairs={{0,8},{4,12},{8,0},{12,4},{16,24},{20,28},{24,16},{28,20},{1,9},{5... | collective-permute-start | bytes 294920 | tf_op jit(solution)/shard_map/ppermute | solution.py:54
  101.4 0.1 collective-permute-start.25
  101.5 2.4 %collective-permute-done.20 = f32[32,768]{1,0:T(8,128)S(1)} collective-permute-done((f32[32,768]{1,0:T(8,128)S(1)}, f32[32,768]{1,0:T(8,128)S(1)}, u32[]{:S(2)}, u32[]{:S(2)}) %collective-permute-start.20) | collective-permute-done | bytes 98336 | tf_op jit(solution)/shard_map/ppermute | solution.py:54
  103.9 0.7 collective-permute-done.19
  104.7 0.1 collective-permute-start.21
  104.8 1.7 %collective-permute-done.21.sums2_ref = f32[128,768]{1,0:T(8,128)S(1)} collective-permute-done((f32[128,768]{1,0:T(8,128)S(1)}, f32[128,768]{1,0:T(8,128)S(1)}, u32[]{:S(2)}, u32[]{:S(2)}) %collective-permute-start.21) | collective-permute-done | bytes 393248 | tf_op jit(solution)/shard_map/ppermute | solution.py:54
  106.5 17.2 %solve.1 = (f32[16,128,512]{2,1,0:T(8,128)}, f32[512,256]{1,0:T(8,128)}) custom-call(s32[7]{0:T(128)S(1)} %pad_add_fusion.index_ref, f32[128,768]{1,0:T(8,128)S(1)} %pad_maximum_fusion.sums_ref, f32[128,768]{1,0:T(8,128)S(1)} %collective-permute-done.21.sums2_ref, f32[256,512]{1,0:T(8,128)S(1)} %constant_dynamic-update-slice_fusion.gram_ref, ...), custom_call_target="tpu_custom_call" | custom-call | tf_op jit(solution)/shard_map/solve/pallas_call | solution.py:447
  (42 shorter events, 0.3 us)
Async XLA Ops:
  2.1 8.4 %collective-permute-start.5 = (f32[8,64,128]{2,1,0:T(8,128)S(1)}, f32[8,64,128]{2,1,0:T(8,128)S(1)}, u32[]{:S(2)}, u32[]{:S(2)}) collective-permute-start(f32[8,64,128]{2,1,0:T(8,128)S(1)} %get-tuple-element.90), channel_id=1, source_target_pairs={{0,4},{4,8},{8,12},{12,16},{16,20},{20,24},{24,28},{1,5},{5,9},{9,... | collective-permute-start | bytes 786440 | tf_op jit(solution)/shard_map/ppermute | solution.py:479
  4.5 6.1 %collective-permute-start.6 = (f32[8,64,128]{2,1,0:T(8,128)S(1)}, f32[8,64,128]{2,1,0:T(8,128)S(1)}, u32[]{:S(2)}, u32[]{:S(2)}) collective-permute-start(f32[8,64,128]{2,1,0:T(8,128)S(1)} %get-tuple-element.91), channel_id=1, source_target_pairs={{4,0},{8,4},{12,8},{16,12},{20,16},{24,20},{28,24},{5,1},{9,5},{13... | collective-permute-start | bytes 786440 | tf_op jit(solution)/shard_map/ppermute | solution.py:480
  5.8 4.6 %copy-start.6 = (s32[4]{0:T(128)S(1)}, s32[4]{0:T(128)}, u32[]{:S(2)}) copy-start(s32[4]{0:T(128)} %constant.45.clone) | copy-start | bytes 52
  5.9 4.7 %copy-start.1 = (f32[64,128]{1,0:T(8,128)S(1)}, f32[64,128]{1,0:T(8,128)}, u32[]{:S(2)}) copy-start(f32[64,128]{1,0:T(8,128)} %stiff_ref.3) | copy-start | bytes 98308
  17.2 45.3 %collective-permute-start.7 = (f32[16,64,128]{2,1,0:T(8,128)}, f32[16,64,128]{2,1,0:T(8,128)S(1)}, u32[]{:S(2)}, u32[]{:S(2)}) collective-permute-start(f32[16,64,128]{2,1,0:T(8,128)} %get-tuple-element.110), channel_id=1, source_target_pairs={{0,1},{1,0},{2,3},{3,2},{4,5},{5,4},{6,7},{7,6},{8,9},{9,8},{10,11... | collective-permute-start | bytes 1572872 | tf_op jit(solution)/shard_map/ppermute | solution.py:54
  19.7 42.8 %collective-permute-start.8 = (f32[16,64,128]{2,1,0:T(8,128)}, f32[16,64,128]{2,1,0:T(8,128)S(1)}, u32[]{:S(2)}, u32[]{:S(2)}) collective-permute-start(f32[16,64,128]{2,1,0:T(8,128)} %get-tuple-element.111), channel_id=1, source_target_pairs={{0,2},{1,3},{2,0},{3,1},{4,6},{5,7},{6,4},{7,5},{8,10},{9,11},{10,... | collective-permute-start | bytes 1572872 | tf_op jit(solution)/shard_map/ppermute | solution.py:54
  22.3 40.2 %collective-permute-start.9 = (f32[16,64,128]{2,1,0:T(8,128)}, f32[16,64,128]{2,1,0:T(8,128)S(1)}, u32[]{:S(2)}, u32[]{:S(2)}) collective-permute-start(f32[16,64,128]{2,1,0:T(8,128)} %get-tuple-element.112), channel_id=1, source_target_pairs={{0,3},{1,2},{2,1},{3,0},{4,7},{5,6},{6,5},{7,4},{8,11},{9,10},{10,... | collective-permute-start | bytes 1572872 | tf_op jit(solution)/shard_map/ppermute | solution.py:54
  23.0 39.6 %copy-start = (f32[16,64,128]{2,1,0:T(8,128)S(1)}, f32[16,64,128]{2,1,0:T(8,128)}, u32[]{:S(2)}) copy-start(f32[16,64,128]{2,1,0:T(8,128)} %get-tuple-element.113.rest_3_) | copy-start | bytes 1572868
  33.3 4.4 %collective-permute-start = (f32[256,512]{1,0:T(8,128)S(1)}, f32[256,512]{1,0:T(8,128)S(1)}, u32[]{:S(2)}, u32[]{:S(2)}) collective-permute-start(f32[256,512]{1,0:T(8,128)S(1)} %get-tuple-element.202), channel_id=1, source_target_pairs={{0,4},{4,0},{8,12},{12,8},{16,20},{20,16},{24,28},{28,24},{1,5},{5... | collective-permute-start | bytes 1572872 | tf_op jit(solution)/shard_map/while/body/ppermute | solution.py:54
  38.3 6.4 %collective-permute-start.2 = (f32[64,512]{1,0:T(8,128)S(1)}, f32[64,512]{1,0:T(8,128)S(1)}, u32[]{:S(2)}, u32[]{:S(2)}) collective-permute-start(f32[64,512]{1,0:T(8,128)S(1)} %get-tuple-element.205), channel_id=1, source_target_pairs={{0,8},{4,12},{8,0},{12,4},{16,24},{20,28},{24,16},{28,20},{1,9},{5... | collective-permute-start | bytes 393224 | tf_op jit(solution)/shard_map/while/body/ppermute | solution.py:54
  40.7 5.9 %collective-permute-start.1 = (f32[64,512]{1,0:T(8,128)S(1)}, f32[64,512]{1,0:T(8,128)S(1)}, u32[]{:S(2)}, u32[]{:S(2)}) collective-permute-start(f32[64,512]{1,0:T(8,128)S(1)} %get-tuple-element.203), channel_id=1, source_target_pairs={{0,16},{4,20},{8,24},{12,28},{16,0},{20,4},{24,8},{28,12},{1,17},{... | collective-permute-start | bytes 393224 | tf_op jit(solution)/shard_map/while/body/ppermute | solution.py:54
  44.7 6.1 %collective-permute-start.3 = (f32[64,512]{1,0:T(8,128)S(1)}, f32[64,512]{1,0:T(8,128)S(1)}, u32[]{:S(2)}, u32[]{:S(2)}) collective-permute-start(f32[64,512]{1,0:T(8,128)S(1)} %get-tuple-element.206), channel_id=1, source_target_pairs={{0,24},{4,28},{8,16},{12,20},{16,8},{20,12},{24,0},{28,4},{1,25},{... | collective-permute-start | bytes 393224 | tf_op jit(solution)/shard_map/while/body/ppermute | solution.py:54
  50.9 11.0 %collective-permute-start.4 = (f32[64,512]{1,0:T(8,128)S(1)}, f32[64,512]{1,0:T(8,128)S(1)}, u32[]{:S(2)}, u32[]{:S(2)}) collective-permute-start(f32[64,512]{1,0:T(8,128)S(1)} %add_add_fusion.4), channel_id=1, source_target_pairs={{0,1},{1,0},{2,3},{3,2},{4,5},{5,4},{6,7},{7,6},{8,9},{9,8},{10,11... | collective-permute-start | bytes 393224 | tf_op jit(solution)/shard_map/while/body/ppermute | solution.py:54
  62.6 5.0 %copy-start.5 = (f32[64,512]{1,0:T(8,128)S(1)}, f32[64,512]{1,0:T(8,128)}, u32[]{:S(2)}) copy-start(f32[64,512]{1,0:T(8,128)} %get-tuple-element.120) | copy-start | bytes 393220
  62.6 43.9 %copy-start.4 = (bf16[2048,512]{1,0:T(8,128)(2,1)S(1)}, bf16[2048,512]{1,0:T(8,128)(2,1)}, u32[]{:S(2)}) copy-start(bf16[2048,512]{1,0:T(8,128)(2,1)} %get-tuple-element.109.low_ref.low_hbm) | copy-start | bytes 6291460
  67.4 39.0 %copy-start.2 = (f32[768,512]{1,0:T(8,128)S(1)}, f32[768,512]{1,0:T(8,128)}, u32[]{:S(2)}) copy-start(f32[768,512]{1,0:T(8,128)} %get-tuple-element.263) | copy-start | bytes 4718596
  67.5 39.0 %copy-start.3 = (bf16[2048,512]{1,0:T(8,128)(2,1)S(1)}, bf16[2048,512]{1,0:T(8,128)(2,1)}, u32[]{:S(2)}) copy-start(bf16[2048,512]{1,0:T(8,128)(2,1)} %get-tuple-element.108.high_ref.high_hbm) | copy-start | bytes 6291460
  67.5 8.1 %collective-permute-start.10 = (f32[128,768]{1,0:T(8,128)S(1)}, f32[128,768]{1,0:T(8,128)S(1)}, u32[]{:S(2)}, u32[]{:S(2)}) collective-permute-start(f32[128,768]{1,0:T(8,128)S(1)} %get-tuple-element.115), channel_id=1, source_target_pairs={{0,4},{4,0},{8,12},{12,8},{16,20},{20,16},{24,28},{28,24},{1,5},{5... | collective-permute-start | bytes 1179656 | tf_op jit(solution)/shard_map/ppermute | solution.py:54
  67.6 14.6 %collective-permute-start.14 = (f32[64,512]{1,0:T(8,128)S(1)}, f32[64,512]{1,0:T(8,128)S(1)}, u32[]{:S(2)}, u32[]{:S(2)}) collective-permute-start(f32[64,512]{1,0:T(8,128)S(1)} %copy-done.5), channel_id=1, source_target_pairs={{0,2},{1,3},{2,0},{3,1},{4,6},{5,7},{6,4},{7,5},{8,10},{9,11},{10,... | collective-permute-start | bytes 393224 | tf_op jit(solution)/shard_map/ppermute | solution.py:54
  76.2 7.1 %collective-permute-start.11 = (f32[32,768]{1,0:T(8,128)S(1)}, f32[32,768]{1,0:T(8,128)S(1)}, u32[]{:S(2)}, u32[]{:S(2)}) collective-permute-start(f32[32,768]{1,0:T(8,128)S(1)} %get-tuple-element.117), channel_id=1, source_target_pairs={{0,8},{4,12},{8,0},{12,4},{16,24},{20,28},{24,16},{28,20},{1,9},{5... | collective-permute-start | bytes 294920 | tf_op jit(solution)/shard_map/ppermute | solution.py:54
  80.3 6.7 %collective-permute-start.12 = (f32[32,768]{1,0:T(8,128)S(1)}, f32[32,768]{1,0:T(8,128)S(1)}, u32[]{:S(2)}, u32[]{:S(2)}) collective-permute-start(f32[32,768]{1,0:T(8,128)S(1)} %get-tuple-element.118), channel_id=1, source_target_pairs={{0,16},{4,20},{8,24},{12,28},{16,0},{20,4},{24,8},{28,12},{1,17},{... | collective-permute-start | bytes 294920 | tf_op jit(solution)/shard_map/ppermute | solution.py:54
  80.3 6.7 %collective-permute-start.13 = (f32[32,768]{1,0:T(8,128)S(1)}, f32[32,768]{1,0:T(8,128)S(1)}, u32[]{:S(2)}, u32[]{:S(2)}) collective-permute-start(f32[32,768]{1,0:T(8,128)S(1)} %get-tuple-element.119), channel_id=1, source_target_pairs={{0,24},{4,28},{8,16},{12,20},{16,8},{20,12},{24,0},{28,4},{1,25},{... | collective-permute-start | bytes 294920 | tf_op jit(solution)/shard_map/ppermute | solution.py:54
  87.0 7.6 %collective-permute-start.17 = (f32[32,768]{1,0:T(8,128)S(1)}, f32[32,768]{1,0:T(8,128)S(1)}, u32[]{:S(2)}, u32[]{:S(2)}) collective-permute-start(f32[32,768]{1,0:T(8,128)S(1)} %add_add_fusion.2), channel_id=1, source_target_pairs={{0,3},{1,2},{2,1},{3,0},{4,7},{5,6},{6,5},{7,4},{8,11},{9,10},{10,... | collective-permute-start | bytes 294920 | tf_op jit(solution)/shard_map/ppermute | solution.py:54
  88.4 9.4 %collective-permute-start.16 = (f32[32,768]{1,0:T(8,128)S(1)}, f32[32,768]{1,0:T(8,128)S(1)}, u32[]{:S(2)}, u32[]{:S(2)}) collective-permute-start(f32[32,768]{1,0:T(8,128)S(1)} %add_add_fusion.2), channel_id=1, source_target_pairs={{0,2},{1,3},{2,0},{3,1},{4,6},{5,7},{6,4},{7,5},{8,10},{9,11},{10,... | collective-permute-start | bytes 294920 | tf_op jit(solution)/shard_map/ppermute | solution.py:54
  89.1 8.7 %collective-permute-start.15 = (f32[32,768]{1,0:T(8,128)S(1)}, f32[32,768]{1,0:T(8,128)S(1)}, u32[]{:S(2)}, u32[]{:S(2)}) collective-permute-start(f32[32,768]{1,0:T(8,128)S(1)} %add_add_fusion.2), channel_id=1, source_target_pairs={{0,1},{1,0},{2,3},{3,2},{4,5},{5,4},{6,7},{7,6},{8,9},{9,8},{10,11... | collective-permute-start | bytes 294920 | tf_op jit(solution)/shard_map/ppermute | solution.py:54
  91.4 10.0 %collective-permute-start.24 = (f32[64,512]{1,0:T(8,128)S(1)}, f32[64,512]{1,0:T(8,128)S(1)}, u32[]{:S(2)}, u32[]{:S(2)}) collective-permute-start(f32[64,512]{1,0:T(8,128)S(1)} %add.52), channel_id=1, source_target_pairs={{0,24},{4,28},{8,16},{12,20},{16,8},{20,12},{24,0},{28,4},{1,25},{... | collective-permute-start | bytes 393224 | tf_op jit(solution)/shard_map/ppermute | solution.py:54
  92.8 8.6 %collective-permute-start.23 = (f32[64,512]{1,0:T(8,128)S(1)}, f32[64,512]{1,0:T(8,128)S(1)}, u32[]{:S(2)}, u32[]{:S(2)}) collective-permute-start(f32[64,512]{1,0:T(8,128)S(1)} %add.52), channel_id=1, source_target_pairs={{0,16},{4,20},{8,24},{12,28},{16,0},{20,4},{24,8},{28,12},{1,17},{... | collective-permute-start | bytes 393224 | tf_op jit(solution)/shard_map/ppermute | solution.py:54
  94.6 5.3 %collective-permute-start.22 = (f32[64,512]{1,0:T(8,128)S(1)}, f32[64,512]{1,0:T(8,128)S(1)}, u32[]{:S(2)}, u32[]{:S(2)}) collective-permute-start(f32[64,512]{1,0:T(8,128)S(1)} %add.52), channel_id=1, source_target_pairs={{0,8},{4,12},{8,0},{12,4},{16,24},{20,28},{24,16},{28,20},{1,9},{5... | collective-permute-start | bytes 393224 | tf_op jit(solution)/shard_map/ppermute | solution.py:54
  97.8 6.1 %collective-permute-start.20 = (f32[32,768]{1,0:T(8,128)S(1)}, f32[32,768]{1,0:T(8,128)S(1)}, u32[]{:S(2)}, u32[]{:S(2)}) collective-permute-start(f32[32,768]{1,0:T(8,128)S(1)} %add_add_fusion.1), channel_id=1, source_target_pairs={{0,24},{4,28},{8,16},{12,20},{16,8},{20,12},{24,0},{28,4},{1,25},{... | collective-permute-start | bytes 294920 | tf_op jit(solution)/shard_map/ppermute | solution.py:54
  99.2 5.4 %collective-permute-start.19 = (f32[32,768]{1,0:T(8,128)S(1)}, f32[32,768]{1,0:T(8,128)S(1)}, u32[]{:S(2)}, u32[]{:S(2)}) collective-permute-start(f32[32,768]{1,0:T(8,128)S(1)} %add_add_fusion.1), channel_id=1, source_target_pairs={{0,16},{4,20},{8,24},{12,28},{16,0},{20,4},{24,8},{28,12},{1,17},{... | collective-permute-start | bytes 294920 | tf_op jit(solution)/shard_map/ppermute | solution.py:54
  99.9 4.8 %collective-permute-start.18 = (f32[32,768]{1,0:T(8,128)S(1)}, f32[32,768]{1,0:T(8,128)S(1)}, u32[]{:S(2)}, u32[]{:S(2)}) collective-permute-start(f32[32,768]{1,0:T(8,128)S(1)} %add_add_fusion.1), channel_id=1, source_target_pairs={{0,8},{4,12},{8,0},{12,4},{16,24},{20,28},{24,16},{28,20},{1,9},{5... | collective-permute-start | bytes 294920 | tf_op jit(solution)/shard_map/ppermute | solution.py:54
  101.4 5.0 %collective-permute-start.25 = (f32[256,512]{1,0:T(8,128)S(1)}, f32[256,512]{1,0:T(8,128)S(1)}, u32[]{:S(2)}, u32[]{:S(2)}) collective-permute-start(f32[256,512]{1,0:T(8,128)S(1)} %constant_dynamic-update-slice_fusion.gram_ref), channel_id=1, source_target_pairs={{0,4},{4,0},{8,12},{12,8},{16,20},{20,16},{24,28},{28,24},{1,5},{5... | collective-permute-start | bytes 1572872 | tf_op jit(solution)/shard_map/ppermute | solution.py:54
  104.7 1.8 %collective-permute-start.21 = (f32[128,768]{1,0:T(8,128)S(1)}, f32[128,768]{1,0:T(8,128)S(1)}, u32[]{:S(2)}, u32[]{:S(2)}) collective-permute-start(f32[128,768]{1,0:T(8,128)S(1)} %pad_maximum_fusion.sums_ref), channel_id=1, source_target_pairs={{0,4},{4,0},{8,12},{12,8},{16,20},{20,16},{24,28},{28,24},{1,5},{5... | collective-permute-start | bytes 1179656 | tf_op jit(solution)/shard_map/ppermute | solution.py:54

commit v14 on v13

--- a/solution.py
+++ b/solution.py
@@ -496,12 +496,12 @@
     empty = room(*[shape(lines * width, rank, dtype=t) for t in (jnp.bfloat16, jnp.bfloat16, jnp.float32)])
     order, gram, high, low, turned = lax.fori_loop(
         0, 1 + (ana >> 20), meanwhile, (order, jnp.zeros((rank // sims, rank), jnp.float32), *empty))
-    gram = ana_sum_by_pairs(gram, bits[-1:])
+    gram_rest = xor_permute(gram, "ana", bits[-1])
 
     send, keep = products(order, high, low, pieces)
     sums = chip_scatter(order, send, keep, chips)
-    sums, gram = lax.optimization_barrier((sums, gram))
-    gram = chip_gather(gram, chips)
+    sums, gram, gram_rest = lax.optimization_barrier((sums, gram, gram_rest))
+    gram = chip_gather(gram + gram_rest, chips)
     sums = ana_sum(sums)
     sums = with_other_core(chip_gather(sums, chips))
     gram = with_other_core(gram)

time: 124 us -> 126 us (1.016)
  starting transfers between devices: 42.2 us -> 43.9 us
    ppermute x24, starting transfers between devices: 38.5 us -> 40.2 us  [xor_permute(): return lax.ppermute(value, axis, [(i, i ^ mask) for i in range(size)])]
  transfers between devices with their start and end apart: 26 -> 26, of which waited for: 12 -> 11; matrix products, arithmetic and copies ran while one was open for 1% -> 1% of each run, Pallas kernels for 13% -> 12%
where the time goes in v14:
time: 126 us
  Pallas kernels  46.1 us (37%)
  starting transfers between devices  43.9 us (35%)
  waiting for transfers between devices  33.2 us (26%)
    ppermute x24, starting transfers between devices, xor_permute(): return lax.ppermute(value, axis, [(i, i ^ mask) for i in range(size)])  40.2 us
    ppermute x24, waiting for transfers between devices, xor_permute(): return lax.ppermute(value, axis, [(i, i ^ mask) for i in range(size)])  33.2 us
    pallas_call x1, Pallas kernels, solve(): pl.pallas_call(functools.partial(solve_kernel, count=float(count), chips=...  17.1 us
    pallas_call x1, Pallas kernels, basis_parts(): pl.pallas_call(basis_kernel, grid=(lines // block,), in_specs=[SCALARS, p...  10.3 us
    pallas_call x1, Pallas kernels, evolve(): pl.pallas_call(functools.partial(evolve_kernel, slots=slots), in_specs=[S...  6.68 us
    pallas_call x1, Pallas kernels, products(): pl.pallas_call(products_kernel, grid=(lines // block,), in_specs=[SCALARS...  4.84 us
    pallas_call x1, Pallas kernels, to_lines(): pl.pallas_call(to_lines_kernel, grid=(members // group,), in_specs=[flat,...  4.58 us
  transfers between devices with their start and end apart: 26, of which 11 were waited for; matrix products, arithmetic and copies ran while one was open for 1% of the time, Pallas kernels for 12%

profile of v14, /device:TPU:0, one launch (start us, length us, event | category | flops | bytes accessed | tf_op | source)
XLA Modules:
  0.0 125.7 jit_solution(17332870083054321755)
XLA Ops:
  0.6 1.5 %edges.1 = (f32[8,64,128]{2,1,0:T(8,128)S(1)}, f32[8,64,128]{2,1,0:T(8,128)S(1)}) custom-call(f32[64,128]{1,0:T(8,128)} %stiff_ref.3, f32[64,64,128]{2,1,0:T(8,128)} %disp_high.1, f32[64,64,128]{2,1,0:T(8,128)} %vel_high.1, f32[64,64,128]{2,1,0:T(8,128)} %disp_high.1, f32[64,64,128]{2,1,0:T(8,128)} %vel_high.1), custom_call_target="tpu_custom_call" | custom-call | tf_op jit(solution)/shard_map/edges/pallas_call | solution.py:76
  2.1 2.4 %collective-permute-start.5 = (f32[8,64,128]{2,1,0:T(8,128)S(1)}, f32[8,64,128]{2,1,0:T(8,128)S(1)}, u32[]{:S(2)}, u32[]{:S(2)}) collective-permute-start(f32[8,64,128]{2,1,0:T(8,128)S(1)} %get-tuple-element.91), channel_id=1, source_target_pairs={{0,4},{4,8},{8,12},{12,16},{16,20},{20,24},{24,28},{1,5},{5,9},{9,... | collective-permute-start | bytes 786440 | tf_op jit(solution)/shard_map/ppermute | solution.py:479
  4.5 1.3 %collective-permute-start.6 = (f32[8,64,128]{2,1,0:T(8,128)S(1)}, f32[8,64,128]{2,1,0:T(8,128)S(1)}, u32[]{:S(2)}, u32[]{:S(2)}) collective-permute-start(f32[8,64,128]{2,1,0:T(8,128)S(1)} %get-tuple-element.92), channel_id=1, source_target_pairs={{4,0},{8,4},{12,8},{16,12},{20,16},{24,20},{28,24},{5,1},{9,5},{13... | collective-permute-start | bytes 786440 | tf_op jit(solution)/shard_map/ppermute | solution.py:480
  5.8 0.0 copy-start.6
  5.9 4.6 %to_lines.1 = (f32[64,64,128]{2,1,0:T(8,128)S(1)}, f32[64,64,128]{2,1,0:T(8,128)S(1)}) custom-call(f32[4096,128]{1,0:T(8,128)} %bitcast.6, f32[4096,128]{1,0:T(8,128)} %bitcast.7), custom_call_target="tpu_custom_call" | custom-call | tf_op jit(solution)/shard_map/to_lines/pallas_call | solution.py:99
  10.5 0.1 pad_add_fusion.index_ref
  10.6 6.7 %evolve.1 = (f32[16,64,128]{2,1,0:T(8,128)}, f32[16,64,128]{2,1,0:T(8,128)}, f32[16,64,128]{2,1,0:T(8,128)}, f32[16,64,128]{2,1,0:T(8,128)}) custom-call(s32[7]{0:T(128)S(1)} %pad_add_fusion.index_ref, f32[64,64,128]{2,1,0:T(8,128)S(1)} %get-tuple-element.96.disp_ref, f32[64,64,128]{2,1,0:T(8,128)S(1)} %get-tuple-element.97.vel_ref, ...), custom_call_target="tpu_custom_call" | custom-call | tf_op jit(solution)/shard_map/evolve/pallas_call | solution.py:158
  17.3 2.5 %collective-permute-start.7 = (f32[16,64,128]{2,1,0:T(8,128)}, f32[16,64,128]{2,1,0:T(8,128)S(1)}, u32[]{:S(2)}, u32[]{:S(2)}) collective-permute-start(f32[16,64,128]{2,1,0:T(8,128)} %get-tuple-element.111), channel_id=1, source_target_pairs={{0,1},{1,0},{2,3},{3,2},{4,5},{5,4},{6,7},{7,6},{8,9},{9,8},{10,11... | collective-permute-start | bytes 1572872 | tf_op jit(solution)/shard_map/ppermute | solution.py:54
  19.7 2.6 %collective-permute-start.8 = (f32[16,64,128]{2,1,0:T(8,128)}, f32[16,64,128]{2,1,0:T(8,128)S(1)}, u32[]{:S(2)}, u32[]{:S(2)}) collective-permute-start(f32[16,64,128]{2,1,0:T(8,128)} %get-tuple-element.112), channel_id=1, source_target_pairs={{0,2},{1,3},{2,0},{3,1},{4,6},{5,7},{6,4},{7,5},{8,10},{9,11},{10,... | collective-permute-start | bytes 1572872 | tf_op jit(solution)/shard_map/ppermute | solution.py:54
  22.3 0.7 broadcast_in_dim.3
  23.0 39.6 %while.18 = (s32[]{:T(128)}, s32[7]{0:T(128)S(1)}, f32[64,512]{1,0:T(8,128)}, bf16[2048,512]{1,0:T(8,128)(2,1)}, bf16[2048,512]{1,0:T(8,128)(2,1)}, /*index=5*/f...) while((s32[]{:T(128)}, s32[7]{0:T(128)S(1)}, ...), condition=%wide.region_1.2_spmd, body=%wide.region_0.1_spmd.sunk | while | flops 131088 | bytes 5243237 | solution.py:497
  23.0 10.3 %basis_parts.1 = (f32[256,512]{1,0:T(8,128)S(1)}, f32[256,512]{1,0:T(8,128)S(1)}, bf16[2048,512]{1,0:T(8,128)(2,1)}, bf16[2048,512]{1,0:T(8,128)(2,1)}, f32[2048,512]{1,0:T(8,128)}) custom-call(s32[7]{0:T(128)S(1)} %get-tuple-element.225.index_ref, f32[768,512]{1,0:T(8,128)} %get-tuple-element.241.rot_ref, f32[16,128,512]{2,1,0:T(8,128)} %get-tuple-element.242.basis_ref), custom_call_target="tpu_custom_call" | custom-call | tf_op jit(solution)/shard_map/while/body/basis_parts/pallas_call | solution.py:209
  33.3 2.9 %collective-permute-start = (f32[256,512]{1,0:T(8,128)S(1)}, f32[256,512]{1,0:T(8,128)S(1)}, u32[]{:S(2)}, u32[]{:S(2)}) collective-permute-start(f32[256,512]{1,0:T(8,128)S(1)} %get-tuple-element.204), channel_id=1, source_target_pairs={{0,4},{4,0},{8,12},{12,8},{16,20},{20,16},{24,28},{28,24},{1,5},{5... | collective-permute-start | bytes 1572872 | tf_op jit(solution)/shard_map/while/body/ppermute | solution.py:54
  36.2 1.5 %collective-permute-done.got_ref = f32[256,512]{1,0:T(8,128)S(1)} collective-permute-done((f32[256,512]{1,0:T(8,128)S(1)}, f32[256,512]{1,0:T(8,128)S(1)}, u32[]{:S(2)}, u32[]{:S(2)}) %collective-permute-start) | collective-permute-done | bytes 524320 | tf_op jit(solution)/shard_map/while/body/ppermute | solution.py:54
  37.7 0.6 split.3
  38.3 2.4 %collective-permute-start.2 = (f32[64,512]{1,0:T(8,128)S(1)}, f32[64,512]{1,0:T(8,128)S(1)}, u32[]{:S(2)}, u32[]{:S(2)}) collective-permute-start(f32[64,512]{1,0:T(8,128)S(1)} %get-tuple-element.207), channel_id=1, source_target_pairs={{0,8},{4,12},{8,0},{12,4},{16,24},{20,28},{24,16},{28,20},{1,9},{5... | collective-permute-start | bytes 393224 | tf_op jit(solution)/shard_map/while/body/ppermute | solution.py:54
  40.7 0.9 collective-permute-start.1
  41.6 3.1 %collective-permute-done.2 = f32[64,512]{1,0:T(8,128)S(1)} collective-permute-done((f32[64,512]{1,0:T(8,128)S(1)}, f32[64,512]{1,0:T(8,128)S(1)}, u32[]{:S(2)}, u32[]{:S(2)}) %collective-permute-start.2) | collective-permute-done | bytes 131104 | tf_op jit(solution)/shard_map/while/body/ppermute | solution.py:54
  44.7 1.8 %collective-permute-start.3 = (f32[64,512]{1,0:T(8,128)S(1)}, f32[64,512]{1,0:T(8,128)S(1)}, u32[]{:S(2)}, u32[]{:S(2)}) collective-permute-start(f32[64,512]{1,0:T(8,128)S(1)} %get-tuple-element.208), channel_id=1, source_target_pairs={{0,24},{4,28},{8,16},{12,20},{16,8},{20,12},{24,0},{28,4},{1,25},{... | collective-permute-start | bytes 393224 | tf_op jit(solution)/shard_map/while/body/ppermute | solution.py:54
  46.6 4.3 %collective-permute-done.3 = f32[64,512]{1,0:T(8,128)S(1)} collective-permute-done((f32[64,512]{1,0:T(8,128)S(1)}, f32[64,512]{1,0:T(8,128)S(1)}, u32[]{:S(2)}, u32[]{:S(2)}) %collective-permute-start.3) | collective-permute-done | bytes 131104 | tf_op jit(solution)/shard_map/while/body/ppermute | solution.py:54
  50.9 0.7 collective-permute-start.4
  51.6 10.3 %collective-permute-done.4 = f32[64,512]{1,0:T(8,128)S(1)} collective-permute-done((f32[64,512]{1,0:T(8,128)S(1)}, f32[64,512]{1,0:T(8,128)S(1)}, u32[]{:S(2)}, u32[]{:S(2)}) %collective-permute-start.4) | collective-permute-done | bytes 131104 | tf_op jit(solution)/shard_map/while/body/ppermute | solution.py:54
  61.9 0.7 add.83
  62.6 4.8 %products.1 = (f32[128,768]{1,0:T(8,128)S(1)}, f32[128,768]{1,0:T(8,128)S(1)}) custom-call(s32[7]{0:T(128)S(1)} %get-tuple-element.108.index_ref, bf16[2048,512]{1,0:T(8,128)(2,1)} %get-tuple-element.109.high_ref.high_hbm, bf16[2048,512]{1,0:T(8,128)(2,1)} %get-tuple-element.110.low_ref.low_hbm, f32[16,64,128]{2,1,0:T(8,128)S(1)} %collective-permute-done.7.rest_0_, ...), custom_call_target="tpu_custom_call" | custom-call | tf_op jit(solution)/shard_map/products/pallas_call | solution.py:257
  67.5 0.1 collective-permute-start.10
  67.6 1.7 %collective-permute-done.10.got_ref = f32[128,768]{1,0:T(8,128)S(1)} collective-permute-done((f32[128,768]{1,0:T(8,128)S(1)}, f32[128,768]{1,0:T(8,128)S(1)}, u32[]{:S(2)}, u32[]{:S(2)}) %collective-permute-start.10) | collective-permute-done | bytes 393248 | tf_op jit(solution)/shard_map/ppermute | solution.py:54
  69.2 0.6 split.2
  69.8 3.2 %collective-permute-start.11 = (f32[32,768]{1,0:T(8,128)S(1)}, f32[32,768]{1,0:T(8,128)S(1)}, u32[]{:S(2)}, u32[]{:S(2)}) collective-permute-start(f32[32,768]{1,0:T(8,128)S(1)} %get-tuple-element.118), channel_id=1, source_target_pairs={{0,8},{4,12},{8,0},{12,4},{16,24},{20,28},{24,16},{28,20},{1,9},{5... | collective-permute-start | bytes 294920 | tf_op jit(solution)/shard_map/ppermute | solution.py:54
  73.0 0.3 collective-permute-start.12
  73.3 1.4 %collective-permute-start.13 = (f32[32,768]{1,0:T(8,128)S(1)}, f32[32,768]{1,0:T(8,128)S(1)}, u32[]{:S(2)}, u32[]{:S(2)}) collective-permute-start(f32[32,768]{1,0:T(8,128)S(1)} %get-tuple-element.120), channel_id=1, source_target_pairs={{0,24},{4,28},{8,16},{12,20},{16,8},{20,12},{24,0},{28,4},{1,25},{... | collective-permute-start | bytes 294920 | tf_op jit(solution)/shard_map/ppermute | solution.py:54
  74.7 8.6 %collective-permute-start.14 = (f32[64,512]{1,0:T(8,128)S(1)}, f32[64,512]{1,0:T(8,128)S(1)}, u32[]{:S(2)}, u32[]{:S(2)}) collective-permute-start(f32[64,512]{1,0:T(8,128)S(1)} %copy-done.5), channel_id=1, source_target_pairs={{0,2},{1,3},{2,0},{3,1},{4,6},{5,7},{6,4},{7,5},{8,10},{9,11},{10,... | collective-permute-start | bytes 393224 | tf_op jit(solution)/shard_map/ppermute | solution.py:54
  83.3 6.3 %collective-permute-done.14 = f32[64,512]{1,0:T(8,128)S(1)} collective-permute-done((f32[64,512]{1,0:T(8,128)S(1)}, f32[64,512]{1,0:T(8,128)S(1)}, u32[]{:S(2)}, u32[]{:S(2)}) %collective-permute-start.14) | collective-permute-done | bytes 131104 | tf_op jit(solution)/shard_map/ppermute | solution.py:54
  89.7 1.1 collective-permute-start.17
  90.8 3.3 %collective-permute-start.15 = (f32[32,768]{1,0:T(8,128)S(1)}, f32[32,768]{1,0:T(8,128)S(1)}, u32[]{:S(2)}, u32[]{:S(2)}) collective-permute-start(f32[32,768]{1,0:T(8,128)S(1)} %add_add_fusion.2), channel_id=1, source_target_pairs={{0,1},{1,0},{2,3},{3,2},{4,5},{5,4},{6,7},{7,6},{8,9},{9,8},{10,11... | collective-permute-start | bytes 294920 | tf_op jit(solution)/shard_map/ppermute | solution.py:54
  94.1 1.6 %collective-permute-start.24 = (f32[64,512]{1,0:T(8,128)S(1)}, f32[64,512]{1,0:T(8,128)S(1)}, u32[]{:S(2)}, u32[]{:S(2)}) collective-permute-start(f32[64,512]{1,0:T(8,128)S(1)} %add.55), channel_id=1, source_target_pairs={{0,24},{4,28},{8,16},{12,20},{16,8},{20,12},{24,0},{28,4},{1,25},{... | collective-permute-start | bytes 393224 | tf_op jit(solution)/shard_map/ppermute | solution.py:54
  95.7 1.9 %collective-permute-start.23 = (f32[64,512]{1,0:T(8,128)S(1)}, f32[64,512]{1,0:T(8,128)S(1)}, u32[]{:S(2)}, u32[]{:S(2)}) collective-permute-start(f32[64,512]{1,0:T(8,128)S(1)} %add.55), channel_id=1, source_target_pairs={{0,16},{4,20},{8,24},{12,28},{16,0},{20,4},{24,8},{28,12},{1,17},{... | collective-permute-start | bytes 393224 | tf_op jit(solution)/shard_map/ppermute | solution.py:54
  97.6 1.3 %collective-permute-start.22 = (f32[64,512]{1,0:T(8,128)S(1)}, f32[64,512]{1,0:T(8,128)S(1)}, u32[]{:S(2)}, u32[]{:S(2)}) collective-permute-start(f32[64,512]{1,0:T(8,128)S(1)} %add.55), channel_id=1, source_target_pairs={{0,8},{4,12},{8,0},{12,4},{16,24},{20,28},{24,16},{28,20},{1,9},{5... | collective-permute-start | bytes 393224 | tf_op jit(solution)/shard_map/ppermute | solution.py:54
  98.9 1.5 %collective-permute-start.20 = (f32[32,768]{1,0:T(8,128)S(1)}, f32[32,768]{1,0:T(8,128)S(1)}, u32[]{:S(2)}, u32[]{:S(2)}) collective-permute-start(f32[32,768]{1,0:T(8,128)S(1)} %add_add_fusion.1), channel_id=1, source_target_pairs={{0,24},{4,28},{8,16},{12,20},{16,8},{20,12},{24,0},{28,4},{1,25},{... | collective-permute-start | bytes 294920 | tf_op jit(solution)/shard_map/ppermute | solution.py:54
  100.4 1.6 %collective-permute-start.19 = (f32[32,768]{1,0:T(8,128)S(1)}, f32[32,768]{1,0:T(8,128)S(1)}, u32[]{:S(2)}, u32[]{:S(2)}) collective-permute-start(f32[32,768]{1,0:T(8,128)S(1)} %add_add_fusion.1), channel_id=1, source_target_pairs={{0,16},{4,20},{8,24},{12,28},{16,0},{20,4},{24,8},{28,12},{1,17},{... | collective-permute-start | bytes 294920 | tf_op jit(solution)/shard_map/ppermute | solution.py:54
  102.0 0.5 collective-permute-start.18
  102.5 1.6 %collective-permute-done.23 = f32[64,512]{1,0:T(8,128)S(1)} collective-permute-done((f32[64,512]{1,0:T(8,128)S(1)}, f32[64,512]{1,0:T(8,128)S(1)}, u32[]{:S(2)}, u32[]{:S(2)}) %collective-permute-start.23) | collective-permute-done | bytes 131104 | tf_op jit(solution)/shard_map/ppermute | solution.py:54
  104.2 0.1 collective-permute-start.25
  104.3 1.2 collective-permute-done.20
  105.5 0.4 collective-permute-done.19
  105.9 0.9 collective-permute-done.18
  106.8 0.1 collective-permute-start.21
  106.9 1.7 %collective-permute-done.21.sums2_ref = f32[128,768]{1,0:T(8,128)S(1)} collective-permute-done((f32[128,768]{1,0:T(8,128)S(1)}, f32[128,768]{1,0:T(8,128)S(1)}, u32[]{:S(2)}, u32[]{:S(2)}) %collective-permute-start.21) | collective-permute-done | bytes 393248 | tf_op jit(solution)/shard_map/ppermute | solution.py:54
  108.6 17.1 %solve.1 = (f32[16,128,512]{2,1,0:T(8,128)}, f32[512,256]{1,0:T(8,128)}) custom-call(s32[7]{0:T(128)S(1)} %pad_add_fusion.index_ref, f32[128,768]{1,0:T(8,128)S(1)} %pad_maximum_fusion.1.sums_ref, f32[128,768]{1,0:T(8,128)S(1)} %collective-permute-done.21.sums2_ref, f32[256,512]{1,0:T(8,128)S(1)} %pad_maximum_fusion.gram_ref, ...), custom_call_target="tpu_custom_call" | custom-call | tf_op jit(solution)/shard_map/solve/pallas_call | solution.py:447
  (39 shorter events, 0.3 us)
Async XLA Ops:
  2.1 8.4 %collective-permute-start.5 = (f32[8,64,128]{2,1,0:T(8,128)S(1)}, f32[8,64,128]{2,1,0:T(8,128)S(1)}, u32[]{:S(2)}, u32[]{:S(2)}) collective-permute-start(f32[8,64,128]{2,1,0:T(8,128)S(1)} %get-tuple-element.91), channel_id=1, source_target_pairs={{0,4},{4,8},{8,12},{12,16},{16,20},{20,24},{24,28},{1,5},{5,9},{9,... | collective-permute-start | bytes 786440 | tf_op jit(solution)/shard_map/ppermute | solution.py:479
  4.5 6.1 %collective-permute-start.6 = (f32[8,64,128]{2,1,0:T(8,128)S(1)}, f32[8,64,128]{2,1,0:T(8,128)S(1)}, u32[]{:S(2)}, u32[]{:S(2)}) collective-permute-start(f32[8,64,128]{2,1,0:T(8,128)S(1)} %get-tuple-element.92), channel_id=1, source_target_pairs={{4,0},{8,4},{12,8},{16,12},{20,16},{24,20},{28,24},{5,1},{9,5},{13... | collective-permute-start | bytes 786440 | tf_op jit(solution)/shard_map/ppermute | solution.py:480
  5.8 4.6 %copy-start.6 = (s32[4]{0:T(128)S(1)}, s32[4]{0:T(128)}, u32[]{:S(2)}) copy-start(s32[4]{0:T(128)} %constant.45.clone) | copy-start | bytes 52
  5.9 4.7 %copy-start.1 = (f32[64,128]{1,0:T(8,128)S(1)}, f32[64,128]{1,0:T(8,128)}, u32[]{:S(2)}) copy-start(f32[64,128]{1,0:T(8,128)} %stiff_ref.3) | copy-start | bytes 98308
  17.3 45.3 %collective-permute-start.7 = (f32[16,64,128]{2,1,0:T(8,128)}, f32[16,64,128]{2,1,0:T(8,128)S(1)}, u32[]{:S(2)}, u32[]{:S(2)}) collective-permute-start(f32[16,64,128]{2,1,0:T(8,128)} %get-tuple-element.111), channel_id=1, source_target_pairs={{0,1},{1,0},{2,3},{3,2},{4,5},{5,4},{6,7},{7,6},{8,9},{9,8},{10,11... | collective-permute-start | bytes 1572872 | tf_op jit(solution)/shard_map/ppermute | solution.py:54
  19.7 42.8 %collective-permute-start.8 = (f32[16,64,128]{2,1,0:T(8,128)}, f32[16,64,128]{2,1,0:T(8,128)S(1)}, u32[]{:S(2)}, u32[]{:S(2)}) collective-permute-start(f32[16,64,128]{2,1,0:T(8,128)} %get-tuple-element.112), channel_id=1, source_target_pairs={{0,2},{1,3},{2,0},{3,1},{4,6},{5,7},{6,4},{7,5},{8,10},{9,11},{10,... | collective-permute-start | bytes 1572872 | tf_op jit(solution)/shard_map/ppermute | solution.py:54
  22.3 40.2 %collective-permute-start.9 = (f32[16,64,128]{2,1,0:T(8,128)}, f32[16,64,128]{2,1,0:T(8,128)S(1)}, u32[]{:S(2)}, u32[]{:S(2)}) collective-permute-start(f32[16,64,128]{2,1,0:T(8,128)} %get-tuple-element.113), channel_id=1, source_target_pairs={{0,3},{1,2},{2,1},{3,0},{4,7},{5,6},{6,5},{7,4},{8,11},{9,10},{10,... | collective-permute-start | bytes 1572872 | tf_op jit(solution)/shard_map/ppermute | solution.py:54
  23.0 39.6 %copy-start = (f32[16,64,128]{2,1,0:T(8,128)S(1)}, f32[16,64,128]{2,1,0:T(8,128)}, u32[]{:S(2)}) copy-start(f32[16,64,128]{2,1,0:T(8,128)} %get-tuple-element.114.rest_3_) | copy-start | bytes 1572868
  33.3 4.4 %collective-permute-start = (f32[256,512]{1,0:T(8,128)S(1)}, f32[256,512]{1,0:T(8,128)S(1)}, u32[]{:S(2)}, u32[]{:S(2)}) collective-permute-start(f32[256,512]{1,0:T(8,128)S(1)} %get-tuple-element.204), channel_id=1, source_target_pairs={{0,4},{4,0},{8,12},{12,8},{16,20},{20,16},{24,28},{28,24},{1,5},{5... | collective-permute-start | bytes 1572872 | tf_op jit(solution)/shard_map/while/body/ppermute | solution.py:54
  38.3 6.4 %collective-permute-start.2 = (f32[64,512]{1,0:T(8,128)S(1)}, f32[64,512]{1,0:T(8,128)S(1)}, u32[]{:S(2)}, u32[]{:S(2)}) collective-permute-start(f32[64,512]{1,0:T(8,128)S(1)} %get-tuple-element.207), channel_id=1, source_target_pairs={{0,8},{4,12},{8,0},{12,4},{16,24},{20,28},{24,16},{28,20},{1,9},{5... | collective-permute-start | bytes 393224 | tf_op jit(solution)/shard_map/while/body/ppermute | solution.py:54
  40.7 5.9 %collective-permute-start.1 = (f32[64,512]{1,0:T(8,128)S(1)}, f32[64,512]{1,0:T(8,128)S(1)}, u32[]{:S(2)}, u32[]{:S(2)}) collective-permute-start(f32[64,512]{1,0:T(8,128)S(1)} %get-tuple-element.205), channel_id=1, source_target_pairs={{0,16},{4,20},{8,24},{12,28},{16,0},{20,4},{24,8},{28,12},{1,17},{... | collective-permute-start | bytes 393224 | tf_op jit(solution)/shard_map/while/body/ppermute | solution.py:54
  44.7 6.1 %collective-permute-start.3 = (f32[64,512]{1,0:T(8,128)S(1)}, f32[64,512]{1,0:T(8,128)S(1)}, u32[]{:S(2)}, u32[]{:S(2)}) collective-permute-start(f32[64,512]{1,0:T(8,128)S(1)} %get-tuple-element.208), channel_id=1, source_target_pairs={{0,24},{4,28},{8,16},{12,20},{16,8},{20,12},{24,0},{28,4},{1,25},{... | collective-permute-start | bytes 393224 | tf_op jit(solution)/shard_map/while/body/ppermute | solution.py:54
  50.9 11.0 %collective-permute-start.4 = (f32[64,512]{1,0:T(8,128)S(1)}, f32[64,512]{1,0:T(8,128)S(1)}, u32[]{:S(2)}, u32[]{:S(2)}) collective-permute-start(f32[64,512]{1,0:T(8,128)S(1)} %add_add_fusion.4), channel_id=1, source_target_pairs={{0,1},{1,0},{2,3},{3,2},{4,5},{5,4},{6,7},{7,6},{8,9},{9,8},{10,11... | collective-permute-start | bytes 393224 | tf_op jit(solution)/shard_map/while/body/ppermute | solution.py:54
  62.6 12.1 %copy-start.5 = (f32[64,512]{1,0:T(8,128)S(1)}, f32[64,512]{1,0:T(8,128)}, u32[]{:S(2)}) copy-start(f32[64,512]{1,0:T(8,128)} %get-tuple-element.123) | copy-start | bytes 393220
  62.6 46.0 %copy-start.4 = (bf16[2048,512]{1,0:T(8,128)(2,1)S(1)}, bf16[2048,512]{1,0:T(8,128)(2,1)}, u32[]{:S(2)}) copy-start(bf16[2048,512]{1,0:T(8,128)(2,1)} %get-tuple-element.110.low_ref.low_hbm) | copy-start | bytes 6291460
  67.4 41.2 %copy-start.2 = (f32[768,512]{1,0:T(8,128)S(1)}, f32[768,512]{1,0:T(8,128)}, u32[]{:S(2)}) copy-start(f32[768,512]{1,0:T(8,128)} %get-tuple-element.265) | copy-start | bytes 4718596
  67.4 41.2 %copy-start.3 = (bf16[2048,512]{1,0:T(8,128)(2,1)S(1)}, bf16[2048,512]{1,0:T(8,128)(2,1)}, u32[]{:S(2)}) copy-start(bf16[2048,512]{1,0:T(8,128)(2,1)} %get-tuple-element.109.high_ref.high_hbm) | copy-start | bytes 6291460
  67.5 1.8 %collective-permute-start.10 = (f32[128,768]{1,0:T(8,128)S(1)}, f32[128,768]{1,0:T(8,128)S(1)}, u32[]{:S(2)}, u32[]{:S(2)}) collective-permute-start(f32[128,768]{1,0:T(8,128)S(1)} %get-tuple-element.116), channel_id=1, source_target_pairs={{0,4},{4,0},{8,12},{12,8},{16,20},{20,16},{24,28},{28,24},{1,5},{5... | collective-permute-start | bytes 1179656 | tf_op jit(solution)/shard_map/ppermute | solution.py:54
  69.8 13.5 %collective-permute-start.11 = (f32[32,768]{1,0:T(8,128)S(1)}, f32[32,768]{1,0:T(8,128)S(1)}, u32[]{:S(2)}, u32[]{:S(2)}) collective-permute-start(f32[32,768]{1,0:T(8,128)S(1)} %get-tuple-element.118), channel_id=1, source_target_pairs={{0,8},{4,12},{8,0},{12,4},{16,24},{20,28},{24,16},{28,20},{1,9},{5... | collective-permute-start | bytes 294920 | tf_op jit(solution)/shard_map/ppermute | solution.py:54
  73.0 10.3 %collective-permute-start.12 = (f32[32,768]{1,0:T(8,128)S(1)}, f32[32,768]{1,0:T(8,128)S(1)}, u32[]{:S(2)}, u32[]{:S(2)}) collective-permute-start(f32[32,768]{1,0:T(8,128)S(1)} %get-tuple-element.119), channel_id=1, source_target_pairs={{0,16},{4,20},{8,24},{12,28},{16,0},{20,4},{24,8},{28,12},{1,17},{... | collective-permute-start | bytes 294920 | tf_op jit(solution)/shard_map/ppermute | solution.py:54
  73.3 10.0 %collective-permute-start.13 = (f32[32,768]{1,0:T(8,128)S(1)}, f32[32,768]{1,0:T(8,128)S(1)}, u32[]{:S(2)}, u32[]{:S(2)}) collective-permute-start(f32[32,768]{1,0:T(8,128)S(1)} %get-tuple-element.120), channel_id=1, source_target_pairs={{0,24},{4,28},{8,16},{12,20},{16,8},{20,12},{24,0},{28,4},{1,25},{... | collective-permute-start | bytes 294920 | tf_op jit(solution)/shard_map/ppermute | solution.py:54
  74.7 15.0 %collective-permute-start.14 = (f32[64,512]{1,0:T(8,128)S(1)}, f32[64,512]{1,0:T(8,128)S(1)}, u32[]{:S(2)}, u32[]{:S(2)}) collective-permute-start(f32[64,512]{1,0:T(8,128)S(1)} %copy-done.5), channel_id=1, source_target_pairs={{0,2},{1,3},{2,0},{3,1},{4,6},{5,7},{6,4},{7,5},{8,10},{9,11},{10,... | collective-permute-start | bytes 393224 | tf_op jit(solution)/shard_map/ppermute | solution.py:54
  89.7 7.9 %collective-permute-start.17 = (f32[32,768]{1,0:T(8,128)S(1)}, f32[32,768]{1,0:T(8,128)S(1)}, u32[]{:S(2)}, u32[]{:S(2)}) collective-permute-start(f32[32,768]{1,0:T(8,128)S(1)} %add_add_fusion.2), channel_id=1, source_target_pairs={{0,3},{1,2},{2,1},{3,0},{4,7},{5,6},{6,5},{7,4},{8,11},{9,10},{10,... | collective-permute-start | bytes 294920 | tf_op jit(solution)/shard_map/ppermute | solution.py:54
  90.8 8.1 %collective-permute-start.16 = (f32[32,768]{1,0:T(8,128)S(1)}, f32[32,768]{1,0:T(8,128)S(1)}, u32[]{:S(2)}, u32[]{:S(2)}) collective-permute-start(f32[32,768]{1,0:T(8,128)S(1)} %add_add_fusion.2), channel_id=1, source_target_pairs={{0,2},{1,3},{2,0},{3,1},{4,6},{5,7},{6,4},{7,5},{8,10},{9,11},{10,... | collective-permute-start | bytes 294920 | tf_op jit(solution)/shard_map/ppermute | solution.py:54
  90.8 8.1 %collective-permute-start.15 = (f32[32,768]{1,0:T(8,128)S(1)}, f32[32,768]{1,0:T(8,128)S(1)}, u32[]{:S(2)}, u32[]{:S(2)}) collective-permute-start(f32[32,768]{1,0:T(8,128)S(1)} %add_add_fusion.2), channel_id=1, source_target_pairs={{0,1},{1,0},{2,3},{3,2},{4,5},{5,4},{6,7},{7,6},{8,9},{9,8},{10,11... | collective-permute-start | bytes 294920 | tf_op jit(solution)/shard_map/ppermute | solution.py:54
  94.1 8.0 %collective-permute-start.24 = (f32[64,512]{1,0:T(8,128)S(1)}, f32[64,512]{1,0:T(8,128)S(1)}, u32[]{:S(2)}, u32[]{:S(2)}) collective-permute-start(f32[64,512]{1,0:T(8,128)S(1)} %add.55), channel_id=1, source_target_pairs={{0,24},{4,28},{8,16},{12,20},{16,8},{20,12},{24,0},{28,4},{1,25},{... | collective-permute-start | bytes 393224 | tf_op jit(solution)/shard_map/ppermute | solution.py:54
  95.7 8.4 %collective-permute-start.23 = (f32[64,512]{1,0:T(8,128)S(1)}, f32[64,512]{1,0:T(8,128)S(1)}, u32[]{:S(2)}, u32[]{:S(2)}) collective-permute-start(f32[64,512]{1,0:T(8,128)S(1)} %add.55), channel_id=1, source_target_pairs={{0,16},{4,20},{8,24},{12,28},{16,0},{20,4},{24,8},{28,12},{1,17},{... | collective-permute-start | bytes 393224 | tf_op jit(solution)/shard_map/ppermute | solution.py:54
  97.6 6.5 %collective-permute-start.22 = (f32[64,512]{1,0:T(8,128)S(1)}, f32[64,512]{1,0:T(8,128)S(1)}, u32[]{:S(2)}, u32[]{:S(2)}) collective-permute-start(f32[64,512]{1,0:T(8,128)S(1)} %add.55), channel_id=1, source_target_pairs={{0,8},{4,12},{8,0},{12,4},{16,24},{20,28},{24,16},{28,20},{1,9},{5... | collective-permute-start | bytes 393224 | tf_op jit(solution)/shard_map/ppermute | solution.py:54
  98.9 6.5 %collective-permute-start.20 = (f32[32,768]{1,0:T(8,128)S(1)}, f32[32,768]{1,0:T(8,128)S(1)}, u32[]{:S(2)}, u32[]{:S(2)}) collective-permute-start(f32[32,768]{1,0:T(8,128)S(1)} %add_add_fusion.1), channel_id=1, source_target_pairs={{0,24},{4,28},{8,16},{12,20},{16,8},{20,12},{24,0},{28,4},{1,25},{... | collective-permute-start | bytes 294920 | tf_op jit(solution)/shard_map/ppermute | solution.py:54
  100.4 5.5 %collective-permute-start.19 = (f32[32,768]{1,0:T(8,128)S(1)}, f32[32,768]{1,0:T(8,128)S(1)}, u32[]{:S(2)}, u32[]{:S(2)}) collective-permute-start(f32[32,768]{1,0:T(8,128)S(1)} %add_add_fusion.1), channel_id=1, source_target_pairs={{0,16},{4,20},{8,24},{12,28},{16,0},{20,4},{24,8},{28,12},{1,17},{... | collective-permute-start | bytes 294920 | tf_op jit(solution)/shard_map/ppermute | solution.py:54
  102.0 4.8 %collective-permute-start.18 = (f32[32,768]{1,0:T(8,128)S(1)}, f32[32,768]{1,0:T(8,128)S(1)}, u32[]{:S(2)}, u32[]{:S(2)}) collective-permute-start(f32[32,768]{1,0:T(8,128)S(1)} %add_add_fusion.1), channel_id=1, source_target_pairs={{0,8},{4,12},{8,0},{12,4},{16,24},{20,28},{24,16},{28,20},{1,9},{5... | collective-permute-start | bytes 294920 | tf_op jit(solution)/shard_map/ppermute | solution.py:54
  104.2 4.4 %collective-permute-start.25 = (f32[256,512]{1,0:T(8,128)S(1)}, f32[256,512]{1,0:T(8,128)S(1)}, u32[]{:S(2)}, u32[]{:S(2)}) collective-permute-start(f32[256,512]{1,0:T(8,128)S(1)} %pad_maximum_fusion.gram_ref), channel_id=1, source_target_pairs={{0,4},{4,0},{8,12},{12,8},{16,20},{20,16},{24,28},{28,24},{1,5},{5... | collective-permute-start | bytes 1572872 | tf_op jit(solution)/shard_map/ppermute | solution.py:54
  106.8 1.8 %collective-permute-start.21 = (f32[128,768]{1,0:T(8,128)S(1)}, f32[128,768]{1,0:T(8,128)S(1)}, u32[]{:S(2)}, u32[]{:S(2)}) collective-permute-start(f32[128,768]{1,0:T(8,128)S(1)} %pad_maximum_fusion.1.sums_ref), channel_id=1, source_target_pairs={{0,4},{4,0},{8,12},{12,8},{16,20},{20,16},{24,28},{28,24},{1,5},{5... | collective-permute-start | bytes 1179656 | tf_op jit(solution)/shard_map/ppermute | solution.py:54
